TPU v7x, 32 devices: a whole 2x2x4 slice. The times are simulated.
32 devices in a mesh: bucket: 4 (over y, x), dp: 8 (over z, core).
Axes of the slice: x: 2, y: 2, z: 4, core: 2. Of those that a mesh axis runs over, the one named last changes fastest.
Arguments:
- token_ids: int32 [32, 1024], P(('bucket', 'dp')), may hold values from 0 to 11263
- segment_ids: int32 [32, 1024], P(('bucket', 'dp')), may hold values from 0 to 17, as said below
- live: int32 [32, 1024], P(('bucket', 'dp')), may hold values from 0 to 1, as said below
- timesteps: int32 [32, 1024], P(('bucket', 'dp')), may hold values from 0 to 1999, as said below
- noise: float32 [32, 1024, 128], P(('bucket', 'dp')), may hold values from -6 to 6
- embedding: float32 [11264, 128], P(('bucket', 'dp')), may hold values from -0.8 to 0.8
- embedding_moment: float32 [11264, 128], P(('bucket', 'dp')), may hold values from -2.1632466e-06 to 2.1632466e-06
- embedding_second: float32 [11264, 128], P(('bucket', 'dp')), may hold values from 1.1280114e-12 to 1.8048183e-11
- up_weight: float32 [128, 768], P(None, ('bucket', 'dp')), may hold values from -0.5 to 0.5
- up_moment: float32 [128, 768], P(None, ('bucket', 'dp')), may hold values from -2.1632466e-06 to 2.1632466e-06
- up_second: float32 [128, 768], P(None, ('bucket', 'dp')), may hold values from 1.1280114e-12 to 1.8048183e-11
- time_weight: float32 [768, 768], P(None, ('bucket', 'dp')), may hold values from -0.21875 to 0.21875
- time_moment: float32 [768, 768], P(None, ('bucket', 'dp')), may hold values from -2.1632466e-06 to 2.1632466e-06
- time_second: float32 [768, 768], P(None, ('bucket', 'dp')), may hold values from 1.1280114e-12 to 1.8048183e-11
- qkv_weight: float32 [768, 2304], P(('bucket', 'dp')), may hold values from -0.21875 to 0.21875
- qkv_moment: float32 [768, 2304], P(('bucket', 'dp')), may hold values from -2.1632466e-06 to 2.1632466e-06
- qkv_second: float32 [768, 2304], P(('bucket', 'dp')), may hold values from 1.1280114e-12 to 1.8048183e-11
- out_weight: float32 [768, 768], P(None, ('bucket', 'dp')), may hold values from -0.875 to 0.875
- out_moment: float32 [768, 768], P(None, ('bucket', 'dp')), may hold values from -2.1632466e-06 to 2.1632466e-06
- out_second: float32 [768, 768], P(None, ('bucket', 'dp')), may hold values from 1.1280114e-12 to 1.8048183e-11
- fc_weight: float32 [768, 3072], P(('bucket', 'dp')), may hold values from -0.21875 to 0.21875
- fc_moment: float32 [768, 3072], P(('bucket', 'dp')), may hold values from -2.1632466e-06 to 2.1632466e-06
- fc_second: float32 [768, 3072], P(('bucket', 'dp')), may hold values from 1.1280114e-12 to 1.8048183e-11
- proj_weight: float32 [3072, 768], P(None, ('bucket', 'dp')), may hold values from -0.109375 to 0.109375
- proj_moment: float32 [3072, 768], P(None, ('bucket', 'dp')), may hold values from -2.1632466e-06 to 2.1632466e-06
- proj_second: float32 [3072, 768], P(None, ('bucket', 'dp')), may hold values from 1.1280114e-12 to 1.8048183e-11
- down_weight: float32 [768, 128], P(('bucket', 'dp')), may hold values from -0.21875 to 0.21875
- down_moment: float32 [768, 128], P(('bucket', 'dp')), may hold values from -2.1632466e-06 to 2.1632466e-06
- down_second: float32 [768, 128], P(('bucket', 'dp')), may hold values from 1.1280114e-12 to 1.8048183e-11
- norm_gains: float32 [3, 768], P(None, ('bucket', 'dp')), may hold values from 0.35 to 2.6
- gains_moment: float32 [3, 768], P(None, ('bucket', 'dp')), may hold values from -2.1632466e-06 to 2.1632466e-06
- gains_second: float32 [3, 768], P(None, ('bucket', 'dp')), may hold values from 1.1280114e-12 to 1.8048183e-11
Outputs:
- loss: float32 [], replicated
- grad_norm: float32 [], replicated
- embedding_moment_new: float32 [11264, 128], P(('bucket', 'dp'))
- embedding_second_new: float32 [11264, 128], P(('bucket', 'dp'))
- embedding_new: float32 [11264, 128], P(('bucket', 'dp'))
- up_moment_new: float32 [128, 768], P(None, ('bucket', 'dp'))
- up_second_new: float32 [128, 768], P(None, ('bucket', 'dp'))
- up_weight_new: float32 [128, 768], P(None, ('bucket', 'dp'))
- time_moment_new: float32 [768, 768], P(None, ('bucket', 'dp'))
- time_second_new: float32 [768, 768], P(None, ('bucket', 'dp'))
- time_weight_new: float32 [768, 768], P(None, ('bucket', 'dp'))
- qkv_moment_new: float32 [768, 2304], P(('bucket', 'dp'))
- qkv_second_new: float32 [768, 2304], P(('bucket', 'dp'))
- qkv_weight_new: float32 [768, 2304], P(('bucket', 'dp'))
- out_moment_new: float32 [768, 768], P(None, ('bucket', 'dp'))
- out_second_new: float32 [768, 768], P(None, ('bucket', 'dp'))
- out_weight_new: float32 [768, 768], P(None, ('bucket', 'dp'))
- fc_moment_new: float32 [768, 3072], P(('bucket', 'dp'))
- fc_second_new: float32 [768, 3072], P(('bucket', 'dp'))
- fc_weight_new: float32 [768, 3072], P(('bucket', 'dp'))
- proj_moment_new: float32 [3072, 768], P(None, ('bucket', 'dp'))
- proj_second_new: float32 [3072, 768], P(None, ('bucket', 'dp'))
- proj_weight_new: float32 [3072, 768], P(None, ('bucket', 'dp'))
- down_moment_new: float32 [768, 128], P(('bucket', 'dp'))
- down_second_new: float32 [768, 128], P(('bucket', 'dp'))
- down_weight_new: float32 [768, 128], P(('bucket', 'dp'))
- gains_moment_new: float32 [3, 768], P(None, ('bucket', 'dp'))
- gains_second_new: float32 [3, 768], P(None, ('bucket', 'dp'))
- norm_gains_new: float32 [3, 768], P(None, ('bucket', 'dp'))
Inputs may be any that keep to these rules, and one draw needn't show every extreme that they name: `segment_ids`: positions of a row that share a number form one item; a row's first item has 64 positions or more, its later items 64 or fewer; padding positions carry 1024 // 64 + 1. `live`: 1 on a row's leading positions, 0 on its padding tail; every row has 64 live positions or more. `timesteps`: equal within an item; rows held by devices whose index along bucket is b have timesteps from b * 500 up to (b+1) * 500 - 1.
All inputs are finite; a program needn't handle non-finite values.
Results may differ from a plain program's by a relative error of at most 0.003.
The roundings to bfloat16 on the way count: a program that leaves them out, or rounds other values in their place, can miss the bound.
Values may be sent and summed in bfloat16 or wider, within the bound.
No kernel may reach another device: no remote copies, remote signals or barrier semaphores. Data moves between devices by JAX's collectives and lax.ppermute only.
A program may use at most 256 MiB of HBM per device.

v0:
```python
import math

import jax
import jax.numpy as jnp
from jax import lax
from jax.sharding import PartitionSpec as P

D = 768
HEAD = 64
EMB = 128
STEPS_T = 2000
ADAM_STEP = 10


NEG_BIG = -1e30
EPS_NORM = 1e-05
BETA_ONE = 0.9
BETA_TWO = 0.95
ADAM_EPS = 1e-08
DECAY_RATE = 0.01
CLIP_NORM = 0.02
RATES = (0.05, 0.05, 0.02, 0.02, 0.02, 0.02, 0.01, 0.02, 0.3)
DECAYS = (DECAY_RATE,) * 8 + (0.0,)
BLOCK_LIMIT = 512


def matmul(left_op, right_op):
    return jnp.dot(left_op, right_op, preferred_element_type=jnp.float32)


def matmul_tn(left_op, right_op):
    return lax.dot_general(
        left_op, right_op, (((0,), (0,)), ((), ())), preferred_element_type=jnp.float32
    )


def matrix_product_transposed(left_op, right_op):
    return lax.dot_general(
        left_op, right_op, (((1,), (1,)), ((), ())), preferred_element_type=jnp.float32
    )


def layer_normalize(hidden, gain_row):
    centre = jnp.mean(hidden, -1, keepdims=True)
    centred = hidden - centre
    spread = jnp.mean(centred * centred, -1, keepdims=True)
    scale_inv = lax.rsqrt(spread + EPS_NORM)
    normed = centred * scale_inv
    return (normed * gain_row, normed, scale_inv)


def norm_back(grad_normed_out, normed, scale_inv, gain_row):
    grad_gain = jnp.sum(grad_normed_out * normed, 0)
    grad_scaled = grad_normed_out * gain_row
    grad_input = scale_inv * (
        grad_scaled
        - jnp.mean(grad_scaled, -1, keepdims=True)
        - normed * jnp.mean(grad_scaled * normed, -1, keepdims=True)
    )
    return (grad_input, grad_gain)


def sinusoid(step_row, model_width):
    half_width = model_width // 2
    freqs = jnp.exp(-math.log(10000.0) * jnp.arange(half_width, dtype=jnp.float32) / half_width)
    angles = step_row.astype(jnp.float32)[:, None] * freqs[None, :]
    return jnp.concatenate([jnp.sin(angles), jnp.cos(angles)], -1)


def block_scores(query_blk, key_heads, seg_blk, segments):
    scores = jnp.einsum(
        "qhd,khd->hqk", query_blk, key_heads, preferred_element_type=jnp.float32
    ) * HEAD ** (-0.5)
    allowed = (seg_blk[:, None] == segments[None, :])[None]
    return jnp.where(allowed, scores, NEG_BIG)


def attention_forward(queries, key_heads, values, segments):
    length = queries.shape[0]
    block_rows = min(BLOCK_LIMIT, length)

    def one_block(block_index):
        row_start = block_index * block_rows
        query_blk = lax.dynamic_slice_in_dim(queries, row_start, block_rows, 0)
        seg_blk = lax.dynamic_slice_in_dim(segments, row_start, block_rows, 0)
        scores = block_scores(query_blk, key_heads, seg_blk, segments)
        row_peak = jnp.max(scores, -1, keepdims=True)
        exp_scores = jnp.exp(scores - row_peak)
        row_total = jnp.sum(exp_scores, -1, keepdims=True)
        probs_low = (exp_scores / row_total).astype(jnp.bfloat16)
        attended = jnp.einsum("hqk,khd->qhd", probs_low, values, preferred_element_type=jnp.float32)
        return (attended, (row_peak + jnp.log(row_total))[..., 0])

    attended, log_sums = lax.map(one_block, jnp.arange(length // block_rows, dtype=jnp.int32))
    return (attended.reshape(length, -1), log_sums)


def attention_backward(queries, key_heads, values, segments, log_sums, grad_attended):
    length = queries.shape[0]
    block_rows = min(BLOCK_LIMIT, length)
    score_scale = HEAD ** (-0.5)

    def one_block(running, block_index):
        grad_keys, grad_values = running
        row_start = block_index * block_rows
        query_blk = lax.dynamic_slice_in_dim(queries, row_start, block_rows, 0)
        seg_blk = lax.dynamic_slice_in_dim(segments, row_start, block_rows, 0)
        grad_blk = lax.dynamic_slice_in_dim(grad_attended, row_start, block_rows, 0)
        scores = block_scores(query_blk, key_heads, seg_blk, segments)
        probs_row = jnp.exp(scores - log_sums[block_index][..., None])
        grad_probs = jnp.einsum(
            "qhd,khd->hqk", grad_blk, values, preferred_element_type=jnp.float32
        )
        row_inner = jnp.sum(probs_row * grad_probs, -1, keepdims=True)
        grad_scores = (probs_row * (grad_probs - row_inner)).astype(jnp.bfloat16)
        grad_values = grad_values + jnp.einsum(
            "hqk,qhd->khd",
            probs_row.astype(jnp.bfloat16),
            grad_blk,
            preferred_element_type=jnp.float32,
        )
        grad_keys = (
            grad_keys
            + jnp.einsum("hqk,qhd->khd", grad_scores, query_blk, preferred_element_type=jnp.float32)
            * score_scale
        )
        grad_query = (
            jnp.einsum("hqk,khd->qhd", grad_scores, key_heads, preferred_element_type=jnp.float32)
            * score_scale
        )
        return ((grad_keys, grad_values), grad_query)

    zero_heads = jnp.zeros(queries.shape, jnp.float32)
    (grad_keys, grad_values), grad_queries = lax.scan(
        one_block, (zero_heads, zero_heads), jnp.arange(length // block_rows, dtype=jnp.int32)
    )
    return (
        grad_queries.reshape(length, -1),
        grad_keys.reshape(length, -1),
        grad_values.reshape(length, -1),
    )


def block_forward(
    hidden_initial,
    segments,
    query_key_value_reduced,
    out_low,
    feedforward_weight_reduced,
    proj_low,
    norm_gain_vector,
):
    length = hidden_initial.shape[0]
    model_width = query_key_value_reduced.shape[0]
    head_count = model_width // HEAD
    normalized_first, centred_scaled_first, inverse_deviation_first = layer_normalize(
        hidden_initial, norm_gain_vector[0]
    )
    normed_one_low = normalized_first.astype(jnp.bfloat16)
    qkv_mixed = matmul(normed_one_low, query_key_value_reduced)
    queries = qkv_mixed[:, :model_width].astype(jnp.bfloat16).reshape(length, head_count, HEAD)
    key_heads = (
        qkv_mixed[:, model_width : 2 * model_width]
        .astype(jnp.bfloat16)
        .reshape(length, head_count, HEAD)
    )
    values = qkv_mixed[:, 2 * model_width :].astype(jnp.bfloat16).reshape(length, head_count, HEAD)
    attended, log_sums = attention_forward(queries, key_heads, values, segments)
    attended_low = attended.astype(jnp.bfloat16)
    hidden_after_first = hidden_initial + matmul(attended_low, out_low)
    normalized_second, centred_scaled_second, inverse_deviation_second = layer_normalize(
        hidden_after_first, norm_gain_vector[1]
    )
    normed_two_low = normalized_second.astype(jnp.bfloat16)
    fc_upper = matmul(normed_two_low, feedforward_weight_reduced)
    active_low = jax.nn.gelu(fc_upper).astype(jnp.bfloat16)
    hidden_after_second = hidden_after_first + matmul(active_low, proj_low)
    saved_acts = (
        centred_scaled_first,
        inverse_deviation_first,
        normed_one_low,
        queries,
        key_heads,
        values,
        log_sums,
        attended_low,
        centred_scaled_second,
        inverse_deviation_second,
        normed_two_low,
        fc_upper,
        active_low,
    )
    return (saved_acts, hidden_after_second)


def block_backward(
    saved_acts,
    grad_two,
    segments,
    query_key_value_reduced,
    out_low,
    feedforward_weight_reduced,
    proj_low,
    norm_gain_vector,
):
    (
        centred_scaled_first,
        inverse_deviation_first,
        normed_one_low,
        queries,
        key_heads,
        values,
        log_sums,
        attended_low,
        centred_scaled_second,
        inverse_deviation_second,
        normed_two_low,
        fc_upper,
        active_low,
    ) = saved_acts
    length, head_count, head_size = queries.shape
    grad_mlp_low = grad_two.astype(jnp.bfloat16)
    grad_proj = matmul_tn(active_low, grad_mlp_low)
    grad_active = matrix_product_transposed(grad_mlp_low, proj_low)
    unused_value, gelu_pull = jax.vjp(jax.nn.gelu, fc_upper)
    (grad_upper,) = gelu_pull(grad_active)
    gradient_upper_reduced = grad_upper.astype(jnp.bfloat16)
    grad_fc = matmul_tn(normed_two_low, gradient_upper_reduced)
    grad_norm_two, grad_gain_two = norm_back(
        matrix_product_transposed(gradient_upper_reduced, feedforward_weight_reduced),
        centred_scaled_second,
        inverse_deviation_second,
        norm_gain_vector[1],
    )
    grad_one = grad_two + grad_norm_two
    grad_branch_low = grad_one.astype(jnp.bfloat16)
    grad_out = matmul_tn(attended_low, grad_branch_low)
    grad_attended = (
        matrix_product_transposed(grad_branch_low, out_low)
        .astype(jnp.bfloat16)
        .reshape(length, head_count, head_size)
    )
    grad_queries, grad_keys, grad_values = attention_backward(
        queries, key_heads, values, segments, log_sums, grad_attended
    )
    gradient_mixed_reduced = jnp.concatenate([grad_queries, grad_keys, grad_values], 1).astype(
        jnp.bfloat16
    )
    grad_qkv = matmul_tn(normed_one_low, gradient_mixed_reduced)
    grad_norm_one, grad_gain_one = norm_back(
        matrix_product_transposed(gradient_mixed_reduced, query_key_value_reduced),
        centred_scaled_first,
        inverse_deviation_first,
        norm_gain_vector[0],
    )
    return (
        grad_one + grad_norm_one,
        (grad_qkv, grad_out, grad_fc, grad_proj, grad_gain_one, grad_gain_two),
    )


def head_pass(pred_low, word_table, tokens, token_weight):
    length = pred_low.shape[0]
    block_rows = min(BLOCK_LIMIT, length)
    vocab_size = word_table.shape[0]

    def one_block(grad_table, block_index):
        row_start = block_index * block_rows
        pred_blk = lax.dynamic_slice_in_dim(pred_low, row_start, block_rows, 0)
        token_blk = lax.dynamic_slice_in_dim(tokens, row_start, block_rows, 0)
        weight_blk = lax.dynamic_slice_in_dim(token_weight, row_start, block_rows, 0)
        logits = matrix_product_transposed(pred_blk, word_table)
        row_peak = jnp.max(logits, -1, keepdims=True)
        log_total = row_peak + jnp.log(jnp.sum(jnp.exp(logits - row_peak), -1, keepdims=True))
        probs_row = jnp.exp(logits - log_total)
        target_hits = jnp.arange(vocab_size, dtype=jnp.int32)[None, :] == token_blk[:, None]
        target = jnp.sum(jnp.where(target_hits, logits, 0.0), -1)
        cross_loss = log_total[:, 0] - target
        grad_logits = (weight_blk[:, None] * (probs_row - target_hits.astype(jnp.float32))).astype(
            jnp.bfloat16
        )
        grad_pred = matmul(grad_logits, word_table)
        return (grad_table + matmul_tn(grad_logits, pred_blk), (cross_loss, grad_pred))

    grad_table, (cross_loss, grad_pred) = lax.scan(
        one_block,
        jnp.zeros(word_table.shape, jnp.float32),
        jnp.arange(length // block_rows, dtype=jnp.int32),
    )
    return (grad_table, cross_loss.reshape(length), grad_pred.reshape(length, -1))


def adam_update(master, moment, second, grad, rate, decay):
    moment_new = BETA_ONE * moment + (1.0 - BETA_ONE) * grad
    second_new = BETA_TWO * second + (1.0 - BETA_TWO) * grad * grad
    moment_hat = moment_new / (1.0 - BETA_ONE**ADAM_STEP)
    second_hat = second_new / (1.0 - BETA_TWO**ADAM_STEP)
    master_new = master - rate * (moment_hat / (jnp.sqrt(second_hat) + ADAM_EPS) + decay * master)
    return [moment_new, second_new, master_new]


def on_device(
    token_ids,
    segment_ids,
    live,
    timesteps,
    noise,
    embedding,
    embedding_moment,
    embedding_second,
    up_weight,
    up_moment,
    up_second,
    time_weight,
    time_moment,
    time_second,
    qkv_weight,
    qkv_moment,
    qkv_second,
    out_weight,
    out_moment,
    out_second,
    fc_weight,
    fc_moment,
    fc_second,
    proj_weight,
    proj_moment,
    proj_second,
    down_weight,
    down_moment,
    down_second,
    norm_gains,
    gains_moment,
    gains_second,
):
    masters = (
        embedding,
        up_weight,
        time_weight,
        qkv_weight,
        out_weight,
        fc_weight,
        proj_weight,
        down_weight,
        norm_gains,
    )
    moments = (
        embedding_moment,
        up_moment,
        time_moment,
        qkv_moment,
        out_moment,
        fc_moment,
        proj_moment,
        down_moment,
        gains_moment,
    )
    seconds = (
        embedding_second,
        up_second,
        time_second,
        qkv_second,
        out_second,
        fc_second,
        proj_second,
        down_second,
        gains_second,
    )
    lowered = [member.astype(jnp.bfloat16) for member in masters]
    gathered = (
        lax.all_gather(lowered[0], ("bucket", "dp"), axis=0, tiled=True),
        lax.all_gather(lowered[1], ("bucket", "dp"), axis=1, tiled=True),
        lax.all_gather(lowered[2], ("bucket", "dp"), axis=1, tiled=True),
        lax.all_gather(lowered[3], ("bucket", "dp"), axis=0, tiled=True),
        lax.all_gather(lowered[4], ("bucket", "dp"), axis=1, tiled=True),
        lax.all_gather(lowered[5], ("bucket", "dp"), axis=0, tiled=True),
        lax.all_gather(lowered[6], ("bucket", "dp"), axis=1, tiled=True),
        lax.all_gather(lowered[7], ("bucket", "dp"), axis=0, tiled=True),
        lax.all_gather(lowered[8], ("bucket", "dp"), axis=1, tiled=True),
    )
    (
        word_table,
        up_low,
        time_low,
        query_key_value_reduced,
        out_low,
        feedforward_weight_reduced,
        proj_low,
        down_weight_reduced,
        gains_low,
    ) = gathered
    norm_gain_vector = gains_low.astype(jnp.float32)
    tokens = token_ids[0]
    segments = segment_ids[0]
    step_row = timesteps[0]
    noise_row = noise[0]
    live_float = live[0].astype(jnp.float32)
    buckets = lax.axis_size("bucket")
    step_span = STEPS_T // buckets
    onehot = (
        (step_row // step_span)[:, None] == jnp.arange(buckets, dtype=jnp.int32)[None, :]
    ).astype(jnp.float32)
    counts = lax.psum(jnp.sum(live_float[:, None] * onehot, 0), ("bucket", "dp"))
    token_weight = live_float * jnp.sum(onehot / counts[None, :], -1) / buckets
    start_emb = word_table[tokens].astype(jnp.float32)
    fraction = step_row.astype(jnp.float32) / STEPS_T
    alpha_bar = 1.0 - jnp.sqrt(fraction + 0.0001)
    keep_root = jnp.sqrt(alpha_bar)[:, None]
    noisy_emb = keep_root * start_emb + jnp.sqrt(1.0 - alpha_bar)[:, None] * noise_row
    noisy_low = noisy_emb.astype(jnp.bfloat16)
    feature_low = sinusoid(step_row, D).astype(jnp.bfloat16)
    hidden_initial = matmul(noisy_low, up_low) + matmul(feature_low, time_low)
    saved_acts, hidden_after_second = block_forward(
        hidden_initial,
        segments,
        query_key_value_reduced,
        out_low,
        feedforward_weight_reduced,
        proj_low,
        norm_gain_vector,
    )
    normalized_final, centred_scaled_final, inverse_deviation_final = layer_normalize(
        hidden_after_second, norm_gain_vector[2]
    )
    normed_top_low = normalized_final.astype(jnp.bfloat16)
    prediction = matmul(normed_top_low, down_weight_reduced)
    pred_low = prediction.astype(jnp.bfloat16)
    grad_table_head, cross_loss, grad_pred_head = head_pass(
        pred_low, word_table, tokens, token_weight
    )
    pred_gap = prediction - start_emb
    loss_local = jnp.sum(token_weight * (jnp.mean(pred_gap * pred_gap, -1) + cross_loss))
    loss_sum = lax.psum(loss_local, ("bucket", "dp"))
    grad_mse = token_weight[:, None] * 2.0 * pred_gap / EMB
    gradient_prediction_reduced = (grad_mse + grad_pred_head).astype(jnp.bfloat16)
    grad_down = matmul_tn(normed_top_low, gradient_prediction_reduced)
    grad_top, grad_gain_top = norm_back(
        matrix_product_transposed(gradient_prediction_reduced, down_weight_reduced),
        centred_scaled_final,
        inverse_deviation_final,
        norm_gain_vector[2],
    )
    grad_zero, block_grads = block_backward(
        saved_acts,
        grad_top,
        segments,
        query_key_value_reduced,
        out_low,
        feedforward_weight_reduced,
        proj_low,
        norm_gain_vector,
    )
    grad_qkv, grad_out, grad_fc, grad_proj, grad_gain_one, grad_gain_two = block_grads
    grad_zero_low = grad_zero.astype(jnp.bfloat16)
    grad_up = matmul_tn(noisy_low, grad_zero_low)
    grad_time = matmul_tn(feature_low, grad_zero_low)
    grad_start = keep_root * matrix_product_transposed(grad_zero_low, up_low) - grad_mse
    grad_table = grad_table_head + jax.ops.segment_sum(
        grad_start, tokens, num_segments=word_table.shape[0]
    )
    grad_gains = jnp.stack([grad_gain_one, grad_gain_two, grad_gain_top], 0)
    shards = (
        lax.psum_scatter(grad_table, ("bucket", "dp"), scatter_dimension=0, tiled=True),
        lax.psum_scatter(grad_up, ("bucket", "dp"), scatter_dimension=1, tiled=True),
        lax.psum_scatter(grad_time, ("bucket", "dp"), scatter_dimension=1, tiled=True),
        lax.psum_scatter(grad_qkv, ("bucket", "dp"), scatter_dimension=0, tiled=True),
        lax.psum_scatter(grad_out, ("bucket", "dp"), scatter_dimension=1, tiled=True),
        lax.psum_scatter(grad_fc, ("bucket", "dp"), scatter_dimension=0, tiled=True),
        lax.psum_scatter(grad_proj, ("bucket", "dp"), scatter_dimension=1, tiled=True),
        lax.psum_scatter(grad_down, ("bucket", "dp"), scatter_dimension=0, tiled=True),
        lax.psum_scatter(grad_gains, ("bucket", "dp"), scatter_dimension=1, tiled=True),
    )
    squares_local = jnp.zeros((), jnp.float32)
    for member in shards:
        squares_local = squares_local + jnp.sum(member * member)
    squares = lax.psum(squares_local, ("bucket", "dp"))
    grad_norm = jnp.sqrt(squares)
    factor = CLIP_NORM / jnp.maximum(grad_norm, CLIP_NORM)
    results = []
    for place in range(9):
        results = results + adam_update(
            masters[place],
            moments[place],
            seconds[place],
            factor * shards[place],
            RATES[place],
            DECAYS[place],
        )
    return (
        loss_sum,
        grad_norm,
        results[0],
        results[1],
        results[2],
        results[3],
        results[4],
        results[5],
        results[6],
        results[7],
        results[8],
        results[9],
        results[10],
        results[11],
        results[12],
        results[13],
        results[14],
        results[15],
        results[16],
        results[17],
        results[18],
        results[19],
        results[20],
        results[21],
        results[22],
        results[23],
        results[24],
        results[25],
        results[26],
    )


def solution(mesh):
    return jax.shard_map(
        on_device,
        mesh=mesh,
        in_specs=(
            P(("bucket", "dp"), None),
            P(("bucket", "dp"), None),
            P(("bucket", "dp"), None),
            P(("bucket", "dp"), None),
            P(("bucket", "dp"), None, None),
            P(("bucket", "dp"), None),
            P(("bucket", "dp"), None),
            P(("bucket", "dp"), None),
            P(None, ("bucket", "dp")),
            P(None, ("bucket", "dp")),
            P(None, ("bucket", "dp")),
            P(None, ("bucket", "dp")),
            P(None, ("bucket", "dp")),
            P(None, ("bucket", "dp")),
            P(("bucket", "dp"), None),
            P(("bucket", "dp"), None),
            P(("bucket", "dp"), None),
            P(None, ("bucket", "dp")),
            P(None, ("bucket", "dp")),
            P(None, ("bucket", "dp")),
            P(("bucket", "dp"), None),
            P(("bucket", "dp"), None),
            P(("bucket", "dp"), None),
            P(None, ("bucket", "dp")),
            P(None, ("bucket", "dp")),
            P(None, ("bucket", "dp")),
            P(("bucket", "dp"), None),
            P(("bucket", "dp"), None),
            P(("bucket", "dp"), None),
            P(None, ("bucket", "dp")),
            P(None, ("bucket", "dp")),
            P(None, ("bucket", "dp")),
        ),
        out_specs=(
            P(),
            P(),
            P(("bucket", "dp"), None),
            P(("bucket", "dp"), None),
            P(("bucket", "dp"), None),
            P(None, ("bucket", "dp")),
            P(None, ("bucket", "dp")),
            P(None, ("bucket", "dp")),
            P(None, ("bucket", "dp")),
            P(None, ("bucket", "dp")),
            P(None, ("bucket", "dp")),
            P(("bucket", "dp"), None),
            P(("bucket", "dp"), None),
            P(("bucket", "dp"), None),
            P(None, ("bucket", "dp")),
            P(None, ("bucket", "dp")),
            P(None, ("bucket", "dp")),
            P(("bucket", "dp"), None),
            P(("bucket", "dp"), None),
            P(("bucket", "dp"), None),
            P(None, ("bucket", "dp")),
            P(None, ("bucket", "dp")),
            P(None, ("bucket", "dp")),
            P(("bucket", "dp"), None),
            P(("bucket", "dp"), None),
            P(("bucket", "dp"), None),
            P(None, ("bucket", "dp")),
            P(None, ("bucket", "dp")),
            P(None, ("bucket", "dp")),
        ),
        check_vma=False,
    )
```

profile of v0, /device:TPU:0, one launch (start us, length us, event | category | flops | bytes accessed | tf_op | source)
XLA Modules:
  0.0 1639.0 jit_solution(11419731851447613199)
XLA Ops:
  22.4 42.0 %psum.21 = f32[4]{0:T(128)S(1)} all-reduce(f32[4]{0:T(128)S(1)} %select_reduce_fusion.1), channel_id=1, replica_groups=mesh['bucket'=4,'dp'=8] {'bucket','dp'}, use_global_device_ids=true, to_apply=%region_1.2 | all-reduce | flops 4 | bytes 32 | tf_op jit(solution)/shard_map/psum | solution.py:403
  65.1 40.3 %all-gather = bf16[32,24,3]{1,2,0:T(4,128)(2,1)S(1)} all-gather(bf16[1,24,3]{1,2,0:T(4,128)(2,1)S(1)} %convert_bitcast_fusion), channel_id=1, replica_groups=mesh['bucket'=4,'dp'=8] {'bucket','dp'}, dimensions={0}, use_global_device_ids=true | all-gather | bytes 4752 | tf_op jit(solution)/shard_map/all_gather | solution.py:379
  106.3 40.3 %all_gather.35 = bf16[768,128]{1,0:T(8,128)(2,1)} all-gather(bf16[24,128]{1,0:T(8,128)(2,1)S(1)} %convert_element_type.150), channel_id=1, replica_groups=mesh['bucket'=4,'dp'=8] {'bucket','dp'}, dimensions={0}, use_global_device_ids=true | all-gather | bytes 202752 | tf_op jit(solution)/shard_map/all_gather | solution.py:378
  146.6 39.3 %all_gather.28 = bf16[128,768]{0,1:T(8,128)(2,1)S(1)} all-gather(bf16[128,24]{0,1:T(8,128)(2,1)S(1)} %convert_element_type.136), channel_id=1, replica_groups=mesh['bucket'=4,'dp'=8] {'bucket','dp'}, dimensions={1}, use_global_device_ids=true | all-gather | bytes 202752 | tf_op jit(solution)/shard_map/all_gather | solution.py:372
  186.1 6.3 fusion.41
  192.5 4.9 fusion.45
  197.5 5.1 gather_fusion
  206.6 7.0 convolution_convert_fusion
  222.4 73.4 %while.42 = (s32[]{:T(128)}, bf16[2,512,12,64]{1,3,2,0:T(8,128)(2,1)}, f32[2,12,512]{2,1,0:T(8,128)S(1)}, s32[2]{0:T(128)S(1)}, s32[1024]{0:T(1024)S(1)}, /*inde...) while((s32[]{:T(128)}, ...), condition=%wide.region_8.9_spmd, body=%wide.region_5.8_spmd.sunk | while | flops 1686628352 | bytes 190286064 | solution.py:94
  224.5 10.7 fusion.151
  235.2 12.4 fusion.152
  250.7 8.6 bitcast_dynamic-update-slice_fusion.6
  261.0 10.7 fusion.151
  271.7 12.4 fusion.152
  287.3 8.5 bitcast_dynamic-update-slice_fusion.6
  295.8 4.2 copy.115
  301.6 4.2 fusion.85
  306.2 9.0 all-gather.16.cloned.1.call-done
  315.3 10.5 fusion.70
  325.7 55.5 %all-gather.18.cloned.1.call-done = bf16[3072,768]{0,1:T(8,128)(2,1)} async-done(((bf16[3072,24]{0,1:T(8,128)(2,1)}), bf16[3072,768]{0,1:T(8,128)(2,1)}) %all-gather.18.cloned.1.call-update) | async-done | bytes 4718608 | tf_op jit(solution)/shard_map/all_gather | solution.py:377
  381.2 20.4 %fusion.86 = (f32[1024]{0:T(1024)S(1)}, f32[1024,768]{0,1:T(8,128)S(1)}) fusion(f32[1024,768]{0,1:T(8,128)S(1)} %get-tuple-element.460, bf16[3072,768]{0,1:T(8,128)(2,1)} %all-gather.18.cloned.1.call-done, f32[1024,3072]{1,0:T(8,128)} %fusion.70), kind=kOutput, calls=%fused_computation.204 | convolution fusion | flops 4861721600 | bytes 23597056 | tf_op jit(solution)/shard_map/dot_general | solution.py:28
  404.7 78.8 %while.43 = (s32[]{:T(128)}, f32[11264,128]{1,0:T(8,128)}, f32[2,512]{1,0:T(2,128)}, f32[2,512,128]{2,1,0:T(8,128)}, s32[2]{0:T(128)S(1)}, /*index=5*/f32[1024]{...) while((s32[]{:T(128)}, f32[11264,128]{1,0:T(8,128)}, ...), condition=%wide.region_18.19_spmd.clone, body=%wide.region_14.18_spmd.clone.sunk | while | flops 4501274112 | bytes 167811312 | solution.py:285
  406.1 5.1 fusion.158
  411.3 8.4 select_reduce_fusion.3
  419.7 8.1 multiply_convert_fusion.14
  429.0 9.1 fusion.160
  438.1 5.1 convolution_add_fusion.5
  444.6 5.1 fusion.158
  449.8 8.4 select_reduce_fusion.3
  458.1 8.1 multiply_convert_fusion.14
  467.5 9.1 fusion.160
  476.6 6.9 convolution_add_fusion.5
  491.1 4.3 multiply_reduce_fusion.1
  498.9 17.8 %fusion.38 = bf16[1024,3072]{1,0:T(8,128)(2,1)S(1)} fusion(f32[1024,3072]{1,0:T(8,128)} %fusion.70, bf16[3072,768]{0,1:T(8,128)(2,1)} %all-gather.18.cloned.1.call-done, f32[1024,768]{0,1:T(8,128)S(1)} %subtract_multiply_fusion), kind=kOutput, calls=%fused_computation.60 | convolution fusion | flops 4895539200 | bytes 26738688 | tf_op jit(solution)/shard_map/dot_general | solution.py:38
  516.8 6.3 multiply_reduce_fusion.2
  528.3 174.1 %while.44 = (s32[]{:T(128)}, f32[1024,12,64]{0,2,1:T(8,128)}, f32[1024,12,64]{0,2,1:T(8,128)}, bf16[2,512,12,64]{1,3,2,0:T(8,128)(2,1)}, s32[2]{0:T(128)S(1)}, /...) while((s32[]{:T(128)}, f32[1024,12,64]{0,2,1:T(8,128)}, ...), condition=%wide.region_27.28_spmd.clone, body=%wide.region_25.27_spmd.clone.sunk | while | flops 4125747200 | bytes 225634640 | solution.py:134
  532.2 11.5 fusion.170
  543.7 13.4 bitcast_add_fusion.5
  557.1 18.1 %multiply_reduce_fusion.25 = (f32[12,512]{1,0:T(8,128)S(1)}, f32[12,512,1024]{2,1,0:T(8,128)}) fusion(f32[12,512,1024]{2,1,0:T(8,128)} %fusion.170, f32[12,512]{1,0:T(8,128)S(1)} %dynamic-slice_bitcast_fusion.2, pred[512,1024]{1,0:T(8,128)(4,1)S(1)} %broadcast_compare_fusion.5, bf16[1024,12,64]{0,2,1:T(8,128)(2,1)} %get-tuple-element.796, ...), kind=kOutput, calls=%fused_computation.30.clone.1 | convolution fusion | flops 836757504 | bytes 53264388 | tf_op jit(solution)/shard_map/while/body/eval_jaxpr/qhd,khd->hqk/dot_general | solution.py:111
  575.2 21.4 %multiply_convert_fusion.15 = bf16[12,512,1024]{2,1,0:T(8,128)(2,1)} fusion(f32[12,512,1024]{2,1,0:T(8,128)} %get-tuple-element.671, f32[12,512,1024]{2,1,0:T(8,128)} %fusion.170, f32[12,512]{1,0:T(8,128)S(1)} %get-tuple-element.672, f32[12,512]{1,0:T(8,128)S(1)} %dynamic-slice_bitcast_fusion.2, pred[512,1024]{1,0:T(8,128)(4,1)S(1)} %broadcast_compare_fusion.5), kind=kLoop, calls=%fused_computation.29.clone.1 | loop fusion | flops 37748736 | bytes 63488000 | tf_op jit(solution)/shard_map/while/body/eval_jaxpr/convert_element_type | solution.py:115
  596.6 9.5 bitcast_dynamic-update-slice_fusion.8
  606.1 8.5 bitcast_add_fusion.4
  618.3 11.5 fusion.170
  629.8 14.2 bitcast_add_fusion.5
  643.9 18.1 %multiply_reduce_fusion.25 = (f32[12,512]{1,0:T(8,128)S(1)}, f32[12,512,1024]{2,1,0:T(8,128)}) fusion(f32[12,512,1024]{2,1,0:T(8,128)} %fusion.170, f32[12,512]{1,0:T(8,128)S(1)} %dynamic-slice_bitcast_fusion.2, pred[512,1024]{1,0:T(8,128)(4,1)S(1)} %broadcast_compare_fusion.5, bf16[1024,12,64]{0,2,1:T(8,128)(2,1)} %get-tuple-element.796, ...), kind=kOutput, calls=%fused_computation.30.clone.1 | convolution fusion | flops 836757504 | bytes 53264388 | tf_op jit(solution)/shard_map/while/body/eval_jaxpr/qhd,khd->hqk/dot_general | solution.py:111
  662.0 21.3 %multiply_convert_fusion.15 = bf16[12,512,1024]{2,1,0:T(8,128)(2,1)} fusion(f32[12,512,1024]{2,1,0:T(8,128)} %get-tuple-element.671, f32[12,512,1024]{2,1,0:T(8,128)} %fusion.170, f32[12,512]{1,0:T(8,128)S(1)} %get-tuple-element.672, f32[12,512]{1,0:T(8,128)S(1)} %dynamic-slice_bitcast_fusion.2, pred[512,1024]{1,0:T(8,128)(4,1)S(1)} %broadcast_compare_fusion.5), kind=kLoop, calls=%fused_computation.29.clone.1 | loop fusion | flops 37748736 | bytes 63488000 | tf_op jit(solution)/shard_map/while/body/eval_jaxpr/convert_element_type | solution.py:115
  683.3 9.5 bitcast_dynamic-update-slice_fusion.8
  692.8 9.5 bitcast_add_fusion.4
  706.4 3.4 convert.28
  711.7 4.9 multiply_reduce_fusion.3
  720.3 5.2 fusion.46
  725.6 4.6 fusion.44
  730.7 9.3 fusion.39
  742.2 10.6 scatter_fusion
  754.7 10.5 fusion.69
  767.2 10.5 fusion.49
  778.8 40.0 %all-reduce.2 = f32[3,768]{1,0:T(4,128)S(1)} all-reduce(f32[3,768]{1,0:T(4,128)S(1)} %pad_maximum_fusion.6), channel_id=10, replica_groups=mesh['bucket'=4,'dp'=8] {'bucket','dp'}, use_global_device_ids=true, to_apply=%region_50.51.clone | all-reduce | flops 2304 | bytes 18432
  822.7 94.7 %reduce-scatter.20.cloned.1.call-done = f32[768,24]{0,1:T(8,128)} async-done(((f32[768,768]{0,1:T(8,128)}), f32[768,24]{0,1:T(8,128)}) %reduce-scatter.20.cloned.1.call-update) | async-done | bytes 73744 | tf_op jit(solution)/shard_map/reduce_scatter | solution.py:467
  918.9 102.6 %reduce-scatter.16.cloned.1.call-done = f32[768,24]{0,1:T(8,128)} async-done(((f32[768,768]{0,1:T(8,128)}), f32[768,24]{0,1:T(8,128)}) %reduce-scatter.16.cloned.1.call-update) | async-done | bytes 73744 | tf_op jit(solution)/shard_map/reduce_scatter | solution.py:465
  1023.0 122.4 %reduce-scatter.18.cloned.1.call-done = f32[24,2304]{1,0:T(8,128)} async-done(((f32[768,2304]{1,0:T(8,128)}), f32[24,2304]{1,0:T(8,128)}) %reduce-scatter.18.cloned.1.call-update) | async-done | bytes 221200 | tf_op jit(solution)/shard_map/reduce_scatter | solution.py:466
  1147.0 145.6 %reduce-scatter.14.cloned.1.call-done = f32[352,128]{1,0:T(8,128)} async-done(((f32[11264,128]{1,0:T(8,128)}), f32[352,128]{1,0:T(8,128)}) %reduce-scatter.14.cloned.1.call-update) | async-done | bytes 180240 | tf_op jit(solution)/shard_map/reduce_scatter | solution.py:463
  1297.5 135.0 %reduce-scatter.22.cloned.1.call-done = f32[24,3072]{1,0:T(8,128)} async-done(((f32[768,3072]{1,0:T(8,128)}), f32[24,3072]{1,0:T(8,128)}) %reduce-scatter.22.cloned.1.call-update) | async-done | bytes 294928 | tf_op jit(solution)/shard_map/reduce_scatter | solution.py:468
  1434.9 138.3 %reduce-scatter.24.cloned.1.call-done = f32[3072,24]{0,1:T(8,128)} async-done(((f32[3072,768]{0,1:T(8,128)}), f32[3072,24]{0,1:T(8,128)}) %reduce-scatter.24.cloned.1.call-update) | async-done | bytes 294928 | tf_op jit(solution)/shard_map/reduce_scatter | solution.py:469
  1576.8 40.1 %all-reduce.3 = (f32[]{:T(128)}, f32[]{:T(128)}) all-reduce(f32[]{:T(128)} %multiply_reduce_fusion.22, f32[]{:T(128)S(6)} %add.360), channel_id=1, replica_groups=mesh['bucket'=4,'dp'=8] {'bucket','dp'}, use_global_device_ids=true, to_apply=%region_20.21 | all-reduce | flops 2 | bytes 16 | tf_op jit(solution)/shard_map/psum | solution.py:433
  (368 shorter events, 109.1 us)
Async XLA Ops:
  7.2 178.7 %copy-start.48 = (f32[1,1024,128]{2,1,0:T(8,128)S(1)}, f32[1,1024,128]{2,1,0:T(8,128)}, u32[]{:S(2)}) copy-start(f32[1,1024,128]{2,1,0:T(8,128)} %param.42) | copy-start | bytes 1572868
  7.2 185.3 %all-gather.10.cloned.1.call-start = ((), (), s32[]{:S(2)}) async-start(), calls=%async_computation.9 | async-start | bytes 1216512 | tf_op jit(solution)/shard_map/all_gather | solution.py:373
  8.8 188.6 %all-gather.8.cloned.1.call-start = ((), (), s32[]{:S(2)}) async-start(), calls=%async_computation.8 | async-start | bytes 2973696 | tf_op jit(solution)/shard_map/all_gather | solution.py:371
  10.5 196.1 %all-gather.12.cloned.1.call-start = ((), (), s32[]{:S(2)}) async-start(), calls=%async_computation.10 | async-start | bytes 3649536 | tf_op jit(solution)/shard_map/all_gather | solution.py:374
  12.2 289.5 %all-gather.14.cloned.1.call-start = ((), (), s32[]{:S(2)}) async-start(), calls=%async_computation.11 | async-start | bytes 1216512 | tf_op jit(solution)/shard_map/all_gather | solution.py:375
  13.7 301.5 %all-gather.16.cloned.1.call-start = ((), (), s32[]{:S(2)}) async-start(), calls=%async_computation.12 | async-start | bytes 4866048 | tf_op jit(solution)/shard_map/all_gather | solution.py:376
  15.5 365.8 %all-gather.18.cloned.1.call-start = ((), (), s32[]{:S(2)}) async-start(), calls=%async_computation.13 | async-start | bytes 4866048 | tf_op jit(solution)/shard_map/all_gather | solution.py:377
  17.2 802.9 %reduce-scatter.28.cloned.1.call-start = ((), (), s32[]{:S(2)}) async-start(), calls=%async_computation.21 | async-start | bytes 405504
  65.1 137.6 %copy-start.82 = (f32[1024]{0:T(1024)}, f32[1024]{0:T(1024)S(1)}, u32[]{:S(2)}) copy-start(f32[1024]{0:T(1024)S(1)} %get-tuple-element.453) | copy-start | bytes 12292
  106.3 100.2 %copy-start.89 = (f32[768]{0:T(1024)}, f32[768]{0:T(1024)S(1)}, u32[]{:S(2)}) copy-start(f32[768]{0:T(1024)S(1)} %get-tuple-element.346) | copy-start | bytes 9220
  185.9 17.6 %copy-start.31 = (bf16[128,768]{0,1:T(8,128)(2,1)}, bf16[128,768]{0,1:T(8,128)(2,1)S(1)}, u32[]{:S(2)}) copy-start(bf16[128,768]{0,1:T(8,128)(2,1)S(1)} %all_gather.28) | copy-start | bytes 589828
  224.5 23.1 %copy-start.7 = (bf16[1024,12,64]{0,2,1:T(8,128)(2,1)S(1)}, bf16[1024,12,64]{0,2,1:T(8,128)(2,1)}, u32[]{:S(2)}) copy-start(bf16[1024,12,64]{0,2,1:T(8,128)(2,1)} %get-tuple-element.707) | copy-start | bytes 4718596 | tf_op jit(solution)/shard_map/while
  235.2 15.5 copy-start
  261.0 23.2 %copy-start.7 = (bf16[1024,12,64]{0,2,1:T(8,128)(2,1)S(1)}, bf16[1024,12,64]{0,2,1:T(8,128)(2,1)}, u32[]{:S(2)}) copy-start(bf16[1024,12,64]{0,2,1:T(8,128)(2,1)} %get-tuple-element.707) | copy-start | bytes 4718596 | tf_op jit(solution)/shard_map/while
  271.7 15.6 copy-start
  305.8 75.4 %copy-start.10 = (f32[1024,768]{0,1:T(8,128)}, f32[1024,768]{0,1:T(8,128)S(1)}, u32[]{:S(2)}) copy-start(f32[1024,768]{0,1:T(8,128)S(1)} %get-tuple-element.460) | copy-start | bytes 9437188
  305.8 9.5 copy-start.52
  305.8 19.9 %copy-start.49 = (f32[1024]{0:T(1024)}, f32[1024]{0:T(1024)S(1)}, u32[]{:S(2)}) copy-start(f32[1024]{0:T(1024)S(1)} %broadcast_multiply_fusion.8) | copy-start | bytes 12292
  306.2 19.5 %copy-start.55 = (f32[1024]{0:T(1024)}, f32[1024]{0:T(1024)S(1)}, u32[]{:S(2)}) copy-start(f32[1024]{0:T(1024)S(1)} %add_rsqrt_fusion.1) | copy-start | bytes 12292
  404.7 81.1 %copy-start.26 = (bf16[1024,128]{0,1:T(8,128)(2,1)S(1)}, bf16[1024,128]{0,1:T(8,128)(2,1)}, u32[]{:S(2)}) copy-start(bf16[1024,128]{0,1:T(8,128)(2,1)} %copy-done.25) | copy-start | bytes 786436
  404.7 81.0 %copy-start.84 = (f32[1024]{0:T(1024)S(1)}, f32[1024]{0:T(1024)}, u32[]{:S(2)}) copy-start(f32[1024]{0:T(1024)} %get-tuple-element.449) | copy-start | bytes 12292
  429.0 9.1 copy-start.1
  467.5 9.1 copy-start.1
  483.5 7.6 copy-start.75
  483.5 7.6 copy-start.77
  495.5 325.9 %reduce-scatter.26.cloned.1.call-start = ((), (), s32[]{:S(2)}) async-start(), calls=%async_computation.20 | async-start | bytes 405504
  496.0 20.7 %slice-start = ((s8[4718592]{0:T(1024)(128)(4,1)}), s8[4194304]{0:T(1024)(128)(4,1)S(1)}, s32[]{:S(2)}) async-start(s8[4718592]{0:T(1024)(128)(4,1)} %bitcast.157), calls=%async_computation.22 | async-start | bytes 8388608
  498.8 24.3 %copy-start.18 = (f32[1024,768]{0,1:T(8,128)}, f32[1024,768]{0,1:T(8,128)S(1)}, u32[]{:S(2)}) copy-start(f32[1024,768]{0,1:T(8,128)S(1)} %subtract_multiply_fusion) | copy-start | bytes 9437188
  498.8 17.9 %copy-start.11 = (f32[1024,768]{0,1:T(8,128)S(1)}, f32[1024,768]{0,1:T(8,128)}, u32[]{:S(2)}) copy-start(f32[1024,768]{0,1:T(8,128)} %copy-done.10) | copy-start | bytes 9437188
  498.8 17.9 %slice-start.1 = ((s8[4718592]{0:T(1024)(128)(4,1)}), s8[524288]{0:T(1024)(128)(4,1)S(1)}, s32[]{:S(2)}) async-start(s8[4718592]{0:T(1024)(128)(4,1)} %bitcast.157), calls=%async_computation.23 | async-start | bytes 1048576
  498.8 17.9 %copy-start.50 = (f32[1024]{0:T(1024)S(1)}, f32[1024]{0:T(1024)}, u32[]{:S(2)}) copy-start(f32[1024]{0:T(1024)} %copy-done.49) | copy-start | bytes 12292
  498.8 17.9 %copy-start.53 = (f32[768]{0:T(1024)S(1)}, f32[768]{0:T(1024)}, u32[]{:S(2)}) copy-start(f32[768]{0:T(1024)} %get-tuple-element.345) | copy-start | bytes 9220
  498.9 17.9 %copy-start.56 = (f32[1024]{0:T(1024)S(1)}, f32[1024]{0:T(1024)}, u32[]{:S(2)}) copy-start(f32[1024]{0:T(1024)} %copy-done.55) | copy-start | bytes 12292
  532.2 11.5 copy-start.22
  596.6 9.5 copy-start.6
  618.3 11.5 copy-start.22
  683.3 9.5 copy-start.6
  706.4 10.3 copy-start.35
  720.3 197.1 %reduce-scatter.20.cloned.1.call-start = ((), (), s32[]{:S(2)}) async-start(), calls=%async_computation.17 | async-start | bytes 2433024 | tf_op jit(solution)/shard_map/reduce_scatter | solution.py:467
  725.5 296.0 %reduce-scatter.16.cloned.1.call-start = ((), (), s32[]{:S(2)}) async-start(), calls=%async_computation.15 | async-start | bytes 2433024 | tf_op jit(solution)/shard_map/reduce_scatter | solution.py:465
  730.2 415.2 %reduce-scatter.18.cloned.1.call-start = ((), (), s32[]{:S(2)}) async-start(), calls=%async_computation.16 | async-start | bytes 7299072 | tf_op jit(solution)/shard_map/reduce_scatter | solution.py:466
  740.0 552.7 %reduce-scatter.14.cloned.1.call-start = ((), (), s32[]{:S(2)}) async-start(), calls=%async_computation.14 | async-start | bytes 5947392 | tf_op jit(solution)/shard_map/reduce_scatter | solution.py:463
  752.8 679.7 %reduce-scatter.22.cloned.1.call-start = ((), (), s32[]{:S(2)}) async-start(), calls=%async_computation.18 | async-start | bytes 9732096 | tf_op jit(solution)/shard_map/reduce_scatter | solution.py:468
  765.3 807.9 %reduce-scatter.24.cloned.1.call-start = ((), (), s32[]{:S(2)}) async-start(), calls=%async_computation.19 | async-start | bytes 9732096 | tf_op jit(solution)/shard_map/reduce_scatter | solution.py:469
  777.7 41.8 %copy-start.73 = (f32[1024]{0:T(1024)S(1)}, f32[1024]{0:T(1024)}, u32[]{:S(2)}) copy-start(f32[1024]{0:T(1024)} %get-tuple-element.717) | copy-start | bytes 12292
  777.7 41.8 %copy-start.91 = (f32[1024]{0:T(1024)S(1)}, f32[1024]{0:T(1024)}, u32[]{:S(2)}) copy-start(f32[1024]{0:T(1024)} %get-tuple-element.448) | copy-start | bytes 12292
  777.7 841.4 %copy-start.78 = (f32[128,24]{0,1:T(8,128)S(1)}, f32[128,24]{0,1:T(8,128)}, u32[]{:S(2)}) copy-start(f32[128,24]{0,1:T(8,128)} %param.46) | copy-start | bytes 36868
  777.7 842.8 %copy-start.79 = (f32[24,128]{1,0:T(8,128)S(1)}, f32[24,128]{1,0:T(8,128)}, u32[]{:S(2)}) copy-start(f32[24,128]{1,0:T(8,128)} %param.64) | copy-start | bytes 36868
  777.7 844.1 %copy-start.64 = (f32[768,24]{0,1:T(8,128)S(1)}, f32[768,24]{0,1:T(8,128)}, u32[]{:S(2)}) copy-start(f32[768,24]{0,1:T(8,128)} %param.55) | copy-start | bytes 221188
  777.7 845.8 %copy-start.65 = (f32[768,24]{0,1:T(8,128)S(1)}, f32[768,24]{0,1:T(8,128)}, u32[]{:S(2)}) copy-start(f32[768,24]{0,1:T(8,128)} %param.49) | copy-start | bytes 221188
  777.7 847.4 %copy-start.47 = (f32[352,128]{1,0:T(8,128)S(1)}, f32[352,128]{1,0:T(8,128)}, u32[]{:S(2)}) copy-start(f32[352,128]{1,0:T(8,128)} %param.43) | copy-start | bytes 540676
  777.8 847.4 %copy-start.67 = (f32[352,128]{1,0:T(8,128)S(1)}, f32[352,128]{1,0:T(8,128)}, u32[]{:S(2)}) copy-start(f32[352,128]{1,0:T(8,128)} %param.45) | copy-start | bytes 540676
  777.8 849.3 %copy-start.44 = (f32[24,2304]{1,0:T(8,128)S(1)}, f32[24,2304]{1,0:T(8,128)}, u32[]{:S(2)}) copy-start(f32[24,2304]{1,0:T(8,128)} %param.52) | copy-start | bytes 663556
  777.8 849.3 %copy-start.66 = (f32[24,2304]{1,0:T(8,128)S(1)}, f32[24,2304]{1,0:T(8,128)}, u32[]{:S(2)}) copy-start(f32[24,2304]{1,0:T(8,128)} %param.54) | copy-start | bytes 663556
  777.8 851.1 %copy-start.37 = (f32[3072,24]{0,1:T(8,128)S(1)}, f32[3072,24]{0,1:T(8,128)}, u32[]{:S(2)}) copy-start(f32[3072,24]{0,1:T(8,128)} %param.61) | copy-start | bytes 884740
  777.8 851.1 %copy-start.60 = (f32[3072,24]{0,1:T(8,128)S(1)}, f32[3072,24]{0,1:T(8,128)}, u32[]{:S(2)}) copy-start(f32[3072,24]{0,1:T(8,128)} %param.63) | copy-start | bytes 884740
  777.8 851.1 %copy-start.61 = (f32[3072,24]{0,1:T(8,128)S(1)}, f32[3072,24]{0,1:T(8,128)}, u32[]{:S(2)}) copy-start(f32[3072,24]{0,1:T(8,128)} %param.62) | copy-start | bytes 884740
  818.8 615.4 %copy-start.86 = (f32[3,768]{1,0:T(4,128)}, f32[3,768]{1,0:T(4,128)S(1)}, u32[]{:S(2)}) copy-start(f32[3,768]{1,0:T(4,128)S(1)} %all-reduce.2) | copy-start | bytes 27652
  1145.4 481.7 %copy-start.43 = (f32[24,2304]{1,0:T(8,128)S(1)}, f32[24,2304]{1,0:T(8,128)}, u32[]{:S(2)}) copy-start(f32[24,2304]{1,0:T(8,128)} %reduce-scatter.18.cloned.1.call-done) | copy-start | bytes 663556
  1434.8 195.2 %copy-start.38 = (f32[24,3072]{1,0:T(8,128)S(1)}, f32[24,3072]{1,0:T(8,128)}, u32[]{:S(2)}) copy-start(f32[24,3072]{1,0:T(8,128)} %param.58) | copy-start | bytes 884740
  1434.9 195.2 %copy-start.39 = (f32[24,3072]{1,0:T(8,128)S(1)}, f32[24,3072]{1,0:T(8,128)}, u32[]{:S(2)}) copy-start(f32[24,3072]{1,0:T(8,128)} %reduce-scatter.22.cloned.1.call-done) | copy-start | bytes 884740
  1434.9 195.2 %copy-start.62 = (f32[24,3072]{1,0:T(8,128)S(1)}, f32[24,3072]{1,0:T(8,128)}, u32[]{:S(2)}) copy-start(f32[24,3072]{1,0:T(8,128)} %param.60) | copy-start | bytes 884740
  1434.9 195.2 %copy-start.63 = (f32[24,3072]{1,0:T(8,128)S(1)}, f32[24,3072]{1,0:T(8,128)}, u32[]{:S(2)}) copy-start(f32[24,3072]{1,0:T(8,128)} %param.59) | copy-start | bytes 884740
  1573.2 55.8 %copy-start.40 = (f32[3072,24]{0,1:T(8,128)S(1)}, f32[3072,24]{0,1:T(8,128)}, u32[]{:S(2)}) copy-start(f32[3072,24]{0,1:T(8,128)} %reduce-scatter.24.cloned.1.call-done) | copy-start | bytes 884740
  (55 other events, 182.7 us)
Sparse Core Ops, SparseCore 0:
  11.6 57.0 all-gather.9
  72.2 57.4 all-gather.7
  133.3 59.3 all-gather.11
  196.1 53.0 all-gather.13
  252.6 62.5 all-gather.15
  318.7 62.4 all-gather.17
  495.6 93.5 reduce-scatter.27
  720.4 93.5 reduce-scatter.25
  819.3 98.0 reduce-scatter.19
  923.4 98.0 reduce-scatter.15
  1027.2 118.1 reduce-scatter.17
  1147.6 145.0 reduce-scatter.13
  1299.6 132.9 reduce-scatter.21
  1438.3 134.8 reduce-scatter.23
where the time goes:
time: 1650 us; the launch traced here: 1640 us
  waiting for transfers between devices  803 us (49%)
  matrix products  334 us (20%)
  blocking collectives  242 us (15%)
  other arithmetic  173 us (10%)
  local copies, waits for them, and re-layouts  53.2 us (3%)
  between operations  23 us (1%)
    reduce_scatter x1, waiting for transfers between devices, on_device(): lax.psum_scatter(grad_table, ('bucket', 'dp'), scatter_dimension=0, tiled...  146 us
    reduce_scatter x1, waiting for transfers between devices, on_device(): lax.psum_scatter(grad_proj, ('bucket', 'dp'), scatter_dimension=1, tiled=...  138 us
    reduce_scatter x1, waiting for transfers between devices, on_device(): lax.psum_scatter(grad_fc, ('bucket', 'dp'), scatter_dimension=0, tiled=True)  135 us
    reduce_scatter x1, waiting for transfers between devices, on_device(): lax.psum_scatter(grad_qkv, ('bucket', 'dp'), scatter_dimension=0, tiled=T...  122 us
    reduce_scatter x1, waiting for transfers between devices, on_device(): lax.psum_scatter(grad_time, ('bucket', 'dp'), scatter_dimension=1, tiled=...  103 us
    reduce_scatter x1, waiting for transfers between devices, on_device(): lax.psum_scatter(grad_out, ('bucket', 'dp'), scatter_dimension=1, tiled=T...  94.7 us
    dot_general x9, matrix products, matmul(): return jnp.dot(left_op, right_op, preferred_element_type=jnp.float32)  69.1 us
    dot_general x9, matrix products, matmul_tn(): lax.dot_general(left_op, right_op, (((0,), (0,)), ((), ())), preferred_el...  56.2 us
  transfers between devices with their start and end apart: 14, of which 8 were waited for; matrix products, arithmetic and copies ran while one was open for 25% of the time, Pallas kernels for 0%

commit v1 on v0

v1 whole, which is shorter than its diff:
```python
import math

import jax
import jax.numpy as jnp
from jax import lax
from jax.experimental import pallas as pl
from jax.experimental.pallas import tpu as pltpu
from jax.sharding import PartitionSpec as P

D = 768
HEAD = 64
EMB = 128
STEPS_T = 2000
ADAM_STEP = 10


NEG_BIG = -1e30
EPS_NORM = 1e-05
BETA_ONE = 0.9
BETA_TWO = 0.95
ADAM_EPS = 1e-08
DECAY_RATE = 0.01
CLIP_NORM = 0.02
RATES = (0.05, 0.05, 0.02, 0.02, 0.02, 0.02, 0.01, 0.02, 0.3)
DECAYS = (DECAY_RATE,) * 8 + (0.0,)


def matmul(left_op, right_op):
    return jnp.dot(left_op, right_op, preferred_element_type=jnp.float32)


def matmul_tn(left_op, right_op):
    return lax.dot_general(
        left_op, right_op, (((0,), (0,)), ((), ())), preferred_element_type=jnp.float32
    )


def matrix_product_transposed(left_op, right_op):
    return lax.dot_general(
        left_op, right_op, (((1,), (1,)), ((), ())), preferred_element_type=jnp.float32
    )


def layer_normalize(hidden, gain_row):
    centre = jnp.mean(hidden, -1, keepdims=True)
    centred = hidden - centre
    spread = jnp.mean(centred * centred, -1, keepdims=True)
    scale_inv = lax.rsqrt(spread + EPS_NORM)
    normed = centred * scale_inv
    return (normed * gain_row, normed, scale_inv)


def norm_back(grad_normed_out, normed, scale_inv, gain_row):
    grad_gain = jnp.sum(grad_normed_out * normed, 0)
    grad_scaled = grad_normed_out * gain_row
    grad_input = scale_inv * (
        grad_scaled
        - jnp.mean(grad_scaled, -1, keepdims=True)
        - normed * jnp.mean(grad_scaled * normed, -1, keepdims=True)
    )
    return (grad_input, grad_gain)


def sinusoid(step_row, model_width):
    half_width = model_width // 2
    freqs = jnp.exp(-math.log(10000.0) * jnp.arange(half_width, dtype=jnp.float32) / half_width)
    angles = step_row.astype(jnp.float32)[:, None] * freqs[None, :]
    return jnp.concatenate([jnp.sin(angles), jnp.cos(angles)], -1)


TILE = 128
LOG2E = math.log2(math.e)


def key_windows(segments):
    length = segments.shape[0]
    blocks = segments.reshape(-1, TILE)
    shared = jnp.any(blocks[:, :, None] == segments[None, None, :], 1)
    places = jnp.arange(length, dtype=jnp.int32)[None, :]
    first = jnp.min(jnp.where(shared, places, length), 1) // 16 * 16
    last = jnp.max(jnp.where(shared, places, -1), 1) + 1
    spans = (last - first + TILE - 1) // TILE
    starts = jnp.minimum(first, length - spans * TILE)
    return jnp.stack([starts, spans]).astype(jnp.int32)


def nt_dot(left, right):
    return lax.dot_general(
        left, right, (((1,), (1,)), ((), ())), preferred_element_type=jnp.float32
    )


def tn_dot(left, right):
    return lax.dot_general(
        left, right, (((0,), (0,)), ((), ())), preferred_element_type=jnp.float32
    )


def probs_window(query, keys, same):
    scores = jnp.where(same, nt_dot(keys, query), NEG_BIG)
    peak = jnp.max(scores, 0, keepdims=True)
    raised = jnp.exp2((scores - peak) * (HEAD ** (-0.5) * LOG2E))
    return raised * (1.0 / jnp.sum(raised, 0, keepdims=True))


def head_halves(pair):
    lanes = lax.broadcasted_iota(jnp.int32, pair.shape, 1)
    zero = jnp.zeros_like(pair)
    return [jnp.where(lanes < HEAD, pair, zero), jnp.where(lanes >= HEAD, pair, zero)]


def over_windows(windows_ref, length, visit):
    def step(block, unused):
        row_start = pl.multiple_of(block * TILE, TILE)
        key_start = pl.multiple_of(windows_ref[0, block], 16)
        for tiles in range(1, length // TILE + 1):

            @pl.when(windows_ref[1, block] == tiles)
            def _():
                visit(row_start, key_start, tiles * TILE)

        return unused

    lax.fori_loop(0, length // TILE, step, 0)


def attention_forward(mixed, seg_row, seg_col, windows):
    length, width = mixed.shape[0], mixed.shape[1] // 3
    pairs = width // TILE

    def kernel(windows_ref, q_ref, k_ref, v_ref, row_ref, col_ref, o_ref):
        def visit(row_start, key_start, span):
            rows = pl.ds(row_start, TILE)
            keys = pl.ds(key_start, span)
            key_blk, value_blk = k_ref[keys, :], v_ref[keys, :]
            same = col_ref[keys, :] == row_ref[:, rows]
            lanes = lax.broadcasted_iota(jnp.int32, (TILE, TILE), 1)
            both = [
                tn_dot(probs_window(half, key_blk, same).astype(jnp.bfloat16), value_blk)
                for half in head_halves(q_ref[rows, :])
            ]
            o_ref[rows, :] = jnp.where(lanes < HEAD, both[0], both[1]).astype(jnp.bfloat16)

        over_windows(windows_ref, length, visit)

    def column(offset):
        return pl.BlockSpec((length, TILE), lambda pair, windows: (0, pair + offset))

    return pl.pallas_call(
        kernel,
        out_shape=jax.ShapeDtypeStruct((length, width), jnp.bfloat16),
        grid_spec=pltpu.PrefetchScalarGridSpec(
            num_scalar_prefetch=1,
            grid=(pairs,),
            in_specs=[
                column(0),
                column(pairs),
                column(2 * pairs),
                pl.BlockSpec((1, length), lambda pair, windows: (0, 0)),
                pl.BlockSpec((length, 1), lambda pair, windows: (0, 0)),
            ],
            out_specs=column(0),
        ),
        compiler_params=pltpu.CompilerParams(vmem_limit_bytes=48 << 20),
        name="attention_forward",
    )(windows, mixed, mixed, mixed, seg_row, seg_col)


def attention_backward(mixed, grad_attended, seg_row, seg_col, windows):
    length, width = mixed.shape[0], mixed.shape[1] // 3
    pairs = width // TILE
    score_scale = HEAD ** (-0.5)

    def kernel(windows_ref, q_ref, k_ref, v_ref, do_ref, row_ref, col_ref, out_ref, dk_acc, dv_acc):
        pair = pl.program_id(0)
        dk_acc[...] = jnp.zeros_like(dk_acc)
        dv_acc[...] = jnp.zeros_like(dv_acc)

        def columns(third):
            return pl.ds(pl.multiple_of((third * pairs + pair) * TILE, TILE), TILE)

        def visit(row_start, key_start, span):
            rows = pl.ds(row_start, TILE)
            keys = pl.ds(key_start, span)
            key_blk, value_blk = k_ref[keys, :], v_ref[keys, :]
            same = col_ref[keys, :] == row_ref[:, rows]
            queries = head_halves(q_ref[rows, :])
            grads = head_halves(do_ref[rows, :])
            probs_low, scores_low = [], []
            for query, grad in zip(queries, grads):
                probs = probs_window(query, key_blk, same)
                grad_probs = nt_dot(value_blk, grad)
                inner = jnp.sum(probs * grad_probs, 0, keepdims=True)
                probs_low.append(probs.astype(jnp.bfloat16))
                scores_low.append((probs * (grad_probs - inner)).astype(jnp.bfloat16))
            scores_both = jnp.concatenate(scores_low, 1)
            dv_acc[keys, :] += jnp.dot(
                jnp.concatenate(probs_low, 1),
                jnp.concatenate(grads, 0),
                preferred_element_type=jnp.float32,
            )
            dk_acc[keys, :] += jnp.dot(
                scores_both,
                jnp.concatenate(queries, 0),
                preferred_element_type=jnp.float32,
            )
            lanes = lax.broadcasted_iota(jnp.int32, (TILE, TILE), 1)
            both = tn_dot(scores_both, key_blk)
            grad_query = jnp.where(lanes < HEAD, both[:TILE], both[TILE:])
            out_ref[rows, columns(0)] = (grad_query * score_scale).astype(jnp.bfloat16)

        over_windows(windows_ref, length, visit)
        out_ref[:, columns(1)] = (dk_acc[...] * score_scale).astype(jnp.bfloat16)
        out_ref[:, columns(2)] = dv_acc[...].astype(jnp.bfloat16)

    def column(offset):
        return pl.BlockSpec((length, TILE), lambda pair, windows: (0, pair + offset))

    return pl.pallas_call(
        kernel,
        out_shape=jax.ShapeDtypeStruct(mixed.shape, jnp.bfloat16),
        grid_spec=pltpu.PrefetchScalarGridSpec(
            num_scalar_prefetch=1,
            grid=(pairs,),
            in_specs=[
                column(0),
                column(pairs),
                column(2 * pairs),
                column(0),
                pl.BlockSpec((1, length), lambda pair, windows: (0, 0)),
                pl.BlockSpec((length, 1), lambda pair, windows: (0, 0)),
            ],
            out_specs=pl.BlockSpec(mixed.shape, lambda pair, windows: (0, 0)),
            scratch_shapes=[pltpu.VMEM((length, TILE), jnp.float32)] * 2,
        ),
        compiler_params=pltpu.CompilerParams(vmem_limit_bytes=48 << 20),
        name="attention_backward",
    )(windows, mixed, mixed, mixed, grad_attended, seg_row, seg_col)


def block_forward(
    hidden_initial,
    segments,
    query_key_value_reduced,
    out_low,
    feedforward_weight_reduced,
    proj_low,
    norm_gain_vector,
):
    normalized_first, centred_scaled_first, inverse_deviation_first = layer_normalize(
        hidden_initial, norm_gain_vector[0]
    )
    normed_one_low = normalized_first.astype(jnp.bfloat16)
    mixed_low = matmul(normed_one_low, query_key_value_reduced).astype(jnp.bfloat16)
    attended_low = attention_forward(mixed_low, *segments)
    hidden_after_first = hidden_initial + matrix_product_transposed(attended_low, out_low)
    normalized_second, centred_scaled_second, inverse_deviation_second = layer_normalize(
        hidden_after_first, norm_gain_vector[1]
    )
    normed_two_low = normalized_second.astype(jnp.bfloat16)
    fc_upper = matmul(normed_two_low, feedforward_weight_reduced)
    active_low = jax.nn.gelu(fc_upper).astype(jnp.bfloat16)
    hidden_after_second = hidden_after_first + matrix_product_transposed(active_low, proj_low)
    saved_acts = (
        centred_scaled_first,
        inverse_deviation_first,
        normed_one_low,
        mixed_low,
        attended_low,
        centred_scaled_second,
        inverse_deviation_second,
        normed_two_low,
        fc_upper,
        active_low,
    )
    return (saved_acts, hidden_after_second)


def block_backward(
    saved_acts,
    grad_two,
    segments,
    query_key_value_reduced,
    out_low,
    feedforward_weight_reduced,
    proj_low,
    norm_gain_vector,
):
    (
        centred_scaled_first,
        inverse_deviation_first,
        normed_one_low,
        mixed_low,
        attended_low,
        centred_scaled_second,
        inverse_deviation_second,
        normed_two_low,
        fc_upper,
        active_low,
    ) = saved_acts
    grad_mlp_low = grad_two.astype(jnp.bfloat16)
    grad_proj = matmul_tn(grad_mlp_low, active_low)
    grad_active = matmul(grad_mlp_low, proj_low)
    unused_value, gelu_pull = jax.vjp(jax.nn.gelu, fc_upper)
    (grad_upper,) = gelu_pull(grad_active)
    gradient_upper_reduced = grad_upper.astype(jnp.bfloat16)
    grad_fc = matmul_tn(normed_two_low, gradient_upper_reduced)
    grad_norm_two, grad_gain_two = norm_back(
        matrix_product_transposed(gradient_upper_reduced, feedforward_weight_reduced),
        centred_scaled_second,
        inverse_deviation_second,
        norm_gain_vector[1],
    )
    grad_one = grad_two + grad_norm_two
    grad_branch_low = grad_one.astype(jnp.bfloat16)
    grad_out = matmul_tn(grad_branch_low, attended_low)
    grad_attended = matmul(grad_branch_low, out_low).astype(jnp.bfloat16)
    gradient_mixed_reduced = attention_backward(mixed_low, grad_attended, *segments)
    grad_qkv = matmul_tn(normed_one_low, gradient_mixed_reduced)
    grad_norm_one, grad_gain_one = norm_back(
        matrix_product_transposed(gradient_mixed_reduced, query_key_value_reduced),
        centred_scaled_first,
        inverse_deviation_first,
        norm_gain_vector[0],
    )
    return (
        grad_one + grad_norm_one,
        (grad_qkv, grad_out, grad_fc, grad_proj, grad_gain_one, grad_gain_two),
    )


def head_pass(pred_low, word_table, token_weight):
    length, width = pred_low.shape
    words = word_table.shape[0]
    tile = 1024

    def kernel(pred_ref, table_ref, weight_ref, grad_table_ref, grad_pred_ref, log_ref, peak, total):
        phase, step = pl.program_id(0), pl.program_id(1)

        @pl.when((phase == 0) & (step == 0))
        def _():
            peak[...] = jnp.full_like(peak, -jnp.inf)
            total[...] = jnp.zeros_like(total)
            grad_pred_ref[...] = jnp.zeros_like(grad_pred_ref)

        table = table_ref[...]
        logits = nt_dot(table, pred_ref[...])

        @pl.when(phase == 0)
        def _():
            old = peak[...]
            new = jnp.maximum(old, jnp.max(logits, 0, keepdims=True))
            raised = jnp.sum(jnp.exp(logits - new), 0, keepdims=True)
            total[...] = total[...] * jnp.exp(old - new) + raised
            peak[...] = new

        @pl.when(phase == 1)
        def _():
            log_total = peak[...] + jnp.log(total[...])
            log_ref[...] = log_total
            grad_logits = (weight_ref[...] * jnp.exp(logits - log_total)).astype(jnp.bfloat16)
            grad_table_ref[...] = jnp.dot(
                grad_logits, pred_ref[...], preferred_element_type=jnp.float32
            )
            grad_pred_ref[...] += tn_dot(table, grad_logits)

    def whole(shape):
        return pl.BlockSpec(shape, lambda phase, step: (0, 0))

    return pl.pallas_call(
        kernel,
        out_shape=(
            jax.ShapeDtypeStruct((words, width), jnp.float32),
            jax.ShapeDtypeStruct((width, length), jnp.float32),
            jax.ShapeDtypeStruct((1, length), jnp.float32),
        ),
        grid_spec=pltpu.PrefetchScalarGridSpec(
            num_scalar_prefetch=0,
            grid=(2, words // tile),
            in_specs=[
                whole((length, width)),
                pl.BlockSpec((tile, width), lambda phase, step: (step, 0)),
                whole((1, length)),
            ],
            out_specs=[
                pl.BlockSpec((tile, width), lambda phase, step: (phase * step, 0)),
                whole((width, length)),
                whole((1, length)),
            ],
            scratch_shapes=[pltpu.VMEM((1, length), jnp.float32)] * 2,
        ),
        compiler_params=pltpu.CompilerParams(vmem_limit_bytes=48 << 20),
        name="head_pass",
    )(pred_low, word_table, token_weight)


def adam_update(master, moment, second, grad, rate, decay):
    moment_new = BETA_ONE * moment + (1.0 - BETA_ONE) * grad
    second_new = BETA_TWO * second + (1.0 - BETA_TWO) * grad * grad
    moment_hat = moment_new / (1.0 - BETA_ONE**ADAM_STEP)
    second_hat = second_new / (1.0 - BETA_TWO**ADAM_STEP)
    master_new = master - rate * (moment_hat / (jnp.sqrt(second_hat) + ADAM_EPS) + decay * master)
    return [moment_new, second_new, master_new]


AXES = ("bucket", "dp")


class Place:
    def __init__(self, buckets, columns):
        self.buckets, self.columns = buckets, columns
        self.count = buckets * columns
        self.line = columns // 2
        self.bits = [1 << place for place in range(1, columns.bit_length() - 1)]
        self.square = lax.axis_index("bucket")
        along = lax.axis_index("dp")
        self.core = along % 2
        self.along = along // 2
        self.flat = self.square * columns + along
        self.step_a = 1 + self.core
        self.step_b = 2 - self.core

    def swap(self, array, pick):
        pairs = [(member, member ^ pick(member)) for member in range(self.count)]
        return lax.ppermute(array, AXES, pairs)

    def swap_core(self, array):
        return self.swap(array, lambda member: 1)

    def swap_a(self, array):
        return self.swap(array, lambda member: self.columns * (1 + member % 2))

    def swap_b(self, array):
        return self.swap(array, lambda member: self.columns * (2 - member % 2))

    def swap_line(self, array, bit):
        return self.swap(array, lambda member: bit)

    def total(self, array):
        spans = [1] + self.bits + [self.columns, 2 * self.columns]
        for bit in spans:
            array = array + self.swap_line(array, bit)
        return array


def assemble(place, pieces):
    line, rows, cols = pieces[0].shape
    flags = jnp.stack([place.square, place.along, place.core]).astype(jnp.int32)

    def kernel(flags_ref, *refs):
        piece_refs, out_ref, held, load_sems, store_sem = refs[:8], *refs[8:]
        square, along, core = flags_ref[0], flags_ref[1], flags_ref[2]
        step_a, step_b = 1 + core, 2 - core
        spots = [
            (square, core),
            (square ^ step_a, core),
            (square ^ step_b, core),
            (square ^ 3, core),
            (square, 1 - core),
            (square ^ step_b, 1 - core),
            (square ^ step_a, 1 - core),
            (square ^ 3, 1 - core),
        ]
        loads = [
            pltpu.make_async_copy(piece_ref, held.at[at], load_sems.at[at])
            for at, piece_ref in enumerate(piece_refs)
        ]
        for load in loads:
            load.start()
        for at, (quarter, side) in enumerate(spots):
            loads[at].wait()
            for offset in range(line):
                pltpu.make_async_copy(
                    held.at[at, offset],
                    out_ref.at[quarter, along ^ offset, side],
                    store_sem,
                ).start()
        pltpu.make_async_copy(out_ref, out_ref, store_sem).wait()

    gathered = pl.pallas_call(
        kernel,
        out_shape=jax.ShapeDtypeStruct((4, line, 2, rows, cols), pieces[0].dtype),
        grid_spec=pltpu.PrefetchScalarGridSpec(
            num_scalar_prefetch=1,
            grid=(1,),
            in_specs=[pl.BlockSpec(memory_space=pl.ANY)] * 8,
            out_specs=pl.BlockSpec(memory_space=pl.ANY),
            scratch_shapes=[
                pltpu.VMEM((8, line, rows, cols), pieces[0].dtype),
                pltpu.SemaphoreType.DMA((8,)),
                pltpu.SemaphoreType.DMA(()),
            ],
        ),
        name="assemble",
    )(flags, *pieces)
    return gathered.reshape(8 * line * rows, cols)


def gather_rows(place, shard):
    own = shard[None]
    for bit in place.bits:
        own = jnp.concatenate([own, place.swap_line(own, bit)], 0)
    near_a = place.swap_a(own)
    near_b = place.swap_b(own)
    far = place.swap_b(near_a)
    mine = [own, near_a, near_b, far]
    return assemble(place, mine + [place.swap_core(piece) for piece in mine])


def scatter_sum(place, keep, send):
    rows = keep.shape[0] // place.count
    cols = keep.shape[1]
    across = place.swap_core(send)
    keep4 = keep.reshape(4, -1, cols)
    across4 = across.reshape(4, -1, cols)

    def quarter(index):
        return (
            lax.dynamic_index_in_dim(keep4, index, 0, False)
            + lax.dynamic_index_in_dim(across4, index, 0, False)
        )

    square = place.square
    first = jnp.stack([quarter(square ^ place.step_a), quarter(square ^ 3)])
    got_a = place.swap_a(first.astype(jnp.bfloat16)).astype(jnp.float32)
    second = (quarter(square ^ place.step_b) + got_a[1]).astype(jnp.bfloat16)
    got_b = place.swap_b(second).astype(jnp.float32)
    own = quarter(square) + got_a[0] + got_b
    own = own.reshape(place.line, 2, rows, cols)
    along = place.along
    for bit in place.bits:
        mine = along % 2
        own = own.reshape((own.shape[0] // 2, 2) + own.shape[1:])
        other = lax.dynamic_index_in_dim(own, 1 - mine, 1, False)
        own = lax.dynamic_index_in_dim(own, mine, 1, False) + place.swap_line(other, bit)
        along = along // 2
    own = own[0]
    other = lax.dynamic_index_in_dim(own, 1 - place.core, 0, False)
    kept = lax.dynamic_index_in_dim(own, place.core, 0, False)
    return kept, place.swap_core(other)


def in_order(place, kept, other, axis):
    return jnp.where(
        place.core == 0,
        jnp.concatenate([kept, other], axis),
        jnp.concatenate([other, kept], axis),
    )


def scatter_columns(place, grad):
    half = grad.shape[1] // 2
    keep = lax.dynamic_slice_in_dim(grad, place.core * half, half, 1)
    send = lax.dynamic_slice_in_dim(grad, (1 - place.core) * half, half, 1)
    kept, other = scatter_sum(place, keep, send)
    return in_order(place, kept, other, 1)


def scatter_table(place, grad):
    cols = grad.shape[1]
    half = grad.shape[0] // place.count // 2
    split = grad.reshape(place.count, 2, half, cols)
    keep = lax.dynamic_index_in_dim(split, place.core, 1, False).reshape(-1, cols)
    send = lax.dynamic_index_in_dim(split, 1 - place.core, 1, False).reshape(-1, cols)
    kept, other = scatter_sum(place, keep, send)
    return in_order(place, kept, other, 0)


def on_device(
    token_ids,
    segment_ids,
    live,
    timesteps,
    noise,
    embedding,
    embedding_moment,
    embedding_second,
    up_weight,
    up_moment,
    up_second,
    time_weight,
    time_moment,
    time_second,
    qkv_weight,
    qkv_moment,
    qkv_second,
    out_weight,
    out_moment,
    out_second,
    fc_weight,
    fc_moment,
    fc_second,
    proj_weight,
    proj_moment,
    proj_second,
    down_weight,
    down_moment,
    down_second,
    norm_gains,
    gains_moment,
    gains_second,
):
    masters = (
        embedding,
        up_weight,
        time_weight,
        qkv_weight,
        out_weight,
        fc_weight,
        proj_weight,
        down_weight,
        norm_gains,
    )
    moments = (
        embedding_moment,
        up_moment,
        time_moment,
        qkv_moment,
        out_moment,
        fc_moment,
        proj_moment,
        down_moment,
        gains_moment,
    )
    seconds = (
        embedding_second,
        up_second,
        time_second,
        qkv_second,
        out_second,
        fc_second,
        proj_second,
        down_second,
        gains_second,
    )
    place = Place(lax.axis_size("bucket"), lax.axis_size("dp"))
    buckets = place.buckets
    step_span = STEPS_T // buckets
    live_float = live[0].astype(jnp.float32)
    step_row = timesteps[0]
    onehot = (
        (step_row // step_span)[:, None] == jnp.arange(buckets, dtype=jnp.int32)[None, :]
    ).astype(jnp.float32)
    counts = place.total(jnp.sum(live_float[:, None] * onehot, 0))
    low = [member.astype(jnp.bfloat16) for member in masters]
    gains_pad = jnp.pad(low[8].T, ((0, 0), (0, EMB - 3)))
    word_table = gather_rows(place, low[0])
    entry_low = gather_rows(place, jnp.concatenate([low[1].T, low[2].T, gains_pad], 1))
    query_key_value_reduced = gather_rows(place, low[3])
    out_low = gather_rows(place, low[4].T)
    feedforward_weight_reduced = gather_rows(place, low[5])
    exit_low = gather_rows(place, jnp.concatenate([low[6].T, low[7]], 1))
    up_low = entry_low[:, :EMB]
    time_low = entry_low[:, EMB : EMB + D]
    gains_low = entry_low[:, EMB + D : EMB + D + 3].T
    ff_width = feedforward_weight_reduced.shape[1]
    proj_low = exit_low[:, :ff_width]
    down_weight_reduced = exit_low[:, ff_width:]
    norm_gain_vector = gains_low.astype(jnp.float32)
    tokens = token_ids[0]
    segments = (segment_ids, segment_ids.T, key_windows(segment_ids[0]))
    noise_row = noise[0]
    token_weight = live_float * jnp.sum(onehot / counts[None, :], -1) / buckets
    start_emb = word_table[tokens].astype(jnp.float32)
    fraction = step_row.astype(jnp.float32) / STEPS_T
    alpha_bar = 1.0 - jnp.sqrt(fraction + 0.0001)
    keep_root = jnp.sqrt(alpha_bar)[:, None]
    noisy_emb = keep_root * start_emb + jnp.sqrt(1.0 - alpha_bar)[:, None] * noise_row
    noisy_low = noisy_emb.astype(jnp.bfloat16)
    feature_low = sinusoid(step_row, D).astype(jnp.bfloat16)
    hidden_initial = matrix_product_transposed(
        noisy_low, up_low
    ) + matrix_product_transposed(feature_low, time_low)
    saved_acts, hidden_after_second = block_forward(
        hidden_initial,
        segments,
        query_key_value_reduced,
        out_low,
        feedforward_weight_reduced,
        proj_low,
        norm_gain_vector,
    )
    normalized_final, centred_scaled_final, inverse_deviation_final = layer_normalize(
        hidden_after_second, norm_gain_vector[2]
    )
    normed_top_low = normalized_final.astype(jnp.bfloat16)
    prediction = matmul(normed_top_low, down_weight_reduced)
    pred_low = prediction.astype(jnp.bfloat16)
    grad_table_head, grad_pred_head, log_total = head_pass(
        pred_low, word_table, token_weight[None, :]
    )
    pred_float = pred_low.astype(jnp.float32)
    target = jnp.sum(pred_float * start_emb, -1)
    cross_loss = log_total[0] - target
    target_prob = jnp.exp(target - log_total[0])
    target_shift = (token_weight * (target_prob - 1.0)).astype(jnp.bfloat16).astype(jnp.float32) - (
        token_weight * target_prob
    ).astype(jnp.bfloat16).astype(jnp.float32)
    target_shift = target_shift[:, None]
    pred_gap = prediction - start_emb
    loss_local = jnp.sum(token_weight * (jnp.mean(pred_gap * pred_gap, -1) + cross_loss))
    grad_mse = token_weight[:, None] * 2.0 * pred_gap / EMB
    gradient_prediction_reduced = (
        grad_mse + grad_pred_head.T + target_shift * start_emb
    ).astype(jnp.bfloat16)
    grad_down = matmul_tn(normed_top_low, gradient_prediction_reduced)
    grad_top, grad_gain_top = norm_back(
        matrix_product_transposed(gradient_prediction_reduced, down_weight_reduced),
        centred_scaled_final,
        inverse_deviation_final,
        norm_gain_vector[2],
    )
    grad_zero, block_grads = block_backward(
        saved_acts,
        grad_top,
        segments,
        query_key_value_reduced,
        out_low,
        feedforward_weight_reduced,
        proj_low,
        norm_gain_vector,
    )
    grad_qkv, grad_out, grad_fc, grad_proj, grad_gain_one, grad_gain_two = block_grads
    grad_zero_low = grad_zero.astype(jnp.bfloat16)
    grad_up = matmul_tn(grad_zero_low, noisy_low)
    grad_time = matmul_tn(grad_zero_low, feature_low)
    grad_start = keep_root * matmul(grad_zero_low, up_low) - grad_mse + target_shift * pred_float
    grad_table = grad_table_head + jax.ops.segment_sum(
        grad_start, tokens, num_segments=word_table.shape[0]
    )
    grad_gains = jnp.stack([grad_gain_one, grad_gain_two, grad_gain_top], 0)
    small = jnp.concatenate([grad_gains.reshape(-1, EMB), jnp.full((1, EMB), loss_local)], 0)
    small = place.total(small)
    loss_sum = small[-1, 0]
    own_cols = D // place.count
    shard_gains = lax.dynamic_slice_in_dim(
        small[:-1].reshape(3, D), place.flat * own_cols, own_cols, 1
    )
    shard_proj = scatter_columns(place, grad_proj)
    shard_fc = scatter_columns(place, grad_fc)
    shard_out = scatter_columns(place, grad_out)
    shard_qkv = scatter_columns(place, grad_qkv)
    shard_rest = scatter_columns(place, jnp.concatenate([grad_up, grad_time, grad_down], 1))
    shard_table = scatter_table(place, grad_table)
    shards = (
        shard_table,
        shard_rest[:, :EMB].T,
        shard_rest[:, EMB : EMB + D].T,
        shard_qkv,
        shard_out.T,
        shard_fc,
        shard_proj.T,
        shard_rest[:, EMB + D :],
        shard_gains,
    )
    squares_local = jnp.zeros((), jnp.float32)
    for member in shards:
        squares_local = squares_local + jnp.sum(member * member)
    squares = place.total(jnp.full((8, EMB), squares_local))[0, 0]
    grad_norm = jnp.sqrt(squares)
    factor = CLIP_NORM / jnp.maximum(grad_norm, CLIP_NORM)
    results = []
    for place in range(9):
        results = results + adam_update(
            masters[place],
            moments[place],
            seconds[place],
            factor * shards[place],
            RATES[place],
            DECAYS[place],
        )
    return (
        loss_sum,
        grad_norm,
        results[0],
        results[1],
        results[2],
        results[3],
        results[4],
        results[5],
        results[6],
        results[7],
        results[8],
        results[9],
        results[10],
        results[11],
        results[12],
        results[13],
        results[14],
        results[15],
        results[16],
        results[17],
        results[18],
        results[19],
        results[20],
        results[21],
        results[22],
        results[23],
        results[24],
        results[25],
        results[26],
    )


def solution(mesh):
    return jax.shard_map(
        on_device,
        mesh=mesh,
        in_specs=(
            P(("bucket", "dp"), None),
            P(("bucket", "dp"), None),
            P(("bucket", "dp"), None),
            P(("bucket", "dp"), None),
            P(("bucket", "dp"), None, None),
            P(("bucket", "dp"), None),
            P(("bucket", "dp"), None),
            P(("bucket", "dp"), None),
            P(None, ("bucket", "dp")),
            P(None, ("bucket", "dp")),
            P(None, ("bucket", "dp")),
            P(None, ("bucket", "dp")),
            P(None, ("bucket", "dp")),
            P(None, ("bucket", "dp")),
            P(("bucket", "dp"), None),
            P(("bucket", "dp"), None),
            P(("bucket", "dp"), None),
            P(None, ("bucket", "dp")),
            P(None, ("bucket", "dp")),
            P(None, ("bucket", "dp")),
            P(("bucket", "dp"), None),
            P(("bucket", "dp"), None),
            P(("bucket", "dp"), None),
            P(None, ("bucket", "dp")),
            P(None, ("bucket", "dp")),
            P(None, ("bucket", "dp")),
            P(("bucket", "dp"), None),
            P(("bucket", "dp"), None),
            P(("bucket", "dp"), None),
            P(None, ("bucket", "dp")),
            P(None, ("bucket", "dp")),
            P(None, ("bucket", "dp")),
        ),
        out_specs=(
            P(),
            P(),
            P(("bucket", "dp"), None),
            P(("bucket", "dp"), None),
            P(("bucket", "dp"), None),
            P(None, ("bucket", "dp")),
            P(None, ("bucket", "dp")),
            P(None, ("bucket", "dp")),
            P(None, ("bucket", "dp")),
            P(None, ("bucket", "dp")),
            P(None, ("bucket", "dp")),
            P(("bucket", "dp"), None),
            P(("bucket", "dp"), None),
            P(("bucket", "dp"), None),
            P(None, ("bucket", "dp")),
            P(None, ("bucket", "dp")),
            P(None, ("bucket", "dp")),
            P(("bucket", "dp"), None),
            P(("bucket", "dp"), None),
            P(("bucket", "dp"), None),
            P(None, ("bucket", "dp")),
            P(None, ("bucket", "dp")),
            P(None, ("bucket", "dp")),
            P(("bucket", "dp"), None),
            P(("bucket", "dp"), None),
            P(("bucket", "dp"), None),
            P(None, ("bucket", "dp")),
            P(None, ("bucket", "dp")),
            P(None, ("bucket", "dp")),
        ),
        check_vma=False,
    )
```

time: 1650 us -> 700 us (0.42)
  waiting for transfers between devices: 803 us -> 167 us
  blocking collectives: 242 us -> 0 us
  matrix products: 334 us -> 114 us
  Pallas kernels: 0 us -> 172 us
  starting transfers between devices: 1.39 us -> 83.5 us
  other arithmetic: 173 us -> 92 us
    reduce_scatter x6 -> x0, waiting for transfers between devices: 739 us -> none  [the longest x1 146 us: on_device(): lax.psum_scatter(grad_table, ('bucket', 'dp'), scatter_dimension=0, tiled...]
    pallas_call x0 -> x9, Pallas kernels: none -> 172 us  [the longest x1 56.5 us: attention_backward(): pl.pallas_call(kernel, out_shape=jax.ShapeDtypeStruct(mixed.shape, jnp.bf...]
    ppermute x0 -> x105, waiting for transfers between devices: none -> 167 us  [swap(): return lax.ppermute(array, AXES, pairs)]
    dot_general x14 -> x0, matrix products: 162 us -> none  [the longest x4 44.3 us: block_scores(): jnp.einsum('qhd,khd->hqk', query_blk, key_heads, preferred_element_type=j...]
    all_gather x3 -> x0, blocking collectives: 120 us -> none  [the longest x1 40.3 us: on_device(): lax.all_gather(lowered[8], ('bucket', 'dp'), axis=1, tiled=True)]
    ppermute x0 -> x105, starting transfers between devices: none -> 83.5 us  [swap(): return lax.ppermute(array, AXES, pairs)]
    psum x2 -> x0, blocking collectives: 82.1 us -> none  [the longest x1 42 us: on_device(): lax.psum(jnp.sum(live_float[:, None] * onehot, 0), ('bucket', 'dp'))]
    all_gather x6 -> x0, waiting for transfers between devices: 64.6 us -> none  [the longest x1 55.5 us: on_device(): lax.all_gather(lowered[6], ('bucket', 'dp'), axis=1, tiled=True)]
  transfers between devices with their start and end apart: 14 -> 105, of which waited for: 8 -> 41; matrix products, arithmetic and copies ran while one was open for 25% -> 20% of each run, Pallas kernels for 0% -> 10%
where the time goes in v1:
time: 700 us; the launch traced here: 692 us
  Pallas kernels  172 us (25%)
  waiting for transfers between devices  167 us (24%)
  matrix products  114 us (16%)
  other arithmetic  92 us (13%)
  starting transfers between devices  83.5 us (12%)
  local copies, waits for them, and re-layouts  52 us (7%)
  between operations  11 us (2%)
    ppermute x105, waiting for transfers between devices, swap(): return lax.ppermute(array, AXES, pairs)  167 us
    ppermute x105, starting transfers between devices, swap(): return lax.ppermute(array, AXES, pairs)  83.5 us
    pallas_call x1, Pallas kernels, attention_backward(): pl.pallas_call(kernel, out_shape=jax.ShapeDtypeStruct(mixed.shape, jnp.bf...  56.5 us
    pallas_call x1, Pallas kernels, attention_forward(): pl.pallas_call(kernel, out_shape=jax.ShapeDtypeStruct((length, width), jn...  54.9 us
    dot_general x6, matrix products, matmul(): return jnp.dot(left_op, right_op, preferred_element_type=jnp.float32)  46.8 us
    pallas_call x1, Pallas kernels, head_pass(): pl.pallas_call(kernel, out_shape=(jax.ShapeDtypeStruct((words, width), jn...  38.6 us
    dot_general x7, matrix products, matrix_product_transposed(): lax.dot_general(left_op, right_op, (((1,), (1,)), ((), ())), preferred_el...  38.2 us
    dot_general x7, matrix products, matmul_tn(): lax.dot_general(left_op, right_op, (((0,), (0,)), ((), ())), preferred_el...  29 us
  transfers between devices with their start and end apart: 105, of which 41 were waited for; matrix products, arithmetic and copies ran while one was open for 20% of the time, Pallas kernels for 10%

profile of v1, /device:TPU:0, one launch (start us, length us, event | category | flops | bytes accessed | tf_op | source)
XLA Modules:
  0.0 691.9 jit_solution(3777611719143127802)
XLA Ops:
  3.2 3.1 collective-permute-start.9
  13.8 7.0 %fusion.14 = (bf16[1024,384]{1,0:T(8,128)(2,1)S(1)}, bf16[1024,384]{1,0:T(8,128)(2,1)}) fusion(f32[384]{0:T(512)S(1)} %multiply_exponential_fusion, f32[1024]{0:T(1024)S(1)} %bitcast.302), kind=kLoop, calls=%fused_computation.46 | loop fusion | flops 1179648 | bytes 1578496 | tf_op jit(solution)/shard_map/convert.13
  28.6 3.0 collective-permute-start.56
  42.5 3.0 collective-permute-start.28
  45.6 3.4 collective-permute-done.28
  49.1 3.4 collective-permute-start.1
  59.9 2.5 collective-permute-start.12
  63.2 6.5 collective-permute-done.19
  69.7 2.9 collective-permute-start.46
  75.5 15.8 %collective-permute-done.37 = bf16[2,24,3072]{2,1,0:T(8,128)(2,1)S(1)} collective-permute-done((bf16[2,24,3072]{2,1,0:T(8,128)(2,1)S(1)}, bf16[2,24,3072]{2,1,0:T(8,128)(2,1)S(1)}, u32[]{:S(2)}, u32[]{:S(2)}) %collective-permute-start.37) | collective-permute-done | bytes 294944 | tf_op jit(solution)/shard_map/ppermute | solution.py:425
  91.3 6.5 collective-permute-done.46
  102.6 2.8 assemble.9
  106.2 2.9 assemble.7
  110.8 2.9 collective-permute-done.20.refs_1_
  115.0 4.6 fusion.24
  121.7 3.7 collective-permute-done.22.refs_3_
  126.7 3.3 assemble.6
  130.0 5.3 gather_fusion
  135.7 2.6 fusion.100
  144.5 3.5 assemble.8
  148.0 9.2 %convolution_convert_fusion.q_ref.k_ref.v_ref = bf16[1024,2304]{1,0:T(8,128)(2,1)} fusion(bf16[768,2304]{1,0:T(8,128)(2,1)} %bitcast.283, f32[1024,768]{0,1:T(8,128)} %copy-done.6, f32[768]{0:T(1024)S(1)} %get-tuple-element.50, f32[1024]{0:T(1024)S(1)} %add_rsqrt_fusion.2, f32[1024]{0:T(1024)S(1)} %broadcast_multiply_fusion.9), kind=kOutput, calls=%fused_computation.12 | convolution fusion | flops 3629383680 | bytes 11414528 | tf_op jit(solution)/shard_map/dot_general | solution.py:29
  157.2 54.9 %attention_forward.1 = bf16[1024,768]{1,0:T(8,128)(2,1)S(1)} custom-call(s32[2,8]{1,0:T(2,128)S(1)} %pad_add_fusion.windows_ref, bf16[1024,2304]{1,0:T(8,128)(2,1)} %convolution_convert_fusion.q_ref.k_ref.v_ref, bf16[1024,2304]{1,0:T(8,128)(2,1)} %convolution_convert_fusion.q_ref.k_ref.v_ref, bf16[1024,2304]{1,0:T(8,128)(2,1)} %convolution_convert_fusion.q_ref.k_ref.v_ref, ...), custom_call_target="tpu_custom_call" | custom-call | tf_op jit(solution)/shard_map/attention_forward/pallas_call | solution.py:149
  217.0 7.7 %collective-permute-done.49.refs_3_ = bf16[4,24,3200]{2,1,0:T(8,128)(2,1)} collective-permute-done((bf16[4,24,3200]{2,1,0:T(8,128)(2,1)}, bf16[4,24,3200]{2,1,0:T(8,128)(2,1)}, u32[]{:S(2)}, u32[]{:S(2)}) %collective-permute-start.49) | collective-permute-done | bytes 614432 | tf_op jit(solution)/shard_map/ppermute | solution.py:425
  224.6 4.7 assemble.10
  229.4 11.1 %fusion.86 = f32[1024,3072]{1,0:T(8,128)} fusion(bf16[768,3072]{1,0:T(8,128)(2,1)} %bitcast.237, f32[1024,768]{0,1:T(8,128)} %copy-done.4, f32[768]{0:T(1024)S(1)} %get-tuple-element.49, f32[1024]{0:T(1024)S(1)} %add_rsqrt_fusion.1, f32[1024]{0:T(1024)S(1)} %broadcast_multiply_fusion.8), kind=kOutput, calls=%fused_computation.325 | convolution fusion | flops 4834983936 | bytes 20458496 | tf_op jit(solution)/shard_map/dot_general | solution.py:29
  240.5 5.0 assemble.11
  245.4 10.3 %fusion.102 = (f32[1024]{0:T(1024)S(1)}, f32[1024,768]{0,1:T(8,128)S(1)}) fusion(f32[1024,768]{0,1:T(8,128)} %copy-done.4, bf16[768,3200]{1,0:T(8,128)(2,1)} %bitcast.270, f32[1024,3072]{1,0:T(8,128)} %fusion.86), kind=kOutput, calls=%fused_computation.328 | convolution fusion | flops 4861721600 | bytes 23597056 | tf_op jit(solution)/shard_map/dot_general | solution.py:39
  257.4 3.4 multiply_reduce_fusion.12
  260.8 38.6 %head_pass.1 = (f32[11264,128]{1,0:T(8,128)}, f32[128,1024]{1,0:T(8,128)S(1)}, f32[1,1024]{1,0:T(1,128)S(1)}) custom-call(bf16[1024,128]{1,0:T(8,128)(2,1)S(1)} %get-tuple-element.80.pred_ref, bf16[11264,128]{1,0:T(8,128)(2,1)S(1)} %bitcast.232, f32[1,1024]{1,0:T(1,128)S(1)} %multiply_multiply_fusion.11.weight_ref), custom_call_target="tpu_custom_call" | custom-call | tf_op jit(solution)/shard_map/head_pass/pallas_call | solution.py:370
  302.6 3.2 multiply_reduce_fusion.5
  307.3 2.5 subtract_multiply_fusion
  309.8 18.9 %fusion.6 = bf16[1024,3072]{1,0:T(8,128)(2,1)} fusion(f32[1024,3072]{1,0:T(8,128)} %fusion.86, bf16[768,3200]{1,0:T(8,128)(2,1)} %bitcast.273, f32[1024,768]{0,1:T(8,128)} %subtract_multiply_fusion), kind=kOutput, calls=%fused_computation.10 | convolution fusion | flops 4895539200 | bytes 26738688 | tf_op jit(solution)/shard_map/dot_general | solution.py:29
  328.7 8.1 %multiply_reduce_fusion.4 = (f32[1024]{0:T(1024)S(1)}, f32[768]{0:T(1024)S(1)}, f32[1024]{0:T(1024)S(1)}, f32[1024,768]{0,1:T(8,128)S(1)}) fusion(f32[1024,768]{0,1:T(8,128)S(1)} %copy-done.5, f32[768]{0:T(1024)S(1)} %get-tuple-element.49, f32[1024]{0:T(1024)S(1)} %add_rsqrt_fusion.1, f32[1024]{0:T(1024)S(1)} %broadcast_multiply_fusion.8, ...), kind=kOutput, calls=%fused_computation.25 | convolution fusion | flops 4838126592 | bytes 17324032 | tf_op jit(solution)/shard_map/dot_general | solution.py:39
  340.9 56.5 %attention_backward.1 = bf16[1024,2304]{1,0:T(8,128)(2,1)} custom-call(s32[2,8]{1,0:T(2,128)S(1)} %pad_add_fusion.windows_ref, bf16[1024,2304]{1,0:T(8,128)(2,1)} %convolution_convert_fusion.q_ref.k_ref.v_ref, bf16[1024,2304]{1,0:T(8,128)(2,1)} %convolution_convert_fusion.q_ref.k_ref.v_ref, bf16[1024,2304]{1,0:T(8,128)(2,1)} %convolution_convert_fusion.q_ref.k_ref.v_ref, ...), custom_call_target="tpu_custom_call" | custom-call | tf_op jit(solution)/shard_map/attention_backward/pallas_call | solution.py:219
  397.4 7.9 %multiply_reduce_fusion = (f32[1024]{0:T(1024)S(1)}, f32[768]{0:T(1024)S(1)}, f32[1024]{0:T(1024)S(1)}, f32[1024,768]{0,1:T(8,128)S(1)}) fusion(f32[1024,768]{0,1:T(8,128)S(1)} %copy-done.8, f32[768]{0:T(1024)S(1)} %get-tuple-element.50, f32[1024]{0:T(1024)S(1)} %add_rsqrt_fusion.2, f32[1024]{0:T(1024)S(1)} %broadcast_multiply_fusion.9, ...), kind=kOutput, calls=%fused_computation.20 | convolution fusion | flops 3630167296 | bytes 14571520 | tf_op jit(solution)/shard_map/dot_general | solution.py:39
  406.4 2.8 fusion.17
  409.2 2.8 fusion.26
  412.7 6.1 fusion.84
  418.8 2.8 fusion.30
  421.6 7.6 %fusion.85 = f32[768,3072]{1,0:T(8,128)} fusion(bf16[1024,3072]{1,0:T(8,128)(2,1)S(1)} %bitcast.311, f32[1024,768]{0,1:T(8,128)S(1)} %copy-done.5, f32[768]{0:T(1024)S(1)} %get-tuple-element.49, f32[1024]{0:T(1024)S(1)} %add_rsqrt_fusion.1, f32[1024]{0:T(1024)S(1)} %broadcast_multiply_fusion.8), kind=kOutput, calls=%fused_computation.324 | convolution fusion | flops 4834983936 | bytes 18885632 | tf_op jit(solution)/shard_map/dot_general | solution.py:33
  429.3 7.6 %fusion.33 = f32[768,3072]{1,0:T(8,128)} fusion(f32[1024,768]{0,1:T(8,128)S(1)} %copy-done.14, f32[1024,3072]{1,0:T(8,128)S(1)} %bitcast.256), kind=kOutput, calls=%fused_computation.86 | convolution fusion | flops 4860936192 | bytes 25165824 | tf_op jit(solution)/shard_map/dot_general | solution.py:33
  439.2 3.2 constant_dynamic-slice_fusion.8
  442.4 10.7 %scatter_fusion = f32[11264,128]{1,0:T(8,128)} fusion(f32[11264,128]{1,0:T(8,128)} %get-tuple-element.34, s32[1024]{0:T(1024)S(1)} %bitcast.307, f32[1024,128]{1,0:T(8,128)S(1)} %copy-done.26), kind=kCustom, calls=%fused_computation.1 | custom fusion | flops 131072 | bytes 1576960 | tf_op jit(solution)/shard_map/scatter-add | solution.py:728
  453.2 5.7 constant_dynamic-slice_fusion.18
  469.0 4.4 constant_dynamic-slice_fusion.3
  473.4 3.0 copy.88
  482.8 3.1 copy.89
  487.5 8.4 %constant_dynamic-slice_fusion.6 = (f32[768,1536]{1,0:T(8,128)}, f32[768,1536]{1,0:T(8,128)}) fusion(f32[768,3072]{1,0:T(8,128)} %fusion.33, s32[]{:T(128)S(6)} %select_n.339, s32[]{:T(128)S(6)} %select_n.340), kind=kLoop, calls=%fused_computation.237 | loop fusion | bytes 18874376 | tf_op jit(solution)/shard_map/dynamic_slice | solution.py:553
  500.1 5.7 collective-permute-done.85
  506.5 4.9 collective-permute-done.72
  521.7 4.7 collective-permute-done.74
  532.5 5.1 collective-permute-done.66
  546.2 3.2 collective-permute-done.67
  554.7 5.7 collective-permute-done.68
  568.7 8.0 %collective-permute-done.79 = f32[2,2,24,1152]{3,2,1,0:T(8,128)S(1)} collective-permute-done((f32[2,2,24,1152]{3,2,1,0:T(8,128)S(1)}, f32[2,2,24,1152]{3,2,1,0:T(8,128)S(1)}, u32[]{:S(2)}, u32[]{:S(2)}) %collective-permute-start.79) | collective-permute-done | bytes 442400 | tf_op jit(solution)/shard_map/ppermute | solution.py:425
  579.8 9.4 %collective-permute-done.80 = f32[1,2,24,1152]{3,2,1,0:T(8,128)S(1)} collective-permute-done((f32[1,2,24,1152]{3,2,1,0:T(8,128)S(1)}, f32[1,2,24,1152]{3,2,1,0:T(8,128)S(1)}, u32[]{:S(2)}, u32[]{:S(2)}) %collective-permute-start.80) | collective-permute-done | bytes 221216 | tf_op jit(solution)/shard_map/ppermute | solution.py:425
  597.7 3.2 collective-permute-done.90
  603.7 3.6 collective-permute-done.96
  609.2 3.2 collective-permute-start.97
  612.5 6.5 collective-permute-done.91
  620.4 16.4 %collective-permute-done.97 = f32[2,2,24,1536]{3,2,1,0:T(8,128)S(1)} collective-permute-done((f32[2,2,24,1536]{3,2,1,0:T(8,128)S(1)}, f32[2,2,24,1536]{3,2,1,0:T(8,128)S(1)}, u32[]{:S(2)}, u32[]{:S(2)}) %collective-permute-start.97) | collective-permute-done | bytes 589856 | tf_op jit(solution)/shard_map/ppermute | solution.py:425
  637.2 13.8 %collective-permute-done.98 = f32[1,2,24,1536]{3,2,1,0:T(8,128)S(1)} collective-permute-done((f32[1,2,24,1536]{3,2,1,0:T(8,128)S(1)}, f32[1,2,24,1536]{3,2,1,0:T(8,128)S(1)}, u32[]{:S(2)}, u32[]{:S(2)}) %collective-permute-start.98) | collective-permute-done | bytes 294944 | tf_op jit(solution)/shard_map/ppermute | solution.py:425
  661.9 3.6 collective-permute-done.101
  666.2 3.8 collective-permute-done.102
  (568 shorter events, 180.8 us)
Async XLA Ops:
  3.2 39.3 %collective-permute-start.9 = (bf16[1,24,1024]{2,1,0:T(8,128)(2,1)S(1)}, bf16[1,24,1024]{2,1,0:T(8,128)(2,1)S(1)}, u32[]{:S(2)}, u32[]{:S(2)}) collective-permute-start(bf16[1,24,1024]{2,1,0:T(8,128)(2,1)S(1)} %fusion.73), channel_id=1, source_target_pairs={{0,2},{1,3},{2,0},{3,1},{4,6},{5,7},{6,4},{7,5},{8,10},{9,11},{10,... | collective-permute-start | bytes 147464 | tf_op jit(solution)/shard_map/ppermute | solution.py:425
  7.2 38.3 %collective-permute-start = (bf16[1,352,128]{2,1,0:T(8,128)(2,1)S(1)}, bf16[1,352,128]{2,1,0:T(8,128)(2,1)S(1)}, u32[]{:S(2)}, u32[]{:S(2)}) collective-permute-start(bf16[1,352,128]{2,1,0:T(8,128)(2,1)S(1)} %convert_bitcast_fusion.3), channel_id=1, source_target_pairs={{0,2},{1,3},{2,0},{3,1},{4,6},{5,7},{6,4},{7,5},{8,10},{9,11},{10,... | collective-permute-start | bytes 270344 | tf_op jit(solution)/shard_map/ppermute | solution.py:425
  8.2 44.3 %collective-permute-start.18 = (bf16[1,24,2304]{2,1,0:T(8,128)(2,1)S(1)}, bf16[1,24,2304]{2,1,0:T(8,128)(2,1)S(1)}, u32[]{:S(2)}, u32[]{:S(2)}) collective-permute-start(bf16[1,24,2304]{2,1,0:T(8,128)(2,1)S(1)} %convert_bitcast_fusion.2), channel_id=1, source_target_pairs={{0,2},{1,3},{2,0},{3,1},{4,6},{5,7},{6,4},{7,5},{8,10},{9,11},{10,... | collective-permute-start | bytes 331784 | tf_op jit(solution)/shard_map/ppermute | solution.py:425
  11.2 31.1 %collective-permute-start.27 = (bf16[1,24,768]{2,1,0:T(8,128)(2,1)S(1)}, bf16[1,24,768]{2,1,0:T(8,128)(2,1)S(1)}, u32[]{:S(2)}, u32[]{:S(2)}) collective-permute-start(bf16[1,24,768]{2,1,0:T(8,128)(2,1)S(1)} %convert_bitcast_fusion.4), channel_id=1, source_target_pairs={{0,2},{1,3},{2,0},{3,1},{4,6},{5,7},{6,4},{7,5},{8,10},{9,11},{10,... | collective-permute-start | bytes 110600 | tf_op jit(solution)/shard_map/ppermute | solution.py:425
  13.5 11.6 %collective-permute-start.54 = (f32[4]{0:T(128)S(1)}, f32[4]{0:T(128)S(1)}, u32[]{:S(2)}, u32[]{:S(2)}) collective-permute-start(f32[4]{0:T(128)S(1)} %select_reduce_fusion.2), channel_id=1, source_target_pairs={{0,1},{1,0},{2,3},{3,2},{4,5},{5,4},{6,7},{7,6},{8,9},{9,8},{10,11... | collective-permute-start | bytes 56 | tf_op jit(solution)/shard_map/ppermute | solution.py:425
  40.3 15.8 %collective-permute-start.45 = (bf16[1,24,3200]{2,1,0:T(8,128)(2,1)S(1)}, bf16[1,24,3200]{2,1,0:T(8,128)(2,1)S(1)}, u32[]{:S(2)}, u32[]{:S(2)}) collective-permute-start(bf16[1,24,3200]{2,1,0:T(8,128)(2,1)S(1)} %maximum_bitcast_fusion), channel_id=1, source_target_pairs={{0,2},{1,3},{2,0},{3,1},{4,6},{5,7},{6,4},{7,5},{8,10},{9,11},{10,... | collective-permute-start | bytes 460808 | tf_op jit(solution)/shard_map/ppermute | solution.py:425
  42.3 13.7 %collective-permute-start.36 = (bf16[1,24,3072]{2,1,0:T(8,128)(2,1)S(1)}, bf16[1,24,3072]{2,1,0:T(8,128)(2,1)S(1)}, u32[]{:S(2)}, u32[]{:S(2)}) collective-permute-start(bf16[1,24,3072]{2,1,0:T(8,128)(2,1)S(1)} %convert_bitcast_fusion.1), channel_id=1, source_target_pairs={{0,2},{1,3},{2,0},{3,1},{4,6},{5,7},{6,4},{7,5},{8,10},{9,11},{10,... | collective-permute-start | bytes 442376 | tf_op jit(solution)/shard_map/ppermute | solution.py:425
  49.1 13.4 %collective-permute-start.1 = (bf16[2,352,128]{2,1,0:T(8,128)(2,1)S(1)}, bf16[2,352,128]{2,1,0:T(8,128)(2,1)S(1)}, u32[]{:S(2)}, u32[]{:S(2)}) collective-permute-start(bf16[2,352,128]{2,1,0:T(8,128)(2,1)S(1)} %pad_maximum_fusion.18), channel_id=1, source_target_pairs={{0,4},{1,5},{2,6},{3,7},{4,0},{5,1},{6,2},{7,3},{8,12},{9,13},{10,... | collective-permute-start | bytes 540680 | tf_op jit(solution)/shard_map/ppermute | solution.py:425
  56.1 13.5 %collective-permute-start.19 = (bf16[2,24,2304]{2,1,0:T(8,128)(2,1)S(1)}, bf16[2,24,2304]{2,1,0:T(8,128)(2,1)S(1)}, u32[]{:S(2)}, u32[]{:S(2)}) collective-permute-start(bf16[2,24,2304]{2,1,0:T(8,128)(2,1)S(1)} %pad_maximum_fusion.16), channel_id=1, source_target_pairs={{0,4},{1,5},{2,6},{3,7},{4,0},{5,1},{6,2},{7,3},{8,12},{9,13},{10,... | collective-permute-start | bytes 663560 | tf_op jit(solution)/shard_map/ppermute | solution.py:425
  57.8 11.9 %collective-permute-start.11 = (bf16[4,24,1024]{2,1,0:T(8,128)(2,1)S(1)}, bf16[4,24,1024]{2,1,0:T(8,128)(2,1)S(1)}, u32[]{:S(2)}, u32[]{:S(2)}) collective-permute-start(bf16[4,24,1024]{2,1,0:T(8,128)(2,1)S(1)} %pad_maximum_fusion.17.refs_0_), channel_id=1, source_target_pairs={{0,8},{1,17},{2,10},{3,19},{4,12},{5,21},{6,14},{7,23},{8,0},{9,25... | collective-permute-start | bytes 589832 | tf_op jit(solution)/shard_map/ppermute | solution.py:425
  59.9 12.6 %collective-permute-start.12 = (bf16[4,24,1024]{2,1,0:T(8,128)(2,1)S(1)}, bf16[4,24,1024]{2,1,0:T(8,128)(2,1)S(1)}, u32[]{:S(2)}, u32[]{:S(2)}) collective-permute-start(bf16[4,24,1024]{2,1,0:T(8,128)(2,1)S(1)} %pad_maximum_fusion.17.refs_0_), channel_id=1, source_target_pairs={{0,16},{1,9},{2,18},{3,11},{4,20},{5,13},{6,22},{7,15},{8,24},{9,1... | collective-permute-start | bytes 589832 | tf_op jit(solution)/shard_map/ppermute | solution.py:425
  62.4 10.7 %collective-permute-start.31 = (bf16[4,24,768]{2,1,0:T(8,128)(2,1)S(1)}, bf16[4,24,768]{2,1,0:T(8,128)(2,1)S(1)}, u32[]{:S(2)}, u32[]{:S(2)}) collective-permute-start(bf16[4,24,768]{2,1,0:T(8,128)(2,1)S(1)} %collective-permute-done.29.refs_1_), channel_id=1, source_target_pairs={{0,16},{1,9},{2,18},{3,11},{4,20},{5,13},{6,22},{7,15},{8,24},{9,1... | collective-permute-start | bytes 442376 | tf_op jit(solution)/shard_map/ppermute | solution.py:425
  69.6 21.6 %collective-permute-start.37 = (bf16[2,24,3072]{2,1,0:T(8,128)(2,1)S(1)}, bf16[2,24,3072]{2,1,0:T(8,128)(2,1)S(1)}, u32[]{:S(2)}, u32[]{:S(2)}) collective-permute-start(bf16[2,24,3072]{2,1,0:T(8,128)(2,1)S(1)} %pad_maximum_fusion.14), channel_id=1, source_target_pairs={{0,4},{1,5},{2,6},{3,7},{4,0},{5,1},{6,2},{7,3},{8,12},{9,13},{10,... | collective-permute-start | bytes 884744 | tf_op jit(solution)/shard_map/ppermute | solution.py:425
  69.7 28.1 %collective-permute-start.46 = (bf16[2,24,3200]{2,1,0:T(8,128)(2,1)S(1)}, bf16[2,24,3200]{2,1,0:T(8,128)(2,1)S(1)}, u32[]{:S(2)}, u32[]{:S(2)}) collective-permute-start(bf16[2,24,3200]{2,1,0:T(8,128)(2,1)S(1)} %pad_maximum_fusion.13), channel_id=1, source_target_pairs={{0,4},{1,5},{2,6},{3,7},{4,0},{5,1},{6,2},{7,3},{8,12},{9,13},{10,... | collective-permute-start | bytes 921608 | tf_op jit(solution)/shard_map/ppermute | solution.py:425
  73.3 27.7 %collective-permute-start.2 = (bf16[4,352,128]{2,1,0:T(8,128)(2,1)S(1)}, bf16[4,352,128]{2,1,0:T(8,128)(2,1)}, u32[]{:S(2)}, u32[]{:S(2)}) collective-permute-start(bf16[4,352,128]{2,1,0:T(8,128)(2,1)S(1)} %pad_maximum_fusion.12.refs_0_), channel_id=1, source_target_pairs={{0,8},{1,17},{2,10},{3,19},{4,12},{5,21},{6,14},{7,23},{8,0},{9,25... | collective-permute-start | bytes 1081352 | tf_op jit(solution)/shard_map/ppermute | solution.py:425
  74.9 23.9 %collective-permute-start.13 = (bf16[4,24,1024]{2,1,0:T(8,128)(2,1)S(1)}, bf16[4,24,1024]{2,1,0:T(8,128)(2,1)S(1)}, u32[]{:S(2)}, u32[]{:S(2)}) collective-permute-start(bf16[4,24,1024]{2,1,0:T(8,128)(2,1)S(1)} %collective-permute-done.11.refs_1_), channel_id=1, source_target_pairs={{0,16},{1,9},{2,18},{3,11},{4,20},{5,13},{6,22},{7,15},{8,24},{9,1... | collective-permute-start | bytes 589832 | tf_op jit(solution)/shard_map/ppermute | solution.py:425
  75.5 23.8 %collective-permute-start.15 = (bf16[4,24,1024]{2,1,0:T(8,128)(2,1)S(1)}, bf16[4,24,1024]{2,1,0:T(8,128)(2,1)S(1)}, u32[]{:S(2)}, u32[]{:S(2)}) collective-permute-start(bf16[4,24,1024]{2,1,0:T(8,128)(2,1)S(1)} %collective-permute-done.11.refs_1_), channel_id=1, source_target_pairs={{0,1},{1,0},{2,3},{3,2},{4,5},{5,4},{6,7},{7,6},{8,9},{9,8},{10,11... | collective-permute-start | bytes 589832 | tf_op jit(solution)/shard_map/ppermute | solution.py:425
  98.8 11.4 %collective-permute-start.3 = (bf16[4,352,128]{2,1,0:T(8,128)(2,1)S(1)}, bf16[4,352,128]{2,1,0:T(8,128)(2,1)}, u32[]{:S(2)}, u32[]{:S(2)}) collective-permute-start(bf16[4,352,128]{2,1,0:T(8,128)(2,1)S(1)} %pad_maximum_fusion.12.refs_0_), channel_id=1, source_target_pairs={{0,16},{1,9},{2,18},{3,11},{4,20},{5,13},{6,22},{7,15},{8,24},{9,1... | collective-permute-start | bytes 1081352 | tf_op jit(solution)/shard_map/ppermute | solution.py:425
  99.2 11.1 %collective-permute-start.5 = (bf16[4,352,128]{2,1,0:T(8,128)(2,1)S(1)}, bf16[4,352,128]{2,1,0:T(8,128)(2,1)}, u32[]{:S(2)}, u32[]{:S(2)}) collective-permute-start(bf16[4,352,128]{2,1,0:T(8,128)(2,1)S(1)} %pad_maximum_fusion.12.refs_0_), channel_id=1, source_target_pairs={{0,1},{1,0},{2,3},{3,2},{4,5},{5,4},{6,7},{7,6},{8,9},{9,8},{10,11... | collective-permute-start | bytes 1081352 | tf_op jit(solution)/shard_map/ppermute | solution.py:425
  100.5 13.2 %collective-permute-start.20 = (bf16[4,24,2304]{2,1,0:T(8,128)(2,1)S(1)}, bf16[4,24,2304]{2,1,0:T(8,128)(2,1)}, u32[]{:S(2)}, u32[]{:S(2)}) collective-permute-start(bf16[4,24,2304]{2,1,0:T(8,128)(2,1)S(1)} %pad_maximum_fusion.10.refs_0_), channel_id=1, source_target_pairs={{0,8},{1,17},{2,10},{3,19},{4,12},{5,21},{6,14},{7,23},{8,0},{9,25... | collective-permute-start | bytes 1327112 | tf_op jit(solution)/shard_map/ppermute | solution.py:425
  101.2 13.7 %collective-permute-start.4 = (bf16[4,352,128]{2,1,0:T(8,128)(2,1)}, bf16[4,352,128]{2,1,0:T(8,128)(2,1)}, u32[]{:S(2)}, u32[]{:S(2)}) collective-permute-start(bf16[4,352,128]{2,1,0:T(8,128)(2,1)} %collective-permute-done.2.refs_1_), channel_id=1, source_target_pairs={{0,16},{1,9},{2,18},{3,11},{4,20},{5,13},{6,22},{7,15},{8,24},{9,1... | collective-permute-start | bytes 1081352 | tf_op jit(solution)/shard_map/ppermute | solution.py:425
  105.4 14.2 %collective-permute-start.21 = (bf16[4,24,2304]{2,1,0:T(8,128)(2,1)S(1)}, bf16[4,24,2304]{2,1,0:T(8,128)(2,1)}, u32[]{:S(2)}, u32[]{:S(2)}) collective-permute-start(bf16[4,24,2304]{2,1,0:T(8,128)(2,1)S(1)} %pad_maximum_fusion.10.refs_0_), channel_id=1, source_target_pairs={{0,16},{1,9},{2,18},{3,11},{4,20},{5,13},{6,22},{7,15},{8,24},{9,1... | collective-permute-start | bytes 1327112 | tf_op jit(solution)/shard_map/ppermute | solution.py:425
  110.3 11.4 %collective-permute-start.7 = (bf16[4,352,128]{2,1,0:T(8,128)(2,1)}, bf16[4,352,128]{2,1,0:T(8,128)(2,1)S(1)}, u32[]{:S(2)}, u32[]{:S(2)}) collective-permute-start(bf16[4,352,128]{2,1,0:T(8,128)(2,1)} %collective-permute-done.3.refs_2_), channel_id=1, source_target_pairs={{0,1},{1,0},{2,3},{3,2},{4,5},{5,4},{6,7},{7,6},{8,9},{9,8},{10,11... | collective-permute-start | bytes 1081352 | tf_op jit(solution)/shard_map/ppermute | solution.py:425
  113.7 11.7 %collective-permute-start.22 = (bf16[4,24,2304]{2,1,0:T(8,128)(2,1)}, bf16[4,24,2304]{2,1,0:T(8,128)(2,1)S(1)}, u32[]{:S(2)}, u32[]{:S(2)}) collective-permute-start(bf16[4,24,2304]{2,1,0:T(8,128)(2,1)} %collective-permute-done.20.refs_1_), channel_id=1, source_target_pairs={{0,16},{1,9},{2,18},{3,11},{4,20},{5,13},{6,22},{7,15},{8,24},{9,1... | collective-permute-start | bytes 1327112 | tf_op jit(solution)/shard_map/ppermute | solution.py:425
  119.6 20.7 %collective-permute-start.23 = (bf16[4,24,2304]{2,1,0:T(8,128)(2,1)S(1)}, bf16[4,24,2304]{2,1,0:T(8,128)(2,1)}, u32[]{:S(2)}, u32[]{:S(2)}) collective-permute-start(bf16[4,24,2304]{2,1,0:T(8,128)(2,1)S(1)} %pad_maximum_fusion.10.refs_0_), channel_id=1, source_target_pairs={{0,1},{1,0},{2,3},{3,2},{4,5},{5,4},{6,7},{7,6},{8,9},{9,8},{10,11... | collective-permute-start | bytes 1327112 | tf_op jit(solution)/shard_map/ppermute | solution.py:425
  120.2 20.3 %collective-permute-start.38 = (bf16[4,24,3072]{2,1,0:T(8,128)(2,1)}, bf16[4,24,3072]{2,1,0:T(8,128)(2,1)}, u32[]{:S(2)}, u32[]{:S(2)}) collective-permute-start(bf16[4,24,3072]{2,1,0:T(8,128)(2,1)} %pad_maximum_fusion.9.refs_0_), channel_id=1, source_target_pairs={{0,8},{1,17},{2,10},{3,19},{4,12},{5,21},{6,14},{7,23},{8,0},{9,25... | collective-permute-start | bytes 1769480 | tf_op jit(solution)/shard_map/ppermute | solution.py:425
  121.7 20.0 %collective-permute-start.24 = (bf16[4,24,2304]{2,1,0:T(8,128)(2,1)}, bf16[4,24,2304]{2,1,0:T(8,128)(2,1)}, u32[]{:S(2)}, u32[]{:S(2)}) collective-permute-start(bf16[4,24,2304]{2,1,0:T(8,128)(2,1)} %collective-permute-done.20.refs_1_), channel_id=1, source_target_pairs={{0,1},{1,0},{2,3},{3,2},{4,5},{5,4},{6,7},{7,6},{8,9},{9,8},{10,11... | collective-permute-start | bytes 1327112 | tf_op jit(solution)/shard_map/ppermute | solution.py:425
  125.4 17.0 %collective-permute-start.25 = (bf16[4,24,2304]{2,1,0:T(8,128)(2,1)}, bf16[4,24,2304]{2,1,0:T(8,128)(2,1)}, u32[]{:S(2)}, u32[]{:S(2)}) collective-permute-start(bf16[4,24,2304]{2,1,0:T(8,128)(2,1)} %collective-permute-done.21.refs_2_), channel_id=1, source_target_pairs={{0,1},{1,0},{2,3},{3,2},{4,5},{5,4},{6,7},{7,6},{8,9},{9,8},{10,11... | collective-permute-start | bytes 1327112 | tf_op jit(solution)/shard_map/ppermute | solution.py:425
  126.3 17.7 %collective-permute-start.26 = (bf16[4,24,2304]{2,1,0:T(8,128)(2,1)S(1)}, bf16[4,24,2304]{2,1,0:T(8,128)(2,1)}, u32[]{:S(2)}, u32[]{:S(2)}) collective-permute-start(bf16[4,24,2304]{2,1,0:T(8,128)(2,1)S(1)} %collective-permute-done.22.refs_3_), channel_id=1, source_target_pairs={{0,1},{1,0},{2,3},{3,2},{4,5},{5,4},{6,7},{7,6},{8,9},{9,8},{10,11... | collective-permute-start | bytes 1327112 | tf_op jit(solution)/shard_map/ppermute | solution.py:425
  140.4 73.2 %collective-permute-start.39 = (bf16[4,24,3072]{2,1,0:T(8,128)(2,1)}, bf16[4,24,3072]{2,1,0:T(8,128)(2,1)}, u32[]{:S(2)}, u32[]{:S(2)}) collective-permute-start(bf16[4,24,3072]{2,1,0:T(8,128)(2,1)} %pad_maximum_fusion.9.refs_0_), channel_id=1, source_target_pairs={{0,16},{1,9},{2,18},{3,11},{4,20},{5,13},{6,22},{7,15},{8,24},{9,1... | collective-permute-start | bytes 1769480 | tf_op jit(solution)/shard_map/ppermute | solution.py:425
  140.5 73.2 %collective-permute-start.41 = (bf16[4,24,3072]{2,1,0:T(8,128)(2,1)}, bf16[4,24,3072]{2,1,0:T(8,128)(2,1)}, u32[]{:S(2)}, u32[]{:S(2)}) collective-permute-start(bf16[4,24,3072]{2,1,0:T(8,128)(2,1)} %pad_maximum_fusion.9.refs_0_), channel_id=1, source_target_pairs={{0,1},{1,0},{2,3},{3,2},{4,5},{5,4},{6,7},{7,6},{8,9},{9,8},{10,11... | collective-permute-start | bytes 1769480 | tf_op jit(solution)/shard_map/ppermute | solution.py:425
  141.7 72.5 %collective-permute-start.47 = (bf16[4,24,3200]{2,1,0:T(8,128)(2,1)S(1)}, bf16[4,24,3200]{2,1,0:T(8,128)(2,1)}, u32[]{:S(2)}, u32[]{:S(2)}) collective-permute-start(bf16[4,24,3200]{2,1,0:T(8,128)(2,1)S(1)} %pad_maximum_fusion.8.refs_0_), channel_id=1, source_target_pairs={{0,8},{1,17},{2,10},{3,19},{4,12},{5,21},{6,14},{7,23},{8,0},{9,25... | collective-permute-start | bytes 1843208 | tf_op jit(solution)/shard_map/ppermute | solution.py:425
  142.4 73.1 %collective-permute-start.48 = (bf16[4,24,3200]{2,1,0:T(8,128)(2,1)S(1)}, bf16[4,24,3200]{2,1,0:T(8,128)(2,1)}, u32[]{:S(2)}, u32[]{:S(2)}) collective-permute-start(bf16[4,24,3200]{2,1,0:T(8,128)(2,1)S(1)} %pad_maximum_fusion.8.refs_0_), channel_id=1, source_target_pairs={{0,16},{1,9},{2,18},{3,11},{4,20},{5,13},{6,22},{7,15},{8,24},{9,1... | collective-permute-start | bytes 1843208 | tf_op jit(solution)/shard_map/ppermute | solution.py:425
  144.0 70.2 %collective-permute-start.40 = (bf16[4,24,3072]{2,1,0:T(8,128)(2,1)}, bf16[4,24,3072]{2,1,0:T(8,128)(2,1)}, u32[]{:S(2)}, u32[]{:S(2)}) collective-permute-start(bf16[4,24,3072]{2,1,0:T(8,128)(2,1)} %collective-permute-done.38.refs_1_), channel_id=1, source_target_pairs={{0,16},{1,9},{2,18},{3,11},{4,20},{5,13},{6,22},{7,15},{8,24},{9,1... | collective-permute-start | bytes 1769480 | tf_op jit(solution)/shard_map/ppermute | solution.py:425
  215.6 24.9 %collective-permute-start.50 = (bf16[4,24,3200]{2,1,0:T(8,128)(2,1)S(1)}, bf16[4,24,3200]{2,1,0:T(8,128)(2,1)}, u32[]{:S(2)}, u32[]{:S(2)}) collective-permute-start(bf16[4,24,3200]{2,1,0:T(8,128)(2,1)S(1)} %pad_maximum_fusion.8.refs_0_), channel_id=1, source_target_pairs={{0,1},{1,0},{2,3},{3,2},{4,5},{5,4},{6,7},{7,6},{8,9},{9,8},{10,11... | collective-permute-start | bytes 1843208 | tf_op jit(solution)/shard_map/ppermute | solution.py:425
  216.0 24.5 %collective-permute-start.51 = (bf16[4,24,3200]{2,1,0:T(8,128)(2,1)}, bf16[4,24,3200]{2,1,0:T(8,128)(2,1)}, u32[]{:S(2)}, u32[]{:S(2)}) collective-permute-start(bf16[4,24,3200]{2,1,0:T(8,128)(2,1)} %collective-permute-done.47.refs_1_), channel_id=1, source_target_pairs={{0,1},{1,0},{2,3},{3,2},{4,5},{5,4},{6,7},{7,6},{8,9},{9,8},{10,11... | collective-permute-start | bytes 1843208 | tf_op jit(solution)/shard_map/ppermute | solution.py:425
  216.8 23.6 %collective-permute-start.52 = (bf16[4,24,3200]{2,1,0:T(8,128)(2,1)}, bf16[4,24,3200]{2,1,0:T(8,128)(2,1)}, u32[]{:S(2)}, u32[]{:S(2)}) collective-permute-start(bf16[4,24,3200]{2,1,0:T(8,128)(2,1)} %collective-permute-done.48.refs_2_), channel_id=1, source_target_pairs={{0,1},{1,0},{2,3},{3,2},{4,5},{5,4},{6,7},{7,6},{8,9},{9,8},{10,11... | collective-permute-start | bytes 1843208 | tf_op jit(solution)/shard_map/ppermute | solution.py:425
  224.6 15.8 %collective-permute-start.53 = (bf16[4,24,3200]{2,1,0:T(8,128)(2,1)}, bf16[4,24,3200]{2,1,0:T(8,128)(2,1)}, u32[]{:S(2)}, u32[]{:S(2)}) collective-permute-start(bf16[4,24,3200]{2,1,0:T(8,128)(2,1)} %collective-permute-done.49.refs_3_), channel_id=1, source_target_pairs={{0,1},{1,0},{2,3},{3,2},{4,5},{5,4},{6,7},{7,6},{8,9},{9,8},{10,11... | collective-permute-start | bytes 1843208 | tf_op jit(solution)/shard_map/ppermute | solution.py:425
  437.7 23.9 %collective-permute-start.59 = (f32[19,128]{1,0:T(8,128)S(1)}, f32[19,128]{1,0:T(8,128)S(1)}, u32[]{:S(2)}, u32[]{:S(2)}) collective-permute-start(f32[19,128]{1,0:T(8,128)S(1)} %concatenate.109), channel_id=1, source_target_pairs={{0,1},{1,0},{2,3},{3,2},{4,5},{5,4},{6,7},{7,6},{8,9},{9,8},{10,11... | collective-permute-start | bytes 29192 | tf_op jit(solution)/shard_map/ppermute | solution.py:425
  442.4 24.1 %collective-permute-start.82 = (f32[768,384]{1,0:T(8,128)}, f32[768,384]{1,0:T(8,128)}, u32[]{:S(2)}, u32[]{:S(2)}) collective-permute-start(f32[768,384]{1,0:T(8,128)} %get-tuple-element.104), channel_id=1, source_target_pairs={{0,1},{1,0},{2,3},{3,2},{4,5},{5,4},{6,7},{7,6},{8,9},{9,8},{10,11... | collective-permute-start | bytes 3538952 | tf_op jit(solution)/shard_map/ppermute | solution.py:425
  458.9 53.7 %collective-permute-start.64 = (f32[5632,128]{1,0:T(8,128)}, f32[5632,128]{1,0:T(8,128)}, u32[]{:S(2)}, u32[]{:S(2)}) collective-permute-start(f32[5632,128]{1,0:T(8,128)} %bitcast.40), channel_id=1, source_target_pairs={{0,1},{1,0},{2,3},{3,2},{4,5},{5,4},{6,7},{7,6},{8,9},{9,8},{10,11... | collective-permute-start | bytes 8650760 | tf_op jit(solution)/shard_map/ppermute | solution.py:425
  461.5 21.3 %collective-permute-start.70 = (f32[768,512]{0,1:T(8,128)}, f32[768,512]{0,1:T(8,128)}, u32[]{:S(2)}, u32[]{:S(2)}) collective-permute-start(f32[768,512]{0,1:T(8,128)} %get-tuple-element.100), channel_id=1, source_target_pairs={{0,1},{1,0},{2,3},{3,2},{4,5},{5,4},{6,7},{7,6},{8,9},{9,8},{10,11... | collective-permute-start | bytes 4718600 | tf_op jit(solution)/shard_map/ppermute | solution.py:425
  465.1 65.0 %collective-permute-start.76 = (f32[768,1152]{1,0:T(8,128)}, f32[768,1152]{1,0:T(8,128)}, u32[]{:S(2)}, u32[]{:S(2)}) collective-permute-start(f32[768,1152]{1,0:T(8,128)} %get-tuple-element.92), channel_id=1, source_target_pairs={{0,1},{1,0},{2,3},{3,2},{4,5},{5,4},{6,7},{7,6},{8,9},{9,8},{10,11... | collective-permute-start | bytes 10616840 | tf_op jit(solution)/shard_map/ppermute | solution.py:425
  477.2 18.8 %collective-permute-start.62 = (f32[19,128]{1,0:T(8,128)S(1)}, f32[19,128]{1,0:T(8,128)}, u32[]{:S(2)}, u32[]{:S(2)}) collective-permute-start(f32[19,128]{1,0:T(8,128)S(1)} %add.787), channel_id=1, source_target_pairs={{0,8},{1,9},{2,10},{3,11},{4,12},{5,13},{6,14},{7,15},{8,0},{9,1},... | collective-permute-start | bytes 29192 | tf_op jit(solution)/shard_map/ppermute | solution.py:425
  482.8 15.1 %collective-permute-start.84 = (bf16[192,384]{1,0:T(8,128)(2,1)}, bf16[192,384]{1,0:T(8,128)(2,1)}, u32[]{:S(2)}, u32[]{:S(2)}) collective-permute-start(bf16[192,384]{1,0:T(8,128)(2,1)} %fusion.66), channel_id=1, source_target_pairs={{0,16},{1,9},{2,18},{3,11},{4,20},{5,13},{6,22},{7,15},{8,24},{9,1... | collective-permute-start | bytes 442376 | tf_op jit(solution)/shard_map/ppermute | solution.py:425
  487.4 11.9 %collective-permute-start.71 = (bf16[2,192,512]{2,1,0:T(8,128)(2,1)S(1)}, bf16[2,192,512]{2,1,0:T(8,128)(2,1)S(1)}, u32[]{:S(2)}, u32[]{:S(2)}) collective-permute-start(bf16[2,192,512]{2,1,0:T(8,128)(2,1)S(1)} %pad_maximum_fusion.11), channel_id=1, source_target_pairs={{0,8},{1,17},{2,10},{3,19},{4,12},{5,21},{6,14},{7,23},{8,0},{9,25... | collective-permute-start | bytes 1179656 | tf_op jit(solution)/shard_map/ppermute | solution.py:425
  495.9 64.6 %collective-permute-start.88 = (f32[768,1536]{1,0:T(8,128)}, f32[768,1536]{1,0:T(8,128)}, u32[]{:S(2)}, u32[]{:S(2)}) collective-permute-start(f32[768,1536]{1,0:T(8,128)} %get-tuple-element.88), channel_id=1, source_target_pairs={{0,1},{1,0},{2,3},{3,2},{4,5},{5,4},{6,7},{7,6},{8,9},{9,8},{10,11... | collective-permute-start | bytes 14155784 | tf_op jit(solution)/shard_map/ppermute | solution.py:425
  497.9 68.7 %collective-permute-start.94 = (f32[768,1536]{1,0:T(8,128)}, f32[768,1536]{1,0:T(8,128)}, u32[]{:S(2)}, u32[]{:S(2)}) collective-permute-start(f32[768,1536]{1,0:T(8,128)} %get-tuple-element.84), channel_id=1, source_target_pairs={{0,1},{1,0},{2,3},{3,2},{4,5},{5,4},{6,7},{7,6},{8,9},{9,8},{10,11... | collective-permute-start | bytes 14155784 | tf_op jit(solution)/shard_map/ppermute | solution.py:425
  517.4 11.3 %collective-permute-start.65 = (bf16[2,1408,128]{2,1,0:T(8,128)(2,1)S(1)}, bf16[2,1408,128]{2,1,0:T(8,128)(2,1)S(1)}, u32[]{:S(2)}, u32[]{:S(2)}) collective-permute-start(bf16[2,1408,128]{2,1,0:T(8,128)(2,1)S(1)} %pad_maximum_fusion.7), channel_id=1, source_target_pairs={{0,8},{1,17},{2,10},{3,19},{4,12},{5,21},{6,14},{7,23},{8,0},{9,25... | collective-permute-start | bytes 2162696 | tf_op jit(solution)/shard_map/ppermute | solution.py:425
  526.4 12.9 %collective-permute-start.63 = (f32[19,128]{1,0:T(8,128)S(1)}, f32[19,128]{1,0:T(8,128)S(1)}, u32[]{:S(2)}, u32[]{:S(2)}) collective-permute-start(f32[19,128]{1,0:T(8,128)S(1)} %add.788), channel_id=1, source_target_pairs={{0,16},{1,17},{2,18},{3,19},{4,20},{5,21},{6,22},{7,23},{8,24},{9,... | collective-permute-start | bytes 29192 | tf_op jit(solution)/shard_map/ppermute | solution.py:425
  528.7 12.1 %collective-permute-start.87 = (f32[24,384]{1,0:T(8,128)S(1)}, f32[24,384]{1,0:T(8,128)}, u32[]{:S(2)}, u32[]{:S(2)}) collective-permute-start(f32[24,384]{1,0:T(8,128)S(1)} %get-tuple-element.115), channel_id=1, source_target_pairs={{0,1},{1,0},{2,3},{3,2},{4,5},{5,4},{6,7},{7,6},{8,9},{9,8},{10,11... | collective-permute-start | bytes 110600 | tf_op jit(solution)/shard_map/ppermute | solution.py:425
  537.6 14.9 %collective-permute-start.77 = (bf16[2,192,1152]{2,1,0:T(8,128)(2,1)S(1)}, bf16[2,192,1152]{2,1,0:T(8,128)(2,1)S(1)}, u32[]{:S(2)}, u32[]{:S(2)}) collective-permute-start(bf16[2,192,1152]{2,1,0:T(8,128)(2,1)S(1)} %pad_maximum_fusion.6), channel_id=1, source_target_pairs={{0,8},{1,17},{2,10},{3,19},{4,12},{5,21},{6,14},{7,23},{8,0},{9,25... | collective-permute-start | bytes 2654216 | tf_op jit(solution)/shard_map/ppermute | solution.py:425
  560.5 91.4 %collective-permute-start.69 = (f32[176,128]{1,0:T(8,128)S(1)}, f32[176,128]{1,0:T(8,128)S(1)}, u32[]{:S(2)}, u32[]{:S(2)}) collective-permute-start(f32[176,128]{1,0:T(8,128)S(1)} %get-tuple-element.111), channel_id=1, source_target_pairs={{0,1},{1,0},{2,3},{3,2},{4,5},{5,4},{6,7},{7,6},{8,9},{9,8},{10,11... | collective-permute-start | bytes 270344 | tf_op jit(solution)/shard_map/ppermute | solution.py:425
  564.0 12.6 %collective-permute-start.79 = (f32[2,2,24,1152]{3,2,1,0:T(8,128)S(1)}, f32[2,2,24,1152]{3,2,1,0:T(8,128)S(1)}, u32[]{:S(2)}, u32[]{:S(2)}) collective-permute-start(f32[2,2,24,1152]{3,2,1,0:T(8,128)S(1)} %dynamic-slice_bitcast_fusion.2), channel_id=1, source_target_pairs={{0,2},{1,3},{2,0},{3,1},{4,6},{5,7},{6,4},{7,5},{8,10},{9,11},{10,... | collective-permute-start | bytes 1327112 | tf_op jit(solution)/shard_map/ppermute | solution.py:425
  564.8 24.4 %collective-permute-start.89 = (bf16[2,192,1536]{2,1,0:T(8,128)(2,1)S(1)}, bf16[2,192,1536]{2,1,0:T(8,128)(2,1)S(1)}, u32[]{:S(2)}, u32[]{:S(2)}) collective-permute-start(bf16[2,192,1536]{2,1,0:T(8,128)(2,1)S(1)} %pad_maximum_fusion.2), channel_id=1, source_target_pairs={{0,8},{1,17},{2,10},{3,19},{4,12},{5,21},{6,14},{7,23},{8,0},{9,25... | collective-permute-start | bytes 3538952 | tf_op jit(solution)/shard_map/ppermute | solution.py:425
  576.7 12.5 %collective-permute-start.80 = (f32[1,2,24,1152]{3,2,1,0:T(8,128)S(1)}, f32[1,2,24,1152]{3,2,1,0:T(8,128)S(1)}, u32[]{:S(2)}, u32[]{:S(2)}) collective-permute-start(f32[1,2,24,1152]{3,2,1,0:T(8,128)S(1)} %constant_dynamic-slice_fusion.9), channel_id=1, source_target_pairs={{0,4},{1,5},{2,6},{3,7},{4,0},{5,1},{6,2},{7,3},{8,12},{9,13},{10,... | collective-permute-start | bytes 663560 | tf_op jit(solution)/shard_map/ppermute | solution.py:425
  578.1 16.4 %collective-permute-start.95 = (bf16[2,192,1536]{2,1,0:T(8,128)(2,1)S(1)}, bf16[2,192,1536]{2,1,0:T(8,128)(2,1)S(1)}, u32[]{:S(2)}, u32[]{:S(2)}) collective-permute-start(bf16[2,192,1536]{2,1,0:T(8,128)(2,1)S(1)} %pad_maximum_fusion.3), channel_id=1, source_target_pairs={{0,8},{1,17},{2,10},{3,19},{4,12},{5,21},{6,14},{7,23},{8,0},{9,25... | collective-permute-start | bytes 3538952 | tf_op jit(solution)/shard_map/ppermute | solution.py:425
  592.6 61.8 %collective-permute-start.81 = (f32[24,1152]{1,0:T(8,128)}, f32[24,1152]{1,0:T(8,128)S(1)}, u32[]{:S(2)}, u32[]{:S(2)}) collective-permute-start(f32[24,1152]{1,0:T(8,128)} %get-tuple-element.109), channel_id=1, source_target_pairs={{0,1},{1,0},{2,3},{3,2},{4,5},{5,4},{6,7},{7,6},{8,9},{9,8},{10,11... | collective-permute-start | bytes 331784 | tf_op jit(solution)/shard_map/ppermute | solution.py:425
  596.4 11.0 %collective-permute-start.96 = (bf16[192,1536]{1,0:T(8,128)(2,1)S(1)}, bf16[192,1536]{1,0:T(8,128)(2,1)S(1)}, u32[]{:S(2)}, u32[]{:S(2)}) collective-permute-start(bf16[192,1536]{1,0:T(8,128)(2,1)S(1)} %fusion.40), channel_id=1, source_target_pairs={{0,16},{1,9},{2,18},{3,11},{4,20},{5,13},{6,22},{7,15},{8,24},{9,1... | collective-permute-start | bytes 1769480 | tf_op jit(solution)/shard_map/ppermute | solution.py:425
  602.7 16.3 %collective-permute-start.91 = (f32[2,2,24,1536]{3,2,1,0:T(8,128)S(1)}, f32[2,2,24,1536]{3,2,1,0:T(8,128)S(1)}, u32[]{:S(2)}, u32[]{:S(2)}) collective-permute-start(f32[2,2,24,1536]{3,2,1,0:T(8,128)S(1)} %dynamic-slice_bitcast_fusion.1), channel_id=1, source_target_pairs={{0,2},{1,3},{2,0},{3,1},{4,6},{5,7},{6,4},{7,5},{8,10},{9,11},{10,... | collective-permute-start | bytes 1769480 | tf_op jit(solution)/shard_map/ppermute | solution.py:425
  609.2 27.5 %collective-permute-start.97 = (f32[2,2,24,1536]{3,2,1,0:T(8,128)S(1)}, f32[2,2,24,1536]{3,2,1,0:T(8,128)S(1)}, u32[]{:S(2)}, u32[]{:S(2)}) collective-permute-start(f32[2,2,24,1536]{3,2,1,0:T(8,128)S(1)} %dynamic-slice_bitcast_fusion), channel_id=1, source_target_pairs={{0,2},{1,3},{2,0},{3,1},{4,6},{5,7},{6,4},{7,5},{8,10},{9,11},{10,... | collective-permute-start | bytes 1769480 | tf_op jit(solution)/shard_map/ppermute | solution.py:425
  619.2 17.8 %collective-permute-start.92 = (f32[1,2,24,1536]{3,2,1,0:T(8,128)S(1)}, f32[1,2,24,1536]{3,2,1,0:T(8,128)S(1)}, u32[]{:S(2)}, u32[]{:S(2)}) collective-permute-start(f32[1,2,24,1536]{3,2,1,0:T(8,128)S(1)} %constant_dynamic-slice_fusion), channel_id=1, source_target_pairs={{0,4},{1,5},{2,6},{3,7},{4,0},{5,1},{6,2},{7,3},{8,12},{9,13},{10,... | collective-permute-start | bytes 884744 | tf_op jit(solution)/shard_map/ppermute | solution.py:425
  636.9 14.1 %collective-permute-start.98 = (f32[1,2,24,1536]{3,2,1,0:T(8,128)S(1)}, f32[1,2,24,1536]{3,2,1,0:T(8,128)S(1)}, u32[]{:S(2)}, u32[]{:S(2)}) collective-permute-start(f32[1,2,24,1536]{3,2,1,0:T(8,128)S(1)} %constant_dynamic-slice_fusion.10), channel_id=1, source_target_pairs={{0,4},{1,5},{2,6},{3,7},{4,0},{5,1},{6,2},{7,3},{8,12},{9,13},{10,... | collective-permute-start | bytes 884744 | tf_op jit(solution)/shard_map/ppermute | solution.py:425
  637.1 19.2 %collective-permute-start.93 = (f32[24,1536]{1,0:T(8,128)S(1)}, f32[24,1536]{1,0:T(8,128)S(1)}, u32[]{:S(2)}, u32[]{:S(2)}) collective-permute-start(f32[24,1536]{1,0:T(8,128)S(1)} %get-tuple-element.107), channel_id=1, source_target_pairs={{0,1},{1,0},{2,3},{3,2},{4,5},{5,4},{6,7},{7,6},{8,9},{9,8},{10,11... | collective-permute-start | bytes 442376 | tf_op jit(solution)/shard_map/ppermute | solution.py:425
  (143 other events, 2623.0 us)

commit v2 on v1

v2 whole, which is shorter than its diff:
```python
import math

import jax
import jax.numpy as jnp
from jax import lax
from jax.experimental import pallas as pl
from jax.experimental.pallas import tpu as pltpu
from jax.sharding import PartitionSpec as P

D = 768
HEAD = 64
EMB = 128
STEPS_T = 2000
ADAM_STEP = 10


NEG_BIG = -1e30
EPS_NORM = 1e-05
BETA_ONE = 0.9
BETA_TWO = 0.95
ADAM_EPS = 1e-08
DECAY_RATE = 0.01
CLIP_NORM = 0.02
RATES = (0.05, 0.05, 0.02, 0.02, 0.02, 0.02, 0.01, 0.02, 0.3)
DECAYS = (DECAY_RATE,) * 8 + (0.0,)


def matmul(left_op, right_op):
    return jnp.dot(left_op, right_op, preferred_element_type=jnp.float32)


def matmul_tn(left_op, right_op):
    return lax.dot_general(
        left_op, right_op, (((0,), (0,)), ((), ())), preferred_element_type=jnp.float32
    )


def matrix_product_transposed(left_op, right_op):
    return lax.dot_general(
        left_op, right_op, (((1,), (1,)), ((), ())), preferred_element_type=jnp.float32
    )


def layer_normalize(hidden, gain_row):
    centre = jnp.mean(hidden, -1, keepdims=True)
    centred = hidden - centre
    spread = jnp.mean(centred * centred, -1, keepdims=True)
    scale_inv = lax.rsqrt(spread + EPS_NORM)
    normed = centred * scale_inv
    return (normed * gain_row, normed, scale_inv)


def norm_back(grad_normed_out, normed, scale_inv, gain_row):
    grad_gain = jnp.sum(grad_normed_out * normed, 0)
    grad_scaled = grad_normed_out * gain_row
    grad_input = scale_inv * (
        grad_scaled
        - jnp.mean(grad_scaled, -1, keepdims=True)
        - normed * jnp.mean(grad_scaled * normed, -1, keepdims=True)
    )
    return (grad_input, grad_gain)


def sinusoid(step_row, model_width):
    half_width = model_width // 2
    freqs = jnp.exp(-math.log(10000.0) * jnp.arange(half_width, dtype=jnp.float32) / half_width)
    angles = step_row.astype(jnp.float32)[:, None] * freqs[None, :]
    return jnp.concatenate([jnp.sin(angles), jnp.cos(angles)], -1)


TILE = 128
LOG2E = math.log2(math.e)
VMEM_LIMIT = 48 << 20


def tie(*arrays):
    return lax.optimization_barrier(arrays)


def key_windows(segments):
    length = segments.shape[0]
    blocks = segments.reshape(-1, TILE)
    shared = jnp.any(blocks[:, :, None] == segments[None, None, :], 1)
    places = jnp.arange(length, dtype=jnp.int32)[None, :]
    first = jnp.min(jnp.where(shared, places, length), 1) // TILE * TILE
    last = jnp.max(jnp.where(shared, places, -1), 1) + 1
    spans = (last - first + TILE - 1) // TILE
    return jnp.stack([first, spans]).astype(jnp.int32)


def nt_dot(left, right):
    return lax.dot_general(
        left, right, (((1,), (1,)), ((), ())), preferred_element_type=jnp.float32
    )


def tn_dot(left, right):
    return lax.dot_general(
        left, right, (((0,), (0,)), ((), ())), preferred_element_type=jnp.float32
    )


def head_stack(pair):
    lanes = lax.broadcasted_iota(jnp.int32, pair.shape, 1)
    zero = jnp.zeros_like(pair)
    return jnp.concatenate(
        [jnp.where(lanes < HEAD, pair, zero), jnp.where(lanes >= HEAD, pair, zero)], 0
    )


def fold(array):
    return array.reshape(-1, 8, array.shape[-1])


PAIRS = D // TILE
WIDE = PAIRS * TILE
LOG_ROWS = -(-2 * PAIRS // 8) * 8


def attention_forward(mixed, seg_row, seg_col, windows):
    length, width = mixed.shape[0], mixed.shape[1] // 3
    groups = width // WIDE
    factor = HEAD ** (-0.5) * LOG2E

    def kernel(windows_ref, q_ref, k_ref, v_ref, row_ref, col_ref, o_ref, log_ref, held, out, flip):
        flip[...] = v_ref[...].T

        def step(block, unused):
            rows = pl.ds(pl.multiple_of(block * TILE, TILE), TILE)
            start, count = windows_ref[0, block], windows_ref[1, block]
            row = row_ref[:, rows]
            queries = [head_stack(q_ref[rows, pl.ds(pair * TILE, TILE)]) for pair in range(PAIRS)]

            def keys_at(at):
                return pl.ds(pl.multiple_of(start + at * TILE, TILE), TILE)

            def held_at(at):
                return pl.ds(pl.multiple_of(at * TILE, TILE), TILE)

            def score(at, state):
                keys = keys_at(at)
                same = col_ref[keys, :] == row
                same = jnp.concatenate([same, same], 1)
                found = []
                for pair in range(PAIRS):
                    old, total = state[pair]
                    scores = nt_dot(k_ref[keys, pl.ds(pair * TILE, TILE)], queries[pair])
                    scores = jnp.where(same, scores * factor, NEG_BIG)
                    held[pair, held_at(at), :] = scores
                    scores = fold(scores)
                    new = jnp.maximum(old, jnp.max(scores, 0))
                    raised = jnp.sum(jnp.exp2(scores - new[None]), 0)
                    found.append((new, total * jnp.exp2(old - new) + raised))
                return tuple(found)

            low = jnp.full((8, 2 * TILE), NEG_BIG, jnp.float32)
            state = lax.fori_loop(0, count, score, ((low, jnp.zeros_like(low)),) * PAIRS)
            logs = []
            for peak, total in state:
                top = jnp.max(peak, 0, keepdims=True)
                total = jnp.sum(total * jnp.exp2(peak - top), 0, keepdims=True)
                logs.append(top + jnp.log2(total))
            out[...] = jnp.zeros_like(out)

            def spread(at, unused):
                for pair in range(PAIRS):
                    probs = jnp.exp2(held[pair, held_at(at), :] - logs[pair]).astype(jnp.bfloat16)
                    out[pair] += jnp.dot(
                        flip[pl.ds(pair * TILE, TILE), keys_at(at)],
                        probs,
                        preferred_element_type=jnp.float32,
                    )
                return unused

            lax.fori_loop(0, count, spread, 0)
            dims = lax.broadcasted_iota(jnp.int32, (TILE, TILE), 0)
            for pair in range(PAIRS):
                both = out[pair]
                chosen = jnp.where(dims < HEAD, both[:, :TILE], both[:, TILE:])
                o_ref[rows, pl.ds(pair * TILE, TILE)] = chosen.T.astype(jnp.bfloat16)
                log_ref[2 * pair : 2 * pair + 1, rows] = logs[pair][:, :TILE]
                log_ref[2 * pair + 1 : 2 * pair + 2, rows] = logs[pair][:, TILE:]
            return unused

        lax.fori_loop(0, length // TILE, step, 0)

    def column(place):
        return pl.BlockSpec((length, WIDE), lambda group, windows: (0, 3 * group + place))

    return pl.pallas_call(
        kernel,
        out_shape=(
            jax.ShapeDtypeStruct((length, width), jnp.bfloat16),
            jax.ShapeDtypeStruct((LOG_ROWS * groups, length), jnp.float32),
        ),
        grid_spec=pltpu.PrefetchScalarGridSpec(
            num_scalar_prefetch=1,
            grid=(groups,),
            in_specs=[
                column(0),
                column(1),
                column(2),
                pl.BlockSpec((1, length), lambda group, windows: (0, 0)),
                pl.BlockSpec((length, TILE), lambda group, windows: (0, 0)),
            ],
            out_specs=[
                pl.BlockSpec((length, WIDE), lambda group, windows: (0, group)),
                pl.BlockSpec((LOG_ROWS, length), lambda group, windows: (group, 0)),
            ],
            scratch_shapes=[
                pltpu.VMEM((PAIRS, length, 2 * TILE), jnp.float32),
                pltpu.VMEM((PAIRS, TILE, 2 * TILE), jnp.float32),
                pltpu.VMEM((WIDE, length), jnp.bfloat16),
            ],
        ),
        compiler_params=pltpu.CompilerParams(vmem_limit_bytes=VMEM_LIMIT),
        name="attention_forward",
    )(windows, mixed, mixed, mixed, seg_row, seg_col)


def attention_backward(mixed, grad_attended, log_sums, seg_row, seg_col, windows):
    length = mixed.shape[0]
    score_scale = HEAD ** (-0.5)
    factor = score_scale * LOG2E

    def kernel(windows_ref, q_ref, k_ref, v_ref, do_ref, log_ref, row_ref, col_ref, *refs):
        out_ref, held, pulled, dq_flip, dq_acc, dk_acc, dv_acc, key_flip = refs
        third = pl.program_id(0)

        def step(block, unused):
            rows = pl.ds(pl.multiple_of(block * TILE, TILE), TILE)
            start, count = windows_ref[0, block], windows_ref[1, block]
            row = row_ref[:, rows]
            pairs = [pl.ds(pair * TILE, TILE) for pair in range(PAIRS)]
            queries = [head_stack(q_ref[rows, cols]) for cols in pairs]
            grads = [head_stack(do_ref[rows, cols]) for cols in pairs]
            logs = [
                jnp.concatenate(
                    [
                        log_ref[2 * pair : 2 * pair + 1, rows],
                        log_ref[2 * pair + 1 : 2 * pair + 2, rows],
                    ],
                    1,
                )
                for pair in range(PAIRS)
            ]

            def keys_at(at):
                return pl.ds(pl.multiple_of(start + at * TILE, TILE), TILE)

            def held_at(at):
                return pl.ds(pl.multiple_of(at * TILE, TILE), TILE)

            def weigh(at, inners):
                keys = keys_at(at)
                same = col_ref[keys, :] == row
                same = jnp.concatenate([same, same], 1)
                found = []
                for pair, cols in enumerate(pairs):
                    scores = nt_dot(k_ref[keys, cols], queries[pair])
                    probs = jnp.where(same, jnp.exp2(scores * factor - logs[pair]), 0.0)
                    grad_probs = nt_dot(v_ref[keys, cols], grads[pair])
                    held[pair, held_at(at), :] = probs
                    pulled[pair, held_at(at), :] = grad_probs
                    found.append(inners[pair] + jnp.sum(fold(probs * grad_probs), 0))
                return tuple(found)

            zero = jnp.zeros((8, 2 * TILE), jnp.float32)
            inners = lax.fori_loop(0, count, weigh, (zero,) * PAIRS)
            inners = [jnp.sum(inner, 0, keepdims=True) for inner in inners]
            dq_flip[...] = jnp.zeros_like(dq_flip)

            def spread(at, unused):
                keys = keys_at(at)
                for pair, cols in enumerate(pairs):
                    probs = held[pair, held_at(at), :]
                    scores = probs * (pulled[pair, held_at(at), :] - inners[pair])
                    scores_low = scores.astype(jnp.bfloat16)
                    dv_acc[keys, cols] += jnp.dot(
                        probs.astype(jnp.bfloat16), grads[pair], preferred_element_type=jnp.float32
                    )
                    dk_acc[keys, cols] += jnp.dot(
                        scores_low, queries[pair], preferred_element_type=jnp.float32
                    )
                    dq_flip[pair] += jnp.dot(
                        key_flip[cols, keys], scores_low, preferred_element_type=jnp.float32
                    )
                return unused

            lax.fori_loop(0, count, spread, 0)
            dims = lax.broadcasted_iota(jnp.int32, (TILE, TILE), 0)
            for pair, cols in enumerate(pairs):
                both = dq_flip[pair]
                dq_acc[rows, cols] = jnp.where(dims < HEAD, both[:, :TILE], both[:, TILE:]).T
            return unused

        @pl.when(third == 0)
        def _():
            dk_acc[...] = jnp.zeros_like(dk_acc)
            dv_acc[...] = jnp.zeros_like(dv_acc)
            key_flip[...] = k_ref[...].T
            lax.fori_loop(0, length // TILE, step, 0)
            out_ref[...] = (dq_acc[...] * score_scale).astype(jnp.bfloat16)

        @pl.when(third == 1)
        def _():
            out_ref[...] = (dk_acc[...] * score_scale).astype(jnp.bfloat16)

        @pl.when(third == 2)
        def _():
            out_ref[...] = dv_acc[...].astype(jnp.bfloat16)

    def column(place):
        return pl.BlockSpec((length, WIDE), lambda third, windows: (0, place))

    return pl.pallas_call(
        kernel,
        out_shape=jax.ShapeDtypeStruct(mixed.shape, jnp.bfloat16),
        grid_spec=pltpu.PrefetchScalarGridSpec(
            num_scalar_prefetch=1,
            grid=(3,),
            in_specs=[
                column(0),
                column(1),
                column(2),
                column(0),
                pl.BlockSpec((LOG_ROWS, length), lambda third, windows: (0, 0)),
                pl.BlockSpec((1, length), lambda third, windows: (0, 0)),
                pl.BlockSpec((length, TILE), lambda third, windows: (0, 0)),
            ],
            out_specs=pl.BlockSpec((length, WIDE), lambda third, windows: (0, third)),
            scratch_shapes=[pltpu.VMEM((PAIRS, length, 2 * TILE), jnp.float32)] * 2
            + [pltpu.VMEM((PAIRS, TILE, 2 * TILE), jnp.float32)]
            + [pltpu.VMEM((length, WIDE), jnp.float32)] * 3
            + [pltpu.VMEM((WIDE, length), jnp.bfloat16)],
        ),
        compiler_params=pltpu.CompilerParams(vmem_limit_bytes=VMEM_LIMIT),
        name="attention_backward",
    )(windows, mixed, mixed, mixed, grad_attended, log_sums, seg_row, seg_col)


def head_pass(pred_low, word_table, token_weight):
    length, width = pred_low.shape
    words = word_table.shape[0]
    tile, across = 1024, 256

    def kernel(
        pred_ref, table_ref, weight_ref, grad_table_ref, grad_pred_ref, log_ref, peak, total, grads
    ):
        phase, step = pl.program_id(0), pl.program_id(1)
        blocks = [
            (pl.ds(row, TILE), pl.ds(col, across))
            for col in range(0, length, across)
            for row in range(0, tile, TILE)
        ]

        @pl.when((phase == 0) & (step == 0))
        def _():
            peak[...] = jnp.full_like(peak, -1e30)
            total[...] = jnp.zeros_like(total)
            grad_pred_ref[...] = jnp.zeros_like(grad_pred_ref)

        @pl.when(phase == 0)
        def _():
            for rows, cols in blocks:
                logits = fold(nt_dot(table_ref[rows, :], pred_ref[cols, :]) * LOG2E)
                old = peak[:, cols]
                new = jnp.maximum(old, jnp.max(logits, 0))
                raised = jnp.sum(jnp.exp2(logits - new[None]), 0)
                total[:, cols] = total[:, cols] * jnp.exp2(old - new) + raised
                peak[:, cols] = new

        @pl.when((phase == 1) & (step == 0))
        def _():
            top = jnp.max(peak[...], 0, keepdims=True)
            sums = jnp.sum(total[...] * jnp.exp2(peak[...] - top), 0, keepdims=True)
            logs = top + jnp.log2(sums)
            log_ref[...] = logs / LOG2E
            weight = weight_ref[...]
            down = jnp.where(weight > 0.0, jnp.log2(weight), -1e30)
            peak[...] = jnp.broadcast_to(logs - down, peak.shape)

        @pl.when(phase == 1)
        def _():
            for rows, cols in blocks:
                logits = nt_dot(table_ref[rows, :], pred_ref[cols, :])
                lowered = fold(logits * LOG2E) - peak[:, cols][None]
                grads[rows, cols] = (
                    jnp.exp2(lowered).reshape(TILE, across).astype(jnp.bfloat16)
                )
            grad_table_ref[...] = jnp.dot(
                grads[...], pred_ref[...], preferred_element_type=jnp.float32
            )
            grad_pred_ref[...] += tn_dot(table_ref[...], grads[...])

    def whole(shape):
        return pl.BlockSpec(shape, lambda phase, step: (0, 0))

    return pl.pallas_call(
        kernel,
        out_shape=(
            jax.ShapeDtypeStruct((words, width), jnp.float32),
            jax.ShapeDtypeStruct((width, length), jnp.float32),
            jax.ShapeDtypeStruct((1, length), jnp.float32),
        ),
        grid_spec=pltpu.PrefetchScalarGridSpec(
            num_scalar_prefetch=0,
            grid=(2, words // tile),
            in_specs=[
                whole((length, width)),
                pl.BlockSpec((tile, width), lambda phase, step: (step, 0)),
                whole((1, length)),
            ],
            out_specs=[
                pl.BlockSpec((tile, width), lambda phase, step: (phase * step, 0)),
                whole((width, length)),
                whole((1, length)),
            ],
            scratch_shapes=[pltpu.VMEM((8, length), jnp.float32)] * 2
            + [pltpu.VMEM((tile, length), jnp.bfloat16)],
        ),
        compiler_params=pltpu.CompilerParams(vmem_limit_bytes=VMEM_LIMIT),
        name="head_pass",
    )(pred_low, word_table, token_weight)


def adam_rule(master, moment, second, grad, rate, decay):
    moment_new = BETA_ONE * moment + (1.0 - BETA_ONE) * grad
    second_new = BETA_TWO * second + (1.0 - BETA_TWO) * grad * grad
    moment_hat = moment_new / (1.0 - BETA_ONE**ADAM_STEP)
    second_hat = second_new / (1.0 - BETA_TWO**ADAM_STEP)
    master_new = master - rate * (moment_hat / (jnp.sqrt(second_hat) + ADAM_EPS) + decay * master)
    return [moment_new, second_new, master_new]


def adam_update(factor, masters, moments, seconds, grads):
    count = len(masters) - 1
    shapes = [member.shape for member in masters[:count]]

    def kernel(factor_ref, *refs):
        small, refs = refs[:4], refs[4:]
        sources, targets = refs[: 4 * count], refs[4 * count : 7 * count]
        small_out, refs = refs[7 * count : 7 * count + 3], refs[7 * count + 3 :]
        held, load_sems, store_sems = refs[:count], refs[count], refs[count + 1]
        loads = []
        for at in range(count):
            for kind in range(4):
                loads.append(
                    pltpu.make_async_copy(
                        sources[kind * count + at], held[at].at[kind], load_sems.at[at, kind]
                    )
                )
                loads[-1].start()
        scale = factor_ref[0]
        values = [ref[...] for ref in small]
        values[3] = scale * values[3]
        for kind, value in enumerate(adam_rule(*values, RATES[count], DECAYS[count])):
            small_out[kind][...] = value
        stores = []
        for at in range(count):
            for kind in range(4):
                loads[4 * at + kind].wait()
            values = [held[at][kind] for kind in range(4)]
            values[3] = scale * values[3]
            for kind, value in enumerate(adam_rule(*values, RATES[at], DECAYS[at])):
                held[at][4 + kind] = value
                stores.append(
                    pltpu.make_async_copy(
                        held[at].at[4 + kind], targets[3 * at + kind], store_sems.at[at, kind]
                    )
                )
                stores[-1].start()
        for store in stores:
            store.wait()

    kinds = (masters, moments, seconds, grads)
    return pl.pallas_call(
        kernel,
        out_shape=[
            jax.ShapeDtypeStruct(member.shape, jnp.float32) for member in masters for kind in range(3)
        ],
        in_specs=[pl.BlockSpec(memory_space=pltpu.SMEM)]
        + [pl.BlockSpec(memory_space=pltpu.VMEM)] * 4
        + [pl.BlockSpec(memory_space=pltpu.HBM)] * (4 * count),
        out_specs=[pl.BlockSpec(memory_space=pltpu.HBM)] * (3 * count)
        + [pl.BlockSpec(memory_space=pltpu.VMEM)] * 3,
        scratch_shapes=[pltpu.VMEM((7,) + shape, jnp.float32) for shape in shapes]
        + [pltpu.SemaphoreType.DMA((count, 4)), pltpu.SemaphoreType.DMA((count, 3))],
        compiler_params=pltpu.CompilerParams(vmem_limit_bytes=60 << 20),
        name="adam_update",
    )(
        factor.reshape(1),
        *[members[count] for members in kinds],
        *[member for members in kinds for member in members[:count]],
    )


AXES = ("bucket", "dp")


class Place:
    def __init__(self, buckets, columns):
        self.buckets, self.columns = buckets, columns
        self.count = buckets * columns
        self.line = columns // 2
        self.bits = [1 << place for place in range(1, columns.bit_length() - 1)]
        self.offsets = [0]
        for bit in reversed(self.bits):
            self.offsets += [offset ^ (bit >> 1) for offset in self.offsets]
        self.square = lax.axis_index("bucket")
        along = lax.axis_index("dp")
        self.core = along % 2
        self.along = along // 2
        self.flat = self.square * columns + along
        self.step_a = 1 + self.core
        self.step_b = 2 - self.core

    def swap(self, array, pick):
        pairs = [(member, member ^ pick(member)) for member in range(self.count)]
        return lax.ppermute(array, AXES, pairs)

    def swap_core(self, array):
        return self.swap(array, lambda member: 1)

    def swap_a(self, array):
        return self.swap(array, lambda member: self.columns * (1 + member % 2))

    def swap_b(self, array):
        return self.swap(array, lambda member: self.columns * (2 - member % 2))

    def swap_line(self, array, bit):
        return self.swap(array, lambda member: bit)

    def total(self, array):
        array = array + self.swap_core(array)
        spans = [self.columns, 2 * self.columns] + self.bits
        for at in range(0, len(spans), 2):
            near, *more = spans[at : at + 2]
            parts = [self.swap_line(array, near)]
            for far in more:
                parts += [self.swap_line(array, far), self.swap_line(array, near ^ far)]
            array = array + sum(parts)
        return array


def assemble(place, pieces):
    twice, rows, cols = pieces[0].shape
    line = twice // 2
    flags = jnp.stack([place.square, place.along, place.core]).astype(jnp.int32)

    def kernel(flags_ref, *refs):
        piece_refs, out_ref, held, load_sems, store_sem = refs[:4], *refs[4:]
        square, along, core = flags_ref[0], flags_ref[1], flags_ref[2]
        step_a, step_b = 1 + core, 2 - core
        spots = [
            (0, (square, square ^ step_a), core),
            (2, (square, square ^ step_b), 1 - core),
            (1, (square ^ step_b, square ^ 3), core),
            (3, (square ^ step_a, square ^ 3), 1 - core),
        ]
        loads = [
            pltpu.make_async_copy(piece_ref, held.at[at], load_sems.at[at])
            for at, piece_ref in enumerate(piece_refs)
        ]
        for load in loads:
            load.start()
        for at, quarters, side in spots:
            loads[at].wait()
            for half, quarter in enumerate(quarters):
                for order, offset in enumerate(place.offsets):
                    pltpu.make_async_copy(
                        held.at[at, half * line + order],
                        out_ref.at[quarter, along ^ offset, side],
                        store_sem,
                    ).start()
        pltpu.make_async_copy(out_ref, out_ref, store_sem).wait()

    gathered = pl.pallas_call(
        kernel,
        out_shape=jax.ShapeDtypeStruct((4, line, 2, rows, cols), pieces[0].dtype),
        grid_spec=pltpu.PrefetchScalarGridSpec(
            num_scalar_prefetch=1,
            grid=(1,),
            in_specs=[pl.BlockSpec(memory_space=pltpu.HBM)] * 4,
            out_specs=pl.BlockSpec(memory_space=pltpu.HBM),
            scratch_shapes=[
                pltpu.VMEM((4, twice, rows, cols), pieces[0].dtype),
                pltpu.SemaphoreType.DMA((4,)),
                pltpu.SemaphoreType.DMA(()),
            ],
        ),
        compiler_params=pltpu.CompilerParams(vmem_limit_bytes=VMEM_LIMIT),
        name="assemble",
    )(flags, *pieces)
    return gathered.reshape(8 * line * rows, cols)


def product_half(left, right):
    half = right.shape[1] // 2

    def half_of(side):
        return matmul_tn(left, lax.dynamic_slice_in_dim(right, side * half, half, 1))

    return half_of


def column_half(array):
    half = array.shape[1] // 2
    return lambda side: lax.dynamic_slice_in_dim(array, side * half, half, 1)


def scatter_halves(place, table, spots, rows):
    words, width = table.shape
    half = words // 2
    each = half // place.count
    length = rows.shape[0]
    flag = place.core.astype(jnp.int32).reshape(1)

    def kernel(spots_ref, flag_ref, table_ref, rows_ref, send_ref, keep_ref, held, load_sem, sems):
        for owner in range(place.count):
            for side in range(2):
                pltpu.make_async_copy(
                    table_ref.at[pl.ds((2 * owner + side) * each, each)],
                    held.at[pl.ds(side * half + owner * each, each)],
                    load_sem,
                ).start()
        pltpu.make_async_copy(table_ref, held, load_sem).wait()

        def step(at, unused):
            for more in range(16):
                place_at = pl.ds(spots_ref[at * 16 + more], 1)
                held[place_at, :] += rows_ref[pl.ds(at * 16 + more, 1), :]
            return unused

        lax.fori_loop(0, length // 16, step, 0)
        core = flag_ref[0]
        first = pltpu.make_async_copy(held.at[pl.ds((1 - core) * half, half)], send_ref, sems.at[0])
        second = pltpu.make_async_copy(held.at[pl.ds(core * half, half)], keep_ref, sems.at[1])
        first.start()
        second.start()
        first.wait()
        second.wait()

    return pl.pallas_call(
        kernel,
        out_shape=[jax.ShapeDtypeStruct((half, width), jnp.float32)] * 2,
        grid_spec=pltpu.PrefetchScalarGridSpec(
            num_scalar_prefetch=2,
            grid=(1,),
            in_specs=[
                pl.BlockSpec(memory_space=pltpu.HBM),
                pl.BlockSpec((length, width), lambda step, spots, flag: (0, 0)),
            ],
            out_specs=[pl.BlockSpec(memory_space=pltpu.HBM)] * 2,
            scratch_shapes=[
                pltpu.VMEM((words, width), jnp.float32),
                pltpu.SemaphoreType.DMA(()),
                pltpu.SemaphoreType.DMA((2,)),
            ],
        ),
        compiler_params=pltpu.CompilerParams(vmem_limit_bytes=VMEM_LIMIT),
        name="scatter_halves",
    )(spots, flag, table, rows)


def join(held, arrived):
    return jnp.concatenate([held, arrived], 0)


class Reduction:
    def __init__(self, place, half_of, stack=False, exact=False, short=False):
        self.place, self.half_of = place, half_of
        self.stack, self.exact, self.short = stack, exact, short

    def whole(self, pieces):
        return pieces[0] if len(pieces) == 1 else jnp.concatenate(pieces, 1)

    def to_core(self):
        return self.half_of(1 - self.place.core)

    def keep(self, pieces=None):
        self.kept_pieces = self.half_of(self.place.core) if pieces is None else pieces
        self.halves = [piece.shape[1] for piece in self.kept_pieces]
        self.quarter_rows = self.kept_pieces[0].shape[0] // 4
        self.rows = self.kept_pieces[0].shape[0] // self.place.count

    def quarter(self, index):
        start = index * self.quarter_rows

        def rows(piece):
            return lax.dynamic_slice_in_dim(piece, start, self.quarter_rows, 0)

        return self.whole(
            [rows(kept) + rows(came) for kept, came in zip(self.kept_pieces, self.across)]
        )

    def lower(self, array):
        if not self.exact:
            return array.astype(jnp.bfloat16)
        last = array[..., -TILE:][..., : TILE // 2]
        rounded = lax.reduce_precision(last, 8, 7)
        both = jnp.concatenate([rounded, last - rounded], -1)
        return jnp.concatenate([array[..., :-TILE], both], -1).astype(jnp.bfloat16)

    def lift(self, array):
        array = array.astype(jnp.float32)
        if not self.exact:
            return array
        rounded, rest = array[..., -TILE : -TILE // 2], array[..., -TILE // 2 :]
        both = jnp.concatenate([rounded + rest, jnp.zeros_like(rest)], -1)
        return jnp.concatenate([array[..., :-TILE], both], -1)

    def to_a(self, across):
        self.across = across
        square = self.place.square
        pair = [self.quarter(square ^ self.place.step_a), self.quarter(square ^ 3)]
        return jnp.stack([self.lower(member) for member in pair])

    def to_b(self, from_a):
        self.from_a = from_a
        mixed = self.quarter(self.place.square ^ self.place.step_b)
        return self.lower(mixed + self.lift(from_a[1]))

    def from_b(self, from_b):
        own = self.quarter(self.place.square)
        own = own + self.lift(self.from_a[0]) + self.lift(from_b)
        self.own = own.reshape(self.place.line, 2, self.rows, own.shape[-1])
        self.along = self.place.along

    def to_line(self):
        split = self.own.reshape((self.own.shape[0] // 2, 2) + self.own.shape[1:])
        mine = self.along % 2
        self.along = self.along // 2
        self.own = lax.dynamic_index_in_dim(split, mine, 1, False)
        other = lax.dynamic_index_in_dim(split, 1 - mine, 1, False)
        return other.astype(jnp.bfloat16) if self.short else other

    def from_line(self, arrived):
        self.own = self.own + arrived.astype(jnp.float32)

    def to_end(self):
        own = self.own[0]
        self.kept = lax.dynamic_index_in_dim(own, self.place.core, 0, False)
        return lax.dynamic_index_in_dim(own, 1 - self.place.core, 0, False)

    def finish(self, other):
        results, start = [], 0
        for half in self.halves:
            kept, came = self.kept[:, start : start + half], other[:, start : start + half]
            start += half
            axis = 0 if self.stack else 1
            results.append(
                jnp.where(
                    self.place.core == 0,
                    jnp.concatenate([kept, came], axis),
                    jnp.concatenate([came, kept], axis),
                )
            )
        return results


def on_device(
    token_ids,
    segment_ids,
    live,
    timesteps,
    noise,
    embedding,
    embedding_moment,
    embedding_second,
    up_weight,
    up_moment,
    up_second,
    time_weight,
    time_moment,
    time_second,
    qkv_weight,
    qkv_moment,
    qkv_second,
    out_weight,
    out_moment,
    out_second,
    fc_weight,
    fc_moment,
    fc_second,
    proj_weight,
    proj_moment,
    proj_second,
    down_weight,
    down_moment,
    down_second,
    norm_gains,
    gains_moment,
    gains_second,
):
    masters = (
        embedding,
        up_weight,
        time_weight,
        qkv_weight,
        out_weight,
        fc_weight,
        proj_weight,
        down_weight,
        norm_gains,
    )
    moments = (
        embedding_moment,
        up_moment,
        time_moment,
        qkv_moment,
        out_moment,
        fc_moment,
        proj_moment,
        down_moment,
        gains_moment,
    )
    seconds = (
        embedding_second,
        up_second,
        time_second,
        qkv_second,
        out_second,
        fc_second,
        proj_second,
        down_second,
        gains_second,
    )
    place = Place(lax.axis_size("bucket"), lax.axis_size("dp"))
    buckets = place.buckets
    step_span = STEPS_T // buckets
    tokens = token_ids[0]
    step_row = timesteps[0]
    live_float = live[0].astype(jnp.float32)
    onehot = (
        (step_row // step_span)[:, None] == jnp.arange(buckets, dtype=jnp.int32)[None, :]
    ).astype(jnp.float32)
    count_own = jnp.sum(live_float[:, None] * onehot, 0)
    count_high = jnp.floor(count_own / 32.0)
    aside = jnp.concatenate([count_high, count_own - 32.0 * count_high]).astype(jnp.bfloat16)
    low = [member.astype(jnp.bfloat16) for member in masters]
    own_rows = low[3].shape[0]
    gains_pad = jnp.concatenate(
        [
            low[8].T,
            jnp.broadcast_to(aside[None, :], (own_rows, 2 * buckets)),
            jnp.zeros((own_rows, EMB - 3 - 2 * buckets), jnp.bfloat16),
        ],
        1,
    )
    model_width = low[3].shape[1] // 3
    ff_width = low[5].shape[1]

    table = low[0][None]
    entry = jnp.concatenate([low[1].T, low[2].T, gains_pad], 1)[None]
    qkv = low[3][None]
    leave = jnp.concatenate([low[4].T, low[5], low[6].T, low[7]], 1)[None]
    fraction = step_row.astype(jnp.float32) / STEPS_T
    alpha_bar = 1.0 - jnp.sqrt(fraction + 0.0001)
    keep_root = jnp.sqrt(alpha_bar)[:, None]
    seg_col = jnp.broadcast_to(segment_ids.T, (segment_ids.shape[1], TILE))
    windows = key_windows(segment_ids[0])
    down_bits = place.bits[::-1]

    for bit in down_bits[:-1]:
        table = join(table, place.swap_line(table, bit))
        entry = join(entry, place.swap_line(entry, bit))
        table, entry, windows = tie(table, entry, windows)
    table = join(table, place.swap_line(table, down_bits[-1]))
    entry = join(entry, place.swap_line(entry, down_bits[-1]))
    for bit in down_bits[:-1]:
        entry, qkv = tie(entry, qkv)
        qkv = join(qkv, place.swap_line(qkv, bit))
    table, entry, qkv, leave, step_row = tie(table, entry, qkv, leave, step_row)
    feature_low = sinusoid(step_row, D).astype(jnp.bfloat16)
    table = join(table, place.swap_a(table))
    entry = join(entry, place.swap_a(entry))
    qkv = join(qkv, place.swap_line(qkv, down_bits[-1]))
    for bit in down_bits[:-1]:
        leave = join(leave, place.swap_line(leave, bit))
    table, entry, qkv = tie(table, entry, qkv)
    table_pieces = [table, place.swap_b(table), place.swap_core(table)]
    entry_pieces = [entry, place.swap_b(entry), place.swap_core(entry)]
    *both, qkv, leave, feature_low = tie(*table_pieces, *entry_pieces, qkv, leave, feature_low)
    table_pieces, entry_pieces = both[:3], both[3:]
    table_pieces.append(place.swap_core(table_pieces[1]))
    entry_pieces.append(place.swap_core(entry_pieces[1]))
    qkv_a = place.swap_a(qkv)
    leave = join(leave, place.swap_line(leave, down_bits[-1]))
    entry_low = assemble(place, entry_pieces)
    word_table = assemble(place, table_pieces)
    word_table, qkv_a, qkv = tie(word_table, qkv_a, qkv)
    qkv_half = join(qkv, qkv_a)
    qkv_pieces = [qkv_half, place.swap_b(qkv_half), place.swap_core(qkv_half)]
    up_low = entry_low[:, :EMB]
    time_low = entry_low[:, EMB : EMB + model_width]
    aside_low = entry_low[:, EMB + model_width :]
    gain_rows = aside_low[:, :3].T.astype(jnp.float32)
    shares = aside_low.reshape(place.count, own_rows, EMB)[:, 0, 3 : 3 + 2 * buckets]
    count_sums = jnp.sum(shares.astype(jnp.float32), 0)
    counts = 32.0 * count_sums[:buckets] + count_sums[buckets:]
    token_weight = live_float * jnp.sum(onehot / counts[None, :], -1) / buckets

    start_emb = word_table[tokens].astype(jnp.float32)
    noisy_emb = keep_root * start_emb + jnp.sqrt(1.0 - alpha_bar)[:, None] * noise[0]
    noisy_low = noisy_emb.astype(jnp.bfloat16)
    hidden_zero = matrix_product_transposed(noisy_low, up_low) + matrix_product_transposed(
        feature_low, time_low
    )
    normed, scaled_one, inverse_one = layer_normalize(hidden_zero, gain_rows[0])
    normed_one_low = normed.astype(jnp.bfloat16)
    *qkv_pieces, normed_one_low, leave = tie(*qkv_pieces, normed_one_low, leave)
    leave_a = place.swap_a(leave)
    qkv_pieces.append(place.swap_core(qkv_pieces[1]))
    qkv_low = assemble(place, qkv_pieces)
    mixed_low = matmul(normed_one_low, qkv_low).astype(jnp.bfloat16)
    segments = (segment_ids, seg_col, windows)
    leave_a, leave, mixed_low = tie(leave_a, leave, mixed_low)
    leave_half, mixed_low = tie(join(leave, leave_a), mixed_low)
    leave_pieces = [leave_half, place.swap_b(leave_half), place.swap_core(leave_half)]
    attended_low, log_sums = attention_forward(mixed_low, *segments)
    *leave_pieces, attended_low = tie(*leave_pieces, attended_low)
    leave_pieces.append(place.swap_core(leave_pieces[1]))
    leave_low = assemble(place, leave_pieces)
    out_low = leave_low[:, :model_width]
    fc_low = leave_low[:, model_width : model_width + ff_width]
    proj_low = leave_low[:, model_width + ff_width : model_width + 2 * ff_width]
    down_low = leave_low[:, model_width + 2 * ff_width :]
    hidden_one = hidden_zero + matrix_product_transposed(attended_low, out_low)
    normed, scaled_two, inverse_two = layer_normalize(hidden_one, gain_rows[1])
    normed_two_low = normed.astype(jnp.bfloat16)
    fc_upper = matmul(normed_two_low, fc_low)
    active_low = jax.nn.gelu(fc_upper).astype(jnp.bfloat16)
    hidden_two = hidden_one + matrix_product_transposed(active_low, proj_low)
    normed, scaled_top, inverse_top = layer_normalize(hidden_two, gain_rows[2])
    normed_top_low = normed.astype(jnp.bfloat16)
    prediction = matmul(normed_top_low, down_low)
    pred_low = prediction.astype(jnp.bfloat16)
    grad_table_head, grad_pred_head, log_total = head_pass(
        pred_low, word_table, token_weight[None, :]
    )

    pred_float = pred_low.astype(jnp.float32)
    target = jnp.sum(pred_float * start_emb, -1)
    cross_loss = log_total[0] - target
    target_prob = jnp.exp(target - log_total[0])
    target_shift = lax.reduce_precision(
        token_weight * (target_prob - 1.0), 8, 7
    ) - lax.reduce_precision(token_weight * target_prob, 8, 7)
    target_shift = target_shift[:, None]
    pred_gap = prediction - start_emb
    loss_local = jnp.sum(token_weight * (jnp.mean(pred_gap * pred_gap, -1) + cross_loss))
    grad_mse = token_weight[:, None] * 2.0 * pred_gap / EMB
    grad_pred_low = (grad_mse + grad_pred_head.T + target_shift * start_emb).astype(jnp.bfloat16)
    grad_down = matmul_tn(normed_top_low, grad_pred_low)
    grad_two, grad_gain_top = norm_back(
        matrix_product_transposed(grad_pred_low, down_low), scaled_top, inverse_top, gain_rows[2]
    )

    bits = list(place.bits)
    grad_two_low = grad_two.astype(jnp.bfloat16)
    proj_half = product_half(grad_two_low, active_low)
    proj = Reduction(place, lambda side: [proj_half(side)], short=True)
    proj_send, grad_two_low = tie(*proj.to_core(), grad_two_low)
    proj_came = place.swap_core(proj_send)
    proj.keep()
    unused_value, gelu_pull = jax.vjp(jax.nn.gelu, fc_upper)
    (grad_upper,) = gelu_pull(matmul(grad_two_low, proj_low))
    grad_upper_low = grad_upper.astype(jnp.bfloat16)
    proj_came, grad_upper_low = tie(proj_came, grad_upper_low)
    proj_send, grad_upper_low = tie(proj.to_a([proj_came]), grad_upper_low)
    proj_came = place.swap_a(proj_send)
    fc_half = product_half(normed_two_low, grad_upper_low)
    fc = Reduction(place, lambda side: [fc_half(side)], short=True)
    fc_send, grad_upper_low = tie(*fc.to_core(), grad_upper_low)
    fc_came = place.swap_core(fc_send)
    fc.keep()
    grad_normed_two = matrix_product_transposed(grad_upper_low, fc_low)
    back_two, grad_gain_two = norm_back(grad_normed_two, scaled_two, inverse_two, gain_rows[1])
    grad_one = grad_two + back_two
    grad_one_low = grad_one.astype(jnp.bfloat16)
    proj_came, fc_came, grad_one_low = tie(proj_came, fc_came, grad_one_low)
    proj_send, fc_send, grad_one_low = tie(
        proj.to_b(proj_came), fc.to_a([fc_came]), grad_one_low
    )
    proj_came, fc_came = place.swap_b(proj_send), place.swap_a(fc_send)
    grad_out = matmul_tn(grad_one_low, attended_low)
    grad_attended = matmul(grad_one_low, out_low).astype(jnp.bfloat16)
    lanes = lax.broadcasted_iota(jnp.int32, (model_width, 2 * TILE), 1)
    exact = jnp.where(lanes == 1, grad_gain_two[:, None], 0.0)
    exact = jnp.where(lanes == 2, grad_gain_top[:, None], exact)
    exact = jnp.where(lanes == 3, loss_local, exact)
    grad_out, exact, grad_attended, proj_came = tie(grad_out, exact, grad_attended, proj_came)
    proj.from_b(proj_came)
    proj_send, grad_attended = tie(proj.to_line(), grad_attended)
    proj_came = place.swap_line(proj_send, bits[0])
    grad_mixed = attention_backward(mixed_low, grad_attended, log_sums, *segments)

    proj_came, fc_came, grad_mixed = tie(proj_came, fc_came, grad_mixed)
    proj.from_line(proj_came)
    proj_send, fc_send, grad_mixed = tie(proj.to_line(), fc.to_b(fc_came), grad_mixed)
    proj_came, fc_came = place.swap_line(proj_send, bits[1]), place.swap_b(fc_send)
    out_half, qkv_half = column_half(grad_out), product_half(normed_one_low, grad_mixed)
    mix = Reduction(place, lambda side: [out_half(side), qkv_half(side)])
    *mix_send, grad_mixed = tie(*mix.to_core(), grad_mixed)
    mix_came = [place.swap_core(piece) for piece in mix_send]
    grad_normed_one = matrix_product_transposed(grad_mixed, qkv_low)
    back_one, grad_gain_one = norm_back(grad_normed_one, scaled_one, inverse_one, gain_rows[0])
    grad_zero = grad_one + back_one
    proj_came, fc_came, grad_zero = tie(proj_came, fc_came, grad_zero)
    proj.from_line(proj_came)
    fc.from_b(fc_came)
    fc_send, grad_zero = tie(fc.to_line(), grad_zero)
    fc_came = place.swap_line(fc_send, bits[0])
    grad_zero_low = grad_zero.astype(jnp.bfloat16)
    grad_start = matmul(grad_zero_low, up_low)
    grad_start = keep_root * grad_start - grad_mse + target_shift * pred_float
    mix.keep()
    *mix_came, grad_start = tie(*mix_came, grad_start)
    mix_send, grad_start = tie(mix.to_a(mix_came), grad_start)
    mix_came = place.swap_a(mix_send)

    own_words = word_table.shape[0] // place.count // 2
    if own_words % 8 == 0:
        owner, spot = tokens // (2 * own_words), tokens % (2 * own_words)
        spot = (spot // own_words * place.count + owner) * own_words + spot % own_words
        words_send, words_kept = scatter_halves(place, grad_table_head, spot, grad_start)
    else:
        grad_table = grad_table_head.at[tokens].add(grad_start)
        split = grad_table.reshape(place.count, 2, own_words, EMB)
        words_send, words_kept = [
            lax.dynamic_index_in_dim(split, side, 1, False).reshape(-1, EMB)
            for side in (1 - place.core, place.core)
        ]
    words = Reduction(place, None, stack=True)
    words.keep([words_kept])
    words_send, fc_came, grad_zero_low = tie(words_send, fc_came, grad_zero_low)
    words_came = place.swap_core(words_send)
    fc.from_line(fc_came)
    time_half = product_half(grad_zero_low, feature_low)
    pair_half = column_half(jnp.concatenate([matmul_tn(grad_zero_low, noisy_low), grad_down], 1))
    exact_half = column_half(jnp.where(lanes == 0, grad_gain_one[:, None], exact))
    rest = Reduction(
        place, lambda side: [time_half(side), pair_half(side), exact_half(side)], exact=True
    )
    *rest_send, mix_came, words_came = tie(*rest.to_core(), mix_came, words_came)
    rest_came = [place.swap_core(piece) for piece in rest_send]
    words_send = words.to_a([words_came])
    words_send, mix_came = tie(words_send, mix_came)
    words_came = place.swap_a(words_send)
    fc_send, mix_send = tie(fc.to_line(), mix.to_b(mix_came))
    fc_came, mix_came = place.swap_line(fc_send, bits[1]), place.swap_b(mix_send)
    rest.keep()
    *rest_came, words_came = tie(*rest_came, words_came)
    words_send, rest_send = tie(words.to_b(words_came), rest.to_a(rest_came))
    words_came, rest_came = place.swap_b(words_send), place.swap_a(rest_send)
    mix_came, words_came = tie(mix_came, words_came)
    mix.from_b(mix_came)
    words.from_b(words_came)
    words_send, mix_send = tie(words.to_line(), mix.to_line())
    words_came = place.swap_line(words_send, bits[0])
    mix_came = place.swap_line(mix_send, bits[0])
    rest_came, fc_came, words_came = tie(rest_came, fc_came, words_came)
    words.from_line(words_came)
    fc.from_line(fc_came)
    words_send, rest_send = tie(words.to_line(), rest.to_b(rest_came))
    words_came, rest_came = place.swap_line(words_send, bits[1]), place.swap_b(rest_send)
    mix_came, rest_came = tie(mix_came, rest_came)
    mix.from_line(mix_came)
    rest.from_b(rest_came)
    rest_send, mix_send = tie(rest.to_line(), mix.to_line())
    rest_came = place.swap_line(rest_send, bits[0])
    mix_came = place.swap_line(mix_send, bits[1])
    words_came, rest_came = tie(words_came, rest_came)
    words.from_line(words_came)
    rest.from_line(rest_came)
    rest_came = place.swap_line(rest.to_line(), bits[1])
    mix_came, rest_came = tie(mix_came, rest_came)
    mix.from_line(mix_came)
    rest.from_line(rest_came)
    members = (proj, fc, mix, rest, words)
    for bit in bits[2:]:
        for member in members:
            member.from_line(place.swap_line(member.to_line(), bit))
    squares_local = jnp.zeros((), jnp.float32)
    for member in members:
        own = member.own[0]
        if member.exact:
            lanes = lax.broadcasted_iota(jnp.int32, own.shape, own.ndim - 1)
            aside = (place.core == 0) & (lanes == own.shape[-1] - TILE + 3)
            own = jnp.where(aside, 0.0, own)
        squares_local = squares_local + jnp.sum(own * own)
    ends = [member.finish(place.swap_core(member.to_end())) for member in members]
    (shard_proj,), (shard_fc,), (shard_out, shard_qkv), rest_ends, (shard_table,) = ends
    shard_time, shard_pair, shard_exact = rest_ends
    loss_sum = shard_exact[0, 3]
    shards = (
        shard_table,
        shard_pair[:, :EMB],
        shard_time,
        shard_qkv,
        shard_out,
        shard_fc,
        shard_proj,
        shard_pair[:, EMB:],
        shard_exact[:, :3].T,
    )
    squares = place.total(jnp.full((8, EMB), squares_local))[0, 0]
    grad_norm = jnp.sqrt(squares)
    factor = CLIP_NORM / jnp.maximum(grad_norm, CLIP_NORM)
    flips = (False, True, True, False, True, False, True, False, False)

    def lay(members):
        return [member.T if flip else member for member, flip in zip(members, flips)]

    results = adam_update(factor, lay(masters), lay(moments), lay(seconds), shards)
    results = [result.T if flips[at // 3] else result for at, result in enumerate(results)]
    return (
        loss_sum,
        grad_norm,
        results[0],
        results[1],
        results[2],
        results[3],
        results[4],
        results[5],
        results[6],
        results[7],
        results[8],
        results[9],
        results[10],
        results[11],
        results[12],
        results[13],
        results[14],
        results[15],
        results[16],
        results[17],
        results[18],
        results[19],
        results[20],
        results[21],
        results[22],
        results[23],
        results[24],
        results[25],
        results[26],
    )


def solution(mesh):
    return jax.shard_map(
        on_device,
        mesh=mesh,
        in_specs=(
            P(("bucket", "dp"), None),
            P(("bucket", "dp"), None),
            P(("bucket", "dp"), None),
            P(("bucket", "dp"), None),
            P(("bucket", "dp"), None, None),
            P(("bucket", "dp"), None),
            P(("bucket", "dp"), None),
            P(("bucket", "dp"), None),
            P(None, ("bucket", "dp")),
            P(None, ("bucket", "dp")),
            P(None, ("bucket", "dp")),
            P(None, ("bucket", "dp")),
            P(None, ("bucket", "dp")),
            P(None, ("bucket", "dp")),
            P(("bucket", "dp"), None),
            P(("bucket", "dp"), None),
            P(("bucket", "dp"), None),
            P(None, ("bucket", "dp")),
            P(None, ("bucket", "dp")),
            P(None, ("bucket", "dp")),
            P(("bucket", "dp"), None),
            P(("bucket", "dp"), None),
            P(("bucket", "dp"), None),
            P(None, ("bucket", "dp")),
            P(None, ("bucket", "dp")),
            P(None, ("bucket", "dp")),
            P(("bucket", "dp"), None),
            P(("bucket", "dp"), None),
            P(("bucket", "dp"), None),
            P(None, ("bucket", "dp")),
            P(None, ("bucket", "dp")),
            P(None, ("bucket", "dp")),
        ),
        out_specs=(
            P(),
            P(),
            P(("bucket", "dp"), None),
            P(("bucket", "dp"), None),
            P(("bucket", "dp"), None),
            P(None, ("bucket", "dp")),
            P(None, ("bucket", "dp")),
            P(None, ("bucket", "dp")),
            P(None, ("bucket", "dp")),
            P(None, ("bucket", "dp")),
            P(None, ("bucket", "dp")),
            P(("bucket", "dp"), None),
            P(("bucket", "dp"), None),
            P(("bucket", "dp"), None),
            P(None, ("bucket", "dp")),
            P(None, ("bucket", "dp")),
            P(None, ("bucket", "dp")),
            P(("bucket", "dp"), None),
            P(("bucket", "dp"), None),
            P(("bucket", "dp"), None),
            P(None, ("bucket", "dp")),
            P(None, ("bucket", "dp")),
            P(None, ("bucket", "dp")),
            P(("bucket", "dp"), None),
            P(("bucket", "dp"), None),
            P(("bucket", "dp"), None),
            P(None, ("bucket", "dp")),
            P(None, ("bucket", "dp")),
            P(None, ("bucket", "dp")),
        ),
        check_vma=False,
    )
```

time: 700 us -> 551 us (0.79)
  waiting for transfers between devices: 167 us -> 118 us
  starting transfers between devices: 83.5 us -> 54 us
  Pallas kernels: 172 us -> 146 us
  local copies, waits for them, and re-layouts: 52 us -> 35.1 us
  other arithmetic: 92 us -> 77.4 us
    ppermute x105 -> x64, waiting for transfers between devices: 167 us -> 118 us  [swap(): return lax.ppermute(array, AXES, pairs)]
    ppermute x105 -> x64, starting transfers between devices: 83.5 us -> 54 us  [swap(): return lax.ppermute(array, AXES, pairs)]
    dynamic_slice x7 -> x2, local copies, waits for them, and re-layouts: 28.9 us -> 0.12 us  [column_half(): return lambda side: lax.dynamic_slice_in_dim(array, side * half, half, 1)]
    unnamed x205 -> x188, local copies, waits for them, and re-layouts: 8.61 us -> 21.7 us
    sub x9 -> x0, other arithmetic: 12 us -> none  [adam_update(): master - rate * (moment_hat / (jnp.sqrt(second_hat) + ADAM_EPS) + decay *...]
    pallas_call x1, Pallas kernels: 56.5 us -> 45.3 us  [attention_backward(): pl.pallas_call(kernel, out_shape=jax.ShapeDtypeStruct(mixed.shape, jnp.bf...]
    scatter-add x1 -> x0, other arithmetic: 10.7 us -> none  [on_device(): jax.ops.segment_sum(grad_start, tokens, num_segments=word_table.shape[0])]
    pallas_call x1 -> x3, Pallas kernels: 54.9 us -> 47.9 us  [the longest x1 33.4 us: attention_forward(): pl.pallas_call(kernel, out_shape=(jax.ShapeDtypeStruct((length, width), j...]
  transfers between devices with their start and end apart: 105 -> 64, of which waited for: 41 -> 27; matrix products, arithmetic and copies ran while one was open for 20% -> 25% of each run, Pallas kernels for 10% -> 18%
where the time goes in v2:
time: 551 us; the launch traced here: 547 us
  Pallas kernels  146 us (26%)
  waiting for transfers between devices  118 us (21%)
  matrix products  108 us (20%)
  other arithmetic  77.4 us (14%)
  starting transfers between devices  54 us (10%)
  local copies, waits for them, and re-layouts  35.1 us (6%)
  between operations  8.03 us (1%)
    ppermute x64, waiting for transfers between devices, swap(): return lax.ppermute(array, AXES, pairs)  118 us
    ppermute x64, starting transfers between devices, swap(): return lax.ppermute(array, AXES, pairs)  54 us
    pallas_call x1, Pallas kernels, attention_backward(): pl.pallas_call(kernel, out_shape=jax.ShapeDtypeStruct(mixed.shape, jnp.bf...  45.3 us
    dot_general x6, matrix products, matmul(): return jnp.dot(left_op, right_op, preferred_element_type=jnp.float32)  45 us
    dot_general x7, matrix products, matrix_product_transposed(): lax.dot_general(left_op, right_op, (((1,), (1,)), ((), ())), preferred_el...  35 us
    pallas_call x1, Pallas kernels, attention_forward(): pl.pallas_call(kernel, out_shape=(jax.ShapeDtypeStruct((length, width), j...  33.4 us
    pallas_call x1, Pallas kernels, head_pass(): pl.pallas_call(kernel, out_shape=(jax.ShapeDtypeStruct((words, width), jn...  32.4 us
    dot_general x11, matrix products, matmul_tn(): lax.dot_general(left_op, right_op, (((0,), (0,)), ((), ())), preferred_el...  27.8 us
  transfers between devices with their start and end apart: 64, of which 27 were waited for; matrix products, arithmetic and copies ran while one was open for 25% of the time, Pallas kernels for 18%

profile of v2, /device:TPU:0, one launch (start us, length us, event | category | flops | bytes accessed | tf_op | source)
XLA Modules:
  0.0 547.3 jit_solution(234343960098527789)
XLA Ops:
  6.2 4.0 collective-permute-start.1
  20.6 3.6 collective-permute-done.3
  24.2 2.9 collective-permute-start.4
  28.2 3.6 collective-permute-done.4
  33.6 3.4 collective-permute-start.12
  37.5 6.5 %fusion.30 = (bf16[1024,384]{1,0:T(8,128)(2,1)S(1)}, bf16[1024,384]{1,0:T(8,128)(2,1)S(1)}) fusion(f32[384]{0:T(512)S(1)} %multiply_exponential_fusion, f32[1024]{0:T(1024)S(1)} %convert_element_type.305), kind=kLoop, calls=%fused_computation.61 | loop fusion | flops 1179648 | bytes 1578496 | tf_op jit(solution)/shard_map/convert.39
  50.6 3.6 collective-permute-done.10.refs_1_
  55.1 6.9 %collective-permute-done.8.refs_1_ = bf16[8,352,128]{2,1,0:T(8,128)(2,1)S(1)} collective-permute-done((bf16[8,352,128]{2,1,0:T(8,128)(2,1)S(1)}, bf16[8,352,128]{2,1,0:T(8,128)(2,1)S(1)}, u32[]{:S(2)}, u32[]{:S(2)}) %collective-permute-start.8) | collective-permute-done | bytes 720928 | tf_op jit(solution)/shard_map/ppermute | solution.py:520
  63.9 3.4 assemble.5
  67.6 4.8 fusion.34
  72.4 8.9 %collective-permute-done.18 = bf16[2,24,7040]{2,1,0:T(8,128)(2,1)} collective-permute-done((bf16[2,24,7040]{2,1,0:T(8,128)(2,1)}, bf16[2,24,7040]{2,1,0:T(8,128)(2,1)}, u32[]{:S(2)}, u32[]{:S(2)}) %collective-permute-start.18) | collective-permute-done | bytes 675872 | tf_op jit(solution)/shard_map/ppermute | solution.py:520
  81.3 2.6 pad_maximum_fusion.2
  85.9 5.5 %assemble.4 = bf16[4,4,2,352,128]{4,3,2,1,0:T(8,128)(2,1)S(1)} custom-call(s32[3]{0:T(128)S(1)} %pad_add_fusion.1.flags_ref, bf16[8,352,128]{2,1,0:T(8,128)(2,1)S(1)} %copy-done.4, bf16[8,352,128]{2,1,0:T(8,128)(2,1)S(1)} %copy-done.10, bf16[8,352,128]{2,1,0:T(8,128)(2,1)S(1)} %copy-done.8, bf16[8,352,128]{2,1,0:T(8,128)(2,1)S(1)} %copy-done.12), custom_call_target="tpu_custom_call" | custom-call | tf_op jit(solution)/shard_map/assemble/pallas_call | solution.py:578
  95.4 3.2 gather_fusion
  100.1 2.7 fusion.124
  104.5 3.9 collective-permute-done.16.refs_1_
  111.0 3.8 assemble.6
  114.8 7.5 %convolution_convert_fusion.q_ref.k_ref.v_ref = bf16[1024,2304]{1,0:T(8,128)(2,1)} fusion(bf16[1024,768]{0,1:T(8,128)(2,1)S(1)} %multiply_convert_fusion.3, bf16[768,2304]{1,0:T(8,128)(2,1)} %bitcast.282), kind=kOutput, calls=%fused_computation.11 | convolution fusion | flops 3626237952 | bytes 9830400 | tf_op jit(solution)/shard_map/dot_general | solution.py:29
  122.3 4.1 collective-permute-done.19
  127.5 33.4 %attention_forward.1 = (bf16[1024,768]{1,0:T(8,128)(2,1)S(1)}, f32[16,1024]{1,0:T(8,128)S(1)}) custom-call(s32[2,8]{1,0:T(2,128)S(1)} %pad_add_fusion.windows_ref, bf16[1024,2304]{1,0:T(8,128)(2,1)} %convolution_convert_fusion.q_ref.k_ref.v_ref, bf16[1024,2304]{1,0:T(8,128)(2,1)} %convolution_convert_fusion.q_ref.k_ref.v_ref, ...), custom_call_target="tpu_custom_call" | custom-call | tf_op jit(solution)/shard_map/attention_forward/pallas_call | solution.py:190
  165.5 3.7 collective-permute-done.23.refs_3_
  171.0 8.2 %assemble.7 = bf16[4,4,2,24,7040]{4,3,2,1,0:T(8,128)(2,1)} custom-call(s32[3]{0:T(128)S(1)} %pad_add_fusion.1.flags_ref, bf16[8,24,7040]{2,1,0:T(8,128)(2,1)S(1)} %copy-done.1, bf16[8,24,7040]{2,1,0:T(8,128)(2,1)} %collective-permute-done.21.refs_1_, bf16[8,24,7040]{2,1,0:T(8,128)(2,1)} %copy-done.48, bf16[8,24,7040]{2,1,0:T(8,128)(2,1)} %collective-permute-done.23.refs_3_), custom_call_target="tpu_custom_call" | custom-call | tf_op jit(solution)/shard_map/assemble/pallas_call | solution.py:578
  179.3 2.8 fusion.125
  183.1 2.1 slice-done.2
  185.2 11.7 %multiply_convert_fusion = (bf16[1024,3072]{1,0:T(8,128)(2,1)}, f32[1024,3072]{1,0:T(8,128)}) fusion(bf16[1024,768]{0,1:T(8,128)(2,1)S(1)} %multiply_convert_fusion.2, bf16[768,7040]{1,0:T(8,128)(2,1)S(1)} %bitcast.270), kind=kOutput, calls=%fused_computation.10 | convolution fusion | flops 4860149760 | bytes 25165824 | tf_op jit(solution)/shard_map/dot_general | solution.py:29
  196.9 7.3 %fusion.126 = (f32[1024]{0:T(1024)S(1)}, f32[1024,768]{0,1:T(8,128)S(1)}) fusion(f32[1024,768]{0,1:T(8,128)S(1)} %get-tuple-element.416, bf16[1024,3072]{1,0:T(8,128)(2,1)} %get-tuple-element.417, bf16[768,7040]{1,0:T(8,128)(2,1)S(1)} %bitcast.271), kind=kOutput, calls=%fused_computation.362 | convolution fusion | flops 4833410048 | bytes 17305600 | tf_op jit(solution)/shard_map/dot_general | solution.py:39
  205.7 2.7 multiply_reduce_fusion.12
  208.5 32.4 %head_pass.1 = (f32[11264,128]{1,0:T(8,128)}, f32[128,1024]{1,0:T(8,128)S(1)}, f32[1,1024]{1,0:T(1,128)S(1)}) custom-call(bf16[1024,128]{1,0:T(8,128)(2,1)S(1)} %get-tuple-element.351.pred_ref, bf16[11264,128]{1,0:T(8,128)(2,1)S(1)} %bitcast.252, f32[1,1024]{1,0:T(1,128)S(1)} %multiply_multiply_fusion.3.weight_ref), custom_call_target="tpu_custom_call" | custom-call | tf_op jit(solution)/shard_map/head_pass/pallas_call | solution.py:399
  245.1 3.3 multiply_reduce_fusion.3
  251.3 2.6 fusion.19
  254.3 2.6 fusion.21
  257.0 18.5 %fusion.6 = bf16[1024,3072]{1,0:T(8,128)(2,1)} fusion(f32[1024,3072]{1,0:T(8,128)} %get-tuple-element.418, bf16[1024,768]{0,1:T(8,128)(2,1)S(1)} %fusion.119, bf16[768,7040]{1,0:T(8,128)(2,1)} %bitcast.265), kind=kOutput, calls=%fused_computation.9 | convolution fusion | flops 4894752768 | bytes 25165824 | tf_op jit(solution)/shard_map/dot_general | solution.py:29
  278.5 2.4 copy-done.83
  280.9 4.2 fusion.17
  285.4 10.0 %multiply_reduce_fusion.2 = (f32[768]{0:T(1024)S(1)}, f32[1024]{0:T(1024)S(1)}, f32[1024]{0:T(1024)S(1)}, f32[1024,768]{0,1:T(8,128)S(1)}) fusion(f32[1024,768]{0,1:T(8,128)} %copy-done.26, f32[1024]{0:T(1024)S(1)} %add_rsqrt_fusion.1, f32[1024]{0:T(1024)S(1)} %broadcast_multiply_fusion.8, f32[768]{0:T(1024)S(1)} %get-tuple-element.335, ...), kind=kOutput, calls=%fused_computation.24 | convolution fusion | flops 4838126592 | bytes 17324032 | tf_op jit(solution)/shard_map/dot_general | solution.py:39
  295.4 2.0 select_select_fusion
  297.5 4.6 fusion.15
  302.2 3.3 fusion.120
  305.8 2.0 fusion.52
  310.9 2.8 fusion.127
  313.8 2.7 convolution_convert_fusion.1.do_ref
  316.5 8.6 %collective-permute-done.27 = bf16[192,1536]{1,0:T(8,128)(2,1)S(1)} collective-permute-done((bf16[192,1536]{1,0:T(8,128)(2,1)S(1)}, bf16[192,1536]{1,0:T(8,128)(2,1)S(1)}, u32[]{:S(2)}, u32[]{:S(2)}) %collective-permute-start.27) | collective-permute-done | bytes 589856 | tf_op jit(solution)/shard_map/ppermute | solution.py:520
  326.1 45.3 %attention_backward.1 = bf16[1024,2304]{1,0:T(8,128)(2,1)} custom-call(s32[2,8]{1,0:T(2,128)S(1)} %pad_add_fusion.windows_ref, bf16[1024,2304]{1,0:T(8,128)(2,1)} %convolution_convert_fusion.q_ref.k_ref.v_ref, bf16[1024,2304]{1,0:T(8,128)(2,1)} %convolution_convert_fusion.q_ref.k_ref.v_ref, bf16[1024,2304]{1,0:T(8,128)(2,1)} %convolution_convert_fusion.q_ref.k_ref.v_ref, ...), custom_call_target="tpu_custom_call" | custom-call | tf_op jit(solution)/shard_map/attention_backward/pallas_call | solution.py:316
  371.5 2.2 fusion.39
  375.4 4.0 fusion.25
  379.9 4.3 multiply_reduce_fusion
  385.3 2.2 fusion.23
  387.6 2.2 fusion.38
  389.9 2.1 collective-permute-start.34
  398.0 8.7 %scatter_halves.1 = (f32[5632,128]{1,0:T(8,128)S(1)}, f32[5632,128]{1,0:T(8,128)}) custom-call(s32[1024]{0:T(1024)S(1)} %get-tuple-element.426.spots_ref, s32[1]{0:T(128)} %bitcast.2.flag_ref, f32[11264,128]{1,0:T(8,128)} %get-tuple-element.216.table_ref, f32[1024,128]{1,0:T(8,128)S(1)} %fusion.33.rows_ref), custom_call_target="tpu_custom_call" | custom-call | tf_op jit(solution)/shard_map/scatter_halves/pallas_call | solution.py:644
  407.4 2.1 fusion.129
  413.1 14.2 %collective-permute-done.35 = bf16[2,192,1536]{2,1,0:T(8,128)(2,1)S(1)} collective-permute-done((bf16[2,192,1536]{2,1,0:T(8,128)(2,1)S(1)}, bf16[2,192,1536]{2,1,0:T(8,128)(2,1)S(1)}, u32[]{:S(2)}, u32[]{:S(2)}) %collective-permute-start.35) | collective-permute-done | bytes 1179680 | tf_op jit(solution)/shard_map/ppermute | solution.py:520
  434.8 9.4 %collective-permute-done.40 = bf16[2,1408,128]{2,1,0:T(8,128)(2,1)S(1)} collective-permute-done((bf16[2,1408,128]{2,1,0:T(8,128)(2,1)S(1)}, bf16[2,1408,128]{2,1,0:T(8,128)(2,1)S(1)}, u32[]{:S(2)}, u32[]{:S(2)}) %collective-permute-start.40) | collective-permute-done | bytes 720928 | tf_op jit(solution)/shard_map/ppermute | solution.py:520
  449.0 3.5 collective-permute-start.44
  452.6 8.0 %collective-permute-done.44 = bf16[1408,128]{1,0:T(8,128)(2,1)} collective-permute-done((bf16[1408,128]{1,0:T(8,128)(2,1)}, bf16[1408,128]{1,0:T(8,128)(2,1)}, u32[]{:S(2)}, u32[]{:S(2)}) %collective-permute-start.44) | collective-permute-done | bytes 360480 | tf_op jit(solution)/shard_map/ppermute | solution.py:520
  465.0 2.8 collective-permute-start.42
  471.1 2.4 collective-permute-done.45
  477.4 8.2 %collective-permute-done.46 = f32[2,2,24,1536]{3,2,1,0:T(8,128)S(1)} collective-permute-done((f32[2,2,24,1536]{3,2,1,0:T(8,128)S(1)}, f32[2,2,24,1536]{3,2,1,0:T(8,128)S(1)}, u32[]{:S(2)}, u32[]{:S(2)}) %collective-permute-start.46) | collective-permute-done | bytes 589856 | tf_op jit(solution)/shard_map/ppermute | solution.py:520
  488.5 2.2 collective-permute-start.48
  492.9 13.6 %collective-permute-done.48 = f32[1,2,176,128]{3,2,1,0:T(8,128)S(1)} collective-permute-done((f32[1,2,176,128]{3,2,1,0:T(8,128)}, f32[1,2,176,128]{3,2,1,0:T(8,128)S(1)}, u32[]{:S(2)}, u32[]{:S(2)}) %collective-permute-start.48) | collective-permute-done | bytes 180256 | tf_op jit(solution)/shard_map/ppermute | solution.py:520
  511.9 6.3 %collective-permute-done.51 = f32[1,2,24,640]{3,2,1,0:T(8,128)S(1)} collective-permute-done((f32[1,2,24,640]{3,2,1,0:T(8,128)S(1)}, f32[1,2,24,640]{3,2,1,0:T(8,128)S(1)}, u32[]{:S(2)}, u32[]{:S(2)}) %collective-permute-start.51) | collective-permute-done | bytes 122912 | tf_op jit(solution)/shard_map/ppermute | solution.py:520
  522.7 2.4 collective-permute-start.56
  530.4 2.9 collective-permute-start.57
  540.0 5.9 %adam_update.1 = (f32[352,128]{1,0:T(8,128)}, f32[352,128]{1,0:T(8,128)}, f32[352,128]{1,0:T(8,128)}, f32[24,128]{1,0:T(8,128)}, f32[24,128]{1,0:T(8,128)}, /*in...) custom-call(f32[1]{0:T(128)} %bitcast.88.factor_ref, ...), custom_call_target="tpu_custom_call" | custom-call | tf_op jit(solution)/shard_map/adam_update/pallas_call | solution.py:477
  (464 shorter events, 125.6 us)
Async XLA Ops:
  6.2 12.2 %collective-permute-start.1 = (bf16[1,24,1024]{2,1,0:T(8,128)(2,1)S(1)}, bf16[1,24,1024]{2,1,0:T(8,128)(2,1)S(1)}, u32[]{:S(2)}, u32[]{:S(2)}) collective-permute-start(bf16[1,24,1024]{2,1,0:T(8,128)(2,1)S(1)} %bitcast.299), channel_id=1, source_target_pairs={{0,4},{1,5},{2,6},{3,7},{4,0},{5,1},{6,2},{7,3},{8,12},{9,13},{10,... | collective-permute-start | bytes 147464 | tf_op jit(solution)/shard_map/ppermute | solution.py:520
  11.2 7.3 %collective-permute-start = (bf16[1,352,128]{2,1,0:T(8,128)(2,1)S(1)}, bf16[1,352,128]{2,1,0:T(8,128)(2,1)S(1)}, u32[]{:S(2)}, u32[]{:S(2)}) collective-permute-start(bf16[1,352,128]{2,1,0:T(8,128)(2,1)S(1)} %convert_bitcast_fusion.2), channel_id=1, source_target_pairs={{0,4},{1,5},{2,6},{3,7},{4,0},{5,1},{6,2},{7,3},{8,12},{9,13},{10,... | collective-permute-start | bytes 270344 | tf_op jit(solution)/shard_map/ppermute | solution.py:520
  18.5 5.7 %collective-permute-start.3 = (bf16[2,24,1024]{2,1,0:T(8,128)(2,1)S(1)}, bf16[2,24,1024]{2,1,0:T(8,128)(2,1)S(1)}, u32[]{:S(2)}, u32[]{:S(2)}) collective-permute-start(bf16[2,24,1024]{2,1,0:T(8,128)(2,1)S(1)} %pad_maximum_fusion.15), channel_id=1, source_target_pairs={{0,2},{1,3},{2,0},{3,1},{4,6},{5,7},{6,4},{7,5},{8,10},{9,11},{10,... | collective-permute-start | bytes 294920 | tf_op jit(solution)/shard_map/ppermute | solution.py:520
  20.4 7.7 %collective-permute-start.2 = (bf16[2,352,128]{2,1,0:T(8,128)(2,1)S(1)}, bf16[2,352,128]{2,1,0:T(8,128)(2,1)S(1)}, u32[]{:S(2)}, u32[]{:S(2)}) collective-permute-start(bf16[2,352,128]{2,1,0:T(8,128)(2,1)S(1)} %pad_maximum_fusion.14), channel_id=1, source_target_pairs={{0,2},{1,3},{2,0},{3,1},{4,6},{5,7},{6,4},{7,5},{8,10},{9,11},{10,... | collective-permute-start | bytes 540680 | tf_op jit(solution)/shard_map/ppermute | solution.py:520
  24.2 7.5 %collective-permute-start.4 = (bf16[1,24,2304]{2,1,0:T(8,128)(2,1)S(1)}, bf16[1,24,2304]{2,1,0:T(8,128)(2,1)S(1)}, u32[]{:S(2)}, u32[]{:S(2)}) collective-permute-start(bf16[1,24,2304]{2,1,0:T(8,128)(2,1)S(1)} %convert_bitcast_fusion.1), channel_id=1, source_target_pairs={{0,4},{1,5},{2,6},{3,7},{4,0},{5,1},{6,2},{7,3},{8,12},{9,13},{10,... | collective-permute-start | bytes 331784 | tf_op jit(solution)/shard_map/ppermute | solution.py:520
  31.8 13.6 %collective-permute-start.6 = (bf16[4,24,1024]{2,1,0:T(8,128)(2,1)S(1)}, bf16[4,24,1024]{2,1,0:T(8,128)(2,1)S(1)}, u32[]{:S(2)}, u32[]{:S(2)}) collective-permute-start(bf16[4,24,1024]{2,1,0:T(8,128)(2,1)S(1)} %pad_maximum_fusion.13), channel_id=1, source_target_pairs={{0,8},{1,17},{2,10},{3,19},{4,12},{5,21},{6,14},{7,23},{8,0},{9,25... | collective-permute-start | bytes 589832 | tf_op jit(solution)/shard_map/ppermute | solution.py:520
  33.5 11.9 %collective-permute-start.7 = (bf16[2,24,2304]{2,1,0:T(8,128)(2,1)S(1)}, bf16[2,24,2304]{2,1,0:T(8,128)(2,1)S(1)}, u32[]{:S(2)}, u32[]{:S(2)}) collective-permute-start(bf16[2,24,2304]{2,1,0:T(8,128)(2,1)S(1)} %pad_maximum_fusion.12), channel_id=1, source_target_pairs={{0,2},{1,3},{2,0},{3,1},{4,6},{5,7},{6,4},{7,5},{8,10},{9,11},{10,... | collective-permute-start | bytes 663560 | tf_op jit(solution)/shard_map/ppermute | solution.py:520
  33.6 16.1 %collective-permute-start.12 = (bf16[1,24,7040]{2,1,0:T(8,128)(2,1)S(1)}, bf16[1,24,7040]{2,1,0:T(8,128)(2,1)S(1)}, u32[]{:S(2)}, u32[]{:S(2)}) collective-permute-start(bf16[1,24,7040]{2,1,0:T(8,128)(2,1)S(1)} %maximum_bitcast_fusion), channel_id=1, source_target_pairs={{0,4},{1,5},{2,6},{3,7},{4,0},{5,1},{6,2},{7,3},{8,12},{9,13},{10,... | collective-permute-start | bytes 1013768 | tf_op jit(solution)/shard_map/ppermute | solution.py:520
  37.0 9.2 %collective-permute-start.5 = (bf16[4,352,128]{2,1,0:T(8,128)(2,1)S(1)}, bf16[4,352,128]{2,1,0:T(8,128)(2,1)S(1)}, u32[]{:S(2)}, u32[]{:S(2)}) collective-permute-start(bf16[4,352,128]{2,1,0:T(8,128)(2,1)S(1)} %pad_maximum_fusion.10), channel_id=1, source_target_pairs={{0,8},{1,17},{2,10},{3,19},{4,12},{5,21},{6,14},{7,23},{8,0},{9,25... | collective-permute-start | bytes 1081352 | tf_op jit(solution)/shard_map/ppermute | solution.py:520
  46.3 4.3 collective-permute-start.11
  46.4 7.8 %collective-permute-start.10 = (bf16[8,24,1024]{2,1,0:T(8,128)(2,1)S(1)}, bf16[8,24,1024]{2,1,0:T(8,128)(2,1)S(1)}, u32[]{:S(2)}, u32[]{:S(2)}) collective-permute-start(bf16[8,24,1024]{2,1,0:T(8,128)(2,1)S(1)} %pad_maximum_fusion.9.refs_0_), channel_id=1, source_target_pairs={{0,16},{1,9},{2,18},{3,11},{4,20},{5,13},{6,22},{7,15},{8,24},{9,1... | collective-permute-start | bytes 1179656 | tf_op jit(solution)/shard_map/ppermute | solution.py:520
  48.1 6.2 %collective-permute-start.9 = (bf16[8,352,128]{2,1,0:T(8,128)(2,1)S(1)}, bf16[8,352,128]{2,1,0:T(8,128)(2,1)S(1)}, u32[]{:S(2)}, u32[]{:S(2)}) collective-permute-start(bf16[8,352,128]{2,1,0:T(8,128)(2,1)S(1)} %pad_maximum_fusion.5.refs_0_), channel_id=1, source_target_pairs={{0,1},{1,0},{2,3},{3,2},{4,5},{5,4},{6,7},{7,6},{8,9},{9,8},{10,11... | collective-permute-start | bytes 2162696 | tf_op jit(solution)/shard_map/ppermute | solution.py:520
  48.1 13.9 %collective-permute-start.8 = (bf16[8,352,128]{2,1,0:T(8,128)(2,1)S(1)}, bf16[8,352,128]{2,1,0:T(8,128)(2,1)S(1)}, u32[]{:S(2)}, u32[]{:S(2)}) collective-permute-start(bf16[8,352,128]{2,1,0:T(8,128)(2,1)S(1)} %pad_maximum_fusion.5.refs_0_), channel_id=1, source_target_pairs={{0,16},{1,9},{2,18},{3,11},{4,20},{5,13},{6,22},{7,15},{8,24},{9,1... | collective-permute-start | bytes 2162696 | tf_op jit(solution)/shard_map/ppermute | solution.py:520
  61.9 1.9 collective-permute-start.15
  62.0 29.4 %collective-permute-start.14 = (bf16[4,24,2304]{2,1,0:T(8,128)(2,1)}, bf16[4,24,2304]{2,1,0:T(8,128)(2,1)}, u32[]{:S(2)}, u32[]{:S(2)}) collective-permute-start(bf16[4,24,2304]{2,1,0:T(8,128)(2,1)} %pad_maximum_fusion.8), channel_id=1, source_target_pairs={{0,8},{1,17},{2,10},{3,19},{4,12},{5,21},{6,14},{7,23},{8,0},{9,25... | collective-permute-start | bytes 1327112 | tf_op jit(solution)/shard_map/ppermute | solution.py:520
  63.5 17.7 %collective-permute-start.18 = (bf16[2,24,7040]{2,1,0:T(8,128)(2,1)}, bf16[2,24,7040]{2,1,0:T(8,128)(2,1)}, u32[]{:S(2)}, u32[]{:S(2)}) collective-permute-start(bf16[2,24,7040]{2,1,0:T(8,128)(2,1)} %pad_maximum_fusion.7), channel_id=1, source_target_pairs={{0,2},{1,3},{2,0},{3,1},{4,6},{5,7},{6,4},{7,5},{8,10},{9,11},{10,... | collective-permute-start | bytes 2027528 | tf_op jit(solution)/shard_map/ppermute | solution.py:520
  63.6 20.4 %collective-permute-start.13 = (bf16[8,352,128]{2,1,0:T(8,128)(2,1)S(1)}, bf16[8,352,128]{2,1,0:T(8,128)(2,1)S(1)}, u32[]{:S(2)}, u32[]{:S(2)}) collective-permute-start(bf16[8,352,128]{2,1,0:T(8,128)(2,1)S(1)} %collective-permute-done.8.refs_1_), channel_id=1, source_target_pairs={{0,1},{1,0},{2,3},{3,2},{4,5},{5,4},{6,7},{7,6},{8,9},{9,8},{10,11... | collective-permute-start | bytes 2162696 | tf_op jit(solution)/shard_map/ppermute | solution.py:520
  95.0 9.4 %collective-permute-start.17 = (bf16[8,24,2304]{2,1,0:T(8,128)(2,1)}, bf16[8,24,2304]{2,1,0:T(8,128)(2,1)}, u32[]{:S(2)}, u32[]{:S(2)}) collective-permute-start(bf16[8,24,2304]{2,1,0:T(8,128)(2,1)} %constant_dynamic-update-slice_fusion.refs_0_), channel_id=1, source_target_pairs={{0,1},{1,0},{2,3},{3,2},{4,5},{5,4},{6,7},{7,6},{8,9},{9,8},{10,11... | collective-permute-start | bytes 2654216 | tf_op jit(solution)/shard_map/ppermute | solution.py:520
  95.0 13.4 %collective-permute-start.16 = (bf16[8,24,2304]{2,1,0:T(8,128)(2,1)}, bf16[8,24,2304]{2,1,0:T(8,128)(2,1)}, u32[]{:S(2)}, u32[]{:S(2)}) collective-permute-start(bf16[8,24,2304]{2,1,0:T(8,128)(2,1)} %constant_dynamic-update-slice_fusion.refs_0_), channel_id=1, source_target_pairs={{0,16},{1,9},{2,18},{3,11},{4,20},{5,13},{6,22},{7,15},{8,24},{9,1... | collective-permute-start | bytes 2654216 | tf_op jit(solution)/shard_map/ppermute | solution.py:520
  108.4 2.6 collective-permute-start.20
  108.4 18.0 %collective-permute-start.19 = (bf16[4,24,7040]{2,1,0:T(8,128)(2,1)S(1)}, bf16[4,24,7040]{2,1,0:T(8,128)(2,1)S(1)}, u32[]{:S(2)}, u32[]{:S(2)}) collective-permute-start(bf16[4,24,7040]{2,1,0:T(8,128)(2,1)S(1)} %copy-done.35), channel_id=1, source_target_pairs={{0,8},{1,17},{2,10},{3,19},{4,12},{5,21},{6,14},{7,23},{8,0},{9,25... | collective-permute-start | bytes 4055048 | tf_op jit(solution)/shard_map/ppermute | solution.py:520
  126.7 35.3 %collective-permute-start.22 = (bf16[8,24,7040]{2,1,0:T(8,128)(2,1)S(1)}, bf16[8,24,7040]{2,1,0:T(8,128)(2,1)S(1)}, u32[]{:S(2)}, u32[]{:S(2)}) collective-permute-start(bf16[8,24,7040]{2,1,0:T(8,128)(2,1)S(1)} %pad_maximum_fusion.refs_0_), channel_id=1, source_target_pairs={{0,1},{1,0},{2,3},{3,2},{4,5},{5,4},{6,7},{7,6},{8,9},{9,8},{10,11... | collective-permute-start | bytes 8110088 | tf_op jit(solution)/shard_map/ppermute | solution.py:520
  126.8 35.3 %collective-permute-start.21 = (bf16[8,24,7040]{2,1,0:T(8,128)(2,1)S(1)}, bf16[8,24,7040]{2,1,0:T(8,128)(2,1)}, u32[]{:S(2)}, u32[]{:S(2)}) collective-permute-start(bf16[8,24,7040]{2,1,0:T(8,128)(2,1)S(1)} %pad_maximum_fusion.refs_0_), channel_id=1, source_target_pairs={{0,16},{1,9},{2,18},{3,11},{4,20},{5,13},{6,22},{7,15},{8,24},{9,1... | collective-permute-start | bytes 8110088 | tf_op jit(solution)/shard_map/ppermute | solution.py:520
  163.6 5.7 %collective-permute-start.23 = (bf16[8,24,7040]{2,1,0:T(8,128)(2,1)}, bf16[8,24,7040]{2,1,0:T(8,128)(2,1)}, u32[]{:S(2)}, u32[]{:S(2)}) collective-permute-start(bf16[8,24,7040]{2,1,0:T(8,128)(2,1)} %collective-permute-done.21.refs_1_), channel_id=1, source_target_pairs={{0,1},{1,0},{2,3},{3,2},{4,5},{5,4},{6,7},{7,6},{8,9},{9,8},{10,11... | collective-permute-start | bytes 8110088 | tf_op jit(solution)/shard_map/ppermute | solution.py:520
  254.0 21.5 %collective-permute-start.24 = (f32[768,1536]{1,0:T(8,128)S(1)}, f32[768,1536]{1,0:T(8,128)S(1)}, u32[]{:S(2)}, u32[]{:S(2)}) collective-permute-start(f32[768,1536]{1,0:T(8,128)S(1)} %fusion.19), channel_id=1, source_target_pairs={{0,1},{1,0},{2,3},{3,2},{4,5},{5,4},{6,7},{7,6},{8,9},{9,8},{10,11... | collective-permute-start | bytes 14155784 | tf_op jit(solution)/shard_map/ppermute | solution.py:520
  285.1 20.4 %collective-permute-start.26 = (f32[768,1536]{1,0:T(8,128)}, f32[768,1536]{1,0:T(8,128)}, u32[]{:S(2)}, u32[]{:S(2)}) collective-permute-start(f32[768,1536]{1,0:T(8,128)} %fusion.17), channel_id=1, source_target_pairs={{0,1},{1,0},{2,3},{3,2},{4,5},{5,4},{6,7},{7,6},{8,9},{9,8},{10,11... | collective-permute-start | bytes 14155784 | tf_op jit(solution)/shard_map/ppermute | solution.py:520
  285.3 20.1 %collective-permute-start.25 = (bf16[2,192,1536]{2,1,0:T(8,128)(2,1)S(1)}, bf16[2,192,1536]{2,1,0:T(8,128)(2,1)S(1)}, u32[]{:S(2)}, u32[]{:S(2)}) collective-permute-start(bf16[2,192,1536]{2,1,0:T(8,128)(2,1)S(1)} %copy-done.65), channel_id=1, source_target_pairs={{0,8},{1,17},{2,10},{3,19},{4,12},{5,21},{6,14},{7,23},{8,0},{9,25... | collective-permute-start | bytes 3538952 | tf_op jit(solution)/shard_map/ppermute | solution.py:520
  309.0 16.1 %collective-permute-start.27 = (bf16[192,1536]{1,0:T(8,128)(2,1)S(1)}, bf16[192,1536]{1,0:T(8,128)(2,1)S(1)}, u32[]{:S(2)}, u32[]{:S(2)}) collective-permute-start(bf16[192,1536]{1,0:T(8,128)(2,1)S(1)} %fusion.41), channel_id=1, source_target_pairs={{0,16},{1,9},{2,18},{3,11},{4,20},{5,13},{6,22},{7,15},{8,24},{9,1... | collective-permute-start | bytes 1769480 | tf_op jit(solution)/shard_map/ppermute | solution.py:520
  309.0 62.6 %collective-permute-start.29 = (bf16[2,192,1536]{2,1,0:T(8,128)(2,1)}, bf16[2,192,1536]{2,1,0:T(8,128)(2,1)}, u32[]{:S(2)}, u32[]{:S(2)}) collective-permute-start(bf16[2,192,1536]{2,1,0:T(8,128)(2,1)} %pad_maximum_fusion.4), channel_id=1, source_target_pairs={{0,8},{1,17},{2,10},{3,19},{4,12},{5,21},{6,14},{7,23},{8,0},{9,25... | collective-permute-start | bytes 3538952 | tf_op jit(solution)/shard_map/ppermute | solution.py:520
  326.1 45.4 %collective-permute-start.28 = (bf16[2,2,24,1536]{3,2,1,0:T(8,128)(2,1)}, bf16[2,2,24,1536]{3,2,1,0:T(8,128)(2,1)}, u32[]{:S(2)}, u32[]{:S(2)}) collective-permute-start(bf16[2,2,24,1536]{3,2,1,0:T(8,128)(2,1)} %fusion.65), channel_id=1, source_target_pairs={{0,2},{1,3},{2,0},{3,1},{4,6},{5,7},{6,4},{7,5},{8,10},{9,11},{10,... | collective-permute-start | bytes 884744 | tf_op jit(solution)/shard_map/ppermute | solution.py:520
  375.2 12.4 %collective-permute-start.32 = (bf16[1,2,24,1536]{3,2,1,0:T(8,128)(2,1)S(1)}, bf16[1,2,24,1536]{3,2,1,0:T(8,128)(2,1)S(1)}, u32[]{:S(2)}, u32[]{:S(2)}) collective-permute-start(bf16[1,2,24,1536]{3,2,1,0:T(8,128)(2,1)S(1)} %dynamic-slice_convert_fusion.1), channel_id=1, source_target_pairs={{0,4},{1,5},{2,6},{3,7},{4,0},{5,1},{6,2},{7,3},{8,12},{9,13},{10,... | collective-permute-start | bytes 442376 | tf_op jit(solution)/shard_map/ppermute | solution.py:520
  375.3 12.3 %collective-permute-start.33 = (bf16[192,1536]{1,0:T(8,128)(2,1)S(1)}, bf16[192,1536]{1,0:T(8,128)(2,1)S(1)}, u32[]{:S(2)}, u32[]{:S(2)}) collective-permute-start(bf16[192,1536]{1,0:T(8,128)(2,1)S(1)} %fusion.39), channel_id=1, source_target_pairs={{0,16},{1,9},{2,18},{3,11},{4,20},{5,13},{6,22},{7,15},{8,24},{9,1... | collective-permute-start | bytes 1769480 | tf_op jit(solution)/shard_map/ppermute | solution.py:520
  379.4 14.5 %collective-permute-start.30 = (f32[768,384]{1,0:T(8,128)S(1)}, f32[768,384]{1,0:T(8,128)S(1)}, u32[]{:S(2)}, u32[]{:S(2)}) collective-permute-start(f32[768,384]{1,0:T(8,128)S(1)} %constant_dynamic-slice_fusion.4), channel_id=1, source_target_pairs={{0,1},{1,0},{2,3},{3,2},{4,5},{5,4},{6,7},{7,6},{8,9},{9,8},{10,11... | collective-permute-start | bytes 3538952 | tf_op jit(solution)/shard_map/ppermute | solution.py:520
  379.4 14.5 %collective-permute-start.31 = (f32[768,1152]{1,0:T(8,128)}, f32[768,1152]{1,0:T(8,128)S(1)}, u32[]{:S(2)}, u32[]{:S(2)}) collective-permute-start(f32[768,1152]{1,0:T(8,128)} %fusion.25), channel_id=1, source_target_pairs={{0,1},{1,0},{2,3},{3,2},{4,5},{5,4},{6,7},{7,6},{8,9},{9,8},{10,11... | collective-permute-start | bytes 10616840 | tf_op jit(solution)/shard_map/ppermute | solution.py:520
  389.9 16.8 %collective-permute-start.34 = (bf16[2,2,24,1536]{3,2,1,0:T(8,128)(2,1)S(1)}, bf16[2,2,24,1536]{3,2,1,0:T(8,128)(2,1)S(1)}, u32[]{:S(2)}, u32[]{:S(2)}) collective-permute-start(bf16[2,2,24,1536]{3,2,1,0:T(8,128)(2,1)S(1)} %fusion.66), channel_id=1, source_target_pairs={{0,2},{1,3},{2,0},{3,1},{4,6},{5,7},{6,4},{7,5},{8,10},{9,11},{10,... | collective-permute-start | bytes 884744 | tf_op jit(solution)/shard_map/ppermute | solution.py:520
  407.4 19.9 %collective-permute-start.36 = (f32[5632,128]{1,0:T(8,128)S(1)}, f32[5632,128]{1,0:T(8,128)}, u32[]{:S(2)}, u32[]{:S(2)}) collective-permute-start(f32[5632,128]{1,0:T(8,128)S(1)} %get-tuple-element.260), channel_id=1, source_target_pairs={{0,1},{1,0},{2,3},{3,2},{4,5},{5,4},{6,7},{7,6},{8,9},{9,8},{10,11... | collective-permute-start | bytes 8650760 | tf_op jit(solution)/shard_map/ppermute | solution.py:520
  411.0 16.3 %collective-permute-start.35 = (bf16[2,192,1536]{2,1,0:T(8,128)(2,1)S(1)}, bf16[2,192,1536]{2,1,0:T(8,128)(2,1)S(1)}, u32[]{:S(2)}, u32[]{:S(2)}) collective-permute-start(bf16[2,192,1536]{2,1,0:T(8,128)(2,1)S(1)} %copy-done.66), channel_id=1, source_target_pairs={{0,8},{1,17},{2,10},{3,19},{4,12},{5,21},{6,14},{7,23},{8,0},{9,25... | collective-permute-start | bytes 3538952 | tf_op jit(solution)/shard_map/ppermute | solution.py:520
  427.3 17.0 %collective-permute-start.37 = (f32[768,384]{1,0:T(8,128)S(1)}, f32[768,384]{1,0:T(8,128)S(1)}, u32[]{:S(2)}, u32[]{:S(2)}) collective-permute-start(f32[768,384]{1,0:T(8,128)S(1)} %fusion.44), channel_id=1, source_target_pairs={{0,1},{1,0},{2,3},{3,2},{4,5},{5,4},{6,7},{7,6},{8,9},{9,8},{10,11... | collective-permute-start | bytes 3538952 | tf_op jit(solution)/shard_map/ppermute | solution.py:520
  429.3 14.9 %collective-permute-start.40 = (bf16[2,1408,128]{2,1,0:T(8,128)(2,1)S(1)}, bf16[2,1408,128]{2,1,0:T(8,128)(2,1)S(1)}, u32[]{:S(2)}, u32[]{:S(2)}) collective-permute-start(bf16[2,1408,128]{2,1,0:T(8,128)(2,1)S(1)} %pad_maximum_fusion.6), channel_id=1, source_target_pairs={{0,8},{1,17},{2,10},{3,19},{4,12},{5,21},{6,14},{7,23},{8,0},{9,25... | collective-permute-start | bytes 2162696 | tf_op jit(solution)/shard_map/ppermute | solution.py:520
  431.1 3.4 collective-permute-start.38
  432.9 1.9 collective-permute-start.39
  433.8 18.8 %collective-permute-start.43 = (bf16[192,1536]{1,0:T(8,128)(2,1)}, bf16[192,1536]{1,0:T(8,128)(2,1)}, u32[]{:S(2)}, u32[]{:S(2)}) collective-permute-start(bf16[192,1536]{1,0:T(8,128)(2,1)} %fusion.36), channel_id=1, source_target_pairs={{0,16},{1,9},{2,18},{3,11},{4,20},{5,13},{6,22},{7,15},{8,24},{9,1... | collective-permute-start | bytes 1769480 | tf_op jit(solution)/shard_map/ppermute | solution.py:520
  449.0 11.6 %collective-permute-start.44 = (bf16[1408,128]{1,0:T(8,128)(2,1)}, bf16[1408,128]{1,0:T(8,128)(2,1)}, u32[]{:S(2)}, u32[]{:S(2)}) collective-permute-start(bf16[1408,128]{1,0:T(8,128)(2,1)} %fusion.49), channel_id=1, source_target_pairs={{0,16},{1,9},{2,18},{3,11},{4,20},{5,13},{6,22},{7,15},{8,24},{9,1... | collective-permute-start | bytes 1081352 | tf_op jit(solution)/shard_map/ppermute | solution.py:520
  452.6 18.5 %collective-permute-start.41 = (bf16[2,192,640]{2,1,0:T(8,128)(2,1)}, bf16[2,192,640]{2,1,0:T(8,128)(2,1)S(1)}, u32[]{:S(2)}, u32[]{:S(2)}) collective-permute-start(bf16[2,192,640]{2,1,0:T(8,128)(2,1)} %maximum_maximum_fusion.1), channel_id=1, source_target_pairs={{0,8},{1,17},{2,10},{3,19},{4,12},{5,21},{6,14},{7,23},{8,0},{9,25... | collective-permute-start | bytes 1474568 | tf_op jit(solution)/shard_map/ppermute | solution.py:520
  463.8 9.7 %collective-permute-start.45 = (f32[2,2,176,128]{3,2,1,0:T(8,128)S(1)}, f32[2,2,176,128]{3,2,1,0:T(8,128)S(1)}, u32[]{:S(2)}, u32[]{:S(2)}) collective-permute-start(f32[2,2,176,128]{3,2,1,0:T(8,128)S(1)} %dynamic-slice_bitcast_fusion.1), channel_id=1, source_target_pairs={{0,2},{1,3},{2,0},{3,1},{4,6},{5,7},{6,4},{7,5},{8,10},{9,11},{10,... | collective-permute-start | bytes 1081352 | tf_op jit(solution)/shard_map/ppermute | solution.py:520
  465.0 6.1 %collective-permute-start.42 = (bf16[1,2,24,1536]{3,2,1,0:T(8,128)(2,1)S(1)}, bf16[1,2,24,1536]{3,2,1,0:T(8,128)(2,1)S(1)}, u32[]{:S(2)}, u32[]{:S(2)}) collective-permute-start(bf16[1,2,24,1536]{3,2,1,0:T(8,128)(2,1)S(1)} %copy-done.76), channel_id=1, source_target_pairs={{0,4},{1,5},{2,6},{3,7},{4,0},{5,1},{6,2},{7,3},{8,12},{9,13},{10,... | collective-permute-start | bytes 442376 | tf_op jit(solution)/shard_map/ppermute | solution.py:520
  467.8 8.7 %collective-permute-start.63 = (f32[24,1536]{1,0:T(8,128)S(1)}, f32[24,1536]{1,0:T(8,128)S(1)}, u32[]{:S(2)}, u32[]{:S(2)}) collective-permute-start(f32[24,1536]{1,0:T(8,128)S(1)} %get-tuple-element.385), channel_id=1, source_target_pairs={{0,1},{1,0},{2,3},{3,2},{4,5},{5,4},{6,7},{7,6},{8,9},{9,8},{10,11... | collective-permute-start | bytes 442376 | tf_op jit(solution)/shard_map/ppermute | solution.py:520
  469.1 16.4 %collective-permute-start.46 = (f32[2,2,24,1536]{3,2,1,0:T(8,128)S(1)}, f32[2,2,24,1536]{3,2,1,0:T(8,128)S(1)}, u32[]{:S(2)}, u32[]{:S(2)}) collective-permute-start(f32[2,2,24,1536]{3,2,1,0:T(8,128)S(1)} %dynamic-slice_bitcast_fusion), channel_id=1, source_target_pairs={{0,2},{1,3},{2,0},{3,1},{4,6},{5,7},{6,4},{7,5},{8,10},{9,11},{10,... | collective-permute-start | bytes 1769480 | tf_op jit(solution)/shard_map/ppermute | solution.py:520
  474.8 10.8 %collective-permute-start.47 = (bf16[192,640]{1,0:T(8,128)(2,1)S(1)}, bf16[192,640]{1,0:T(8,128)(2,1)S(1)}, u32[]{:S(2)}, u32[]{:S(2)}) collective-permute-start(bf16[192,640]{1,0:T(8,128)(2,1)S(1)} %pad_maximum_fusion.11), channel_id=1, source_target_pairs={{0,16},{1,9},{2,18},{3,11},{4,20},{5,13},{6,22},{7,15},{8,24},{9,1... | collective-permute-start | bytes 737288 | tf_op jit(solution)/shard_map/ppermute | solution.py:520
  486.7 19.7 %collective-permute-start.49 = (f32[2,2,24,640]{3,2,1,0:T(8,128)S(1)}, f32[2,2,24,640]{3,2,1,0:T(8,128)S(1)}, u32[]{:S(2)}, u32[]{:S(2)}) collective-permute-start(f32[2,2,24,640]{3,2,1,0:T(8,128)S(1)} %dynamic-slice_bitcast_fusion.2), channel_id=1, source_target_pairs={{0,2},{1,3},{2,0},{3,1},{4,6},{5,7},{6,4},{7,5},{8,10},{9,11},{10,... | collective-permute-start | bytes 737288 | tf_op jit(solution)/shard_map/ppermute | solution.py:520
  488.5 17.9 %collective-permute-start.48 = (f32[1,2,176,128]{3,2,1,0:T(8,128)}, f32[1,2,176,128]{3,2,1,0:T(8,128)S(1)}, u32[]{:S(2)}, u32[]{:S(2)}) collective-permute-start(f32[1,2,176,128]{3,2,1,0:T(8,128)} %constant_dynamic-slice_fusion.2), channel_id=1, source_target_pairs={{0,4},{1,5},{2,6},{3,7},{4,0},{5,1},{6,2},{7,3},{8,12},{9,13},{10,... | collective-permute-start | bytes 540680 | tf_op jit(solution)/shard_map/ppermute | solution.py:520
  490.7 18.3 %collective-permute-start.62 = (f32[24,1536]{1,0:T(8,128)S(1)}, f32[24,1536]{1,0:T(8,128)S(1)}, u32[]{:S(2)}, u32[]{:S(2)}) collective-permute-start(f32[24,1536]{1,0:T(8,128)S(1)} %get-tuple-element.387), channel_id=1, source_target_pairs={{0,1},{1,0},{2,3},{3,2},{4,5},{5,4},{6,7},{7,6},{8,9},{9,8},{10,11... | collective-permute-start | bytes 442376 | tf_op jit(solution)/shard_map/ppermute | solution.py:520
  492.1 19.8 %collective-permute-start.50 = (f32[1,2,24,1536]{3,2,1,0:T(8,128)}, f32[1,2,24,1536]{3,2,1,0:T(8,128)S(1)}, u32[]{:S(2)}, u32[]{:S(2)}) collective-permute-start(f32[1,2,24,1536]{3,2,1,0:T(8,128)} %constant_dynamic-slice_fusion.1), channel_id=1, source_target_pairs={{0,4},{1,5},{2,6},{3,7},{4,0},{5,1},{6,2},{7,3},{8,12},{9,13},{10,... | collective-permute-start | bytes 884744 | tf_op jit(solution)/shard_map/ppermute | solution.py:520
  508.8 1.4 collective-permute-start.60
  508.9 9.3 %collective-permute-start.51 = (f32[1,2,24,640]{3,2,1,0:T(8,128)S(1)}, f32[1,2,24,640]{3,2,1,0:T(8,128)S(1)}, u32[]{:S(2)}, u32[]{:S(2)}) collective-permute-start(f32[1,2,24,640]{3,2,1,0:T(8,128)S(1)} %constant_dynamic-slice_fusion), channel_id=1, source_target_pairs={{0,4},{1,5},{2,6},{3,7},{4,0},{5,1},{6,2},{7,3},{8,12},{9,13},{10,... | collective-permute-start | bytes 368648 | tf_op jit(solution)/shard_map/ppermute | solution.py:520
  521.5 1.2 collective-permute-start.53
  522.7 4.5 collective-permute-start.56
  525.2 3.6 collective-permute-start.55
  525.2 3.6 collective-permute-start.54
  528.8 5.5 collective-permute-start.59
  530.4 4.5 collective-permute-start.58
  530.4 4.5 collective-permute-start.57
  533.3 2.9 collective-permute-start.52
  533.4 5.3 collective-permute-start.61
  (93 other events, 820.1 us)

commit v3 on v2

--- a/solution.py
+++ b/solution.py
@@ -50,6 +50,15 @@
     return (normed * gain_row, normed, scale_inv)
 
 
+def gelu_and_slope(upper):
+    root, cube = math.sqrt(2.0 / math.pi), 0.044715
+    square = upper * upper
+    bend = jnp.tanh(upper * (root + root * cube * square))
+    half = 0.5 + 0.5 * bend
+    steep = root + 3.0 * root * cube * square
+    return upper * half, half + 0.5 * upper * (1.0 - bend * bend) * steep
+
+
 def norm_back(grad_normed_out, normed, scale_inv, gain_row):
     grad_gain = jnp.sum(grad_normed_out * normed, 0)
     grad_scaled = grad_normed_out * gain_row
@@ -70,7 +79,6 @@
 
 TILE = 128
 LOG2E = math.log2(math.e)
-VMEM_LIMIT = 48 << 20
 
 
 def tie(*arrays):
@@ -84,7 +92,8 @@
     places = jnp.arange(length, dtype=jnp.int32)[None, :]
     first = jnp.min(jnp.where(shared, places, length), 1) // TILE * TILE
     last = jnp.max(jnp.where(shared, places, -1), 1) + 1
-    spans = (last - first + TILE - 1) // TILE
+    spans = (last - first + KEYS - 1) // KEYS
+    first = jnp.minimum(first, length - spans * KEYS)
     return jnp.stack([first, spans]).astype(jnp.int32)
 
 
@@ -114,6 +123,7 @@
 
 PAIRS = D // TILE
 WIDE = PAIRS * TILE
+KEYS = 256
 LOG_ROWS = -(-2 * PAIRS // 8) * 8
 
 
@@ -132,10 +142,10 @@
             queries = [head_stack(q_ref[rows, pl.ds(pair * TILE, TILE)]) for pair in range(PAIRS)]
 
             def keys_at(at):
-                return pl.ds(pl.multiple_of(start + at * TILE, TILE), TILE)
+                return pl.ds(pl.multiple_of(start + at * KEYS, TILE), KEYS)
 
             def held_at(at):
-                return pl.ds(pl.multiple_of(at * TILE, TILE), TILE)
+                return pl.ds(pl.multiple_of(at * KEYS, KEYS), KEYS)
 
             def score(at, state):
                 keys = keys_at(at)
@@ -213,7 +223,7 @@
                 pltpu.VMEM((WIDE, length), jnp.bfloat16),
             ],
         ),
-        compiler_params=pltpu.CompilerParams(vmem_limit_bytes=VMEM_LIMIT),
+        compiler_params=pltpu.CompilerParams(vmem_limit_bytes=28 << 20),
         name="attention_forward",
     )(windows, mixed, mixed, mixed, seg_row, seg_col)
 
@@ -246,10 +256,10 @@
             ]
 
             def keys_at(at):
-                return pl.ds(pl.multiple_of(start + at * TILE, TILE), TILE)
+                return pl.ds(pl.multiple_of(start + at * KEYS, TILE), KEYS)
 
             def held_at(at):
-                return pl.ds(pl.multiple_of(at * TILE, TILE), TILE)
+                return pl.ds(pl.multiple_of(at * KEYS, KEYS), KEYS)
 
             def weigh(at, inners):
                 keys = keys_at(at)
@@ -334,7 +344,7 @@
             + [pltpu.VMEM((length, WIDE), jnp.float32)] * 3
             + [pltpu.VMEM((WIDE, length), jnp.bfloat16)],
         ),
-        compiler_params=pltpu.CompilerParams(vmem_limit_bytes=VMEM_LIMIT),
+        compiler_params=pltpu.CompilerParams(vmem_limit_bytes=44 << 20),
         name="attention_backward",
     )(windows, mixed, mixed, mixed, grad_attended, log_sums, seg_row, seg_col)
 
@@ -419,7 +429,7 @@
             scratch_shapes=[pltpu.VMEM((8, length), jnp.float32)] * 2
             + [pltpu.VMEM((tile, length), jnp.bfloat16)],
         ),
-        compiler_params=pltpu.CompilerParams(vmem_limit_bytes=VMEM_LIMIT),
+        compiler_params=pltpu.CompilerParams(vmem_limit_bytes=18 << 20),
         name="head_pass",
     )(pred_low, word_table, token_weight)
 
@@ -589,7 +599,7 @@
                 pltpu.SemaphoreType.DMA(()),
             ],
         ),
-        compiler_params=pltpu.CompilerParams(vmem_limit_bytes=VMEM_LIMIT),
+        compiler_params=pltpu.CompilerParams(vmem_limit_bytes=(2 << 20) + 8 * twice * cols * (-(-rows // 8) * 8)),
         name="assemble",
     )(flags, *pieces)
     return gathered.reshape(8 * line * rows, cols)
@@ -658,7 +668,7 @@
                 pltpu.SemaphoreType.DMA((2,)),
             ],
         ),
-        compiler_params=pltpu.CompilerParams(vmem_limit_bytes=VMEM_LIMIT),
+        compiler_params=pltpu.CompilerParams(vmem_limit_bytes=9 << 20),
         name="scatter_halves",
     )(spots, flag, table, rows)
 
@@ -668,95 +678,280 @@
 
 
 class Reduction:
-    def __init__(self, place, half_of, stack=False, exact=False, short=False):
-        self.place, self.half_of = place, half_of
-        self.stack, self.exact, self.short = stack, exact, short
-
-    def whole(self, pieces):
-        return pieces[0] if len(pieces) == 1 else jnp.concatenate(pieces, 1)
-
-    def to_core(self):
-        return self.half_of(1 - self.place.core)
-
-    def keep(self, pieces=None):
-        self.kept_pieces = self.half_of(self.place.core) if pieces is None else pieces
-        self.halves = [piece.shape[1] for piece in self.kept_pieces]
-        self.quarter_rows = self.kept_pieces[0].shape[0] // 4
-        self.rows = self.kept_pieces[0].shape[0] // self.place.count
-
-    def quarter(self, index):
-        start = index * self.quarter_rows
-
-        def rows(piece):
-            return lax.dynamic_slice_in_dim(piece, start, self.quarter_rows, 0)
-
-        return self.whole(
-            [rows(kept) + rows(came) for kept, came in zip(self.kept_pieces, self.across)]
+    def __init__(self, place, kept, across, axis=1, exact=False, short=0):
+        self.place, self.axis, self.exact, self.short = place, axis, exact, short
+        self.rows = [piece.shape[0] // place.count for piece in kept]
+        shapes = [
+            (4, place.line // 2, 2, 2 * rows, piece.shape[1]) for rows, piece in zip(self.rows, kept)
+        ]
+        kept = [piece.reshape(shape) for piece, shape in zip(kept, shapes)]
+        across = [piece.reshape(shape) for piece, shape in zip(across, shapes)]
+        if axis == 1:
+            self.parts = [(own, came, own.shape[4], 0) for own, came in zip(kept, across)]
+        else:
+            self.parts = [
+                (own, came, TILE, block)
+                for own, came in zip(kept, across)
+                for block in range(own.shape[4] // TILE)
+            ]
+            self.rows = [own.shape[3] // 2 for own, unused, cols, block in self.parts]
+        self.cols = [part[2] for part in self.parts]
+        if axis == 1:
+            self.span = (2 * self.rows[0], sum(self.cols))
+        else:
+            self.span = (2 * sum(self.rows), self.cols[0])
+        self.level = 0
+
+    def where(self, at):
+        if self.axis == 1:
+            start = sum(self.cols[:at])
+            return slice(0, self.span[0]), slice(start, start + self.cols[at])
+        start = 2 * sum(self.rows[:at])
+        return slice(start, start + 2 * self.rows[at]), slice(0, self.span[1])
+
+    def lower(self, at, value):
+        if self.exact and at == len(self.cols) - 1:
+            last = value[..., : TILE // 2]
+            rounded = last.astype(jnp.bfloat16).astype(jnp.float32)
+            value = jnp.concatenate([rounded, last - rounded], -1)
+        return value.astype(jnp.bfloat16)
+
+    def lift(self, at, value):
+        value = value.astype(jnp.float32)
+        if self.exact and at == len(self.cols) - 1:
+            rounded, rest = value[..., : TILE // 2], value[..., TILE // 2 :]
+            value = jnp.concatenate([rounded + rest, jnp.zeros_like(rest)], -1)
+        return value
+
+    def cast(self, at, value, ref):
+        return self.lower(at, value) if ref.dtype == jnp.bfloat16 else value
+
+    def took(self, at, value):
+        return self.lift(at, value) if value.dtype == jnp.bfloat16 else value
+
+    def call(self, name, kernel, steps, flags, inputs, outputs):
+        return pl.pallas_call(
+            kernel,
+            out_shape=[entry for entry, unused, index in outputs],
+            grid_spec=pltpu.PrefetchScalarGridSpec(
+                num_scalar_prefetch=1,
+                grid=(steps,),
+                in_specs=[pl.BlockSpec(block, index) for unused, block, index in inputs],
+                out_specs=[pl.BlockSpec(block, index) for unused, block, index in outputs],
+            ),
+            compiler_params=pltpu.CompilerParams(vmem_limit_bytes=40 << 20),
+            name=name,
+        )(jnp.stack(flags).astype(jnp.int32), *[array for array, unused, index in inputs])
+
+    def pieces(self, block, index):
+        entries = []
+        for kept, across, cols, place in self.parts:
+
+            def at_place(step, flags, place=place):
+                return index(step, flags) + (place,)
+
+            for array in (kept, across):
+                entries.append((array, block + (array.shape[3], cols), at_place))
+        return entries
+
+    def to_a(self):
+        square, line = self.place.square, self.place.line
+        count = len(self.cols)
+
+        def kernel(flags_ref, *refs):
+            out_ref = refs[-1]
+            for at in range(count):
+                rows, cols = self.where(at)
+                value = refs[2 * at][0] + refs[2 * at + 1][0]
+                out_ref[0, :, :, rows, cols] = self.lower(at, value)
+
+        shape = (2, line // 2, 2) + self.span
+        (result,) = self.call(
+            "reduce_first",
+            kernel,
+            2,
+            [square ^ self.place.step_a, square ^ 3],
+            self.pieces((1, line // 2, 2), lambda step, flags: (flags[step], 0, 0, 0)),
+            [
+                (
+                    jax.ShapeDtypeStruct(shape, jnp.bfloat16),
+                    (1,) + shape[1:],
+                    lambda step, flags: (step, 0, 0, 0, 0),
+                )
+            ],
         )
-
-    def lower(self, array):
-        if not self.exact:
-            return array.astype(jnp.bfloat16)
-        last = array[..., -TILE:][..., : TILE // 2]
-        rounded = lax.reduce_precision(last, 8, 7)
-        both = jnp.concatenate([rounded, last - rounded], -1)
-        return jnp.concatenate([array[..., :-TILE], both], -1).astype(jnp.bfloat16)
-
-    def lift(self, array):
-        array = array.astype(jnp.float32)
-        if not self.exact:
-            return array
-        rounded, rest = array[..., -TILE : -TILE // 2], array[..., -TILE // 2 :]
-        both = jnp.concatenate([rounded + rest, jnp.zeros_like(rest)], -1)
-        return jnp.concatenate([array[..., :-TILE], both], -1)
-
-    def to_a(self, across):
-        self.across = across
-        square = self.place.square
-        pair = [self.quarter(square ^ self.place.step_a), self.quarter(square ^ 3)]
-        return jnp.stack([self.lower(member) for member in pair])
+        return result
+
+    def came_a(self, refs, at, index):
+        rows, cols = self.where(at)
+        if len(self.from_a) > 1:
+            return self.lift(at, refs[at][index + (slice(None), slice(None))])
+        return self.lift(at, refs[0][index + (rows, cols)])
 
     def to_b(self, from_a):
         self.from_a = from_a
-        mixed = self.quarter(self.place.square ^ self.place.step_b)
-        return self.lower(mixed + self.lift(from_a[1]))
-
-    def from_b(self, from_b):
-        own = self.quarter(self.place.square)
-        own = own + self.lift(self.from_a[0]) + self.lift(from_b)
-        self.own = own.reshape(self.place.line, 2, self.rows, own.shape[-1])
-        self.along = self.place.along
-
-    def to_line(self):
-        split = self.own.reshape((self.own.shape[0] // 2, 2) + self.own.shape[1:])
+        line, count = self.place.line, len(self.cols)
+
+        def kernel(flags_ref, *refs):
+            out_ref, firsts = refs[-1], refs[2 * count : -1]
+            for at in range(count):
+                rows, cols = self.where(at)
+                value = refs[2 * at][0] + refs[2 * at + 1][0]
+                value = value + self.came_a(firsts, at, (0, slice(None), slice(None)))
+                out_ref[:, :, rows, cols] = self.lower(at, value)
+
+        shape = (line // 2, 2) + self.span
+        (result,) = self.call(
+            "reduce_second",
+            kernel,
+            1,
+            [self.place.square ^ self.place.step_b],
+            self.pieces((1, line // 2, 2), lambda step, flags: (flags[0], 0, 0, 0))
+            + [
+                (array, (1,) + array.shape[1:], lambda step, flags: (1, 0, 0, 0, 0))
+                for array in from_a
+            ],
+            [(jax.ShapeDtypeStruct(shape, jnp.bfloat16), shape, lambda step, flags: (0, 0, 0, 0))],
+        )
+        return result
+
+    def halves(self, lines):
+        self.level += 1
+        kinds = (jnp.bfloat16 if self.level <= self.short else jnp.float32, jnp.float32)
+        shape = (lines,) + self.span
+        return [
+            (jax.ShapeDtypeStruct(shape, kind), shape, lambda step, flags: (0, 0, 0))
+            for kind in kinds
+        ]
+
+    def to_line(self, from_b):
+        line, count = self.place.line, len(self.cols)
+        mine = self.place.along % 2
+        self.along = self.place.along // 2
+
+        def kernel(flags_ref, *refs):
+            firsts, second_ref = refs[2 * count : -3], refs[-3]
+            for step, out_ref in enumerate(refs[-2:]):
+
+                @pl.when(pl.program_id(0) == step)
+                def _():
+                    for at in range(count):
+                        rows, cols = self.where(at)
+                        value = refs[2 * at][0, :, 0] + refs[2 * at + 1][0, :, 0]
+                        value = value + self.came_a(firsts, at, (0, slice(None), 0))
+                        value = value + self.lift(at, second_ref[:, 0, rows, cols])
+                        out_ref[:, rows, cols] = self.cast(at, value, out_ref)
+
+        send, self.own = self.call(
+            "reduce_third",
+            kernel,
+            2,
+            [self.place.square, 1 - mine, mine],
+            self.pieces((1, line // 2, 1), lambda step, flags: (flags[0], 0, flags[1 + step], 0))
+            + [
+                (
+                    array,
+                    (1, line // 2, 1) + array.shape[3:],
+                    lambda step, flags: (0, 0, flags[1 + step], 0, 0),
+                )
+                for array in self.from_a
+            ]
+            + [
+                (
+                    from_b,
+                    (line // 2, 1) + self.span,
+                    lambda step, flags: (0, flags[1 + step], 0, 0),
+                )
+            ],
+            self.halves(line // 2),
+        )
+        return send
+
+    def next_line(self, came):
+        lines, count = self.own.shape[0] // 2, len(self.cols)
         mine = self.along % 2
         self.along = self.along // 2
-        self.own = lax.dynamic_index_in_dim(split, mine, 1, False)
-        other = lax.dynamic_index_in_dim(split, 1 - mine, 1, False)
-        return other.astype(jnp.bfloat16) if self.short else other
-
-    def from_line(self, arrived):
-        self.own = self.own + arrived.astype(jnp.float32)
-
-    def to_end(self):
-        own = self.own[0]
-        self.kept = lax.dynamic_index_in_dim(own, self.place.core, 0, False)
-        return lax.dynamic_index_in_dim(own, 1 - self.place.core, 0, False)
-
-    def finish(self, other):
+        entries = [
+            (
+                array.reshape((lines, 2) + self.span),
+                (lines, 1) + self.span,
+                lambda step, flags: (0, flags[step], 0, 0),
+            )
+            for array in (self.own, came)
+        ]
+
+        def kernel(flags_ref, own_ref, came_ref, *out_refs):
+            for step, out_ref in enumerate(out_refs):
+
+                @pl.when(pl.program_id(0) == step)
+                def _():
+                    for at in range(count):
+                        rows, cols = self.where(at)
+                        value = own_ref[:, 0, rows, cols] + self.took(at, came_ref[:, 0, rows, cols])
+                        out_ref[:, rows, cols] = self.cast(at, value, out_ref)
+
+        send, self.own = self.call(
+            "reduce_line", kernel, 2, [1 - mine, mine], entries, self.halves(lines)
+        )
+        return send
+
+    def to_end(self, came):
+        half, count = (self.span[0] // 2, self.span[1]), len(self.cols)
+
+        def kernel(flags_ref, own_ref, came_ref, send_ref, keep_ref, squares_ref):
+            first = flags_ref[0] == 0
+            if came_ref.dtype == jnp.bfloat16 and self.exact:
+                pieces = [self.took(at, came_ref[(0,) + self.where(at)]) for at in range(count)]
+                came = jnp.concatenate(pieces, self.axis)
+            else:
+                came = came_ref[0].astype(jnp.float32)
+            value = own_ref[0] + came
+            squared = value * value
+            if self.exact:
+                spot_row = lax.broadcasted_iota(jnp.int32, squared.shape, 0)
+                spot_lane = lax.broadcasted_iota(jnp.int32, squared.shape, 1)
+                aside = (spot_lane == 3) & (spot_row >= self.span[0] - 2 * self.rows[-1])
+                squared = jnp.where(aside & first, 0.0, squared)
+            squares_ref[...] = jnp.full(squares_ref.shape, jnp.sum(squared), jnp.float32)
+            groups = [self.rows[0]] if self.axis == 1 else self.rows
+            start = 0
+            for rows in groups:
+                low, high = value[2 * start : 2 * start + rows], value[2 * start + rows : 2 * start + 2 * rows]
+                send_ref[start : start + rows] = jnp.where(first, high, low)
+                keep_ref[start : start + rows] = jnp.where(first, low, high)
+                start += rows
+
+        whole = (1,) + self.span
+        send, self.last, self.squares = self.call(
+            "reduce_last",
+            kernel,
+            1,
+            [self.place.core],
+            [(array, whole, lambda step, flags: (0, 0, 0)) for array in (self.own, came)],
+            [
+                (jax.ShapeDtypeStruct(shape, jnp.float32), shape, lambda step, flags: (0, 0))
+                for shape in (half, half, (8, TILE))
+            ],
+        )
+        return send
+
+    def unpack(self, array):
         results, start = [], 0
-        for half in self.halves:
-            kept, came = self.kept[:, start : start + half], other[:, start : start + half]
-            start += half
-            axis = 0 if self.stack else 1
-            results.append(
-                jnp.where(
-                    self.place.core == 0,
-                    jnp.concatenate([kept, came], axis),
-                    jnp.concatenate([came, kept], axis),
-                )
-            )
+        for size in self.cols if self.axis == 1 else self.rows:
+            results.append(lax.slice_in_dim(array, start, start + size, axis=self.axis))
+            start += size
         return results
+
+    def finish(self, came):
+        return self.unpack(self.last), self.unpack(came)
+
+
+def in_order(place, kept, came, axis):
+    return jnp.where(
+        place.core == 0,
+        jnp.concatenate([kept, came], axis),
+        jnp.concatenate([came, kept], axis),
+    )
 
 
 def on_device(
@@ -871,27 +1066,31 @@
     for bit in down_bits[:-1]:
         entry, qkv = tie(entry, qkv)
         qkv = join(qkv, place.swap_line(qkv, bit))
-    table, entry, qkv, leave, step_row = tie(table, entry, qkv, leave, step_row)
-    feature_low = sinusoid(step_row, D).astype(jnp.bfloat16)
-    table = join(table, place.swap_a(table))
-    entry = join(entry, place.swap_a(entry))
-    qkv = join(qkv, place.swap_line(qkv, down_bits[-1]))
+    table, entry, qkv, leave = tie(table, entry, qkv, leave)
+    table_came, entry_came = place.swap_a(table), place.swap_a(entry)
+    qkv_came = place.swap_line(qkv, down_bits[-1])
     for bit in down_bits[:-1]:
         leave = join(leave, place.swap_line(leave, bit))
-    table, entry, qkv = tie(table, entry, qkv)
+    table_came, entry_came, qkv_came, step_row = tie(table_came, entry_came, qkv_came, step_row)
+    feature_low = sinusoid(step_row, D).astype(jnp.bfloat16)
+    table, entry, qkv = join(table, table_came), join(entry, entry_came), join(qkv, qkv_came)
     table_pieces = [table, place.swap_b(table), place.swap_core(table)]
     entry_pieces = [entry, place.swap_b(entry), place.swap_core(entry)]
-    *both, qkv, leave, feature_low = tie(*table_pieces, *entry_pieces, qkv, leave, feature_low)
+    leave_came = place.swap_line(leave, down_bits[-1])
+    *both, qkv, feature_low = tie(*table_pieces, *entry_pieces, qkv, feature_low)
     table_pieces, entry_pieces = both[:3], both[3:]
     table_pieces.append(place.swap_core(table_pieces[1]))
     entry_pieces.append(place.swap_core(entry_pieces[1]))
-    qkv_a = place.swap_a(qkv)
-    leave = join(leave, place.swap_line(leave, down_bits[-1]))
+    qkv_came = place.swap_a(qkv)
     entry_low = assemble(place, entry_pieces)
+    entry_low, qkv_came = tie(entry_low, qkv_came)
+    qkv = join(qkv, qkv_came)
+    qkv_pieces = [qkv, place.swap_b(qkv), place.swap_core(qkv)]
+    qkv, table_pieces[0] = tie(qkv, table_pieces[0])
     word_table = assemble(place, table_pieces)
-    word_table, qkv_a, qkv = tie(word_table, qkv_a, qkv)
-    qkv_half = join(qkv, qkv_a)
-    qkv_pieces = [qkv_half, place.swap_b(qkv_half), place.swap_core(qkv_half)]
+    word_table, leave_came = tie(word_table, leave_came)
+    leave = join(leave, leave_came)
+    leave_came = place.swap_a(leave)
     up_low = entry_low[:, :EMB]
     time_low = entry_low[:, EMB : EMB + model_width]
     aside_low = entry_low[:, EMB + model_width :]
@@ -909,15 +1108,14 @@
     )
     normed, scaled_one, inverse_one = layer_normalize(hidden_zero, gain_rows[0])
     normed_one_low = normed.astype(jnp.bfloat16)
-    *qkv_pieces, normed_one_low, leave = tie(*qkv_pieces, normed_one_low, leave)
-    leave_a = place.swap_a(leave)
+    *qkv_pieces, normed_one_low = tie(*qkv_pieces, normed_one_low)
     qkv_pieces.append(place.swap_core(qkv_pieces[1]))
     qkv_low = assemble(place, qkv_pieces)
+    leave_came, qkv_low = tie(leave_came, qkv_low)
+    leave = join(leave, leave_came)
+    leave_pieces = [leave, place.swap_b(leave), place.swap_core(leave)]
     mixed_low = matmul(normed_one_low, qkv_low).astype(jnp.bfloat16)
     segments = (segment_ids, seg_col, windows)
-    leave_a, leave, mixed_low = tie(leave_a, leave, mixed_low)
-    leave_half, mixed_low = tie(join(leave, leave_a), mixed_low)
-    leave_pieces = [leave_half, place.swap_b(leave_half), place.swap_core(leave_half)]
     attended_low, log_sums = attention_forward(mixed_low, *segments)
     *leave_pieces, attended_low = tie(*leave_pieces, attended_low)
     leave_pieces.append(place.swap_core(leave_pieces[1]))
@@ -929,8 +1127,8 @@
     hidden_one = hidden_zero + matrix_product_transposed(attended_low, out_low)
     normed, scaled_two, inverse_two = layer_normalize(hidden_one, gain_rows[1])
     normed_two_low = normed.astype(jnp.bfloat16)
-    fc_upper = matmul(normed_two_low, fc_low)
-    active_low = jax.nn.gelu(fc_upper).astype(jnp.bfloat16)
+    active, slope = gelu_and_slope(matmul(normed_two_low, fc_low))
+    active_low, slope = tie(active.astype(jnp.bfloat16), slope)
     hidden_two = hidden_one + matrix_product_transposed(active_low, proj_low)
     normed, scaled_top, inverse_top = layer_normalize(hidden_two, gain_rows[2])
     normed_top_low = normed.astype(jnp.bfloat16)
@@ -958,66 +1156,59 @@
     )
 
     bits = list(place.bits)
+    core = place.core
     grad_two_low = grad_two.astype(jnp.bfloat16)
     proj_half = product_half(grad_two_low, active_low)
-    proj = Reduction(place, lambda side: [proj_half(side)], short=True)
-    proj_send, grad_two_low = tie(*proj.to_core(), grad_two_low)
+    proj_send, grad_two_low = tie(proj_half(1 - core), grad_two_low)
     proj_came = place.swap_core(proj_send)
-    proj.keep()
-    unused_value, gelu_pull = jax.vjp(jax.nn.gelu, fc_upper)
-    (grad_upper,) = gelu_pull(matmul(grad_two_low, proj_low))
-    grad_upper_low = grad_upper.astype(jnp.bfloat16)
+    proj_kept = proj_half(core)
+    grad_upper_low = (slope * matmul(grad_two_low, proj_low)).astype(jnp.bfloat16)
     proj_came, grad_upper_low = tie(proj_came, grad_upper_low)
-    proj_send, grad_upper_low = tie(proj.to_a([proj_came]), grad_upper_low)
-    proj_came = place.swap_a(proj_send)
+    proj = Reduction(place, [proj_kept], [proj_came])
+    proj_send, grad_upper_low = tie(proj.to_a(), grad_upper_low)
+    proj_a = place.swap_a(proj_send)
     fc_half = product_half(normed_two_low, grad_upper_low)
-    fc = Reduction(place, lambda side: [fc_half(side)], short=True)
-    fc_send, grad_upper_low = tie(*fc.to_core(), grad_upper_low)
+    fc_send, grad_upper_low = tie(fc_half(1 - core), grad_upper_low)
     fc_came = place.swap_core(fc_send)
-    fc.keep()
+    fc_kept = fc_half(core)
     grad_normed_two = matrix_product_transposed(grad_upper_low, fc_low)
     back_two, grad_gain_two = norm_back(grad_normed_two, scaled_two, inverse_two, gain_rows[1])
     grad_one = grad_two + back_two
     grad_one_low = grad_one.astype(jnp.bfloat16)
-    proj_came, fc_came, grad_one_low = tie(proj_came, fc_came, grad_one_low)
-    proj_send, fc_send, grad_one_low = tie(
-        proj.to_b(proj_came), fc.to_a([fc_came]), grad_one_low
-    )
-    proj_came, fc_came = place.swap_b(proj_send), place.swap_a(fc_send)
-    grad_out = matmul_tn(grad_one_low, attended_low)
+    proj_a, fc_came, grad_one_low = tie(proj_a, fc_came, grad_one_low)
+    fc = Reduction(place, [fc_kept], [fc_came])
+    fc_send, grad_one_low = tie(fc.to_a(), grad_one_low)
+    fc_a = place.swap_a(fc_send)
+    out_half = product_half(grad_one_low, attended_low)
+    out_send, out_kept = out_half(1 - core), out_half(core)
     grad_attended = matmul(grad_one_low, out_low).astype(jnp.bfloat16)
     lanes = lax.broadcasted_iota(jnp.int32, (model_width, 2 * TILE), 1)
     exact = jnp.where(lanes == 1, grad_gain_two[:, None], 0.0)
     exact = jnp.where(lanes == 2, grad_gain_top[:, None], exact)
     exact = jnp.where(lanes == 3, loss_local, exact)
-    grad_out, exact, grad_attended, proj_came = tie(grad_out, exact, grad_attended, proj_came)
-    proj.from_b(proj_came)
-    proj_send, grad_attended = tie(proj.to_line(), grad_attended)
-    proj_came = place.swap_line(proj_send, bits[0])
+    out_send, out_kept, exact, grad_attended = tie(out_send, out_kept, exact, grad_attended)
+    out_came = place.swap_core(out_send)
     grad_mixed = attention_backward(mixed_low, grad_attended, log_sums, *segments)
 
-    proj_came, fc_came, grad_mixed = tie(proj_came, fc_came, grad_mixed)
-    proj.from_line(proj_came)
-    proj_send, fc_send, grad_mixed = tie(proj.to_line(), fc.to_b(fc_came), grad_mixed)
-    proj_came, fc_came = place.swap_line(proj_send, bits[1]), place.swap_b(fc_send)
-    out_half, qkv_half = column_half(grad_out), product_half(normed_one_low, grad_mixed)
-    mix = Reduction(place, lambda side: [out_half(side), qkv_half(side)])
-    *mix_send, grad_mixed = tie(*mix.to_core(), grad_mixed)
-    mix_came = [place.swap_core(piece) for piece in mix_send]
+    fc_a, out_came, grad_mixed = tie(fc_a, out_came, grad_mixed)
+    feed = Reduction(place, [proj_kept, fc_kept], [proj_came, fc_came], short=len(bits))
+    feed_send, grad_mixed = tie(feed.to_b([proj_a, fc_a]), grad_mixed)
+    feed_came = place.swap_b(feed_send)
+    qkv_half = product_half(normed_one_low, grad_mixed)
+    qkv_send, grad_mixed = tie(qkv_half(1 - core), grad_mixed)
+    qkv_came = place.swap_core(qkv_send)
     grad_normed_one = matrix_product_transposed(grad_mixed, qkv_low)
     back_one, grad_gain_one = norm_back(grad_normed_one, scaled_one, inverse_one, gain_rows[0])
     grad_zero = grad_one + back_one
-    proj_came, fc_came, grad_zero = tie(proj_came, fc_came, grad_zero)
-    proj.from_line(proj_came)
-    fc.from_b(fc_came)
-    fc_send, grad_zero = tie(fc.to_line(), grad_zero)
-    fc_came = place.swap_line(fc_send, bits[0])
+    feed_came, grad_zero = tie(feed_came, grad_zero)
+    feed_send, grad_zero = tie(feed.to_line(feed_came), grad_zero)
+    feed_came = place.swap_line(feed_send, bits[0])
     grad_zero_low = grad_zero.astype(jnp.bfloat16)
     grad_start = matmul(grad_zero_low, up_low)
     grad_start = keep_root * grad_start - grad_mse + target_shift * pred_float
-    mix.keep()
-    *mix_came, grad_start = tie(*mix_came, grad_start)
-    mix_send, grad_start = tie(mix.to_a(mix_came), grad_start)
+    qkv_kept, qkv_came, grad_start = tie(qkv_half(core), qkv_came, grad_start)
+    mix = Reduction(place, [out_kept, qkv_kept], [out_came, qkv_came], short=1)
+    mix_send, grad_start = tie(mix.to_a(), grad_start)
     mix_came = place.swap_a(mix_send)
 
     own_words = word_table.shape[0] // place.count // 2
@@ -1030,82 +1221,69 @@
         split = grad_table.reshape(place.count, 2, own_words, EMB)
         words_send, words_kept = [
             lax.dynamic_index_in_dim(split, side, 1, False).reshape(-1, EMB)
-            for side in (1 - place.core, place.core)
+            for side in (1 - core, core)
         ]
-    words = Reduction(place, None, stack=True)
-    words.keep([words_kept])
-    words_send, fc_came, grad_zero_low = tie(words_send, fc_came, grad_zero_low)
+    words_send, mix_came, feed_came, grad_zero_low = tie(
+        words_send, mix_came, feed_came, grad_zero_low
+    )
     words_came = place.swap_core(words_send)
-    fc.from_line(fc_came)
+    feed_send, mix_send, grad_zero_low = tie(
+        feed.next_line(feed_came), mix.to_b([mix_came]), grad_zero_low
+    )
+    feed_came, mix_came = place.swap_line(feed_send, bits[1]), place.swap_b(mix_send)
     time_half = product_half(grad_zero_low, feature_low)
     pair_half = column_half(jnp.concatenate([matmul_tn(grad_zero_low, noisy_low), grad_down], 1))
     exact_half = column_half(jnp.where(lanes == 0, grad_gain_one[:, None], exact))
-    rest = Reduction(
-        place, lambda side: [time_half(side), pair_half(side), exact_half(side)], exact=True
-    )
-    *rest_send, mix_came, words_came = tie(*rest.to_core(), mix_came, words_came)
+
+    def rest_half(side):
+        return time_half(side), jnp.concatenate([pair_half(side), exact_half(side)], 1)
+
+    rest_send = tie(*rest_half(1 - core))
     rest_came = [place.swap_core(piece) for piece in rest_send]
-    words_send = words.to_a([words_came])
-    words_send, mix_came = tie(words_send, mix_came)
-    words_came = place.swap_a(words_send)
-    fc_send, mix_send = tie(fc.to_line(), mix.to_b(mix_came))
-    fc_came, mix_came = place.swap_line(fc_send, bits[1]), place.swap_b(mix_send)
-    rest.keep()
-    *rest_came, words_came = tie(*rest_came, words_came)
-    words_send, rest_send = tie(words.to_b(words_came), rest.to_a(rest_came))
-    words_came, rest_came = place.swap_b(words_send), place.swap_a(rest_send)
-    mix_came, words_came = tie(mix_came, words_came)
-    mix.from_b(mix_came)
-    words.from_b(words_came)
-    words_send, mix_send = tie(words.to_line(), mix.to_line())
-    words_came = place.swap_line(words_send, bits[0])
-    mix_came = place.swap_line(mix_send, bits[0])
-    rest_came, fc_came, words_came = tie(rest_came, fc_came, words_came)
-    words.from_line(words_came)
-    fc.from_line(fc_came)
-    words_send, rest_send = tie(words.to_line(), rest.to_b(rest_came))
-    words_came, rest_came = place.swap_line(words_send, bits[1]), place.swap_b(rest_send)
-    mix_came, rest_came = tie(mix_came, rest_came)
-    mix.from_line(mix_came)
-    rest.from_b(rest_came)
-    rest_send, mix_send = tie(rest.to_line(), mix.to_line())
-    rest_came = place.swap_line(rest_send, bits[0])
-    mix_came = place.swap_line(mix_send, bits[1])
-    words_came, rest_came = tie(words_came, rest_came)
-    words.from_line(words_came)
-    rest.from_line(rest_came)
-    rest_came = place.swap_line(rest.to_line(), bits[1])
-    mix_came, rest_came = tie(mix_came, rest_came)
-    mix.from_line(mix_came)
-    rest.from_line(rest_came)
-    members = (proj, fc, mix, rest, words)
+    rest_kept = rest_half(core)
+    words_came, *rest_came = tie(words_came, *rest_came)
+    late = Reduction(
+        place, [words_kept, *rest_kept], [words_came, *rest_came], axis=0, exact=True
+    )
+    late_send, mix_came = tie(late.to_a(), mix_came)
+    late_came = place.swap_a(late_send)
+    mix_came = place.swap_line(mix.to_line(mix_came), bits[0])
+    late_came, mix_came, feed_came = tie(late_came, mix_came, feed_came)
+    late_send, mix_send = tie(late.to_b([late_came]), mix.next_line(mix_came))
+    late_came, mix_came = place.swap_b(late_send), place.swap_line(mix_send, bits[1])
+    (late_came,) = tie(late_came)
+    late_came = place.swap_line(late.to_line(late_came), bits[0])
+    late_came, mix_came = tie(late_came, mix_came)
+    late_came = place.swap_line(late.next_line(late_came), bits[1])
+    members, arrived = (feed, mix, late), [feed_came, mix_came, late_came]
     for bit in bits[2:]:
-        for member in members:
-            member.from_line(place.swap_line(member.to_line(), bit))
-    squares_local = jnp.zeros((), jnp.float32)
-    for member in members:
-        own = member.own[0]
-        if member.exact:
-            lanes = lax.broadcasted_iota(jnp.int32, own.shape, own.ndim - 1)
-            aside = (place.core == 0) & (lanes == own.shape[-1] - TILE + 3)
-            own = jnp.where(aside, 0.0, own)
-        squares_local = squares_local + jnp.sum(own * own)
-    ends = [member.finish(place.swap_core(member.to_end())) for member in members]
-    (shard_proj,), (shard_fc,), (shard_out, shard_qkv), rest_ends, (shard_table,) = ends
-    shard_time, shard_pair, shard_exact = rest_ends
+        arrived = [
+            place.swap_line(member.next_line(came), bit) for member, came in zip(members, arrived)
+        ]
+    ends = [
+        member.finish(place.swap_core(member.to_end(came))) for member, came in zip(members, arrived)
+    ]
+    squares_local = feed.squares + mix.squares + late.squares
+    (proj_end, fc_end), (out_end, qkv_end), (words_end, *rest_ends) = [
+        list(zip(*end)) for end in ends
+    ]
+    time_end = [jnp.concatenate(sides[:-2], 1) for sides in zip(*rest_ends)]
+    pair_end, exact_end = rest_ends[-2:]
+    shard_pair = in_order(place, *pair_end, 1)
+    shard_exact = jnp.where(core == 0, *exact_end)
     loss_sum = shard_exact[0, 3]
     shards = (
-        shard_table,
+        in_order(place, *words_end, 0),
         shard_pair[:, :EMB],
-        shard_time,
-        shard_qkv,
-        shard_out,
-        shard_fc,
-        shard_proj,
+        in_order(place, *time_end, 1),
+        in_order(place, *qkv_end, 1),
+        in_order(place, *out_end, 1),
+        in_order(place, *fc_end, 1),
+        in_order(place, *proj_end, 1),
         shard_pair[:, EMB:],
         shard_exact[:, :3].T,
     )
-    squares = place.total(jnp.full((8, EMB), squares_local))[0, 0]
+    squares = place.total(squares_local)[0, 0]
     grad_norm = jnp.sqrt(squares)
     factor = CLIP_NORM / jnp.maximum(grad_norm, CLIP_NORM)
     flips = (False, True, True, False, True, False, True, False, False)

time: 551 us -> 517 us (0.938)
  waiting for transfers between devices: 118 us -> 79.8 us
  other arithmetic: 77.4 us -> 46.2 us
  local copies, waits for them, and re-layouts: 35.1 us -> 56.7 us
  Pallas kernels: 146 us -> 166 us
    ppermute x64 -> x54, waiting for transfers between devices: 118 us -> 79.8 us  [swap(): return lax.ppermute(array, AXES, pairs)]
    pallas_call x0 -> x16, Pallas kernels: none -> 34.2 us  [call(): pl.pallas_call(kernel, out_shape=[entry for entry, unused, index in outpu...]
    unnamed x188 -> x281, local copies, waits for them, and re-layouts: 21.7 us -> 41.9 us
    add x19 -> x1, other arithmetic: 14.4 us -> 0.01 us  [on_device(): squares_local = feed.squares + mix.squares + late.squares]
    pallas_call x1, Pallas kernels: 45.3 us -> 35.5 us  [attention_backward(): pl.pallas_call(kernel, out_shape=jax.ShapeDtypeStruct(mixed.shape, jnp.bf...]
    another operation x11 -> x5, other arithmetic: 15.2 us -> 6.72 us  [the longest x8 8.63 us: to_a(): return jnp.stack([self.lower(member) for member in pair])]
    dot_general x6, matrix products: 45 us -> 37 us  [matmul(): return jnp.dot(left_op, right_op, preferred_element_type=jnp.float32)]
    pallas_call x1, Pallas kernels: 33.4 us -> 25.8 us  [attention_forward(): pl.pallas_call(kernel, out_shape=(jax.ShapeDtypeStruct((length, width), j...]
  transfers between devices with their start and end apart: 64 -> 54, of which waited for: 27 -> 21; matrix products, arithmetic and copies ran while one was open for 25% -> 21% of each run, Pallas kernels for 18% -> 21%
where the time goes in v3:
time: 517 us; the launch traced here: 512 us
  Pallas kernels  166 us (32%)
  matrix products  105 us (20%)
  waiting for transfers between devices  79.8 us (15%)
  local copies, waits for them, and re-layouts  56.7 us (11%)
  starting transfers between devices  53.3 us (10%)
  other arithmetic  46.2 us (9%)
    ppermute x54, waiting for transfers between devices, swap(): return lax.ppermute(array, AXES, pairs)  79.8 us
    ppermute x54, starting transfers between devices, swap(): return lax.ppermute(array, AXES, pairs)  53.3 us
    unnamed x281, local copies, waits for them, and re-layouts  41.9 us
    dot_general x6, matrix products, matmul(): return jnp.dot(left_op, right_op, preferred_element_type=jnp.float32)  37 us
    dot_general x7, matrix products, matrix_product_transposed(): lax.dot_general(left_op, right_op, (((1,), (1,)), ((), ())), preferred_el...  36.5 us
    pallas_call x1, Pallas kernels, attention_backward(): pl.pallas_call(kernel, out_shape=jax.ShapeDtypeStruct(mixed.shape, jnp.bf...  35.5 us
    pallas_call x16, Pallas kernels, call(): pl.pallas_call(kernel, out_shape=[entry for entry, unused, index in outpu...  34.2 us
    dot_general x12, matrix products, matmul_tn(): lax.dot_general(left_op, right_op, (((0,), (0,)), ((), ())), preferred_el...  31.9 us
  transfers between devices with their start and end apart: 54, of which 21 were waited for; matrix products, arithmetic and copies ran while one was open for 21% of the time, Pallas kernels for 21%

profile of v3, /device:TPU:0, one launch (start us, length us, event | category | flops | bytes accessed | tf_op | source)
XLA Modules:
  0.0 512.2 jit_solution(274103403669617302)
XLA Ops:
  6.2 4.0 collective-permute-start.1
  22.6 3.6 collective-permute-done.3
  26.1 2.9 collective-permute-start.4
  30.1 3.8 collective-permute-done.4
  37.7 6.6 %collective-permute-start.7 = (bf16[2,24,2304]{2,1,0:T(8,128)(2,1)S(1)}, bf16[2,24,2304]{2,1,0:T(8,128)(2,1)S(1)}, u32[]{:S(2)}, u32[]{:S(2)}) collective-permute-start(bf16[2,24,2304]{2,1,0:T(8,128)(2,1)S(1)} %pad_maximum_fusion.7), channel_id=1, source_target_pairs={{0,2},{1,3},{2,0},{3,1},{4,6},{5,7},{6,4},{7,5},{8,10},{9,11},{10,... | collective-permute-start | bytes 663560 | tf_op jit(solution)/shard_map/ppermute | solution.py:530
  44.4 5.7 %collective-permute-done.7 = bf16[2,24,2304]{2,1,0:T(8,128)(2,1)S(1)} collective-permute-done((bf16[2,24,2304]{2,1,0:T(8,128)(2,1)S(1)}, bf16[2,24,2304]{2,1,0:T(8,128)(2,1)S(1)}, u32[]{:S(2)}, u32[]{:S(2)}) %collective-permute-start.7) | collective-permute-done | bytes 221216 | tf_op jit(solution)/shard_map/ppermute | solution.py:530
  53.7 6.5 %fusion.22 = (bf16[1024,384]{1,0:T(8,128)(2,1)S(1)}, bf16[1024,384]{1,0:T(8,128)(2,1)S(1)}) fusion(f32[384]{0:T(512)S(1)} %multiply_exponential_fusion, f32[1024]{0:T(1024)S(1)} %convert_element_type.133), kind=kLoop, calls=%fused_computation.55 | loop fusion | flops 1179648 | bytes 1578496 | tf_op jit(solution)/shard_map/convert.1
  61.6 4.2 collective-permute-done.8.refs_1_
  70.0 3.4 assemble.4
  78.9 4.7 fusion.26
  85.6 5.5 %assemble.5 = bf16[4,4,2,352,128]{4,3,2,1,0:T(8,128)(2,1)S(1)} custom-call(s32[3]{0:T(128)S(1)} %pad_add_fusion.3.flags_ref, bf16[8,352,128]{2,1,0:T(8,128)(2,1)S(1)} %copy-done.45, bf16[8,352,128]{2,1,0:T(8,128)(2,1)S(1)} %copy-done.53, bf16[8,352,128]{2,1,0:T(8,128)(2,1)S(1)} %copy-done.51, bf16[8,352,128]{2,1,0:T(8,128)(2,1)S(1)} %copy-done.55), custom_call_target="tpu_custom_call" | custom-call | tf_op jit(solution)/shard_map/assemble/pallas_call | solution.py:588
  91.2 2.4 pad_maximum_fusion.1
  95.0 3.2 gather_fusion
  99.7 2.7 fusion.78
  107.1 6.3 %assemble.6 = bf16[4,4,2,24,2304]{4,3,2,1,0:T(8,128)(2,1)S(1)} custom-call(s32[3]{0:T(128)S(1)} %pad_add_fusion.3.flags_ref, bf16[8,24,2304]{2,1,0:T(8,128)(2,1)} %constant_dynamic-update-slice_fusion.4.refs_0_, bf16[8,24,2304]{2,1,0:T(8,128)(2,1)} %collective-permute-done.18.refs_1_, bf16[8,24,2304]{2,1,0:T(8,128)(2,1)} %collective-permute-done.19.refs_2_, ...), custom_call_target="tpu_custom_call" | custom-call | tf_op jit(solution)/shard_map/assemble/pallas_call | solution.py:588
  113.4 2.5 constant_dynamic-update-slice_fusion.6.refs_0_
  116.6 4.2 convolution_convert_fusion.q_ref.k_ref.v_ref
  121.1 25.8 %attention_forward.1 = (bf16[1024,768]{1,0:T(8,128)(2,1)S(1)}, f32[16,1024]{1,0:T(8,128)S(1)}) custom-call(s32[2,8]{1,0:T(2,128)S(1)} %pad_add_fusion.windows_ref, bf16[1024,2304]{1,0:T(8,128)(2,1)S(1)} %convolution_convert_fusion.q_ref.k_ref.v_ref, bf16[1024,2304]{1,0:T(8,128)(2,1)S(1)} %convolution_convert_fusion.q_ref.k_ref.v_ref, ...), custom_call_target="tpu_custom_call" | custom-call | tf_op jit(solution)/shard_map/attention_forward/pallas_call | solution.py:200
  151.8 3.9 collective-permute-done.23.refs_3_
  159.2 5.1 assemble.7
  166.6 12.7 %multiply_add_fusion = (f32[1024,3072]{1,0:T(8,128)}, bf16[1024,3072]{1,0:T(8,128)(2,1)S(1)}) fusion(bf16[1024,768]{0,1:T(8,128)(2,1)S(1)} %multiply_convert_fusion.3, bf16[768,7040]{1,0:T(8,128)(2,1)S(1)} %bitcast.206), kind=kOutput, calls=%fused_computation.2 | convolution fusion | flops 4882169856 | bytes 25165824 | tf_op jit(solution)/shard_map/dot_general | solution.py:29
  179.4 5.1 fusion.80
  187.7 31.3 %head_pass.1 = (f32[11264,128]{1,0:T(8,128)S(1)}, f32[128,1024]{1,0:T(8,128)S(1)}, f32[1,1024]{1,0:T(1,128)S(1)}) custom-call(bf16[1024,128]{1,0:T(8,128)(2,1)S(1)} %get-tuple-element.341.pred_ref, bf16[11264,128]{1,0:T(8,128)(2,1)S(1)} %bitcast.204, f32[1,1024]{1,0:T(1,128)S(1)} %multiply_multiply_fusion.1.weight_ref), custom_call_target="tpu_custom_call" | custom-call | tf_op jit(solution)/shard_map/head_pass/pallas_call | solution.py:409
  219.1 2.6 copy-done.24
  224.0 3.3 multiply_reduce_fusion.3
  230.3 4.3 fusion.11
  234.9 4.5 fusion.13
  239.4 11.3 %multiply_convert_fusion = bf16[1024,3072]{1,0:T(8,128)(2,1)S(1)} fusion(f32[1024,3072]{1,0:T(8,128)} %get-tuple-element.218, bf16[1024,768]{0,1:T(8,128)(2,1)S(1)} %fusion.73, bf16[768,7040]{1,0:T(8,128)(2,1)} %bitcast.210), kind=kOutput, calls=%fused_computation.1 | convolution fusion | flops 4838129664 | bytes 25165824 | tf_op jit(solution)/shard_map/dot_general | solution.py:29
  250.7 4.6 reduce_first.4
  255.3 4.4 fusion.7
  260.1 10.0 %multiply_reduce_fusion.2 = (f32[768]{0:T(1024)S(1)}, f32[1024]{0:T(1024)S(1)}, f32[1024]{0:T(1024)S(1)}, f32[1024,768]{0,1:T(8,128)S(1)}) fusion(f32[1024,768]{0,1:T(8,128)} %copy-done.78, f32[1024]{0:T(1024)S(1)} %add_rsqrt_fusion.1, f32[1024]{0:T(1024)S(1)} %broadcast_multiply_fusion.8, f32[768]{0:T(1024)S(1)} %get-tuple-element.335, ...), kind=kOutput, calls=%fused_computation.19 | convolution fusion | flops 4838126592 | bytes 17324032 | tf_op jit(solution)/shard_map/dot_general | solution.py:39
  271.8 2.6 fusion.9
  275.8 3.3 fusion.74
  279.1 3.1 reduce_first.5
  282.2 4.1 convolution_convert_fusion.1.do_ref
  295.8 35.5 %attention_backward.1 = bf16[1024,2304]{1,0:T(8,128)(2,1)S(1)} custom-call(s32[2,8]{1,0:T(2,128)S(1)} %pad_add_fusion.windows_ref, bf16[1024,2304]{1,0:T(8,128)(2,1)} %copy-done, bf16[1024,2304]{1,0:T(8,128)(2,1)} %copy-done, bf16[1024,2304]{1,0:T(8,128)(2,1)} %copy-done, bf16[1024,768]{1,0:T(8,128)(2,1)S(1)} %copy-done.46, f32[16,1024]{1,0:T(8,128)S(1)} %copy-done.62, ...), custom_call_target="tpu_custom_call" | custom-call | tf_op jit(solution)/shard_map/attention_backward/pallas_call | solution.py:326
  331.4 4.7 reduce_second.3
  336.3 4.0 fusion.15
  340.4 9.3 %multiply_reduce_fusion = (f32[768]{0:T(1024)}, f32[1024]{0:T(1024)S(1)}, f32[1024]{0:T(1024)S(1)}, f32[1024,768]{0,1:T(8,128)S(1)}) fusion(f32[1024,768]{0,1:T(8,128)} %copy-done.73, f32[1024]{0:T(1024)} %copy-done.105, f32[1024]{0:T(1024)S(1)} %copy-done.104, f32[768]{0:T(1024)} %copy-done.107, bf16[1024,2304]{1,0:T(8,128)(2,1)} %copy-done.34, ...), kind=kOutput, calls=%fused_computation.16 | convolution fusion | flops 3630167296 | bytes 14571520 | tf_op jit(solution)/shard_map/dot_general | solution.py:39
  349.8 2.2 fusion.17
  353.8 3.0 collective-permute-done.30.refs_6_
  356.9 3.7 reduce_third.3
  360.6 3.1 fusion.25.rows_ref
  363.8 2.2 reduce_first.6
  366.9 2.6 copy-done.25
  370.6 13.0 %scatter_halves.1 = (f32[5632,128]{1,0:T(8,128)}, f32[5632,128]{1,0:T(8,128)S(1)}) custom-call(s32[1024]{0:T(1024)S(1)} %get-tuple-element.387.spots_ref, s32[1]{0:T(128)} %bitcast.flag_ref.flags_ref, f32[11264,128]{1,0:T(8,128)S(1)} %copy-done.25, f32[1024,128]{1,0:T(8,128)S(1)} %copy-done.43), custom_call_target="tpu_custom_call" | custom-call | tf_op jit(solution)/shard_map/scatter_halves/pallas_call | solution.py:654
  387.7 2.2 reduce_second.4
  398.4 2.6 fusion.30
  401.0 2.3 copy.82
  406.3 2.5 reduce_first.7
  408.8 2.1 collective-permute-start.37
  412.5 2.1 reduce_third.4
  414.6 2.1 collective-permute-start.38
  416.7 10.0 %collective-permute-done.39.came_ref = bf16[1,48,3072]{2,1,0:T(8,128)(2,1)S(1)} collective-permute-done((bf16[1,48,3072]{2,1,0:T(8,128)(2,1)S(1)}, bf16[1,48,3072]{2,1,0:T(8,128)(2,1)S(1)}, u32[]{:S(2)}, u32[]{:S(2)}) %collective-permute-start.39) | collective-permute-done | bytes 294944 | tf_op jit(solution)/shard_map/ppermute | solution.py:530
  428.7 2.7 reduce_second.5
  435.7 8.2 %collective-permute-done.40.refs_13_ = bf16[2,2,592,128]{3,2,1,0:T(8,128)(2,1)} collective-permute-done((bf16[2,2,592,128]{3,2,1,0:T(8,128)(2,1)}, bf16[2,2,592,128]{3,2,1,0:T(8,128)(2,1)}, u32[]{:S(2)}, u32[]{:S(2)}) %collective-permute-start.40) | collective-permute-done | bytes 606240 | tf_op jit(solution)/shard_map/ppermute | solution.py:530
  448.2 2.4 reduce_third.5
  450.7 2.8 collective-permute-start.42
  453.6 15.2 %collective-permute-done.42.came_ref = f32[1,48,1536]{2,1,0:T(8,128)S(1)} collective-permute-done((f32[1,48,1536]{2,1,0:T(8,128)S(1)}, f32[1,48,1536]{2,1,0:T(8,128)S(1)}, u32[]{:S(2)}, u32[]{:S(2)}) %collective-permute-start.42) | collective-permute-done | bytes 294944 | tf_op jit(solution)/shard_map/ppermute | solution.py:530
  468.7 2.2 collective-permute-done.41
  473.9 12.2 %collective-permute-done.43.came_ref = f32[1,592,128]{2,1,0:T(8,128)S(1)} collective-permute-done((f32[1,592,128]{2,1,0:T(8,128)S(1)}, f32[1,592,128]{2,1,0:T(8,128)S(1)}, u32[]{:S(2)}, u32[]{:S(2)}) %collective-permute-start.43) | collective-permute-done | bytes 303136 | tf_op jit(solution)/shard_map/ppermute | solution.py:530
  488.6 2.2 collective-permute-start.47
  495.8 2.9 collective-permute-start.49
  504.9 5.9 %adam_update.1 = (f32[352,128]{1,0:T(8,128)}, f32[352,128]{1,0:T(8,128)}, f32[352,128]{1,0:T(8,128)}, f32[24,128]{1,0:T(8,128)}, f32[24,128]{1,0:T(8,128)}, /*in...) custom-call(f32[1]{0:T(128)} %bitcast.61.factor_ref, ...), custom_call_target="tpu_custom_call" | custom-call | tf_op jit(solution)/shard_map/adam_update/pallas_call | solution.py:487
  (500 shorter events, 127.5 us)
Async XLA Ops:
  6.2 14.1 %collective-permute-start.1 = (bf16[1,24,1024]{2,1,0:T(8,128)(2,1)S(1)}, bf16[1,24,1024]{2,1,0:T(8,128)(2,1)S(1)}, u32[]{:S(2)}, u32[]{:S(2)}) collective-permute-start(bf16[1,24,1024]{2,1,0:T(8,128)(2,1)S(1)} %bitcast.243), channel_id=1, source_target_pairs={{0,4},{1,5},{2,6},{3,7},{4,0},{5,1},{6,2},{7,3},{8,12},{9,13},{10,... | collective-permute-start | bytes 147464 | tf_op jit(solution)/shard_map/ppermute | solution.py:530
  11.2 9.2 %collective-permute-start = (bf16[1,352,128]{2,1,0:T(8,128)(2,1)S(1)}, bf16[1,352,128]{2,1,0:T(8,128)(2,1)S(1)}, u32[]{:S(2)}, u32[]{:S(2)}) collective-permute-start(bf16[1,352,128]{2,1,0:T(8,128)(2,1)S(1)} %convert_bitcast_fusion.2), channel_id=1, source_target_pairs={{0,4},{1,5},{2,6},{3,7},{4,0},{5,1},{6,2},{7,3},{8,12},{9,13},{10,... | collective-permute-start | bytes 270344 | tf_op jit(solution)/shard_map/ppermute | solution.py:530
  13.3 85.0 %copy-start.109 = (f32[1024]{0:T(1024)}, f32[1024]{0:T(1024)S(1)}, u32[]{:S(2)}) copy-start(f32[1024]{0:T(1024)S(1)} %get-tuple-element.368) | copy-start | bytes 12292
  19.2 34.5 %copy-start.115 = (s32[1,1024]{1,0:T(1,128)S(1)}, s32[1,1024]{1,0:T(1,128)}, u32[]{:S(2)}) copy-start(s32[1,1024]{1,0:T(1,128)} %param.35) | copy-start | bytes 12292
  20.4 5.7 %collective-permute-start.3 = (bf16[2,24,1024]{2,1,0:T(8,128)(2,1)S(1)}, bf16[2,24,1024]{2,1,0:T(8,128)(2,1)S(1)}, u32[]{:S(2)}, u32[]{:S(2)}) collective-permute-start(bf16[2,24,1024]{2,1,0:T(8,128)(2,1)S(1)} %pad_maximum_fusion.10), channel_id=1, source_target_pairs={{0,2},{1,3},{2,0},{3,1},{4,6},{5,7},{6,4},{7,5},{8,10},{9,11},{10,... | collective-permute-start | bytes 294920 | tf_op jit(solution)/shard_map/ppermute | solution.py:530
  22.4 7.7 %collective-permute-start.2 = (bf16[2,352,128]{2,1,0:T(8,128)(2,1)S(1)}, bf16[2,352,128]{2,1,0:T(8,128)(2,1)S(1)}, u32[]{:S(2)}, u32[]{:S(2)}) collective-permute-start(bf16[2,352,128]{2,1,0:T(8,128)(2,1)S(1)} %pad_maximum_fusion.9), channel_id=1, source_target_pairs={{0,2},{1,3},{2,0},{3,1},{4,6},{5,7},{6,4},{7,5},{8,10},{9,11},{10,... | collective-permute-start | bytes 540680 | tf_op jit(solution)/shard_map/ppermute | solution.py:530
  26.1 7.7 %collective-permute-start.4 = (bf16[1,24,2304]{2,1,0:T(8,128)(2,1)S(1)}, bf16[1,24,2304]{2,1,0:T(8,128)(2,1)S(1)}, u32[]{:S(2)}, u32[]{:S(2)}) collective-permute-start(bf16[1,24,2304]{2,1,0:T(8,128)(2,1)S(1)} %convert_bitcast_fusion.1), channel_id=1, source_target_pairs={{0,4},{1,5},{2,6},{3,7},{4,0},{5,1},{6,2},{7,3},{8,12},{9,13},{10,... | collective-permute-start | bytes 331784 | tf_op jit(solution)/shard_map/ppermute | solution.py:530
  33.9 33.5 %collective-permute-start.15 = (bf16[1,24,7040]{2,1,0:T(8,128)(2,1)S(1)}, bf16[1,24,7040]{2,1,0:T(8,128)(2,1)S(1)}, u32[]{:S(2)}, u32[]{:S(2)}) collective-permute-start(bf16[1,24,7040]{2,1,0:T(8,128)(2,1)S(1)} %maximum_bitcast_fusion), channel_id=1, source_target_pairs={{0,4},{1,5},{2,6},{3,7},{4,0},{5,1},{6,2},{7,3},{8,12},{9,13},{10,... | collective-permute-start | bytes 1013768 | tf_op jit(solution)/shard_map/ppermute | solution.py:530
  34.9 15.3 %collective-permute-start.5 = (bf16[4,352,128]{2,1,0:T(8,128)(2,1)S(1)}, bf16[4,352,128]{2,1,0:T(8,128)(2,1)S(1)}, u32[]{:S(2)}, u32[]{:S(2)}) collective-permute-start(bf16[4,352,128]{2,1,0:T(8,128)(2,1)S(1)} %pad_maximum_fusion.6), channel_id=1, source_target_pairs={{0,8},{1,17},{2,10},{3,19},{4,12},{5,21},{6,14},{7,23},{8,0},{9,25... | collective-permute-start | bytes 1081352 | tf_op jit(solution)/shard_map/ppermute | solution.py:530
  37.1 7.3 %collective-permute-start.6 = (bf16[4,24,1024]{2,1,0:T(8,128)(2,1)S(1)}, bf16[4,24,1024]{2,1,0:T(8,128)(2,1)S(1)}, u32[]{:S(2)}, u32[]{:S(2)}) collective-permute-start(bf16[4,24,1024]{2,1,0:T(8,128)(2,1)S(1)} %pad_maximum_fusion.8), channel_id=1, source_target_pairs={{0,8},{1,17},{2,10},{3,19},{4,12},{5,21},{6,14},{7,23},{8,0},{9,25... | collective-permute-start | bytes 589832 | tf_op jit(solution)/shard_map/ppermute | solution.py:530
  37.7 12.5 %collective-permute-start.7 = (bf16[2,24,2304]{2,1,0:T(8,128)(2,1)S(1)}, bf16[2,24,2304]{2,1,0:T(8,128)(2,1)S(1)}, u32[]{:S(2)}, u32[]{:S(2)}) collective-permute-start(bf16[2,24,2304]{2,1,0:T(8,128)(2,1)S(1)} %pad_maximum_fusion.7), channel_id=1, source_target_pairs={{0,2},{1,3},{2,0},{3,1},{4,6},{5,7},{6,4},{7,5},{8,10},{9,11},{10,... | collective-permute-start | bytes 663560 | tf_op jit(solution)/shard_map/ppermute | solution.py:530
  50.2 11.4 %collective-permute-start.11 = (bf16[8,24,1024]{2,1,0:T(8,128)(2,1)S(1)}, bf16[8,24,1024]{2,1,0:T(8,128)(2,1)S(1)}, u32[]{:S(2)}, u32[]{:S(2)}) collective-permute-start(bf16[8,24,1024]{2,1,0:T(8,128)(2,1)S(1)} %constant_dynamic-update-slice_fusion.2.refs_0_), channel_id=1, source_target_pairs={{0,1},{1,0},{2,3},{3,2},{4,5},{5,4},{6,7},{7,6},{8,9},{9,8},{10,11... | collective-permute-start | bytes 1179656 | tf_op jit(solution)/shard_map/ppermute | solution.py:530
  50.2 11.4 %collective-permute-start.10 = (bf16[8,24,1024]{2,1,0:T(8,128)(2,1)S(1)}, bf16[8,24,1024]{2,1,0:T(8,128)(2,1)S(1)}, u32[]{:S(2)}, u32[]{:S(2)}) collective-permute-start(bf16[8,24,1024]{2,1,0:T(8,128)(2,1)S(1)} %constant_dynamic-update-slice_fusion.2.refs_0_), channel_id=1, source_target_pairs={{0,16},{1,9},{2,18},{3,11},{4,20},{5,13},{6,22},{7,15},{8,24},{9,1... | collective-permute-start | bytes 1179656 | tf_op jit(solution)/shard_map/ppermute | solution.py:530
  52.0 9.6 %collective-permute-start.9 = (bf16[8,352,128]{2,1,0:T(8,128)(2,1)S(1)}, bf16[8,352,128]{2,1,0:T(8,128)(2,1)S(1)}, u32[]{:S(2)}, u32[]{:S(2)}) collective-permute-start(bf16[8,352,128]{2,1,0:T(8,128)(2,1)S(1)} %constant_dynamic-update-slice_fusion.refs_0_), channel_id=1, source_target_pairs={{0,1},{1,0},{2,3},{3,2},{4,5},{5,4},{6,7},{7,6},{8,9},{9,8},{10,11... | collective-permute-start | bytes 2162696 | tf_op jit(solution)/shard_map/ppermute | solution.py:530
  52.2 13.6 %collective-permute-start.8 = (bf16[8,352,128]{2,1,0:T(8,128)(2,1)S(1)}, bf16[8,352,128]{2,1,0:T(8,128)(2,1)S(1)}, u32[]{:S(2)}, u32[]{:S(2)}) collective-permute-start(bf16[8,352,128]{2,1,0:T(8,128)(2,1)S(1)} %constant_dynamic-update-slice_fusion.refs_0_), channel_id=1, source_target_pairs={{0,16},{1,9},{2,18},{3,11},{4,20},{5,13},{6,22},{7,15},{8,24},{9,1... | collective-permute-start | bytes 2162696 | tf_op jit(solution)/shard_map/ppermute | solution.py:530
  65.8 4.2 collective-permute-start.12
  65.8 8.3 %collective-permute-start.13 = (bf16[4,24,2304]{2,1,0:T(8,128)(2,1)S(1)}, bf16[4,24,2304]{2,1,0:T(8,128)(2,1)S(1)}, u32[]{:S(2)}, u32[]{:S(2)}) collective-permute-start(bf16[4,24,2304]{2,1,0:T(8,128)(2,1)S(1)} %pad_maximum_fusion.5), channel_id=1, source_target_pairs={{0,8},{1,17},{2,10},{3,19},{4,12},{5,21},{6,14},{7,23},{8,0},{9,25... | collective-permute-start | bytes 1327112 | tf_op jit(solution)/shard_map/ppermute | solution.py:530
  68.4 22.7 %collective-permute-start.16 = (bf16[2,24,7040]{2,1,0:T(8,128)(2,1)}, bf16[2,24,7040]{2,1,0:T(8,128)(2,1)}, u32[]{:S(2)}, u32[]{:S(2)}) collective-permute-start(bf16[2,24,7040]{2,1,0:T(8,128)(2,1)} %pad_maximum_fusion.4), channel_id=1, source_target_pairs={{0,2},{1,3},{2,0},{3,1},{4,6},{5,7},{6,4},{7,5},{8,10},{9,11},{10,... | collective-permute-start | bytes 2027528 | tf_op jit(solution)/shard_map/ppermute | solution.py:530
  69.2 14.4 %collective-permute-start.14 = (bf16[8,352,128]{2,1,0:T(8,128)(2,1)S(1)}, bf16[8,352,128]{2,1,0:T(8,128)(2,1)S(1)}, u32[]{:S(2)}, u32[]{:S(2)}) collective-permute-start(bf16[8,352,128]{2,1,0:T(8,128)(2,1)S(1)} %collective-permute-done.8.refs_1_), channel_id=1, source_target_pairs={{0,1},{1,0},{2,3},{3,2},{4,5},{5,4},{6,7},{7,6},{8,9},{9,8},{10,11... | collective-permute-start | bytes 2162696 | tf_op jit(solution)/shard_map/ppermute | solution.py:530
  74.9 29.2 %collective-permute-start.19 = (bf16[8,24,2304]{2,1,0:T(8,128)(2,1)}, bf16[8,24,2304]{2,1,0:T(8,128)(2,1)}, u32[]{:S(2)}, u32[]{:S(2)}) collective-permute-start(bf16[8,24,2304]{2,1,0:T(8,128)(2,1)} %constant_dynamic-update-slice_fusion.4.refs_0_), channel_id=1, source_target_pairs={{0,1},{1,0},{2,3},{3,2},{4,5},{5,4},{6,7},{7,6},{8,9},{9,8},{10,11... | collective-permute-start | bytes 2654216 | tf_op jit(solution)/shard_map/ppermute | solution.py:530
  74.9 29.2 %collective-permute-start.18 = (bf16[8,24,2304]{2,1,0:T(8,128)(2,1)}, bf16[8,24,2304]{2,1,0:T(8,128)(2,1)}, u32[]{:S(2)}, u32[]{:S(2)}) collective-permute-start(bf16[8,24,2304]{2,1,0:T(8,128)(2,1)} %constant_dynamic-update-slice_fusion.4.refs_0_), channel_id=1, source_target_pairs={{0,16},{1,9},{2,18},{3,11},{4,20},{5,13},{6,22},{7,15},{8,24},{9,1... | collective-permute-start | bytes 2654216 | tf_op jit(solution)/shard_map/ppermute | solution.py:530
  93.5 19.9 %collective-permute-start.17 = (bf16[4,24,7040]{2,1,0:T(8,128)(2,1)}, bf16[4,24,7040]{2,1,0:T(8,128)(2,1)}, u32[]{:S(2)}, u32[]{:S(2)}) collective-permute-start(bf16[4,24,7040]{2,1,0:T(8,128)(2,1)} %pad_maximum_fusion.1), channel_id=1, source_target_pairs={{0,8},{1,17},{2,10},{3,19},{4,12},{5,21},{6,14},{7,23},{8,0},{9,25... | collective-permute-start | bytes 4055048 | tf_op jit(solution)/shard_map/ppermute | solution.py:530
  98.2 87.0 %copy-start.85 = (bf16[1024,128]{1,0:T(8,128)(2,1)}, bf16[1024,128]{1,0:T(8,128)(2,1)S(1)}, u32[]{:S(2)}) copy-start(bf16[1024,128]{1,0:T(8,128)(2,1)S(1)} %gather_fusion) | copy-start | bytes 786436
  104.1 3.0 collective-permute-start.20
  116.0 32.8 %collective-permute-start.22 = (bf16[8,24,7040]{2,1,0:T(8,128)(2,1)S(1)}, bf16[8,24,7040]{2,1,0:T(8,128)(2,1)S(1)}, u32[]{:S(2)}, u32[]{:S(2)}) collective-permute-start(bf16[8,24,7040]{2,1,0:T(8,128)(2,1)S(1)} %constant_dynamic-update-slice_fusion.6.refs_0_), channel_id=1, source_target_pairs={{0,1},{1,0},{2,3},{3,2},{4,5},{5,4},{6,7},{7,6},{8,9},{9,8},{10,11... | collective-permute-start | bytes 8110088 | tf_op jit(solution)/shard_map/ppermute | solution.py:530
  116.1 34.3 %collective-permute-start.21 = (bf16[8,24,7040]{2,1,0:T(8,128)(2,1)S(1)}, bf16[8,24,7040]{2,1,0:T(8,128)(2,1)}, u32[]{:S(2)}, u32[]{:S(2)}) collective-permute-start(bf16[8,24,7040]{2,1,0:T(8,128)(2,1)S(1)} %constant_dynamic-update-slice_fusion.6.refs_0_), channel_id=1, source_target_pairs={{0,16},{1,9},{2,18},{3,11},{4,20},{5,13},{6,22},{7,15},{8,24},{9,1... | collective-permute-start | bytes 8110088 | tf_op jit(solution)/shard_map/ppermute | solution.py:530
  121.1 30.5 %copy-start.117 = (s32[1024]{0:T(1024)S(1)}, s32[1024]{0:T(1024)}, u32[]{:S(2)}) copy-start(s32[1024]{0:T(1024)} %copy-done.116) | copy-start | bytes 12292
  121.1 30.6 %copy-start.120 = (s32[1,1024]{1,0:T(1,128)S(1)}, s32[1,1024]{1,0:T(1,128)}, u32[]{:S(2)}) copy-start(s32[1,1024]{1,0:T(1,128)} %param.34) | copy-start | bytes 12292
  150.3 5.4 %collective-permute-start.23 = (bf16[8,24,7040]{2,1,0:T(8,128)(2,1)}, bf16[8,24,7040]{2,1,0:T(8,128)(2,1)}, u32[]{:S(2)}, u32[]{:S(2)}) collective-permute-start(bf16[8,24,7040]{2,1,0:T(8,128)(2,1)} %collective-permute-done.21.refs_1_), channel_id=1, source_target_pairs={{0,1},{1,0},{2,3},{3,2},{4,5},{5,4},{6,7},{7,6},{8,9},{9,8},{10,11... | collective-permute-start | bytes 8110088 | tf_op jit(solution)/shard_map/ppermute | solution.py:530
  186.1 32.9 %copy-start.82 = (bf16[1024,768]{0,1:T(8,128)(2,1)}, bf16[1024,768]{0,1:T(8,128)(2,1)S(1)}, u32[]{:S(2)}) copy-start(bf16[1024,768]{0,1:T(8,128)(2,1)S(1)} %multiply_convert_fusion.2) | copy-start | bytes 4718596
  187.7 31.4 %copy-start.41 = (bf16[1024,128]{1,0:T(8,128)(2,1)}, bf16[1024,128]{1,0:T(8,128)(2,1)S(1)}, u32[]{:S(2)}) copy-start(bf16[1024,128]{1,0:T(8,128)(2,1)S(1)} %get-tuple-element.341.pred_ref) | copy-start | bytes 786436
  234.6 16.1 %collective-permute-start.24 = (f32[768,1536]{1,0:T(8,128)}, f32[768,1536]{1,0:T(8,128)}, u32[]{:S(2)}, u32[]{:S(2)}) collective-permute-start(f32[768,1536]{1,0:T(8,128)} %fusion.11), channel_id=1, source_target_pairs={{0,1},{1,0},{2,3},{3,2},{4,5},{5,4},{6,7},{7,6},{8,9},{9,8},{10,11... | collective-permute-start | bytes 14155784 | tf_op jit(solution)/shard_map/ppermute | solution.py:530
  259.6 19.5 %collective-permute-start.26 = (f32[768,1536]{1,0:T(8,128)}, f32[768,1536]{1,0:T(8,128)}, u32[]{:S(2)}, u32[]{:S(2)}) collective-permute-start(f32[768,1536]{1,0:T(8,128)} %fusion.7), channel_id=1, source_target_pairs={{0,1},{1,0},{2,3},{3,2},{4,5},{5,4},{6,7},{7,6},{8,9},{9,8},{10,11... | collective-permute-start | bytes 14155784 | tf_op jit(solution)/shard_map/ppermute | solution.py:530
  260.0 19.1 %collective-permute-start.25 = (bf16[2,2,2,48,1536]{4,3,2,1,0:T(8,128)(2,1)S(1)}, bf16[2,2,2,48,1536]{4,3,2,1,0:T(8,128)(2,1)S(1)}, u32[]{:S(2)}, u32[]{:S(2)}) collective-permute-start(bf16[2,2,2,48,1536]{4,3,2,1,0:T(8,128)(2,1)S(1)} %reduce_first.4), channel_id=1, source_target_pairs={{0,8},{1,17},{2,10},{3,19},{4,12},{5,21},{6,14},{7,23},{8,0},{9,25... | collective-permute-start | bytes 3538952 | tf_op jit(solution)/shard_map/ppermute | solution.py:530
  279.1 52.3 %copy-start.28 = (bf16[2,2,2,48,1536]{4,3,2,1,0:T(8,128)(2,1)}, bf16[2,2,2,48,1536]{4,3,2,1,0:T(8,128)(2,1)S(1)}, u32[]{:S(2)}) copy-start(bf16[2,2,2,48,1536]{4,3,2,1,0:T(8,128)(2,1)S(1)} %collective-permute-done.25.refs_4_) | copy-start | bytes 3538948
  290.3 41.0 %collective-permute-start.28 = (f32[768,384]{1,0:T(8,128)}, f32[768,384]{1,0:T(8,128)S(1)}, u32[]{:S(2)}, u32[]{:S(2)}) collective-permute-start(f32[768,384]{1,0:T(8,128)} %fusion.36), channel_id=1, source_target_pairs={{0,1},{1,0},{2,3},{3,2},{4,5},{5,4},{6,7},{7,6},{8,9},{9,8},{10,11... | collective-permute-start | bytes 3538952 | tf_op jit(solution)/shard_map/ppermute | solution.py:530
  290.5 40.9 %collective-permute-start.27 = (bf16[2,2,2,48,1536]{4,3,2,1,0:T(8,128)(2,1)}, bf16[2,2,2,48,1536]{4,3,2,1,0:T(8,128)(2,1)S(1)}, u32[]{:S(2)}, u32[]{:S(2)}) collective-permute-start(bf16[2,2,2,48,1536]{4,3,2,1,0:T(8,128)(2,1)} %reduce_first.5), channel_id=1, source_target_pairs={{0,8},{1,17},{2,10},{3,19},{4,12},{5,21},{6,14},{7,23},{8,0},{9,25... | collective-permute-start | bytes 3538952 | tf_op jit(solution)/shard_map/ppermute | solution.py:530
  292.2 39.2 %slice-start = ((s8[4718592]{0:T(1024)(128)(4,1)}), s8[4194304]{0:T(1024)(128)(4,1)S(1)}, s32[]{:S(2)}) async-start(s8[4718592]{0:T(1024)(128)(4,1)} %bitcast.173), calls=%async_computation | async-start | bytes 8388608
  295.8 35.5 %slice-start.1 = ((s8[4718592]{0:T(1024)(128)(4,1)}), s8[524288]{0:T(1024)(128)(4,1)S(1)}, s32[]{:S(2)}) async-start(s8[4718592]{0:T(1024)(128)(4,1)} %bitcast.173), calls=%async_computation.1 | async-start | bytes 1048576
  340.3 23.5 %collective-permute-start.29 = (f32[768,1152]{1,0:T(8,128)}, f32[768,1152]{1,0:T(8,128)S(1)}, u32[]{:S(2)}, u32[]{:S(2)}) collective-permute-start(f32[768,1152]{1,0:T(8,128)} %fusion.15), channel_id=1, source_target_pairs={{0,1},{1,0},{2,3},{3,2},{4,5},{5,4},{6,7},{7,6},{8,9},{9,8},{10,11... | collective-permute-start | bytes 10616840 | tf_op jit(solution)/shard_map/ppermute | solution.py:530
  340.4 16.4 %collective-permute-start.30 = (bf16[2,2,48,3072]{3,2,1,0:T(8,128)(2,1)}, bf16[2,2,48,3072]{3,2,1,0:T(8,128)(2,1)S(1)}, u32[]{:S(2)}, u32[]{:S(2)}) collective-permute-start(bf16[2,2,48,3072]{3,2,1,0:T(8,128)(2,1)} %copy-done.47), channel_id=1, source_target_pairs={{0,16},{1,9},{2,18},{3,11},{4,20},{5,13},{6,22},{7,15},{8,24},{9,1... | collective-permute-start | bytes 3538952 | tf_op jit(solution)/shard_map/ppermute | solution.py:530
  366.0 19.3 %collective-permute-start.31 = (bf16[2,2,2,48,1536]{4,3,2,1,0:T(8,128)(2,1)}, bf16[2,2,2,48,1536]{4,3,2,1,0:T(8,128)(2,1)}, u32[]{:S(2)}, u32[]{:S(2)}) collective-permute-start(bf16[2,2,2,48,1536]{4,3,2,1,0:T(8,128)(2,1)} %reduce_first.6), channel_id=1, source_target_pairs={{0,8},{1,17},{2,10},{3,19},{4,12},{5,21},{6,14},{7,23},{8,0},{9,25... | collective-permute-start | bytes 3538952 | tf_op jit(solution)/shard_map/ppermute | solution.py:530
  366.0 19.3 %collective-permute-start.32 = (bf16[2,48,3072]{2,1,0:T(8,128)(2,1)}, bf16[2,48,3072]{2,1,0:T(8,128)(2,1)}, u32[]{:S(2)}, u32[]{:S(2)}) collective-permute-start(bf16[2,48,3072]{2,1,0:T(8,128)(2,1)} %get-tuple-element.253), channel_id=1, source_target_pairs={{0,2},{1,3},{2,0},{3,1},{4,6},{5,7},{6,4},{7,5},{8,10},{9,11},{10,... | collective-permute-start | bytes 1769480 | tf_op jit(solution)/shard_map/ppermute | solution.py:530
  385.3 15.7 %collective-permute-start.33 = (f32[5632,128]{1,0:T(8,128)}, f32[5632,128]{1,0:T(8,128)}, u32[]{:S(2)}, u32[]{:S(2)}) collective-permute-start(f32[5632,128]{1,0:T(8,128)} %get-tuple-element.254), channel_id=1, source_target_pairs={{0,1},{1,0},{2,3},{3,2},{4,5},{5,4},{6,7},{7,6},{8,9},{9,8},{10,11... | collective-permute-start | bytes 8650760 | tf_op jit(solution)/shard_map/ppermute | solution.py:530
  395.7 5.4 %collective-permute-start.34 = (f32[768,384]{1,0:T(8,128)}, f32[768,384]{1,0:T(8,128)S(1)}, u32[]{:S(2)}, u32[]{:S(2)}) collective-permute-start(f32[768,384]{1,0:T(8,128)} %fusion.32), channel_id=1, source_target_pairs={{0,1},{1,0},{2,3},{3,2},{4,5},{5,4},{6,7},{7,6},{8,9},{9,8},{10,11... | collective-permute-start | bytes 3538952 | tf_op jit(solution)/shard_map/ppermute | solution.py:530
  395.9 5.1 collective-permute-start.35
  396.2 12.7 %collective-permute-start.36 = (bf16[2,2,48,1536]{3,2,1,0:T(8,128)(2,1)}, bf16[2,2,48,1536]{3,2,1,0:T(8,128)(2,1)}, u32[]{:S(2)}, u32[]{:S(2)}) collective-permute-start(bf16[2,2,48,1536]{3,2,1,0:T(8,128)(2,1)} %reduce_second.4), channel_id=1, source_target_pairs={{0,16},{1,9},{2,18},{3,11},{4,20},{5,13},{6,22},{7,15},{8,24},{9,1... | collective-permute-start | bytes 1769480 | tf_op jit(solution)/shard_map/ppermute | solution.py:530
  408.8 19.9 %collective-permute-start.37 = (bf16[2,2,2,592,128]{4,3,2,1,0:T(8,128)(2,1)S(1)}, bf16[2,2,2,592,128]{4,3,2,1,0:T(8,128)(2,1)S(1)}, u32[]{:S(2)}, u32[]{:S(2)}) collective-permute-start(bf16[2,2,2,592,128]{4,3,2,1,0:T(8,128)(2,1)S(1)} %reduce_first.7), channel_id=1, source_target_pairs={{0,8},{1,17},{2,10},{3,19},{4,12},{5,21},{6,14},{7,23},{8,0},{9,25... | collective-permute-start | bytes 3637256 | tf_op jit(solution)/shard_map/ppermute | solution.py:530
  410.9 15.7 %collective-permute-start.39 = (bf16[1,48,3072]{2,1,0:T(8,128)(2,1)S(1)}, bf16[1,48,3072]{2,1,0:T(8,128)(2,1)S(1)}, u32[]{:S(2)}, u32[]{:S(2)}) collective-permute-start(bf16[1,48,3072]{2,1,0:T(8,128)(2,1)S(1)} %copy-done.67), channel_id=1, source_target_pairs={{0,4},{1,5},{2,6},{3,7},{4,0},{5,1},{6,2},{7,3},{8,12},{9,13},{10,... | collective-permute-start | bytes 884744 | tf_op jit(solution)/shard_map/ppermute | solution.py:530
  414.6 14.1 %collective-permute-start.38 = (bf16[2,48,1536]{2,1,0:T(8,128)(2,1)S(1)}, bf16[2,48,1536]{2,1,0:T(8,128)(2,1)S(1)}, u32[]{:S(2)}, u32[]{:S(2)}) collective-permute-start(bf16[2,48,1536]{2,1,0:T(8,128)(2,1)S(1)} %get-tuple-element.270), channel_id=1, source_target_pairs={{0,2},{1,3},{2,0},{3,1},{4,6},{5,7},{6,4},{7,5},{8,10},{9,11},{10,... | collective-permute-start | bytes 884744 | tf_op jit(solution)/shard_map/ppermute | solution.py:530
  433.5 10.4 %collective-permute-start.40 = (bf16[2,2,592,128]{3,2,1,0:T(8,128)(2,1)}, bf16[2,2,592,128]{3,2,1,0:T(8,128)(2,1)}, u32[]{:S(2)}, u32[]{:S(2)}) collective-permute-start(bf16[2,2,592,128]{3,2,1,0:T(8,128)(2,1)} %reduce_second.5), channel_id=1, source_target_pairs={{0,16},{1,9},{2,18},{3,11},{4,20},{5,13},{6,22},{7,15},{8,24},{9,1... | collective-permute-start | bytes 1818632 | tf_op jit(solution)/shard_map/ppermute | solution.py:530
  435.3 18.2 %collective-permute-start.53 = (f32[24,3072]{1,0:T(8,128)S(1)}, f32[24,3072]{1,0:T(8,128)S(1)}, u32[]{:S(2)}, u32[]{:S(2)}) collective-permute-start(f32[24,3072]{1,0:T(8,128)S(1)} %get-tuple-element.295), channel_id=1, source_target_pairs={{0,1},{1,0},{2,3},{3,2},{4,5},{5,4},{6,7},{7,6},{8,9},{9,8},{10,11... | collective-permute-start | bytes 884744 | tf_op jit(solution)/shard_map/ppermute | solution.py:530
  450.6 20.4 %collective-permute-start.41 = (f32[2,592,128]{2,1,0:T(8,128)S(1)}, f32[2,592,128]{2,1,0:T(8,128)S(1)}, u32[]{:S(2)}, u32[]{:S(2)}) collective-permute-start(f32[2,592,128]{2,1,0:T(8,128)S(1)} %get-tuple-element.278), channel_id=1, source_target_pairs={{0,2},{1,3},{2,0},{3,1},{4,6},{5,7},{6,4},{7,5},{8,10},{9,11},{10,... | collective-permute-start | bytes 1818632 | tf_op jit(solution)/shard_map/ppermute | solution.py:530
  450.7 18.0 %collective-permute-start.42 = (f32[1,48,1536]{2,1,0:T(8,128)S(1)}, f32[1,48,1536]{2,1,0:T(8,128)S(1)}, u32[]{:S(2)}, u32[]{:S(2)}) collective-permute-start(f32[1,48,1536]{2,1,0:T(8,128)S(1)} %copy-done.69), channel_id=1, source_target_pairs={{0,4},{1,5},{2,6},{3,7},{4,0},{5,1},{6,2},{7,3},{8,12},{9,13},{10,... | collective-permute-start | bytes 884744 | tf_op jit(solution)/shard_map/ppermute | solution.py:530
  471.6 14.5 %collective-permute-start.43 = (f32[1,592,128]{2,1,0:T(8,128)S(1)}, f32[1,592,128]{2,1,0:T(8,128)S(1)}, u32[]{:S(2)}, u32[]{:S(2)}) collective-permute-start(f32[1,592,128]{2,1,0:T(8,128)S(1)} %get-tuple-element.282), channel_id=1, source_target_pairs={{0,4},{1,5},{2,6},{3,7},{4,0},{5,1},{6,2},{7,3},{8,12},{9,13},{10,... | collective-permute-start | bytes 909320 | tf_op jit(solution)/shard_map/ppermute | solution.py:530
  473.8 13.3 %collective-permute-start.52 = (f32[24,1536]{1,0:T(8,128)S(1)}, f32[24,1536]{1,0:T(8,128)S(1)}, u32[]{:S(2)}, u32[]{:S(2)}) collective-permute-start(f32[24,1536]{1,0:T(8,128)S(1)} %get-tuple-element.293), channel_id=1, source_target_pairs={{0,1},{1,0},{2,3},{3,2},{4,5},{5,4},{6,7},{7,6},{8,9},{9,8},{10,11... | collective-permute-start | bytes 442376 | tf_op jit(solution)/shard_map/ppermute | solution.py:530
  486.3 1.2 collective-permute-start.45
  487.6 4.5 collective-permute-start.48
  488.6 3.8 collective-permute-start.47
  490.8 3.6 collective-permute-start.46
  494.4 5.4 %collective-permute-start.51 = (f32[8,128]{1,0:T(8,128)S(1)}, f32[8,128]{1,0:T(8,128)S(1)}, u32[]{:S(2)}, u32[]{:S(2)}) collective-permute-start(f32[8,128]{1,0:T(8,128)S(1)} %add_add_fusion.1), channel_id=1, source_target_pairs={{0,6},{1,7},{2,4},{3,5},{4,2},{5,3},{6,0},{7,1},{8,14},{9,15},{10,... | collective-permute-start | bytes 12296 | tf_op jit(solution)/shard_map/ppermute | solution.py:530
  495.8 4.5 collective-permute-start.50
  495.8 4.5 collective-permute-start.49
  499.4 2.2 collective-permute-start.44
  (124 other events, 801.7 us)

commit v4 on v3

--- a/solution.py
+++ b/solution.py
@@ -321,7 +321,9 @@
             out_ref[...] = dv_acc[...].astype(jnp.bfloat16)
 
     def column(place):
-        return pl.BlockSpec((length, WIDE), lambda third, windows: (0, place))
+        return pl.BlockSpec(
+            (length, WIDE), lambda third, windows: (0, place), pipeline_mode=pl.Buffered(1)
+        )
 
     return pl.pallas_call(
         kernel,
@@ -344,18 +346,18 @@
             + [pltpu.VMEM((length, WIDE), jnp.float32)] * 3
             + [pltpu.VMEM((WIDE, length), jnp.bfloat16)],
         ),
-        compiler_params=pltpu.CompilerParams(vmem_limit_bytes=44 << 20),
+        compiler_params=pltpu.CompilerParams(vmem_limit_bytes=38 << 20),
         name="attention_backward",
     )(windows, mixed, mixed, mixed, grad_attended, log_sums, seg_row, seg_col)
 
 
-def head_pass(pred_low, word_table, token_weight):
+def head_pass(pred_low, word_table, token_weight, small):
     length, width = pred_low.shape
     words = word_table.shape[0]
     tile, across = 1024, 256
 
     def kernel(
-        pred_ref, table_ref, weight_ref, grad_table_ref, grad_pred_ref, log_ref, peak, total, grads
+        small_ref, pred_ref, table_ref, weight_ref, grad_table_ref, grad_pred_ref, log_ref, peak, total, grads
     ):
         phase, step = pl.program_id(0), pl.program_id(1)
         blocks = [
@@ -366,11 +368,17 @@
 
         @pl.when((phase == 0) & (step == 0))
         def _():
-            peak[...] = jnp.full_like(peak, -1e30)
+            peak[...] = jnp.full_like(peak, jnp.where(small_ref[0] == 1, 0.0, -1e30))
             total[...] = jnp.zeros_like(total)
             grad_pred_ref[...] = jnp.zeros_like(grad_pred_ref)
 
-        @pl.when(phase == 0)
+        @pl.when((phase == 0) & (small_ref[0] == 1))
+        def _():
+            for rows, cols in blocks:
+                logits = fold(nt_dot(table_ref[rows, :], pred_ref[cols, :]) * LOG2E)
+                total[:, cols] += jnp.sum(jnp.exp2(logits), 0)
+
+        @pl.when((phase == 0) & (small_ref[0] == 0))
         def _():
             for rows, cols in blocks:
                 logits = fold(nt_dot(table_ref[rows, :], pred_ref[cols, :]) * LOG2E)
@@ -404,7 +412,7 @@
             grad_pred_ref[...] += tn_dot(table_ref[...], grads[...])
 
     def whole(shape):
-        return pl.BlockSpec(shape, lambda phase, step: (0, 0))
+        return pl.BlockSpec(shape, lambda phase, step, small: (0, 0))
 
     return pl.pallas_call(
         kernel,
@@ -414,24 +422,24 @@
             jax.ShapeDtypeStruct((1, length), jnp.float32),
         ),
         grid_spec=pltpu.PrefetchScalarGridSpec(
-            num_scalar_prefetch=0,
+            num_scalar_prefetch=1,
             grid=(2, words // tile),
             in_specs=[
                 whole((length, width)),
-                pl.BlockSpec((tile, width), lambda phase, step: (step, 0)),
+                pl.BlockSpec((tile, width), lambda phase, step, small: (step, 0)),
                 whole((1, length)),
             ],
             out_specs=[
-                pl.BlockSpec((tile, width), lambda phase, step: (phase * step, 0)),
+                pl.BlockSpec((tile, width), lambda phase, step, small: (phase * step, 0)),
                 whole((width, length)),
                 whole((1, length)),
             ],
             scratch_shapes=[pltpu.VMEM((8, length), jnp.float32)] * 2
             + [pltpu.VMEM((tile, length), jnp.bfloat16)],
         ),
-        compiler_params=pltpu.CompilerParams(vmem_limit_bytes=18 << 20),
+        compiler_params=pltpu.CompilerParams(vmem_limit_bytes=60 << 20),
         name="head_pass",
-    )(pred_low, word_table, token_weight)
+    )(small, pred_low, word_table, token_weight)
 
 
 def adam_rule(master, moment, second, grad, rate, decay):
@@ -541,7 +549,7 @@
     def swap_line(self, array, bit):
         return self.swap(array, lambda member: bit)
 
-    def total(self, array):
+    def total(self, array, beside):
         array = array + self.swap_core(array)
         spans = [self.columns, 2 * self.columns] + self.bits
         for at in range(0, len(spans), 2):
@@ -550,7 +558,9 @@
             for far in more:
                 parts += [self.swap_line(array, far), self.swap_line(array, near ^ far)]
             array = array + sum(parts)
-        return array
+            if at == 0:
+                array, *beside = tie(array, *beside)
+        return array, beside
 
 
 def assemble(place, pieces):
@@ -668,7 +678,7 @@
                 pltpu.SemaphoreType.DMA((2,)),
             ],
         ),
-        compiler_params=pltpu.CompilerParams(vmem_limit_bytes=9 << 20),
+        compiler_params=pltpu.CompilerParams(vmem_limit_bytes=48 << 20),
         name="scatter_halves",
     )(spots, flag, table, rows)
 
@@ -1038,8 +1048,7 @@
     gains_pad = jnp.concatenate(
         [
             low[8].T,
-            jnp.broadcast_to(aside[None, :], (own_rows, 2 * buckets)),
-            jnp.zeros((own_rows, EMB - 3 - 2 * buckets), jnp.bfloat16),
+            jnp.zeros((own_rows, EMB - 3), jnp.bfloat16),
         ],
         1,
     )
@@ -1049,7 +1058,8 @@
     table = low[0][None]
     entry = jnp.concatenate([low[1].T, low[2].T, gains_pad], 1)[None]
     qkv = low[3][None]
-    leave = jnp.concatenate([low[4].T, low[5], low[6].T, low[7]], 1)[None]
+    aside_pad = jnp.pad(aside[None, :], ((0, own_rows - 1), (0, EMB - 2 * buckets)))
+    leave = jnp.concatenate([low[4].T, low[5], low[6].T, low[7], aside_pad], 1)[None]
     fraction = step_row.astype(jnp.float32) / STEPS_T
     alpha_bar = 1.0 - jnp.sqrt(fraction + 0.0001)
     keep_root = jnp.sqrt(alpha_bar)[:, None]
@@ -1066,17 +1076,21 @@
     for bit in down_bits[:-1]:
         entry, qkv = tie(entry, qkv)
         qkv = join(qkv, place.swap_line(qkv, bit))
-    table, entry, qkv, leave = tie(table, entry, qkv, leave)
+    table, entry, qkv = tie(table, entry, qkv)
     table_came, entry_came = place.swap_a(table), place.swap_a(entry)
-    qkv_came = place.swap_line(qkv, down_bits[-1])
-    for bit in down_bits[:-1]:
-        leave = join(leave, place.swap_line(leave, bit))
-    table_came, entry_came, qkv_came, step_row = tie(table_came, entry_came, qkv_came, step_row)
+    table_came, entry_came, qkv, leave, step_row = tie(
+        table_came, entry_came, qkv, leave, step_row
+    )
     feature_low = sinusoid(step_row, D).astype(jnp.bfloat16)
-    table, entry, qkv = join(table, table_came), join(entry, entry_came), join(qkv, qkv_came)
+    table, entry = join(table, table_came), join(entry, entry_came)
     table_pieces = [table, place.swap_b(table), place.swap_core(table)]
     entry_pieces = [entry, place.swap_b(entry), place.swap_core(entry)]
-    leave_came = place.swap_line(leave, down_bits[-1])
+    qkv_came = place.swap_line(qkv, down_bits[-1])
+    for bit in down_bits[:-2]:
+        leave = join(leave, place.swap_line(leave, bit))
+    leave_came = place.swap_line(leave, down_bits[-2])
+    (qkv_came,) = tie(qkv_came)
+    qkv = join(qkv, qkv_came)
     *both, qkv, feature_low = tie(*table_pieces, *entry_pieces, qkv, feature_low)
     table_pieces, entry_pieces = both[:3], both[3:]
     table_pieces.append(place.swap_core(table_pieces[1]))
@@ -1085,6 +1099,9 @@
     entry_low = assemble(place, entry_pieces)
     entry_low, qkv_came = tie(entry_low, qkv_came)
     qkv = join(qkv, qkv_came)
+    entry_low, leave_came, qkv = tie(entry_low, leave_came, qkv)
+    leave = join(leave, leave_came)
+    leave_came = place.swap_line(leave, down_bits[-1])
     qkv_pieces = [qkv, place.swap_b(qkv), place.swap_core(qkv)]
     qkv, table_pieces[0] = tie(qkv, table_pieces[0])
     word_table = assemble(place, table_pieces)
@@ -1093,12 +1110,9 @@
     leave_came = place.swap_a(leave)
     up_low = entry_low[:, :EMB]
     time_low = entry_low[:, EMB : EMB + model_width]
-    aside_low = entry_low[:, EMB + model_width :]
-    gain_rows = aside_low[:, :3].T.astype(jnp.float32)
-    shares = aside_low.reshape(place.count, own_rows, EMB)[:, 0, 3 : 3 + 2 * buckets]
-    count_sums = jnp.sum(shares.astype(jnp.float32), 0)
-    counts = 32.0 * count_sums[:buckets] + count_sums[buckets:]
-    token_weight = live_float * jnp.sum(onehot / counts[None, :], -1) / buckets
+    gain_rows = entry_low[:, EMB + model_width :][:, :3].T.astype(jnp.float32)
+
+    table_size = jnp.max(jnp.sum(jnp.square(word_table.astype(jnp.float32)), 1))
 
     start_emb = word_table[tokens].astype(jnp.float32)
     noisy_emb = keep_root * start_emb + jnp.sqrt(1.0 - alpha_bar)[:, None] * noise[0]
@@ -1123,7 +1137,12 @@
     out_low = leave_low[:, :model_width]
     fc_low = leave_low[:, model_width : model_width + ff_width]
     proj_low = leave_low[:, model_width + ff_width : model_width + 2 * ff_width]
-    down_low = leave_low[:, model_width + 2 * ff_width :]
+    down_low = leave_low[:, model_width + 2 * ff_width : model_width + 2 * ff_width + EMB]
+    shares = leave_low[:, model_width + 2 * ff_width + EMB :]
+    shares = shares.reshape(place.count, own_rows, EMB)[:, 0, : 2 * buckets]
+    count_sums = jnp.sum(shares.astype(jnp.float32), 0)
+    counts = 32.0 * count_sums[:buckets] + count_sums[buckets:]
+    token_weight = live_float * jnp.sum(onehot / counts[None, :], -1) / buckets
     hidden_one = hidden_zero + matrix_product_transposed(attended_low, out_low)
     normed, scaled_two, inverse_two = layer_normalize(hidden_one, gain_rows[1])
     normed_two_low = normed.astype(jnp.bfloat16)
@@ -1134,8 +1153,10 @@
     normed_top_low = normed.astype(jnp.bfloat16)
     prediction = matmul(normed_top_low, down_low)
     pred_low = prediction.astype(jnp.bfloat16)
+    size = jnp.sqrt(jnp.max(jnp.sum(jnp.square(prediction), 1)) * table_size)
+    small = (size < 40.0).astype(jnp.int32).reshape(1)
     grad_table_head, grad_pred_head, log_total = head_pass(
-        pred_low, word_table, token_weight[None, :]
+        pred_low, word_table, token_weight[None, :], small
     )
 
     pred_float = pred_low.astype(jnp.float32)
@@ -1283,7 +1304,8 @@
         shard_pair[:, EMB:],
         shard_exact[:, :3].T,
     )
-    squares = place.total(squares_local)[0, 0]
+    squares, shards = place.total(squares_local, shards)
+    squares = squares[0, 0]
     grad_norm = jnp.sqrt(squares)
     factor = CLIP_NORM / jnp.maximum(grad_norm, CLIP_NORM)
     flips = (False, True, True, False, True, False, True, False, False)

time: 517 us -> 510 us (0.986)
  starting transfers between devices: 53.3 us -> 39.9 us
  waiting for transfers between devices: 79.8 us -> 92.1 us
  local copies, waits for them, and re-layouts: 56.7 us -> 49.4 us
    ppermute x54, starting transfers between devices: 53.3 us -> 39.9 us  [swap(): return lax.ppermute(array, AXES, pairs)]
    ppermute x54, waiting for transfers between devices: 79.8 us -> 92.1 us  [swap(): return lax.ppermute(array, AXES, pairs)]
    unnamed x281 -> x260, local copies, waits for them, and re-layouts: 41.9 us -> 34.6 us
  transfers between devices with their start and end apart: 54 -> 54, of which waited for: 21 -> 23; matrix products, arithmetic and copies ran while one was open for 21% -> 22% of each run, Pallas kernels for 21% -> 20%
where the time goes in v4:
time: 510 us; the launch traced here: 505 us
  Pallas kernels  163 us (32%)
  matrix products  104 us (20%)
  waiting for transfers between devices  92.1 us (18%)
  other arithmetic  50.1 us (10%)
  local copies, waits for them, and re-layouts  49.4 us (10%)
  starting transfers between devices  39.9 us (8%)
  between operations  6.13 us (1%)
    ppermute x54, waiting for transfers between devices, swap(): return lax.ppermute(array, AXES, pairs)  92.1 us
    ppermute x54, starting transfers between devices, swap(): return lax.ppermute(array, AXES, pairs)  39.9 us
    dot_general x7, matrix products, matrix_product_transposed(): lax.dot_general(left_op, right_op, (((1,), (1,)), ((), ())), preferred_el...  36.3 us
    dot_general x6, matrix products, matmul(): return jnp.dot(left_op, right_op, preferred_element_type=jnp.float32)  35.9 us
    unnamed x260, local copies, waits for them, and re-layouts  34.6 us
    pallas_call x1, Pallas kernels, head_pass(): pl.pallas_call(kernel, out_shape=(jax.ShapeDtypeStruct((words, width), jn...  34.2 us
    pallas_call x16, Pallas kernels, call(): pl.pallas_call(kernel, out_shape=[entry for entry, unused, index in outpu...  34 us
    pallas_call x1, Pallas kernels, attention_backward(): pl.pallas_call(kernel, out_shape=jax.ShapeDtypeStruct(mixed.shape, jnp.bf...  33.4 us
  transfers between devices with their start and end apart: 54, of which 23 were waited for; matrix products, arithmetic and copies ran while one was open for 22% of the time, Pallas kernels for 20%

profile of v4, /device:TPU:0, one launch (start us, length us, event | category | flops | bytes accessed | tf_op | source)
XLA Modules:
  0.0 505.3 jit_solution(16498359930247114818)
XLA Ops:
  3.2 4.1 collective-permute-start.1
  21.2 3.6 collective-permute-done.3
  24.9 2.9 collective-permute-start.4
  28.8 3.6 collective-permute-done.4
  34.7 7.3 %collective-permute-done.6 = bf16[4,24,1024]{2,1,0:T(8,128)(2,1)S(1)} collective-permute-done((bf16[4,24,1024]{2,1,0:T(8,128)(2,1)S(1)}, bf16[4,24,1024]{2,1,0:T(8,128)(2,1)S(1)}, u32[]{:S(2)}, u32[]{:S(2)}) %collective-permute-start.6) | collective-permute-done | bytes 196640 | tf_op jit(solution)/shard_map/ppermute | solution.py:538
  45.8 6.5 %fusion.22 = (bf16[1024,384]{1,0:T(8,128)(2,1)S(1)}, bf16[1024,384]{1,0:T(8,128)(2,1)S(1)}) fusion(f32[384]{0:T(512)S(1)} %multiply_exponential_fusion, f32[1024]{0:T(1024)S(1)} %convert_element_type.142), kind=kLoop, calls=%fused_computation.56 | loop fusion | flops 1179648 | bytes 1578496 | tf_op jit(solution)/shard_map/convert.2
  53.6 3.4 collective-permute-start.14
  60.3 3.4 assemble.4
  63.8 2.2 collective-permute-done.13
  67.0 5.4 %collective-permute-done.14 = bf16[1,24,7168]{2,1,0:T(8,128)(2,1)S(1)} collective-permute-done((bf16[1,24,7168]{2,1,0:T(8,128)(2,1)S(1)}, bf16[1,24,7168]{2,1,0:T(8,128)(2,1)S(1)}, u32[]{:S(2)}, u32[]{:S(2)}) %collective-permute-start.14) | collective-permute-done | bytes 344096 | tf_op jit(solution)/shard_map/ppermute | solution.py:538
  77.0 4.6 fusion.26
  83.7 5.5 %assemble.5 = bf16[4,4,2,352,128]{4,3,2,1,0:T(8,128)(2,1)S(1)} custom-call(s32[3]{0:T(128)S(1)} %pad_add_fusion.3.flags_ref, bf16[8,352,128]{2,1,0:T(8,128)(2,1)S(1)} %copy-done.38, bf16[8,352,128]{2,1,0:T(8,128)(2,1)S(1)} %copy-done.46, bf16[8,352,128]{2,1,0:T(8,128)(2,1)S(1)} %copy-done.44, bf16[8,352,128]{2,1,0:T(8,128)(2,1)S(1)} %copy-done.48), custom_call_target="tpu_custom_call" | custom-call | tf_op jit(solution)/shard_map/assemble/pallas_call | solution.py:598
  89.2 2.6 collective-permute-done.16
  91.8 2.3 pad_maximum_fusion.1
  95.6 3.2 gather_fusion
  100.3 2.7 fusion.83
  107.7 6.3 %assemble.6 = bf16[4,4,2,24,2304]{4,3,2,1,0:T(8,128)(2,1)S(1)} custom-call(s32[3]{0:T(128)S(1)} %pad_add_fusion.3.flags_ref, bf16[8,24,2304]{2,1,0:T(8,128)(2,1)} %pad_maximum_fusion.2.refs_0_, bf16[8,24,2304]{2,1,0:T(8,128)(2,1)} %collective-permute-done.18.refs_1_, bf16[8,24,2304]{2,1,0:T(8,128)(2,1)} %collective-permute-done.19.refs_2_, ...), custom_call_target="tpu_custom_call" | custom-call | tf_op jit(solution)/shard_map/assemble/pallas_call | solution.py:598
  114.1 2.5 constant_dynamic-update-slice_fusion.7.refs_0_
  117.2 4.2 convolution_convert_fusion.q_ref.k_ref.v_ref
  121.7 25.8 %attention_forward.1 = (bf16[1024,768]{1,0:T(8,128)(2,1)S(1)}, f32[16,1024]{1,0:T(8,128)S(1)}) custom-call(s32[2,8]{1,0:T(2,128)S(1)} %pad_add_fusion.windows_ref, bf16[1024,2304]{1,0:T(8,128)(2,1)S(1)} %convolution_convert_fusion.q_ref.k_ref.v_ref, bf16[1024,2304]{1,0:T(8,128)(2,1)S(1)} %convolution_convert_fusion.q_ref.k_ref.v_ref, ...), custom_call_target="tpu_custom_call" | custom-call | tf_op jit(solution)/shard_map/attention_forward/pallas_call | solution.py:200
  152.7 3.0 collective-permute-done.23.refs_3_
  159.3 5.5 %assemble.7 = bf16[4,4,2,24,7168]{4,3,2,1,0:T(8,128)(2,1)S(1)} custom-call(s32[3]{0:T(128)S(1)} %pad_add_fusion.3.flags_ref, bf16[8,24,7168]{2,1,0:T(8,128)(2,1)S(1)} %copy-done.33, bf16[8,24,7168]{2,1,0:T(8,128)(2,1)} %collective-permute-done.21.refs_1_, bf16[8,24,7168]{2,1,0:T(8,128)(2,1)S(1)} %copy-done.35, ...), custom_call_target="tpu_custom_call" | custom-call | tf_op jit(solution)/shard_map/assemble/pallas_call | solution.py:598
  168.5 12.9 %multiply_add_fusion = (f32[1024,3072]{1,0:T(8,128)}, bf16[1024,3072]{1,0:T(8,128)(2,1)S(1)}) fusion(bf16[1024,768]{0,1:T(8,128)(2,1)S(1)} %multiply_convert_fusion.3, bf16[768,7168]{1,0:T(8,128)(2,1)S(1)} %bitcast.213), kind=kOutput, calls=%fused_computation.2 | convolution fusion | flops 4882169856 | bytes 25165824 | tf_op jit(solution)/shard_map/dot_general | solution.py:29
  181.4 5.1 %fusion.85 = (f32[1024]{0:T(1024)S(1)}, f32[1024,768]{0,1:T(8,128)S(1)}) fusion(f32[1024,768]{0,1:T(8,128)S(1)} %get-tuple-element.405, bf16[1024,3072]{1,0:T(8,128)(2,1)S(1)} %get-tuple-element.229, bf16[768,7168]{1,0:T(8,128)(2,1)S(1)} %bitcast.214), kind=kOutput, calls=%fused_computation.261 | convolution fusion | flops 4833410048 | bytes 17305600 | tf_op jit(solution)/shard_map/dot_general | solution.py:39
  192.5 34.2 %head_pass.1 = (f32[11264,128]{1,0:T(8,128)}, f32[128,1024]{1,0:T(8,128)}, f32[1,1024]{1,0:T(1,128)}) custom-call(s32[1]{0:T(128)} %bitcast.34.small_ref, bf16[1024,128]{1,0:T(8,128)(2,1)} %get-tuple-element.367.pred_ref, bf16[11264,128]{1,0:T(8,128)(2,1)} %bitcast.189, f32[1,1024]{1,0:T(1,128)} %multiply_multiply_fusion.1.weight_ref), custom_call_target="tpu_custom_call" | custom-call | tf_op jit(solution)/shard_map/head_pass/pallas_call | solution.py:417
  229.6 3.3 multiply_reduce_fusion.4
  235.9 4.3 fusion.11
  240.5 4.5 fusion.13
  245.0 11.3 %multiply_convert_fusion = bf16[1024,3072]{1,0:T(8,128)(2,1)S(1)} fusion(f32[1024,3072]{1,0:T(8,128)} %get-tuple-element.234, bf16[1024,768]{0,1:T(8,128)(2,1)S(1)} %fusion.78, bf16[768,7168]{1,0:T(8,128)(2,1)} %bitcast.217), kind=kOutput, calls=%fused_computation.1 | convolution fusion | flops 4838129664 | bytes 25165824 | tf_op jit(solution)/shard_map/dot_general | solution.py:29
  256.3 4.6 reduce_first.4
  260.9 4.5 fusion.7
  266.1 9.8 %multiply_reduce_fusion.3 = (f32[768]{0:T(1024)S(1)}, f32[1024]{0:T(1024)S(1)}, f32[1024]{0:T(1024)S(1)}, f32[1024,768]{0,1:T(8,128)S(1)}) fusion(f32[1024,768]{0,1:T(8,128)} %copy-done.68, f32[1024]{0:T(1024)S(1)} %add_rsqrt_fusion.1, f32[1024]{0:T(1024)S(1)} %broadcast_multiply_fusion.8, f32[768]{0:T(1024)S(1)} %copy-done.109, ...), kind=kOutput, calls=%fused_computation.20 | convolution fusion | flops 4838126592 | bytes 17324032 | tf_op jit(solution)/shard_map/dot_general | solution.py:39
  277.7 2.6 fusion.9
  281.6 3.3 fusion.79
  284.9 3.1 reduce_first.5
  288.1 4.0 convolution_convert_fusion.1.do_ref
  296.0 2.1 collective-permute-start.27
  298.1 2.3 copy-done.1
  301.8 33.4 %attention_backward.1 = bf16[1024,2304]{1,0:T(8,128)(2,1)S(1)} custom-call(s32[2,8]{1,0:T(2,128)S(1)} %pad_add_fusion.windows_ref, bf16[1024,2304]{1,0:T(8,128)(2,1)S(1)} %copy-done.1, bf16[1024,2304]{1,0:T(8,128)(2,1)S(1)} %copy-done.1, bf16[1024,2304]{1,0:T(8,128)(2,1)S(1)} %copy-done.1, bf16[1024,768]{1,0:T(8,128)(2,1)S(1)} %copy-done.39, ...), custom_call_target="tpu_custom_call" | custom-call | tf_op jit(solution)/shard_map/attention_backward/pallas_call | solution.py:328
  335.4 4.5 reduce_second.3
  340.0 4.0 fusion.15
  344.1 9.3 %multiply_reduce_fusion.1 = (f32[768]{0:T(1024)}, f32[1024]{0:T(1024)S(1)}, f32[1024]{0:T(1024)S(1)}, f32[1024,768]{0,1:T(8,128)S(1)}) fusion(f32[1024,768]{0,1:T(8,128)} %copy-done.63, f32[1024]{0:T(1024)} %copy-done.96, f32[1024]{0:T(1024)S(1)} %broadcast_multiply_fusion.9, f32[768]{0:T(1024)} %copy-done.98, bf16[1024,2304]{1,0:T(8,128)(2,1)} %copy-done.29, ...), kind=kOutput, calls=%fused_computation.17 | convolution fusion | flops 3630167296 | bytes 14571520 | tf_op jit(solution)/shard_map/dot_general | solution.py:39
  353.6 2.2 fusion.17
  357.5 3.0 collective-permute-done.30.refs_6_
  360.5 3.8 reduce_third.3
  364.5 3.1 fusion.25.rows_ref
  367.6 2.3 reduce_first.6
  371.4 9.4 %scatter_halves.1 = (f32[5632,128]{1,0:T(8,128)}, f32[5632,128]{1,0:T(8,128)}) custom-call(s32[1024]{0:T(1024)S(1)} %get-tuple-element.414.spots_ref, s32[1]{0:T(128)} %bitcast.flag_ref.flags_ref, f32[11264,128]{1,0:T(8,128)} %get-tuple-element.230.table_ref, f32[1024,128]{1,0:T(8,128)S(1)} %copy-done.36), custom_call_target="tpu_custom_call" | custom-call | tf_op jit(solution)/shard_map/scatter_halves/pallas_call | solution.py:664
  380.8 4.9 collective-permute-done.32
  387.5 2.2 reduce_second.4
  393.3 2.0 fusion.32
  397.8 2.6 fusion.30
  400.4 2.3 copy.82
  405.6 2.5 reduce_first.7
  409.8 2.1 reduce_third.4
  412.4 12.9 %collective-permute-done.39.came_ref = bf16[1,48,3072]{2,1,0:T(8,128)(2,1)S(1)} collective-permute-done((bf16[1,48,3072]{2,1,0:T(8,128)(2,1)S(1)}, bf16[1,48,3072]{2,1,0:T(8,128)(2,1)S(1)}, u32[]{:S(2)}, u32[]{:S(2)}) %collective-permute-start.39) | collective-permute-done | bytes 294944 | tf_op jit(solution)/shard_map/ppermute | solution.py:538
  426.9 2.7 reduce_second.5
  434.8 7.2 %collective-permute-done.40.refs_13_ = bf16[2,2,592,128]{3,2,1,0:T(8,128)(2,1)} collective-permute-done((bf16[2,2,592,128]{3,2,1,0:T(8,128)(2,1)}, bf16[2,2,592,128]{3,2,1,0:T(8,128)(2,1)}, u32[]{:S(2)}, u32[]{:S(2)}) %collective-permute-start.40) | collective-permute-done | bytes 606240 | tf_op jit(solution)/shard_map/ppermute | solution.py:538
  446.3 2.4 reduce_third.5
  450.7 12.9 %collective-permute-done.41 = f32[2,592,128]{2,1,0:T(8,128)S(1)} collective-permute-done((f32[2,592,128]{2,1,0:T(8,128)S(1)}, f32[2,592,128]{2,1,0:T(8,128)S(1)}, u32[]{:S(2)}, u32[]{:S(2)}) %collective-permute-start.41) | collective-permute-done | bytes 606240 | tf_op jit(solution)/shard_map/ppermute | solution.py:538
  465.4 15.2 %collective-permute-done.43.came_ref = f32[1,592,128]{2,1,0:T(8,128)S(1)} collective-permute-done((f32[1,592,128]{2,1,0:T(8,128)S(1)}, f32[1,592,128]{2,1,0:T(8,128)S(1)}, u32[]{:S(2)}, u32[]{:S(2)}) %collective-permute-start.43) | collective-permute-done | bytes 303136 | tf_op jit(solution)/shard_map/ppermute | solution.py:538
  482.0 2.3 collective-permute-start.48
  492.1 2.4 collective-permute-start.51
  497.9 6.0 %adam_update.1 = (f32[352,128]{1,0:T(8,128)}, f32[352,128]{1,0:T(8,128)}, f32[352,128]{1,0:T(8,128)}, f32[24,128]{1,0:T(8,128)}, f32[24,128]{1,0:T(8,128)}, /*in...) custom-call(f32[1]{0:T(128)} %bitcast.65.factor_ref, ...), custom_call_target="tpu_custom_call" | custom-call | tf_op jit(solution)/shard_map/adam_update/pallas_call | solution.py:495
  (483 shorter events, 119.1 us)
Async XLA Ops:
  3.1 42.5 %copy-start.108 = (s32[1,1024]{1,0:T(1,128)S(1)}, s32[1,1024]{1,0:T(1,128)}, u32[]{:S(2)}) copy-start(s32[1,1024]{1,0:T(1,128)} %param.35) | copy-start | bytes 12292
  3.2 15.9 %collective-permute-start.1 = (bf16[1,24,1024]{2,1,0:T(8,128)(2,1)S(1)}, bf16[1,24,1024]{2,1,0:T(8,128)(2,1)S(1)}, u32[]{:S(2)}, u32[]{:S(2)}) collective-permute-start(bf16[1,24,1024]{2,1,0:T(8,128)(2,1)S(1)} %maximum_bitcast_fusion), channel_id=1, source_target_pairs={{0,4},{1,5},{2,6},{3,7},{4,0},{5,1},{6,2},{7,3},{8,12},{9,13},{10,... | collective-permute-start | bytes 147464 | tf_op jit(solution)/shard_map/ppermute | solution.py:538
  8.2 10.9 %collective-permute-start = (bf16[1,352,128]{2,1,0:T(8,128)(2,1)S(1)}, bf16[1,352,128]{2,1,0:T(8,128)(2,1)S(1)}, u32[]{:S(2)}, u32[]{:S(2)}) collective-permute-start(bf16[1,352,128]{2,1,0:T(8,128)(2,1)S(1)} %convert_bitcast_fusion.1), channel_id=1, source_target_pairs={{0,4},{1,5},{2,6},{3,7},{4,0},{5,1},{6,2},{7,3},{8,12},{9,13},{10,... | collective-permute-start | bytes 270344 | tf_op jit(solution)/shard_map/ppermute | solution.py:538
  11.1 41.2 %copy-start.106 = (f32[1,1024]{1,0:T(1,128)}, f32[1,1024]{1,0:T(1,128)S(1)}, u32[]{:S(2)}) copy-start(f32[1,1024]{1,0:T(1,128)S(1)} %convert_element_type.140) | copy-start | bytes 12292
  13.6 85.2 %copy-start.100 = (f32[1024]{0:T(1024)}, f32[1024]{0:T(1024)S(1)}, u32[]{:S(2)}) copy-start(f32[1024]{0:T(1024)S(1)} %get-tuple-element.394) | copy-start | bytes 12292
  19.1 5.7 %collective-permute-start.3 = (bf16[2,24,1024]{2,1,0:T(8,128)(2,1)S(1)}, bf16[2,24,1024]{2,1,0:T(8,128)(2,1)S(1)}, u32[]{:S(2)}, u32[]{:S(2)}) collective-permute-start(bf16[2,24,1024]{2,1,0:T(8,128)(2,1)S(1)} %pad_maximum_fusion.11), channel_id=1, source_target_pairs={{0,2},{1,3},{2,0},{3,1},{4,6},{5,7},{6,4},{7,5},{8,10},{9,11},{10,... | collective-permute-start | bytes 294920 | tf_op jit(solution)/shard_map/ppermute | solution.py:538
  21.1 7.7 %collective-permute-start.2 = (bf16[2,352,128]{2,1,0:T(8,128)(2,1)S(1)}, bf16[2,352,128]{2,1,0:T(8,128)(2,1)S(1)}, u32[]{:S(2)}, u32[]{:S(2)}) collective-permute-start(bf16[2,352,128]{2,1,0:T(8,128)(2,1)S(1)} %pad_maximum_fusion.10), channel_id=1, source_target_pairs={{0,2},{1,3},{2,0},{3,1},{4,6},{5,7},{6,4},{7,5},{8,10},{9,11},{10,... | collective-permute-start | bytes 540680 | tf_op jit(solution)/shard_map/ppermute | solution.py:538
  24.9 7.5 %collective-permute-start.4 = (bf16[1,24,2304]{2,1,0:T(8,128)(2,1)S(1)}, bf16[1,24,2304]{2,1,0:T(8,128)(2,1)S(1)}, u32[]{:S(2)}, u32[]{:S(2)}) collective-permute-start(bf16[1,24,2304]{2,1,0:T(8,128)(2,1)S(1)} %convert_bitcast_fusion), channel_id=1, source_target_pairs={{0,4},{1,5},{2,6},{3,7},{4,0},{5,1},{6,2},{7,3},{8,12},{9,13},{10,... | collective-permute-start | bytes 331784 | tf_op jit(solution)/shard_map/ppermute | solution.py:538
  32.4 9.6 %collective-permute-start.5 = (bf16[4,352,128]{2,1,0:T(8,128)(2,1)S(1)}, bf16[4,352,128]{2,1,0:T(8,128)(2,1)S(1)}, u32[]{:S(2)}, u32[]{:S(2)}) collective-permute-start(bf16[4,352,128]{2,1,0:T(8,128)(2,1)S(1)} %pad_maximum_fusion.7), channel_id=1, source_target_pairs={{0,8},{1,17},{2,10},{3,19},{4,12},{5,21},{6,14},{7,23},{8,0},{9,25... | collective-permute-start | bytes 1081352 | tf_op jit(solution)/shard_map/ppermute | solution.py:538
  34.3 7.8 %collective-permute-start.6 = (bf16[4,24,1024]{2,1,0:T(8,128)(2,1)S(1)}, bf16[4,24,1024]{2,1,0:T(8,128)(2,1)S(1)}, u32[]{:S(2)}, u32[]{:S(2)}) collective-permute-start(bf16[4,24,1024]{2,1,0:T(8,128)(2,1)S(1)} %pad_maximum_fusion.9), channel_id=1, source_target_pairs={{0,8},{1,17},{2,10},{3,19},{4,12},{5,21},{6,14},{7,23},{8,0},{9,25... | collective-permute-start | bytes 589832 | tf_op jit(solution)/shard_map/ppermute | solution.py:538
  42.0 15.0 %collective-permute-start.10 = (bf16[8,24,1024]{2,1,0:T(8,128)(2,1)S(1)}, bf16[8,24,1024]{2,1,0:T(8,128)(2,1)S(1)}, u32[]{:S(2)}, u32[]{:S(2)}) collective-permute-start(bf16[8,24,1024]{2,1,0:T(8,128)(2,1)S(1)} %constant_dynamic-update-slice_fusion.5.refs_0_), channel_id=1, source_target_pairs={{0,1},{1,0},{2,3},{3,2},{4,5},{5,4},{6,7},{7,6},{8,9},{9,8},{10,11... | collective-permute-start | bytes 1179656 | tf_op jit(solution)/shard_map/ppermute | solution.py:538
  42.1 14.9 %collective-permute-start.9 = (bf16[8,24,1024]{2,1,0:T(8,128)(2,1)S(1)}, bf16[8,24,1024]{2,1,0:T(8,128)(2,1)S(1)}, u32[]{:S(2)}, u32[]{:S(2)}) collective-permute-start(bf16[8,24,1024]{2,1,0:T(8,128)(2,1)S(1)} %constant_dynamic-update-slice_fusion.5.refs_0_), channel_id=1, source_target_pairs={{0,16},{1,9},{2,18},{3,11},{4,20},{5,13},{6,22},{7,15},{8,24},{9,1... | collective-permute-start | bytes 1179656 | tf_op jit(solution)/shard_map/ppermute | solution.py:538
  43.9 13.2 %collective-permute-start.8 = (bf16[8,352,128]{2,1,0:T(8,128)(2,1)S(1)}, bf16[8,352,128]{2,1,0:T(8,128)(2,1)S(1)}, u32[]{:S(2)}, u32[]{:S(2)}) collective-permute-start(bf16[8,352,128]{2,1,0:T(8,128)(2,1)S(1)} %constant_dynamic-update-slice_fusion.3.refs_0_), channel_id=1, source_target_pairs={{0,1},{1,0},{2,3},{3,2},{4,5},{5,4},{6,7},{7,6},{8,9},{9,8},{10,11... | collective-permute-start | bytes 2162696 | tf_op jit(solution)/shard_map/ppermute | solution.py:538
  44.1 13.6 %collective-permute-start.7 = (bf16[8,352,128]{2,1,0:T(8,128)(2,1)S(1)}, bf16[8,352,128]{2,1,0:T(8,128)(2,1)S(1)}, u32[]{:S(2)}, u32[]{:S(2)}) collective-permute-start(bf16[8,352,128]{2,1,0:T(8,128)(2,1)S(1)} %constant_dynamic-update-slice_fusion.3.refs_0_), channel_id=1, source_target_pairs={{0,16},{1,9},{2,18},{3,11},{4,20},{5,13},{6,22},{7,15},{8,24},{9,1... | collective-permute-start | bytes 2162696 | tf_op jit(solution)/shard_map/ppermute | solution.py:538
  45.6 8.0 %collective-permute-start.11 = (bf16[2,24,2304]{2,1,0:T(8,128)(2,1)S(1)}, bf16[2,24,2304]{2,1,0:T(8,128)(2,1)S(1)}, u32[]{:S(2)}, u32[]{:S(2)}) collective-permute-start(bf16[2,24,2304]{2,1,0:T(8,128)(2,1)S(1)} %pad_maximum_fusion.8), channel_id=1, source_target_pairs={{0,2},{1,3},{2,0},{3,1},{4,6},{5,7},{6,4},{7,5},{8,10},{9,11},{10,... | collective-permute-start | bytes 663560 | tf_op jit(solution)/shard_map/ppermute | solution.py:538
  53.6 18.8 %collective-permute-start.14 = (bf16[1,24,7168]{2,1,0:T(8,128)(2,1)S(1)}, bf16[1,24,7168]{2,1,0:T(8,128)(2,1)S(1)}, u32[]{:S(2)}, u32[]{:S(2)}) collective-permute-start(bf16[1,24,7168]{2,1,0:T(8,128)(2,1)S(1)} %bitcast.242), channel_id=1, source_target_pairs={{0,4},{1,5},{2,6},{3,7},{4,0},{5,1},{6,2},{7,3},{8,12},{9,13},{10,... | collective-permute-start | bytes 1032200 | tf_op jit(solution)/shard_map/ppermute | solution.py:538
  57.7 2.6 collective-permute-start.12
  57.7 8.3 %collective-permute-start.13 = (bf16[4,24,2304]{2,1,0:T(8,128)(2,1)S(1)}, bf16[4,24,2304]{2,1,0:T(8,128)(2,1)S(1)}, u32[]{:S(2)}, u32[]{:S(2)}) collective-permute-start(bf16[4,24,2304]{2,1,0:T(8,128)(2,1)S(1)} %pad_maximum_fusion.6), channel_id=1, source_target_pairs={{0,8},{1,17},{2,10},{3,19},{4,12},{5,21},{6,14},{7,23},{8,0},{9,25... | collective-permute-start | bytes 1327112 | tf_op jit(solution)/shard_map/ppermute | solution.py:538
  60.1 21.6 %collective-permute-start.15 = (bf16[8,352,128]{2,1,0:T(8,128)(2,1)S(1)}, bf16[8,352,128]{2,1,0:T(8,128)(2,1)S(1)}, u32[]{:S(2)}, u32[]{:S(2)}) collective-permute-start(bf16[8,352,128]{2,1,0:T(8,128)(2,1)S(1)} %collective-permute-done.7.refs_1_), channel_id=1, source_target_pairs={{0,1},{1,0},{2,3},{3,2},{4,5},{5,4},{6,7},{7,6},{8,9},{9,8},{10,11... | collective-permute-start | bytes 2162696 | tf_op jit(solution)/shard_map/ppermute | solution.py:538
  72.4 32.3 %collective-permute-start.19 = (bf16[8,24,2304]{2,1,0:T(8,128)(2,1)}, bf16[8,24,2304]{2,1,0:T(8,128)(2,1)}, u32[]{:S(2)}, u32[]{:S(2)}) collective-permute-start(bf16[8,24,2304]{2,1,0:T(8,128)(2,1)} %pad_maximum_fusion.2.refs_0_), channel_id=1, source_target_pairs={{0,1},{1,0},{2,3},{3,2},{4,5},{5,4},{6,7},{7,6},{8,9},{9,8},{10,11... | collective-permute-start | bytes 2654216 | tf_op jit(solution)/shard_map/ppermute | solution.py:538
  72.4 32.3 %collective-permute-start.18 = (bf16[8,24,2304]{2,1,0:T(8,128)(2,1)}, bf16[8,24,2304]{2,1,0:T(8,128)(2,1)}, u32[]{:S(2)}, u32[]{:S(2)}) collective-permute-start(bf16[8,24,2304]{2,1,0:T(8,128)(2,1)} %pad_maximum_fusion.2.refs_0_), channel_id=1, source_target_pairs={{0,16},{1,9},{2,18},{3,11},{4,20},{5,13},{6,22},{7,15},{8,24},{9,1... | collective-permute-start | bytes 2654216 | tf_op jit(solution)/shard_map/ppermute | solution.py:538
  74.1 17.7 %collective-permute-start.16 = (bf16[2,24,7168]{2,1,0:T(8,128)(2,1)}, bf16[2,24,7168]{2,1,0:T(8,128)(2,1)}, u32[]{:S(2)}, u32[]{:S(2)}) collective-permute-start(bf16[2,24,7168]{2,1,0:T(8,128)(2,1)} %pad_maximum_fusion.5), channel_id=1, source_target_pairs={{0,2},{1,3},{2,0},{3,1},{4,6},{5,7},{6,4},{7,5},{8,10},{9,11},{10,... | collective-permute-start | bytes 2064392 | tf_op jit(solution)/shard_map/ppermute | solution.py:538
  77.0 26.4 %copy-start.98 = (f32[768]{0:T(1024)}, f32[768]{0:T(1024)S(1)}, u32[]{:S(2)}) copy-start(f32[768]{0:T(1024)S(1)} %get-tuple-element.362) | copy-start | bytes 9220
  89.2 61.2 %copy-start.4 = (bf16[4,4,2,352,128]{4,3,2,1,0:T(8,128)(2,1)}, bf16[4,4,2,352,128]{4,3,2,1,0:T(8,128)(2,1)S(1)}, u32[]{:S(2)}) copy-start(bf16[4,4,2,352,128]{4,3,2,1,0:T(8,128)(2,1)S(1)} %assemble.5) | copy-start | bytes 8650756
  94.1 19.9 %collective-permute-start.17 = (bf16[4,24,7168]{2,1,0:T(8,128)(2,1)}, bf16[4,24,7168]{2,1,0:T(8,128)(2,1)}, u32[]{:S(2)}, u32[]{:S(2)}) collective-permute-start(bf16[4,24,7168]{2,1,0:T(8,128)(2,1)} %pad_maximum_fusion.1), channel_id=1, source_target_pairs={{0,8},{1,17},{2,10},{3,19},{4,12},{5,21},{6,14},{7,23},{8,0},{9,25... | collective-permute-start | bytes 4128776 | tf_op jit(solution)/shard_map/ppermute | solution.py:538
  104.7 3.0 collective-permute-start.20
  116.5 32.1 %collective-permute-start.22 = (bf16[8,24,7168]{2,1,0:T(8,128)(2,1)S(1)}, bf16[8,24,7168]{2,1,0:T(8,128)(2,1)S(1)}, u32[]{:S(2)}, u32[]{:S(2)}) collective-permute-start(bf16[8,24,7168]{2,1,0:T(8,128)(2,1)S(1)} %constant_dynamic-update-slice_fusion.7.refs_0_), channel_id=1, source_target_pairs={{0,1},{1,0},{2,3},{3,2},{4,5},{5,4},{6,7},{7,6},{8,9},{9,8},{10,11... | collective-permute-start | bytes 8257544 | tf_op jit(solution)/shard_map/ppermute | solution.py:538
  116.6 33.6 %collective-permute-start.21 = (bf16[8,24,7168]{2,1,0:T(8,128)(2,1)S(1)}, bf16[8,24,7168]{2,1,0:T(8,128)(2,1)}, u32[]{:S(2)}, u32[]{:S(2)}) collective-permute-start(bf16[8,24,7168]{2,1,0:T(8,128)(2,1)S(1)} %constant_dynamic-update-slice_fusion.7.refs_0_), channel_id=1, source_target_pairs={{0,16},{1,9},{2,18},{3,11},{4,20},{5,13},{6,22},{7,15},{8,24},{9,1... | collective-permute-start | bytes 8257544 | tf_op jit(solution)/shard_map/ppermute | solution.py:538
  150.3 5.4 %collective-permute-start.23 = (bf16[8,24,7168]{2,1,0:T(8,128)(2,1)}, bf16[8,24,7168]{2,1,0:T(8,128)(2,1)}, u32[]{:S(2)}, u32[]{:S(2)}) collective-permute-start(bf16[8,24,7168]{2,1,0:T(8,128)(2,1)} %collective-permute-done.21.refs_1_), channel_id=1, source_target_pairs={{0,1},{1,0},{2,3},{3,2},{4,5},{5,4},{6,7},{7,6},{8,9},{9,8},{10,11... | collective-permute-start | bytes 8257544 | tf_op jit(solution)/shard_map/ppermute | solution.py:538
  191.4 36.6 %copy-start.107 = (f32[1,1024]{1,0:T(1,128)S(1)}, f32[1,1024]{1,0:T(1,128)}, u32[]{:S(2)}) copy-start(f32[1,1024]{1,0:T(1,128)} %copy-done.106) | copy-start | bytes 12292
  191.6 38.0 %copy-start.75 = (f32[1024,128]{1,0:T(8,128)}, f32[1024,128]{1,0:T(8,128)S(1)}, u32[]{:S(2)}) copy-start(f32[1024,128]{1,0:T(8,128)S(1)} %copy.78) | copy-start | bytes 1572868
  240.3 16.1 %collective-permute-start.24 = (f32[768,1536]{1,0:T(8,128)}, f32[768,1536]{1,0:T(8,128)}, u32[]{:S(2)}, u32[]{:S(2)}) collective-permute-start(f32[768,1536]{1,0:T(8,128)} %fusion.11), channel_id=1, source_target_pairs={{0,1},{1,0},{2,3},{3,2},{4,5},{5,4},{6,7},{7,6},{8,9},{9,8},{10,11... | collective-permute-start | bytes 14155784 | tf_op jit(solution)/shard_map/ppermute | solution.py:538
  265.4 19.5 %collective-permute-start.26 = (f32[768,1536]{1,0:T(8,128)}, f32[768,1536]{1,0:T(8,128)}, u32[]{:S(2)}, u32[]{:S(2)}) collective-permute-start(f32[768,1536]{1,0:T(8,128)} %fusion.7), channel_id=1, source_target_pairs={{0,1},{1,0},{2,3},{3,2},{4,5},{5,4},{6,7},{7,6},{8,9},{9,8},{10,11... | collective-permute-start | bytes 14155784 | tf_op jit(solution)/shard_map/ppermute | solution.py:538
  265.9 19.1 %collective-permute-start.25 = (bf16[2,2,2,48,1536]{4,3,2,1,0:T(8,128)(2,1)S(1)}, bf16[2,2,2,48,1536]{4,3,2,1,0:T(8,128)(2,1)S(1)}, u32[]{:S(2)}, u32[]{:S(2)}) collective-permute-start(bf16[2,2,2,48,1536]{4,3,2,1,0:T(8,128)(2,1)S(1)} %reduce_first.4), channel_id=1, source_target_pairs={{0,8},{1,17},{2,10},{3,19},{4,12},{5,21},{6,14},{7,23},{8,0},{9,25... | collective-permute-start | bytes 3538952 | tf_op jit(solution)/shard_map/ppermute | solution.py:538
  284.9 50.4 %copy-start.27 = (bf16[2,2,2,48,1536]{4,3,2,1,0:T(8,128)(2,1)}, bf16[2,2,2,48,1536]{4,3,2,1,0:T(8,128)(2,1)S(1)}, u32[]{:S(2)}) copy-start(bf16[2,2,2,48,1536]{4,3,2,1,0:T(8,128)(2,1)S(1)} %collective-permute-done.25.refs_4_) | copy-start | bytes 3538948
  294.0 41.3 %slice-start = ((s8[4718592]{0:T(1024)(128)(4,1)}), s8[524288]{0:T(1024)(128)(4,1)S(1)}, s32[]{:S(2)}) async-start(s8[4718592]{0:T(1024)(128)(4,1)} %bitcast.178), calls=%async_computation | async-start | bytes 1048576
  296.0 39.2 %collective-permute-start.28 = (f32[768,384]{1,0:T(8,128)}, f32[768,384]{1,0:T(8,128)S(1)}, u32[]{:S(2)}, u32[]{:S(2)}) collective-permute-start(f32[768,384]{1,0:T(8,128)} %fusion.36), channel_id=1, source_target_pairs={{0,1},{1,0},{2,3},{3,2},{4,5},{5,4},{6,7},{7,6},{8,9},{9,8},{10,11... | collective-permute-start | bytes 3538952 | tf_op jit(solution)/shard_map/ppermute | solution.py:538
  296.0 39.3 %collective-permute-start.27 = (bf16[2,2,2,48,1536]{4,3,2,1,0:T(8,128)(2,1)}, bf16[2,2,2,48,1536]{4,3,2,1,0:T(8,128)(2,1)}, u32[]{:S(2)}, u32[]{:S(2)}) collective-permute-start(bf16[2,2,2,48,1536]{4,3,2,1,0:T(8,128)(2,1)} %reduce_first.5), channel_id=1, source_target_pairs={{0,8},{1,17},{2,10},{3,19},{4,12},{5,21},{6,14},{7,23},{8,0},{9,25... | collective-permute-start | bytes 3538952 | tf_op jit(solution)/shard_map/ppermute | solution.py:538
  301.8 33.5 %slice-start.1 = ((s8[4718592]{0:T(1024)(128)(4,1)}), s8[4194304]{0:T(1024)(128)(4,1)S(1)}, s32[]{:S(2)}) async-start(s8[4718592]{0:T(1024)(128)(4,1)} %bitcast.178), calls=%async_computation.1 | async-start | bytes 8388608
  344.0 23.6 %collective-permute-start.29 = (f32[768,1152]{1,0:T(8,128)}, f32[768,1152]{1,0:T(8,128)S(1)}, u32[]{:S(2)}, u32[]{:S(2)}) collective-permute-start(f32[768,1152]{1,0:T(8,128)} %fusion.15), channel_id=1, source_target_pairs={{0,1},{1,0},{2,3},{3,2},{4,5},{5,4},{6,7},{7,6},{8,9},{9,8},{10,11... | collective-permute-start | bytes 10616840 | tf_op jit(solution)/shard_map/ppermute | solution.py:538
  344.1 16.4 %collective-permute-start.30 = (bf16[2,2,48,3072]{3,2,1,0:T(8,128)(2,1)}, bf16[2,2,48,3072]{3,2,1,0:T(8,128)(2,1)S(1)}, u32[]{:S(2)}, u32[]{:S(2)}) collective-permute-start(bf16[2,2,48,3072]{3,2,1,0:T(8,128)(2,1)} %copy-done.40), channel_id=1, source_target_pairs={{0,16},{1,9},{2,18},{3,11},{4,20},{5,13},{6,22},{7,15},{8,24},{9,1... | collective-permute-start | bytes 3538952 | tf_op jit(solution)/shard_map/ppermute | solution.py:538
  369.9 16.5 %collective-permute-start.31 = (bf16[2,2,2,48,1536]{4,3,2,1,0:T(8,128)(2,1)}, bf16[2,2,2,48,1536]{4,3,2,1,0:T(8,128)(2,1)}, u32[]{:S(2)}, u32[]{:S(2)}) collective-permute-start(bf16[2,2,2,48,1536]{4,3,2,1,0:T(8,128)(2,1)} %reduce_first.6), channel_id=1, source_target_pairs={{0,8},{1,17},{2,10},{3,19},{4,12},{5,21},{6,14},{7,23},{8,0},{9,25... | collective-permute-start | bytes 3538952 | tf_op jit(solution)/shard_map/ppermute | solution.py:538
  369.9 15.8 %collective-permute-start.32 = (bf16[2,48,3072]{2,1,0:T(8,128)(2,1)}, bf16[2,48,3072]{2,1,0:T(8,128)(2,1)}, u32[]{:S(2)}, u32[]{:S(2)}) collective-permute-start(bf16[2,48,3072]{2,1,0:T(8,128)(2,1)} %get-tuple-element.269), channel_id=1, source_target_pairs={{0,2},{1,3},{2,0},{3,1},{4,6},{5,7},{6,4},{7,5},{8,10},{9,11},{10,... | collective-permute-start | bytes 1769480 | tf_op jit(solution)/shard_map/ppermute | solution.py:538
  386.4 13.9 %collective-permute-start.33 = (f32[5632,128]{1,0:T(8,128)}, f32[5632,128]{1,0:T(8,128)}, u32[]{:S(2)}, u32[]{:S(2)}) collective-permute-start(f32[5632,128]{1,0:T(8,128)} %get-tuple-element.270), channel_id=1, source_target_pairs={{0,1},{1,0},{2,3},{3,2},{4,5},{5,4},{6,7},{7,6},{8,9},{9,8},{10,11... | collective-permute-start | bytes 8650760 | tf_op jit(solution)/shard_map/ppermute | solution.py:538
  395.3 5.1 %collective-permute-start.34 = (f32[768,384]{1,0:T(8,128)}, f32[768,384]{1,0:T(8,128)S(1)}, u32[]{:S(2)}, u32[]{:S(2)}) collective-permute-start(f32[768,384]{1,0:T(8,128)} %fusion.32), channel_id=1, source_target_pairs={{0,1},{1,0},{2,3},{3,2},{4,5},{5,4},{6,7},{7,6},{8,9},{9,8},{10,11... | collective-permute-start | bytes 3538952 | tf_op jit(solution)/shard_map/ppermute | solution.py:538
  395.8 4.5 collective-permute-start.35
  395.9 12.3 %collective-permute-start.36 = (bf16[2,2,48,1536]{3,2,1,0:T(8,128)(2,1)}, bf16[2,2,48,1536]{3,2,1,0:T(8,128)(2,1)}, u32[]{:S(2)}, u32[]{:S(2)}) collective-permute-start(bf16[2,2,48,1536]{3,2,1,0:T(8,128)(2,1)} %reduce_second.4), channel_id=1, source_target_pairs={{0,16},{1,9},{2,18},{3,11},{4,20},{5,13},{6,22},{7,15},{8,24},{9,1... | collective-permute-start | bytes 1769480 | tf_op jit(solution)/shard_map/ppermute | solution.py:538
  408.2 18.7 %collective-permute-start.37 = (bf16[2,2,2,592,128]{4,3,2,1,0:T(8,128)(2,1)S(1)}, bf16[2,2,2,592,128]{4,3,2,1,0:T(8,128)(2,1)S(1)}, u32[]{:S(2)}, u32[]{:S(2)}) collective-permute-start(bf16[2,2,2,592,128]{4,3,2,1,0:T(8,128)(2,1)S(1)} %reduce_first.7), channel_id=1, source_target_pairs={{0,8},{1,17},{2,10},{3,19},{4,12},{5,21},{6,14},{7,23},{8,0},{9,25... | collective-permute-start | bytes 3637256 | tf_op jit(solution)/shard_map/ppermute | solution.py:538
  409.3 16.1 %collective-permute-start.39 = (bf16[1,48,3072]{2,1,0:T(8,128)(2,1)S(1)}, bf16[1,48,3072]{2,1,0:T(8,128)(2,1)S(1)}, u32[]{:S(2)}, u32[]{:S(2)}) collective-permute-start(bf16[1,48,3072]{2,1,0:T(8,128)(2,1)S(1)} %copy-done.58), channel_id=1, source_target_pairs={{0,4},{1,5},{2,6},{3,7},{4,0},{5,1},{6,2},{7,3},{8,12},{9,13},{10,... | collective-permute-start | bytes 884744 | tf_op jit(solution)/shard_map/ppermute | solution.py:538
  411.9 15.0 %collective-permute-start.38 = (bf16[2,48,1536]{2,1,0:T(8,128)(2,1)S(1)}, bf16[2,48,1536]{2,1,0:T(8,128)(2,1)S(1)}, u32[]{:S(2)}, u32[]{:S(2)}) collective-permute-start(bf16[2,48,1536]{2,1,0:T(8,128)(2,1)S(1)} %get-tuple-element.286), channel_id=1, source_target_pairs={{0,2},{1,3},{2,0},{3,1},{4,6},{5,7},{6,4},{7,5},{8,10},{9,11},{10,... | collective-permute-start | bytes 884744 | tf_op jit(solution)/shard_map/ppermute | solution.py:538
  431.7 10.4 %collective-permute-start.40 = (bf16[2,2,592,128]{3,2,1,0:T(8,128)(2,1)}, bf16[2,2,592,128]{3,2,1,0:T(8,128)(2,1)}, u32[]{:S(2)}, u32[]{:S(2)}) collective-permute-start(bf16[2,2,592,128]{3,2,1,0:T(8,128)(2,1)} %reduce_second.5), channel_id=1, source_target_pairs={{0,16},{1,9},{2,18},{3,11},{4,20},{5,13},{6,22},{7,15},{8,24},{9,1... | collective-permute-start | bytes 1818632 | tf_op jit(solution)/shard_map/ppermute | solution.py:538
  434.6 14.2 %collective-permute-start.50 = (f32[24,3072]{1,0:T(8,128)S(1)}, f32[24,3072]{1,0:T(8,128)S(1)}, u32[]{:S(2)}, u32[]{:S(2)}) collective-permute-start(f32[24,3072]{1,0:T(8,128)S(1)} %get-tuple-element.311), channel_id=1, source_target_pairs={{0,1},{1,0},{2,3},{3,2},{4,5},{5,4},{6,7},{7,6},{8,9},{9,8},{10,11... | collective-permute-start | bytes 884744 | tf_op jit(solution)/shard_map/ppermute | solution.py:538
  434.7 15.9 %collective-permute-start.42 = (f32[1,48,1536]{2,1,0:T(8,128)}, f32[1,48,1536]{2,1,0:T(8,128)S(1)}, u32[]{:S(2)}, u32[]{:S(2)}) collective-permute-start(f32[1,48,1536]{2,1,0:T(8,128)} %copy-done.59), channel_id=1, source_target_pairs={{0,4},{1,5},{2,6},{3,7},{4,0},{5,1},{6,2},{7,3},{8,12},{9,13},{10,... | collective-permute-start | bytes 884744 | tf_op jit(solution)/shard_map/ppermute | solution.py:538
  448.7 14.8 %collective-permute-start.41 = (f32[2,592,128]{2,1,0:T(8,128)S(1)}, f32[2,592,128]{2,1,0:T(8,128)S(1)}, u32[]{:S(2)}, u32[]{:S(2)}) collective-permute-start(f32[2,592,128]{2,1,0:T(8,128)S(1)} %get-tuple-element.294), channel_id=1, source_target_pairs={{0,2},{1,3},{2,0},{3,1},{4,6},{5,7},{6,4},{7,5},{8,10},{9,11},{10,... | collective-permute-start | bytes 1818632 | tf_op jit(solution)/shard_map/ppermute | solution.py:538
  463.8 1.6 collective-permute-start.49
  464.5 16.0 %collective-permute-start.43 = (f32[1,592,128]{2,1,0:T(8,128)S(1)}, f32[1,592,128]{2,1,0:T(8,128)S(1)}, u32[]{:S(2)}, u32[]{:S(2)}) collective-permute-start(f32[1,592,128]{2,1,0:T(8,128)S(1)} %get-tuple-element.298), channel_id=1, source_target_pairs={{0,4},{1,5},{2,6},{3,7},{4,0},{5,1},{6,2},{7,3},{8,12},{9,13},{10,... | collective-permute-start | bytes 909320 | tf_op jit(solution)/shard_map/ppermute | solution.py:538
  480.8 1.2 collective-permute-start.45
  482.0 4.5 collective-permute-start.48
  484.3 3.6 collective-permute-start.47
  484.5 3.6 collective-permute-start.46
  486.1 2.0 collective-permute-start.44
  490.2 5.6 %collective-permute-start.53 = (f32[8,128]{1,0:T(8,128)S(1)}, f32[8,128]{1,0:T(8,128)S(1)}, u32[]{:S(2)}, u32[]{:S(2)}) collective-permute-start(f32[8,128]{1,0:T(8,128)S(1)} %add_add_fusion.1), channel_id=1, source_target_pairs={{0,6},{1,7},{2,4},{3,5},{4,2},{5,3},{6,0},{7,1},{8,14},{9,15},{10,... | collective-permute-start | bytes 12296 | tf_op jit(solution)/shard_map/ppermute | solution.py:538
  492.1 4.5 collective-permute-start.52
  492.1 4.5 collective-permute-start.51
  (114 other events, 716.9 us)

commit v5 on v4

--- a/solution.py
+++ b/solution.py
@@ -1203,7 +1203,7 @@
     out_half = product_half(grad_one_low, attended_low)
     out_send, out_kept = out_half(1 - core), out_half(core)
     grad_attended = matmul(grad_one_low, out_low).astype(jnp.bfloat16)
-    lanes = lax.broadcasted_iota(jnp.int32, (model_width, 2 * TILE), 1)
+    lanes = lax.broadcasted_iota(jnp.int32, (model_width, TILE), 1)
     exact = jnp.where(lanes == 1, grad_gain_two[:, None], 0.0)
     exact = jnp.where(lanes == 2, grad_gain_top[:, None], exact)
     exact = jnp.where(lanes == 3, loss_local, exact)
@@ -1253,11 +1253,12 @@
     )
     feed_came, mix_came = place.swap_line(feed_send, bits[1]), place.swap_b(mix_send)
     time_half = product_half(grad_zero_low, feature_low)
-    pair_half = column_half(jnp.concatenate([matmul_tn(grad_zero_low, noisy_low), grad_down], 1))
-    exact_half = column_half(jnp.where(lanes == 0, grad_gain_one[:, None], exact))
+    grad_up = matmul_tn(grad_zero_low, noisy_low)
+    exact = jnp.where(lanes == 0, grad_gain_one[:, None], exact)
 
     def rest_half(side):
-        return time_half(side), jnp.concatenate([pair_half(side), exact_half(side)], 1)
+        first = side == 0
+        return time_half(side), jnp.where(first, grad_up, grad_down), jnp.where(first, exact, 0.0)
 
     rest_send = tie(*rest_half(1 - core))
     rest_came = [place.swap_core(piece) for piece in rest_send]

time: 510 us -> 503 us (0.986)
  waiting for transfers between devices: 92.1 us -> 101 us
  Pallas kernels: 163 us -> 156 us
  local copies, waits for them, and re-layouts: 49.4 us -> 43.1 us
    ppermute x54 -> x55, waiting for transfers between devices: 92.1 us -> 101 us  [swap(): return lax.ppermute(array, AXES, pairs)]
    pallas_call x16, Pallas kernels: 34 us -> 26.4 us  [call(): pl.pallas_call(kernel, out_shape=[entry for entry, unused, index in outpu...]
    unnamed x260 -> x230, local copies, waits for them, and re-layouts: 34.6 us -> 30.9 us
    ppermute x54 -> x55, starting transfers between devices: 39.9 us -> 40.9 us  [swap(): return lax.ppermute(array, AXES, pairs)]
  transfers between devices with their start and end apart: 54 -> 55, of which waited for: 23 -> 25; matrix products, arithmetic and copies ran while one was open for 22% -> 21% of each run, Pallas kernels for 20% -> 19%
where the time goes in v5:
time: 503 us; the launch traced here: 499 us
  Pallas kernels  156 us (31%)
  matrix products  102 us (20%)
  waiting for transfers between devices  101 us (20%)
  other arithmetic  50 us (10%)
  local copies, waits for them, and re-layouts  43.1 us (9%)
  starting transfers between devices  40.9 us (8%)
  between operations  5.95 us (1%)
    ppermute x55, waiting for transfers between devices, swap(): return lax.ppermute(array, AXES, pairs)  101 us
    ppermute x55, starting transfers between devices, swap(): return lax.ppermute(array, AXES, pairs)  40.9 us
    dot_general x7, matrix products, matrix_product_transposed(): lax.dot_general(left_op, right_op, (((1,), (1,)), ((), ())), preferred_el...  36.3 us
    dot_general x6, matrix products, matmul(): return jnp.dot(left_op, right_op, preferred_element_type=jnp.float32)  34.7 us
    pallas_call x1, Pallas kernels, head_pass(): pl.pallas_call(kernel, out_shape=(jax.ShapeDtypeStruct((words, width), jn...  33.9 us
    pallas_call x1, Pallas kernels, attention_backward(): pl.pallas_call(kernel, out_shape=jax.ShapeDtypeStruct(mixed.shape, jnp.bf...  33.6 us
    unnamed x230, local copies, waits for them, and re-layouts  30.9 us
    dot_general x12, matrix products, matmul_tn(): lax.dot_general(left_op, right_op, (((0,), (0,)), ((), ())), preferred_el...  30.7 us
  transfers between devices with their start and end apart: 55, of which 25 were waited for; matrix products, arithmetic and copies ran while one was open for 21% of the time, Pallas kernels for 19%

profile of v5, /device:TPU:0, one launch (start us, length us, event | category | flops | bytes accessed | tf_op | source)
XLA Modules:
  0.0 498.9 jit_solution(5961933570594733540)
XLA Ops:
  3.2 4.1 collective-permute-start.1
  19.1 2.0 collective-permute-start.3
  21.2 3.6 collective-permute-done.3
  24.9 2.9 collective-permute-start.4
  28.8 3.6 collective-permute-done.4
  34.7 7.3 %collective-permute-done.6 = bf16[4,24,1024]{2,1,0:T(8,128)(2,1)S(1)} collective-permute-done((bf16[4,24,1024]{2,1,0:T(8,128)(2,1)S(1)}, bf16[4,24,1024]{2,1,0:T(8,128)(2,1)S(1)}, u32[]{:S(2)}, u32[]{:S(2)}) %collective-permute-start.6) | collective-permute-done | bytes 196640 | tf_op jit(solution)/shard_map/ppermute | solution.py:538
  45.8 6.6 %fusion.22 = (bf16[1024,384]{1,0:T(8,128)(2,1)S(1)}, bf16[1024,384]{1,0:T(8,128)(2,1)S(1)}) fusion(f32[384]{0:T(512)S(1)} %multiply_exponential_fusion, f32[1024]{0:T(1024)S(1)} %convert_element_type.142), kind=kLoop, calls=%fused_computation.56 | loop fusion | flops 1179648 | bytes 1578496 | tf_op jit(solution)/shard_map/convert.2
  53.7 3.4 collective-permute-start.14
  60.3 3.4 assemble.4
  63.7 2.2 collective-permute-done.13
  67.0 5.5 %collective-permute-done.14 = bf16[1,24,7168]{2,1,0:T(8,128)(2,1)S(1)} collective-permute-done((bf16[1,24,7168]{2,1,0:T(8,128)(2,1)S(1)}, bf16[1,24,7168]{2,1,0:T(8,128)(2,1)S(1)}, u32[]{:S(2)}, u32[]{:S(2)}) %collective-permute-start.14) | collective-permute-done | bytes 344096 | tf_op jit(solution)/shard_map/ppermute | solution.py:538
  77.1 4.7 fusion.26
  83.7 5.5 %assemble.5 = bf16[4,4,2,352,128]{4,3,2,1,0:T(8,128)(2,1)S(1)} custom-call(s32[3]{0:T(128)S(1)} %pad_add_fusion.3.flags_ref, bf16[8,352,128]{2,1,0:T(8,128)(2,1)S(1)} %copy-done.29, bf16[8,352,128]{2,1,0:T(8,128)(2,1)S(1)} %copy-done.37, bf16[8,352,128]{2,1,0:T(8,128)(2,1)S(1)} %copy-done.35, bf16[8,352,128]{2,1,0:T(8,128)(2,1)S(1)} %copy-done.39), custom_call_target="tpu_custom_call" | custom-call | tf_op jit(solution)/shard_map/assemble/pallas_call | solution.py:598
  89.3 2.6 collective-permute-done.16
  91.8 2.4 pad_maximum_fusion.1
  95.7 3.2 gather_fusion
  100.4 2.7 fusion.81
  107.8 6.3 %assemble.6 = bf16[4,4,2,24,2304]{4,3,2,1,0:T(8,128)(2,1)S(1)} custom-call(s32[3]{0:T(128)S(1)} %pad_add_fusion.3.flags_ref, bf16[8,24,2304]{2,1,0:T(8,128)(2,1)} %pad_maximum_fusion.2.refs_0_, bf16[8,24,2304]{2,1,0:T(8,128)(2,1)} %collective-permute-done.18.refs_1_, bf16[8,24,2304]{2,1,0:T(8,128)(2,1)} %collective-permute-done.19.refs_2_, ...), custom_call_target="tpu_custom_call" | custom-call | tf_op jit(solution)/shard_map/assemble/pallas_call | solution.py:598
  114.1 2.5 constant_dynamic-update-slice_fusion.7.refs_0_
  117.3 4.2 convolution_convert_fusion.q_ref.k_ref.v_ref
  121.7 25.8 %attention_forward.1 = (bf16[1024,768]{1,0:T(8,128)(2,1)S(1)}, f32[16,1024]{1,0:T(8,128)S(1)}) custom-call(s32[2,8]{1,0:T(2,128)S(1)} %pad_add_fusion.windows_ref, bf16[1024,2304]{1,0:T(8,128)(2,1)S(1)} %convolution_convert_fusion.q_ref.k_ref.v_ref, bf16[1024,2304]{1,0:T(8,128)(2,1)S(1)} %convolution_convert_fusion.q_ref.k_ref.v_ref, ...), custom_call_target="tpu_custom_call" | custom-call | tf_op jit(solution)/shard_map/attention_forward/pallas_call | solution.py:200
  152.7 3.0 collective-permute-done.23.refs_3_
  159.3 5.8 %assemble.7 = bf16[4,4,2,24,7168]{4,3,2,1,0:T(8,128)(2,1)S(1)} custom-call(s32[3]{0:T(128)S(1)} %pad_add_fusion.3.flags_ref, bf16[8,24,7168]{2,1,0:T(8,128)(2,1)S(1)} %copy-done.25, bf16[8,24,7168]{2,1,0:T(8,128)(2,1)} %collective-permute-done.21.refs_1_, bf16[8,24,7168]{2,1,0:T(8,128)(2,1)S(1)} %copy-done.27, ...), custom_call_target="tpu_custom_call" | custom-call | tf_op jit(solution)/shard_map/assemble/pallas_call | solution.py:598
  168.9 12.9 %multiply_add_fusion = (f32[1024,3072]{1,0:T(8,128)}, bf16[1024,3072]{1,0:T(8,128)(2,1)S(1)}) fusion(bf16[1024,768]{0,1:T(8,128)(2,1)S(1)} %multiply_convert_fusion.3, bf16[768,7168]{1,0:T(8,128)(2,1)S(1)} %bitcast.203), kind=kOutput, calls=%fused_computation.2 | convolution fusion | flops 4882169856 | bytes 25165824 | tf_op jit(solution)/shard_map/dot_general | solution.py:29
  181.7 5.1 %fusion.83 = (f32[1024]{0:T(1024)S(1)}, f32[1024,768]{0,1:T(8,128)S(1)}) fusion(f32[1024,768]{0,1:T(8,128)S(1)} %get-tuple-element.409, bf16[1024,3072]{1,0:T(8,128)(2,1)S(1)} %get-tuple-element.231, bf16[768,7168]{1,0:T(8,128)(2,1)S(1)} %bitcast.204), kind=kOutput, calls=%fused_computation.254 | convolution fusion | flops 4833410048 | bytes 17305600 | tf_op jit(solution)/shard_map/dot_general | solution.py:39
  192.8 33.9 %head_pass.1 = (f32[11264,128]{1,0:T(8,128)}, f32[128,1024]{1,0:T(8,128)}, f32[1,1024]{1,0:T(1,128)}) custom-call(s32[1]{0:T(128)} %bitcast.34.small_ref, bf16[1024,128]{1,0:T(8,128)(2,1)} %get-tuple-element.371.pred_ref, bf16[11264,128]{1,0:T(8,128)(2,1)} %bitcast.191, f32[1,1024]{1,0:T(1,128)} %multiply_multiply_fusion.1.weight_ref), custom_call_target="tpu_custom_call" | custom-call | tf_op jit(solution)/shard_map/head_pass/pallas_call | solution.py:417
  229.7 3.3 multiply_reduce_fusion.4
  236.0 4.3 fusion.11
  240.6 4.5 fusion.13
  245.1 11.3 %multiply_convert_fusion = bf16[1024,3072]{1,0:T(8,128)(2,1)S(1)} fusion(f32[1024,3072]{1,0:T(8,128)} %get-tuple-element.236, bf16[1024,768]{0,1:T(8,128)(2,1)S(1)} %fusion.76, bf16[768,7168]{1,0:T(8,128)(2,1)} %bitcast.207), kind=kOutput, calls=%fused_computation.1 | convolution fusion | flops 4838129664 | bytes 25165824 | tf_op jit(solution)/shard_map/dot_general | solution.py:29
  256.4 4.6 reduce_first.4
  260.9 4.5 fusion.7
  266.1 9.8 %multiply_reduce_fusion.3 = (f32[768]{0:T(1024)S(1)}, f32[1024]{0:T(1024)S(1)}, f32[1024]{0:T(1024)S(1)}, f32[1024,768]{0,1:T(8,128)S(1)}) fusion(f32[1024,768]{0,1:T(8,128)} %copy-done.56, f32[1024]{0:T(1024)S(1)} %add_rsqrt_fusion.1, f32[1024]{0:T(1024)S(1)} %broadcast_multiply_fusion.8, f32[768]{0:T(1024)S(1)} %copy-done.94, ...), kind=kOutput, calls=%fused_computation.20 | convolution fusion | flops 4838126592 | bytes 17324032 | tf_op jit(solution)/shard_map/dot_general | solution.py:39
  277.6 2.6 fusion.9
  281.6 3.3 fusion.77
  284.9 3.1 reduce_first.5
  288.0 4.0 convolution_convert_fusion.1.do_ref
  292.0 2.0 fusion.34
  294.0 2.0 fusion.36
  296.1 2.1 collective-permute-start.27
  298.1 2.3 copy-done.1
  301.9 33.6 %attention_backward.1 = bf16[1024,2304]{1,0:T(8,128)(2,1)S(1)} custom-call(s32[2,8]{1,0:T(2,128)S(1)} %pad_add_fusion.windows_ref, bf16[1024,2304]{1,0:T(8,128)(2,1)S(1)} %copy-done.1, bf16[1024,2304]{1,0:T(8,128)(2,1)S(1)} %copy-done.1, bf16[1024,2304]{1,0:T(8,128)(2,1)S(1)} %copy-done.1, bf16[1024,768]{1,0:T(8,128)(2,1)S(1)} %copy-done.30, ...), custom_call_target="tpu_custom_call" | custom-call | tf_op jit(solution)/shard_map/attention_backward/pallas_call | solution.py:328
  335.6 4.5 reduce_second.3
  340.3 4.0 fusion.15
  344.3 9.3 %multiply_reduce_fusion.1 = (f32[768]{0:T(1024)}, f32[1024]{0:T(1024)S(1)}, f32[1024]{0:T(1024)S(1)}, f32[1024,768]{0,1:T(8,128)S(1)}) fusion(f32[1024,768]{0,1:T(8,128)} %copy-done.51, f32[1024]{0:T(1024)} %copy-done.81, f32[1024]{0:T(1024)S(1)} %broadcast_multiply_fusion.9, f32[768]{0:T(1024)} %copy-done.83, bf16[1024,2304]{1,0:T(8,128)(2,1)} %copy-done.18, ...), kind=kOutput, calls=%fused_computation.17 | convolution fusion | flops 3630167296 | bytes 14571520 | tf_op jit(solution)/shard_map/dot_general | solution.py:39
  353.7 2.2 fusion.17
  357.7 3.0 collective-permute-done.30.refs_6_
  360.7 3.1 reduce_third.3
  364.9 2.0 fusion.25.rows_ref
  368.5 9.1 %scatter_halves.1 = (f32[5632,128]{1,0:T(8,128)}, f32[5632,128]{1,0:T(8,128)}) custom-call(s32[1024]{0:T(1024)S(1)} %get-tuple-element.418.spots_ref, s32[1]{0:T(128)} %bitcast.flag_ref.flags_ref, f32[11264,128]{1,0:T(8,128)} %get-tuple-element.232.table_ref, f32[1024,128]{1,0:T(8,128)S(1)} %fusion.25.rows_ref), custom_call_target="tpu_custom_call" | custom-call | tf_op jit(solution)/shard_map/scatter_halves/pallas_call | solution.py:664
  377.6 5.9 %collective-permute-done.32 = bf16[2,48,3072]{2,1,0:T(8,128)(2,1)S(1)} collective-permute-done((bf16[2,48,3072]{2,1,0:T(8,128)(2,1)S(1)}, bf16[2,48,3072]{2,1,0:T(8,128)(2,1)S(1)}, u32[]{:S(2)}, u32[]{:S(2)}) %collective-permute-start.32) | collective-permute-done | bytes 589856 | tf_op jit(solution)/shard_map/ppermute | solution.py:538
  385.4 2.1 fusion.84
  388.8 2.0 copy-done.6
  400.6 2.4 reduce_first.7
  403.0 3.5 collective-permute-done.37.refs_5_
  409.9 13.4 %collective-permute-done.40.came_ref = bf16[1,48,3072]{2,1,0:T(8,128)(2,1)S(1)} collective-permute-done((bf16[1,48,3072]{2,1,0:T(8,128)(2,1)S(1)}, bf16[1,48,3072]{2,1,0:T(8,128)(2,1)S(1)}, u32[]{:S(2)}, u32[]{:S(2)}) %collective-permute-start.40) | collective-permute-done | bytes 294944 | tf_op jit(solution)/shard_map/ppermute | solution.py:538
  427.4 8.4 %collective-permute-done.41.refs_13_ = bf16[2,2,592,128]{3,2,1,0:T(8,128)(2,1)S(1)} collective-permute-done((bf16[2,2,592,128]{3,2,1,0:T(8,128)(2,1)S(1)}, bf16[2,2,592,128]{3,2,1,0:T(8,128)(2,1)S(1)}, u32[]{:S(2)}, u32[]{:S(2)}) %collective-permute-start.41) | collective-permute-done | bytes 606240 | tf_op jit(solution)/shard_map/ppermute | solution.py:538
  435.9 2.2 reduce_third.5
  438.9 5.0 %collective-permute-done.43.came_ref = f32[1,48,1536]{2,1,0:T(8,128)S(1)} collective-permute-done((f32[1,48,1536]{2,1,0:T(8,128)S(1)}, f32[1,48,1536]{2,1,0:T(8,128)S(1)}, u32[]{:S(2)}, u32[]{:S(2)}) %collective-permute-start.43) | collective-permute-done | bytes 294944 | tf_op jit(solution)/shard_map/ppermute | solution.py:538
  443.9 12.9 %collective-permute-done.42 = f32[2,592,128]{2,1,0:T(8,128)S(1)} collective-permute-done((f32[2,592,128]{2,1,0:T(8,128)S(1)}, f32[2,592,128]{2,1,0:T(8,128)S(1)}, u32[]{:S(2)}, u32[]{:S(2)}) %collective-permute-start.42) | collective-permute-done | bytes 606240 | tf_op jit(solution)/shard_map/ppermute | solution.py:538
  458.6 15.2 %collective-permute-done.44.came_ref = f32[1,592,128]{2,1,0:T(8,128)S(1)} collective-permute-done((f32[1,592,128]{2,1,0:T(8,128)S(1)}, f32[1,592,128]{2,1,0:T(8,128)S(1)}, u32[]{:S(2)}, u32[]{:S(2)}) %collective-permute-start.44) | collective-permute-done | bytes 303136 | tf_op jit(solution)/shard_map/ppermute | solution.py:538
  484.0 1.8 collective-permute-start.54
  485.8 2.6 collective-permute-start.52
  491.6 6.0 %adam_update.1 = (f32[352,128]{1,0:T(8,128)}, f32[352,128]{1,0:T(8,128)}, f32[352,128]{1,0:T(8,128)}, f32[24,128]{1,0:T(8,128)}, f32[24,128]{1,0:T(8,128)}, /*in...) custom-call(f32[1]{0:T(128)} %bitcast.67.factor_ref, ...), custom_call_target="tpu_custom_call" | custom-call | tf_op jit(solution)/shard_map/adam_update/pallas_call | solution.py:495
  (449 shorter events, 110.3 us)
Async XLA Ops:
  3.1 42.5 %copy-start.93 = (s32[1,1024]{1,0:T(1,128)S(1)}, s32[1,1024]{1,0:T(1,128)}, u32[]{:S(2)}) copy-start(s32[1,1024]{1,0:T(1,128)} %param.35) | copy-start | bytes 12292
  3.2 15.9 %collective-permute-start.1 = (bf16[1,24,1024]{2,1,0:T(8,128)(2,1)S(1)}, bf16[1,24,1024]{2,1,0:T(8,128)(2,1)S(1)}, u32[]{:S(2)}, u32[]{:S(2)}) collective-permute-start(bf16[1,24,1024]{2,1,0:T(8,128)(2,1)S(1)} %maximum_bitcast_fusion), channel_id=1, source_target_pairs={{0,4},{1,5},{2,6},{3,7},{4,0},{5,1},{6,2},{7,3},{8,12},{9,13},{10,... | collective-permute-start | bytes 147464 | tf_op jit(solution)/shard_map/ppermute | solution.py:538
  8.2 10.9 %collective-permute-start = (bf16[1,352,128]{2,1,0:T(8,128)(2,1)S(1)}, bf16[1,352,128]{2,1,0:T(8,128)(2,1)S(1)}, u32[]{:S(2)}, u32[]{:S(2)}) collective-permute-start(bf16[1,352,128]{2,1,0:T(8,128)(2,1)S(1)} %convert_bitcast_fusion.1), channel_id=1, source_target_pairs={{0,4},{1,5},{2,6},{3,7},{4,0},{5,1},{6,2},{7,3},{8,12},{9,13},{10,... | collective-permute-start | bytes 270344 | tf_op jit(solution)/shard_map/ppermute | solution.py:538
  11.1 41.3 %copy-start.91 = (f32[1,1024]{1,0:T(1,128)}, f32[1,1024]{1,0:T(1,128)S(1)}, u32[]{:S(2)}) copy-start(f32[1,1024]{1,0:T(1,128)S(1)} %convert_element_type.140) | copy-start | bytes 12292
  13.6 85.3 %copy-start.85 = (f32[1024]{0:T(1024)}, f32[1024]{0:T(1024)S(1)}, u32[]{:S(2)}) copy-start(f32[1024]{0:T(1024)S(1)} %get-tuple-element.398) | copy-start | bytes 12292
  19.1 5.7 %collective-permute-start.3 = (bf16[2,24,1024]{2,1,0:T(8,128)(2,1)S(1)}, bf16[2,24,1024]{2,1,0:T(8,128)(2,1)S(1)}, u32[]{:S(2)}, u32[]{:S(2)}) collective-permute-start(bf16[2,24,1024]{2,1,0:T(8,128)(2,1)S(1)} %pad_maximum_fusion.9), channel_id=1, source_target_pairs={{0,2},{1,3},{2,0},{3,1},{4,6},{5,7},{6,4},{7,5},{8,10},{9,11},{10,... | collective-permute-start | bytes 294920 | tf_op jit(solution)/shard_map/ppermute | solution.py:538
  21.1 7.7 %collective-permute-start.2 = (bf16[2,352,128]{2,1,0:T(8,128)(2,1)S(1)}, bf16[2,352,128]{2,1,0:T(8,128)(2,1)S(1)}, u32[]{:S(2)}, u32[]{:S(2)}) collective-permute-start(bf16[2,352,128]{2,1,0:T(8,128)(2,1)S(1)} %pad_maximum_fusion.8), channel_id=1, source_target_pairs={{0,2},{1,3},{2,0},{3,1},{4,6},{5,7},{6,4},{7,5},{8,10},{9,11},{10,... | collective-permute-start | bytes 540680 | tf_op jit(solution)/shard_map/ppermute | solution.py:538
  24.9 7.5 %collective-permute-start.4 = (bf16[1,24,2304]{2,1,0:T(8,128)(2,1)S(1)}, bf16[1,24,2304]{2,1,0:T(8,128)(2,1)S(1)}, u32[]{:S(2)}, u32[]{:S(2)}) collective-permute-start(bf16[1,24,2304]{2,1,0:T(8,128)(2,1)S(1)} %convert_bitcast_fusion), channel_id=1, source_target_pairs={{0,4},{1,5},{2,6},{3,7},{4,0},{5,1},{6,2},{7,3},{8,12},{9,13},{10,... | collective-permute-start | bytes 331784 | tf_op jit(solution)/shard_map/ppermute | solution.py:538
  32.4 9.6 %collective-permute-start.5 = (bf16[4,352,128]{2,1,0:T(8,128)(2,1)S(1)}, bf16[4,352,128]{2,1,0:T(8,128)(2,1)S(1)}, u32[]{:S(2)}, u32[]{:S(2)}) collective-permute-start(bf16[4,352,128]{2,1,0:T(8,128)(2,1)S(1)} %pad_maximum_fusion.5), channel_id=1, source_target_pairs={{0,8},{1,17},{2,10},{3,19},{4,12},{5,21},{6,14},{7,23},{8,0},{9,25... | collective-permute-start | bytes 1081352 | tf_op jit(solution)/shard_map/ppermute | solution.py:538
  34.3 7.8 %collective-permute-start.6 = (bf16[4,24,1024]{2,1,0:T(8,128)(2,1)S(1)}, bf16[4,24,1024]{2,1,0:T(8,128)(2,1)S(1)}, u32[]{:S(2)}, u32[]{:S(2)}) collective-permute-start(bf16[4,24,1024]{2,1,0:T(8,128)(2,1)S(1)} %pad_maximum_fusion.7), channel_id=1, source_target_pairs={{0,8},{1,17},{2,10},{3,19},{4,12},{5,21},{6,14},{7,23},{8,0},{9,25... | collective-permute-start | bytes 589832 | tf_op jit(solution)/shard_map/ppermute | solution.py:538
  42.0 15.1 %collective-permute-start.10 = (bf16[8,24,1024]{2,1,0:T(8,128)(2,1)S(1)}, bf16[8,24,1024]{2,1,0:T(8,128)(2,1)S(1)}, u32[]{:S(2)}, u32[]{:S(2)}) collective-permute-start(bf16[8,24,1024]{2,1,0:T(8,128)(2,1)S(1)} %constant_dynamic-update-slice_fusion.5.refs_0_), channel_id=1, source_target_pairs={{0,1},{1,0},{2,3},{3,2},{4,5},{5,4},{6,7},{7,6},{8,9},{9,8},{10,11... | collective-permute-start | bytes 1179656 | tf_op jit(solution)/shard_map/ppermute | solution.py:538
  42.1 15.0 %collective-permute-start.9 = (bf16[8,24,1024]{2,1,0:T(8,128)(2,1)S(1)}, bf16[8,24,1024]{2,1,0:T(8,128)(2,1)S(1)}, u32[]{:S(2)}, u32[]{:S(2)}) collective-permute-start(bf16[8,24,1024]{2,1,0:T(8,128)(2,1)S(1)} %constant_dynamic-update-slice_fusion.5.refs_0_), channel_id=1, source_target_pairs={{0,16},{1,9},{2,18},{3,11},{4,20},{5,13},{6,22},{7,15},{8,24},{9,1... | collective-permute-start | bytes 1179656 | tf_op jit(solution)/shard_map/ppermute | solution.py:538
  43.9 13.3 %collective-permute-start.8 = (bf16[8,352,128]{2,1,0:T(8,128)(2,1)S(1)}, bf16[8,352,128]{2,1,0:T(8,128)(2,1)S(1)}, u32[]{:S(2)}, u32[]{:S(2)}) collective-permute-start(bf16[8,352,128]{2,1,0:T(8,128)(2,1)S(1)} %constant_dynamic-update-slice_fusion.3.refs_0_), channel_id=1, source_target_pairs={{0,1},{1,0},{2,3},{3,2},{4,5},{5,4},{6,7},{7,6},{8,9},{9,8},{10,11... | collective-permute-start | bytes 2162696 | tf_op jit(solution)/shard_map/ppermute | solution.py:538
  44.1 13.6 %collective-permute-start.7 = (bf16[8,352,128]{2,1,0:T(8,128)(2,1)S(1)}, bf16[8,352,128]{2,1,0:T(8,128)(2,1)S(1)}, u32[]{:S(2)}, u32[]{:S(2)}) collective-permute-start(bf16[8,352,128]{2,1,0:T(8,128)(2,1)S(1)} %constant_dynamic-update-slice_fusion.3.refs_0_), channel_id=1, source_target_pairs={{0,16},{1,9},{2,18},{3,11},{4,20},{5,13},{6,22},{7,15},{8,24},{9,1... | collective-permute-start | bytes 2162696 | tf_op jit(solution)/shard_map/ppermute | solution.py:538
  45.6 8.1 %collective-permute-start.11 = (bf16[2,24,2304]{2,1,0:T(8,128)(2,1)S(1)}, bf16[2,24,2304]{2,1,0:T(8,128)(2,1)S(1)}, u32[]{:S(2)}, u32[]{:S(2)}) collective-permute-start(bf16[2,24,2304]{2,1,0:T(8,128)(2,1)S(1)} %pad_maximum_fusion.6), channel_id=1, source_target_pairs={{0,2},{1,3},{2,0},{3,1},{4,6},{5,7},{6,4},{7,5},{8,10},{9,11},{10,... | collective-permute-start | bytes 663560 | tf_op jit(solution)/shard_map/ppermute | solution.py:538
  53.7 18.8 %collective-permute-start.14 = (bf16[1,24,7168]{2,1,0:T(8,128)(2,1)S(1)}, bf16[1,24,7168]{2,1,0:T(8,128)(2,1)S(1)}, u32[]{:S(2)}, u32[]{:S(2)}) collective-permute-start(bf16[1,24,7168]{2,1,0:T(8,128)(2,1)S(1)} %bitcast.245), channel_id=1, source_target_pairs={{0,4},{1,5},{2,6},{3,7},{4,0},{5,1},{6,2},{7,3},{8,12},{9,13},{10,... | collective-permute-start | bytes 1032200 | tf_op jit(solution)/shard_map/ppermute | solution.py:538
  57.7 2.6 collective-permute-start.12
  57.7 8.3 %collective-permute-start.13 = (bf16[4,24,2304]{2,1,0:T(8,128)(2,1)S(1)}, bf16[4,24,2304]{2,1,0:T(8,128)(2,1)S(1)}, u32[]{:S(2)}, u32[]{:S(2)}) collective-permute-start(bf16[4,24,2304]{2,1,0:T(8,128)(2,1)S(1)} %pad_maximum_fusion.4), channel_id=1, source_target_pairs={{0,8},{1,17},{2,10},{3,19},{4,12},{5,21},{6,14},{7,23},{8,0},{9,25... | collective-permute-start | bytes 1327112 | tf_op jit(solution)/shard_map/ppermute | solution.py:538
  60.1 21.7 %collective-permute-start.15 = (bf16[8,352,128]{2,1,0:T(8,128)(2,1)S(1)}, bf16[8,352,128]{2,1,0:T(8,128)(2,1)S(1)}, u32[]{:S(2)}, u32[]{:S(2)}) collective-permute-start(bf16[8,352,128]{2,1,0:T(8,128)(2,1)S(1)} %collective-permute-done.7.refs_1_), channel_id=1, source_target_pairs={{0,1},{1,0},{2,3},{3,2},{4,5},{5,4},{6,7},{7,6},{8,9},{9,8},{10,11... | collective-permute-start | bytes 2162696 | tf_op jit(solution)/shard_map/ppermute | solution.py:538
  72.5 32.2 %collective-permute-start.19 = (bf16[8,24,2304]{2,1,0:T(8,128)(2,1)}, bf16[8,24,2304]{2,1,0:T(8,128)(2,1)}, u32[]{:S(2)}, u32[]{:S(2)}) collective-permute-start(bf16[8,24,2304]{2,1,0:T(8,128)(2,1)} %pad_maximum_fusion.2.refs_0_), channel_id=1, source_target_pairs={{0,1},{1,0},{2,3},{3,2},{4,5},{5,4},{6,7},{7,6},{8,9},{9,8},{10,11... | collective-permute-start | bytes 2654216 | tf_op jit(solution)/shard_map/ppermute | solution.py:538
  72.5 32.2 %collective-permute-start.18 = (bf16[8,24,2304]{2,1,0:T(8,128)(2,1)}, bf16[8,24,2304]{2,1,0:T(8,128)(2,1)}, u32[]{:S(2)}, u32[]{:S(2)}) collective-permute-start(bf16[8,24,2304]{2,1,0:T(8,128)(2,1)} %pad_maximum_fusion.2.refs_0_), channel_id=1, source_target_pairs={{0,16},{1,9},{2,18},{3,11},{4,20},{5,13},{6,22},{7,15},{8,24},{9,1... | collective-permute-start | bytes 2654216 | tf_op jit(solution)/shard_map/ppermute | solution.py:538
  74.1 17.7 %collective-permute-start.16 = (bf16[2,24,7168]{2,1,0:T(8,128)(2,1)}, bf16[2,24,7168]{2,1,0:T(8,128)(2,1)}, u32[]{:S(2)}, u32[]{:S(2)}) collective-permute-start(bf16[2,24,7168]{2,1,0:T(8,128)(2,1)} %pad_maximum_fusion.3), channel_id=1, source_target_pairs={{0,2},{1,3},{2,0},{3,1},{4,6},{5,7},{6,4},{7,5},{8,10},{9,11},{10,... | collective-permute-start | bytes 2064392 | tf_op jit(solution)/shard_map/ppermute | solution.py:538
  89.2 61.2 %copy-start.4 = (bf16[4,4,2,352,128]{4,3,2,1,0:T(8,128)(2,1)}, bf16[4,4,2,352,128]{4,3,2,1,0:T(8,128)(2,1)S(1)}, u32[]{:S(2)}) copy-start(bf16[4,4,2,352,128]{4,3,2,1,0:T(8,128)(2,1)S(1)} %assemble.5) | copy-start | bytes 8650756
  94.2 19.9 %collective-permute-start.17 = (bf16[4,24,7168]{2,1,0:T(8,128)(2,1)}, bf16[4,24,7168]{2,1,0:T(8,128)(2,1)}, u32[]{:S(2)}, u32[]{:S(2)}) collective-permute-start(bf16[4,24,7168]{2,1,0:T(8,128)(2,1)} %pad_maximum_fusion.1), channel_id=1, source_target_pairs={{0,8},{1,17},{2,10},{3,19},{4,12},{5,21},{6,14},{7,23},{8,0},{9,25... | collective-permute-start | bytes 4128776 | tf_op jit(solution)/shard_map/ppermute | solution.py:538
  104.7 3.1 collective-permute-start.20
  116.6 32.1 %collective-permute-start.22 = (bf16[8,24,7168]{2,1,0:T(8,128)(2,1)S(1)}, bf16[8,24,7168]{2,1,0:T(8,128)(2,1)S(1)}, u32[]{:S(2)}, u32[]{:S(2)}) collective-permute-start(bf16[8,24,7168]{2,1,0:T(8,128)(2,1)S(1)} %constant_dynamic-update-slice_fusion.7.refs_0_), channel_id=1, source_target_pairs={{0,1},{1,0},{2,3},{3,2},{4,5},{5,4},{6,7},{7,6},{8,9},{9,8},{10,11... | collective-permute-start | bytes 8257544 | tf_op jit(solution)/shard_map/ppermute | solution.py:538
  116.7 33.6 %collective-permute-start.21 = (bf16[8,24,7168]{2,1,0:T(8,128)(2,1)S(1)}, bf16[8,24,7168]{2,1,0:T(8,128)(2,1)}, u32[]{:S(2)}, u32[]{:S(2)}) collective-permute-start(bf16[8,24,7168]{2,1,0:T(8,128)(2,1)S(1)} %constant_dynamic-update-slice_fusion.7.refs_0_), channel_id=1, source_target_pairs={{0,16},{1,9},{2,18},{3,11},{4,20},{5,13},{6,22},{7,15},{8,24},{9,1... | collective-permute-start | bytes 8257544 | tf_op jit(solution)/shard_map/ppermute | solution.py:538
  150.3 5.4 %collective-permute-start.23 = (bf16[8,24,7168]{2,1,0:T(8,128)(2,1)}, bf16[8,24,7168]{2,1,0:T(8,128)(2,1)}, u32[]{:S(2)}, u32[]{:S(2)}) collective-permute-start(bf16[8,24,7168]{2,1,0:T(8,128)(2,1)} %collective-permute-done.21.refs_1_), channel_id=1, source_target_pairs={{0,1},{1,0},{2,3},{3,2},{4,5},{5,4},{6,7},{7,6},{8,9},{9,8},{10,11... | collective-permute-start | bytes 8257544 | tf_op jit(solution)/shard_map/ppermute | solution.py:538
  191.7 36.3 %copy-start.92 = (f32[1,1024]{1,0:T(1,128)S(1)}, f32[1,1024]{1,0:T(1,128)}, u32[]{:S(2)}) copy-start(f32[1,1024]{1,0:T(1,128)} %copy-done.91) | copy-start | bytes 12292
  191.9 37.8 %copy-start.62 = (f32[1024,128]{1,0:T(8,128)}, f32[1024,128]{1,0:T(8,128)S(1)}, u32[]{:S(2)}) copy-start(f32[1024,128]{1,0:T(8,128)S(1)} %copy.74) | copy-start | bytes 1572868
  240.3 16.1 %collective-permute-start.24 = (f32[768,1536]{1,0:T(8,128)}, f32[768,1536]{1,0:T(8,128)}, u32[]{:S(2)}, u32[]{:S(2)}) collective-permute-start(f32[768,1536]{1,0:T(8,128)} %fusion.11), channel_id=1, source_target_pairs={{0,1},{1,0},{2,3},{3,2},{4,5},{5,4},{6,7},{7,6},{8,9},{9,8},{10,11... | collective-permute-start | bytes 14155784 | tf_op jit(solution)/shard_map/ppermute | solution.py:538
  265.4 19.5 %collective-permute-start.26 = (f32[768,1536]{1,0:T(8,128)}, f32[768,1536]{1,0:T(8,128)}, u32[]{:S(2)}, u32[]{:S(2)}) collective-permute-start(f32[768,1536]{1,0:T(8,128)} %fusion.7), channel_id=1, source_target_pairs={{0,1},{1,0},{2,3},{3,2},{4,5},{5,4},{6,7},{7,6},{8,9},{9,8},{10,11... | collective-permute-start | bytes 14155784 | tf_op jit(solution)/shard_map/ppermute | solution.py:538
  265.9 19.0 %collective-permute-start.25 = (bf16[2,2,2,48,1536]{4,3,2,1,0:T(8,128)(2,1)S(1)}, bf16[2,2,2,48,1536]{4,3,2,1,0:T(8,128)(2,1)S(1)}, u32[]{:S(2)}, u32[]{:S(2)}) collective-permute-start(bf16[2,2,2,48,1536]{4,3,2,1,0:T(8,128)(2,1)S(1)} %reduce_first.4), channel_id=1, source_target_pairs={{0,8},{1,17},{2,10},{3,19},{4,12},{5,21},{6,14},{7,23},{8,0},{9,25... | collective-permute-start | bytes 3538952 | tf_op jit(solution)/shard_map/ppermute | solution.py:538
  284.9 50.6 %copy-start.16 = (bf16[2,2,2,48,1536]{4,3,2,1,0:T(8,128)(2,1)}, bf16[2,2,2,48,1536]{4,3,2,1,0:T(8,128)(2,1)S(1)}, u32[]{:S(2)}) copy-start(bf16[2,2,2,48,1536]{4,3,2,1,0:T(8,128)(2,1)S(1)} %collective-permute-done.25.refs_4_) | copy-start | bytes 3538948
  294.0 41.5 %slice-start = ((s8[4718592]{0:T(1024)(128)(4,1)}), s8[524288]{0:T(1024)(128)(4,1)S(1)}, s32[]{:S(2)}) async-start(s8[4718592]{0:T(1024)(128)(4,1)} %bitcast.180), calls=%async_computation | async-start | bytes 1048576
  296.0 39.5 %collective-permute-start.28 = (f32[768,384]{1,0:T(8,128)}, f32[768,384]{1,0:T(8,128)S(1)}, u32[]{:S(2)}, u32[]{:S(2)}) collective-permute-start(f32[768,384]{1,0:T(8,128)} %fusion.36), channel_id=1, source_target_pairs={{0,1},{1,0},{2,3},{3,2},{4,5},{5,4},{6,7},{7,6},{8,9},{9,8},{10,11... | collective-permute-start | bytes 3538952 | tf_op jit(solution)/shard_map/ppermute | solution.py:538
  296.1 39.5 %collective-permute-start.27 = (bf16[2,2,2,48,1536]{4,3,2,1,0:T(8,128)(2,1)}, bf16[2,2,2,48,1536]{4,3,2,1,0:T(8,128)(2,1)}, u32[]{:S(2)}, u32[]{:S(2)}) collective-permute-start(bf16[2,2,2,48,1536]{4,3,2,1,0:T(8,128)(2,1)} %reduce_first.5), channel_id=1, source_target_pairs={{0,8},{1,17},{2,10},{3,19},{4,12},{5,21},{6,14},{7,23},{8,0},{9,25... | collective-permute-start | bytes 3538952 | tf_op jit(solution)/shard_map/ppermute | solution.py:538
  301.9 33.7 %slice-start.1 = ((s8[4718592]{0:T(1024)(128)(4,1)}), s8[4194304]{0:T(1024)(128)(4,1)S(1)}, s32[]{:S(2)}) async-start(s8[4718592]{0:T(1024)(128)(4,1)} %bitcast.180), calls=%async_computation.1 | async-start | bytes 8388608
  344.2 22.7 %collective-permute-start.29 = (f32[768,1152]{1,0:T(8,128)}, f32[768,1152]{1,0:T(8,128)S(1)}, u32[]{:S(2)}, u32[]{:S(2)}) collective-permute-start(f32[768,1152]{1,0:T(8,128)} %fusion.15), channel_id=1, source_target_pairs={{0,1},{1,0},{2,3},{3,2},{4,5},{5,4},{6,7},{7,6},{8,9},{9,8},{10,11... | collective-permute-start | bytes 10616840 | tf_op jit(solution)/shard_map/ppermute | solution.py:538
  344.3 16.4 %collective-permute-start.30 = (bf16[2,2,48,3072]{3,2,1,0:T(8,128)(2,1)}, bf16[2,2,48,3072]{3,2,1,0:T(8,128)(2,1)S(1)}, u32[]{:S(2)}, u32[]{:S(2)}) collective-permute-start(bf16[2,2,48,3072]{3,2,1,0:T(8,128)(2,1)} %copy-done.31), channel_id=1, source_target_pairs={{0,16},{1,9},{2,18},{3,11},{4,20},{5,13},{6,22},{7,15},{8,24},{9,1... | collective-permute-start | bytes 3538952 | tf_op jit(solution)/shard_map/ppermute | solution.py:538
  367.9 16.4 %collective-permute-start.31 = (bf16[2,2,2,48,1536]{4,3,2,1,0:T(8,128)(2,1)S(1)}, bf16[2,2,2,48,1536]{4,3,2,1,0:T(8,128)(2,1)S(1)}, u32[]{:S(2)}, u32[]{:S(2)}) collective-permute-start(bf16[2,2,2,48,1536]{4,3,2,1,0:T(8,128)(2,1)S(1)} %reduce_first.6), channel_id=1, source_target_pairs={{0,8},{1,17},{2,10},{3,19},{4,12},{5,21},{6,14},{7,23},{8,0},{9,25... | collective-permute-start | bytes 3538952 | tf_op jit(solution)/shard_map/ppermute | solution.py:538
  368.0 15.5 %collective-permute-start.32 = (bf16[2,48,3072]{2,1,0:T(8,128)(2,1)S(1)}, bf16[2,48,3072]{2,1,0:T(8,128)(2,1)S(1)}, u32[]{:S(2)}, u32[]{:S(2)}) collective-permute-start(bf16[2,48,3072]{2,1,0:T(8,128)(2,1)S(1)} %get-tuple-element.271), channel_id=1, source_target_pairs={{0,2},{1,3},{2,0},{3,1},{4,6},{5,7},{6,4},{7,5},{8,10},{9,11},{10,... | collective-permute-start | bytes 1769480 | tf_op jit(solution)/shard_map/ppermute | solution.py:538
  385.3 15.3 %collective-permute-start.33 = (f32[5632,128]{1,0:T(8,128)}, f32[5632,128]{1,0:T(8,128)}, u32[]{:S(2)}, u32[]{:S(2)}) collective-permute-start(f32[5632,128]{1,0:T(8,128)} %get-tuple-element.272), channel_id=1, source_target_pairs={{0,1},{1,0},{2,3},{3,2},{4,5},{5,4},{6,7},{7,6},{8,9},{9,8},{10,11... | collective-permute-start | bytes 8650760 | tf_op jit(solution)/shard_map/ppermute | solution.py:538
  396.1 4.5 collective-permute-start.34
  396.6 9.9 %collective-permute-start.37 = (bf16[2,2,48,1536]{3,2,1,0:T(8,128)(2,1)S(1)}, bf16[2,2,48,1536]{3,2,1,0:T(8,128)(2,1)S(1)}, u32[]{:S(2)}, u32[]{:S(2)}) collective-permute-start(bf16[2,2,48,1536]{3,2,1,0:T(8,128)(2,1)S(1)} %reduce_second.4), channel_id=1, source_target_pairs={{0,16},{1,9},{2,18},{3,11},{4,20},{5,13},{6,22},{7,15},{8,24},{9,1... | collective-permute-start | bytes 1769480 | tf_op jit(solution)/shard_map/ppermute | solution.py:538
  398.3 1.7 collective-permute-start.35
  398.3 2.3 collective-permute-start.36
  406.5 17.1 %collective-permute-start.38 = (bf16[2,2,2,592,128]{4,3,2,1,0:T(8,128)(2,1)S(1)}, bf16[2,2,2,592,128]{4,3,2,1,0:T(8,128)(2,1)S(1)}, u32[]{:S(2)}, u32[]{:S(2)}) collective-permute-start(bf16[2,2,2,592,128]{4,3,2,1,0:T(8,128)(2,1)S(1)} %reduce_first.7), channel_id=1, source_target_pairs={{0,8},{1,17},{2,10},{3,19},{4,12},{5,21},{6,14},{7,23},{8,0},{9,25... | collective-permute-start | bytes 3637256 | tf_op jit(solution)/shard_map/ppermute | solution.py:538
  408.1 15.1 %collective-permute-start.40 = (bf16[1,48,3072]{2,1,0:T(8,128)(2,1)S(1)}, bf16[1,48,3072]{2,1,0:T(8,128)(2,1)S(1)}, u32[]{:S(2)}, u32[]{:S(2)}) collective-permute-start(bf16[1,48,3072]{2,1,0:T(8,128)(2,1)S(1)} %copy-done.47), channel_id=1, source_target_pairs={{0,4},{1,5},{2,6},{3,7},{4,0},{5,1},{6,2},{7,3},{8,12},{9,13},{10,... | collective-permute-start | bytes 884744 | tf_op jit(solution)/shard_map/ppermute | solution.py:538
  409.4 14.3 %collective-permute-start.39 = (bf16[2,48,1536]{2,1,0:T(8,128)(2,1)S(1)}, bf16[2,48,1536]{2,1,0:T(8,128)(2,1)S(1)}, u32[]{:S(2)}, u32[]{:S(2)}) collective-permute-start(bf16[2,48,1536]{2,1,0:T(8,128)(2,1)S(1)} %get-tuple-element.290), channel_id=1, source_target_pairs={{0,2},{1,3},{2,0},{3,1},{4,6},{5,7},{6,4},{7,5},{8,10},{9,11},{10,... | collective-permute-start | bytes 884744 | tf_op jit(solution)/shard_map/ppermute | solution.py:538
  425.7 10.1 %collective-permute-start.41 = (bf16[2,2,592,128]{3,2,1,0:T(8,128)(2,1)S(1)}, bf16[2,2,592,128]{3,2,1,0:T(8,128)(2,1)S(1)}, u32[]{:S(2)}, u32[]{:S(2)}) collective-permute-start(bf16[2,2,592,128]{3,2,1,0:T(8,128)(2,1)S(1)} %reduce_second.5), channel_id=1, source_target_pairs={{0,16},{1,9},{2,18},{3,11},{4,20},{5,13},{6,22},{7,15},{8,24},{9,1... | collective-permute-start | bytes 1818632 | tf_op jit(solution)/shard_map/ppermute | solution.py:538
  427.2 10.9 %collective-permute-start.51 = (f32[24,3072]{1,0:T(8,128)S(1)}, f32[24,3072]{1,0:T(8,128)S(1)}, u32[]{:S(2)}, u32[]{:S(2)}) collective-permute-start(f32[24,3072]{1,0:T(8,128)S(1)} %get-tuple-element.315), channel_id=1, source_target_pairs={{0,1},{1,0},{2,3},{3,2},{4,5},{5,4},{6,7},{7,6},{8,9},{9,8},{10,11... | collective-permute-start | bytes 884744 | tf_op jit(solution)/shard_map/ppermute | solution.py:538
  427.3 16.6 %collective-permute-start.43 = (f32[1,48,1536]{2,1,0:T(8,128)S(1)}, f32[1,48,1536]{2,1,0:T(8,128)S(1)}, u32[]{:S(2)}, u32[]{:S(2)}) collective-permute-start(f32[1,48,1536]{2,1,0:T(8,128)S(1)} %get-tuple-element.299), channel_id=1, source_target_pairs={{0,4},{1,5},{2,6},{3,7},{4,0},{5,1},{6,2},{7,3},{8,12},{9,13},{10,... | collective-permute-start | bytes 884744 | tf_op jit(solution)/shard_map/ppermute | solution.py:538
  438.1 18.7 %collective-permute-start.42 = (f32[2,592,128]{2,1,0:T(8,128)S(1)}, f32[2,592,128]{2,1,0:T(8,128)S(1)}, u32[]{:S(2)}, u32[]{:S(2)}) collective-permute-start(f32[2,592,128]{2,1,0:T(8,128)S(1)} %get-tuple-element.298), channel_id=1, source_target_pairs={{0,2},{1,3},{2,0},{3,1},{4,6},{5,7},{6,4},{7,5},{8,10},{9,11},{10,... | collective-permute-start | bytes 1818632 | tf_op jit(solution)/shard_map/ppermute | solution.py:538
  457.0 1.6 collective-permute-start.50
  457.8 16.0 %collective-permute-start.44 = (f32[1,592,128]{2,1,0:T(8,128)S(1)}, f32[1,592,128]{2,1,0:T(8,128)S(1)}, u32[]{:S(2)}, u32[]{:S(2)}) collective-permute-start(f32[1,592,128]{2,1,0:T(8,128)S(1)} %get-tuple-element.302), channel_id=1, source_target_pairs={{0,4},{1,5},{2,6},{3,7},{4,0},{5,1},{6,2},{7,3},{8,12},{9,13},{10,... | collective-permute-start | bytes 909320 | tf_op jit(solution)/shard_map/ppermute | solution.py:538
  474.0 1.2 collective-permute-start.46
  475.3 4.5 collective-permute-start.49
  476.7 3.6 collective-permute-start.48
  478.3 3.6 collective-permute-start.47
  479.4 2.5 collective-permute-start.45
  484.0 5.6 %collective-permute-start.54 = (f32[8,128]{1,0:T(8,128)S(1)}, f32[8,128]{1,0:T(8,128)S(1)}, u32[]{:S(2)}, u32[]{:S(2)}) collective-permute-start(f32[8,128]{1,0:T(8,128)S(1)} %add_add_fusion.1), channel_id=1, source_target_pairs={{0,6},{1,7},{2,4},{3,5},{4,2},{5,3},{6,0},{7,1},{8,14},{9,15},{10,... | collective-permute-start | bytes 12296 | tf_op jit(solution)/shard_map/ppermute | solution.py:538
  485.8 4.5 collective-permute-start.53
  485.8 4.5 collective-permute-start.52
  (100 other events, 587.6 us)
